TPU v7x, 128 devices: a whole 4x4x4 slice. The times are simulated.
128 devices in a mesh: gx: 4 (over x), gy: 8 (over z, core), gz: 4 (over y).
Axes of the slice: x: 4, y: 4, z: 4, core: 2. Of those that a mesh axis runs over, the one named last changes fastest.
Arguments:
- source_field: float32 [128, 256, 512], P('gx', 'gy', 'gz'), may hold values from -20 to 20
- beta_field: float32 [128, 256, 512], P('gx', 'gy', 'gz'), may hold values from 0.5 to 4
Outputs:
- solution: float32 [128, 256, 512], P('gx', 'gy', 'gz')
All inputs are finite; a program needn't handle non-finite values.
Results may differ from a plain program's by a relative error of at most 0.0001.
Values sent between devices are 32-bit elements; how exact they have to be, the bound alone decides.
No kernel may reach another device: no remote copies, remote signals or barrier semaphores. Data moves between devices by JAX's collectives and lax.ppermute only.
A program may use at most 128 MiB of HBM per device.

v0:
```python
import jax
import jax.numpy as jnp
from jax import lax
from jax.sharding import PartitionSpec as P

LEVELS = 4
SMOOTH = 4
BOTTOM = 12


LOW_EIG = 0.3
HIGH_EIG = 2.0
BOTTOM_LOW = 0.02


def with_halo(block, sides, width):
    for axis, dim in sides:
        count = lax.axis_size(axis)
        forward = [(i, i + 1) for i in range(count - 1)]
        backward = [(target, source) for source, target in forward]
        low = lax.ppermute(
            lax.slice_in_dim(block, block.shape[dim] - width, None, axis=dim), axis, forward
        )
        high = lax.ppermute(lax.slice_in_dim(block, 0, width, axis=dim), axis, backward)
        block = jnp.concatenate([low, block, high], axis=dim)
    return block


def cheb_plan(degree, lowest, highest):
    centre = 0.5 * (highest + lowest)
    radius = 0.5 * (highest - lowest)
    ratio_s = centre / radius
    rho_old = 1.0 / ratio_s
    recipe = [(0.0, 1.0 / centre)]
    for position in range(1, degree):
        rho_new = 1.0 / (2.0 * ratio_s - rho_old)
        recipe.append((rho_new * rho_old, 2.0 * rho_new / radius))
        rho_old = rho_new
    return recipe


def face_terms(padded):
    face_x = 0.5 * (padded[1:, 1:-1, 1:-1] + padded[:-1, 1:-1, 1:-1])
    face_y = 0.5 * (padded[1:-1, 1:, 1:-1] + padded[1:-1, :-1, 1:-1])
    face_z = 0.5 * (padded[1:-1, 1:-1, 1:] + padded[1:-1, 1:-1, :-1])
    diagonal = (
        face_x[:-1]
        + face_x[1:]
        + face_y[:, :-1]
        + face_y[:, 1:]
        + face_z[:, :, :-1]
        + face_z[:, :, 1:]
    )
    return (face_x, face_y, face_z, diagonal)


def apply_operator(padded, values, operator_terms, spacing):
    face_x, face_y, face_z, diagonal = operator_terms
    beside = face_x[:-1] * padded[:-2, 1:-1, 1:-1] + face_x[1:] * padded[2:, 1:-1, 1:-1]
    beside = (
        beside + face_y[:, :-1] * padded[1:-1, :-2, 1:-1] + face_y[:, 1:] * padded[1:-1, 2:, 1:-1]
    )
    beside = (
        beside
        + face_z[:, :, :-1] * padded[1:-1, 1:-1, :-2]
        + face_z[:, :, 1:] * padded[1:-1, 1:-1, 2:]
    )
    return spacing * (diagonal * values - beside)


def run_steps(values, source, operator_terms, inverse, spacing, recipe, from_zero, padder):
    update = None
    for position, (retain, factor) in enumerate(recipe):
        if position == 0 and from_zero:
            remain = source
        else:
            remain = source - apply_operator(padder(values), values, operator_terms, spacing)
        if position == 0:
            update = factor * (inverse * remain)
        else:
            update = retain * update + factor * (inverse * remain)
        values = values + update
    return values


def pad_faces(values):
    return with_halo(values, (("gx", 0), ("gy", 1), ("gz", 2)), 1)


def pad_bottom(values):
    return with_halo(values, (("gx", 0), ("gy", 1), ("gz", 2)), 1)


def restrict(values):
    first, second, third = values.shape
    return values.reshape(first // 2, 2, second // 2, 2, third // 2, 2).mean(axis=(1, 3, 5))


def prolong(values):
    first, second, third = values.shape
    spread_out = jnp.broadcast_to(
        values[:, None, :, None, :, None], (first, 2, second, 2, third, 2)
    )
    return spread_out.reshape(2 * first, 2 * second, 2 * third)


def per_device(source_field, beta_field):
    beta_levels = [beta_field]
    for level_idx in range(1, LEVELS):
        beta_levels.append(restrict(beta_levels[-1]))
    recipe = cheb_plan(SMOOTH, LOW_EIG, HIGH_EIG)
    bottom_recipe = cheb_plan(BOTTOM, BOTTOM_LOW, HIGH_EIG)
    sources = [source_field]
    iterates = []
    saved = []
    for level_idx in range(LEVELS - 1):
        spacing = 0.25**level_idx
        padded_beta = with_halo(beta_levels[level_idx], (("gx", 0), ("gy", 1), ("gz", 2)), 1)
        operator_terms = face_terms(padded_beta)
        inverse = 1.0 / (spacing * operator_terms[3])
        level_source = sources[level_idx]
        values = run_steps(
            jnp.zeros_like(level_source),
            level_source,
            operator_terms,
            inverse,
            spacing,
            recipe,
            True,
            pad_faces,
        )
        remain = level_source - apply_operator(pad_faces(values), values, operator_terms, spacing)
        iterates.append(values)
        sources.append(restrict(remain))
        saved.append((operator_terms, inverse, level_source))
    last_level = LEVELS - 1
    spacing = 0.25**last_level
    bottom_source = sources[last_level]
    bottom_beta = beta_levels[last_level]
    padded_beta = with_halo(bottom_beta, (("gx", 0), ("gy", 1), ("gz", 2)), 1)
    operator_terms = face_terms(padded_beta)
    inverse = 1.0 / (spacing * operator_terms[3])
    coarse = run_steps(
        jnp.zeros_like(bottom_source),
        bottom_source,
        operator_terms,
        inverse,
        spacing,
        bottom_recipe,
        True,
        pad_bottom,
    )
    for level_idx in reversed(range(LEVELS - 1)):
        spacing = 0.25**level_idx
        operator_terms, inverse, level_source = saved[level_idx]
        values = iterates[level_idx] + prolong(coarse)
        coarse = run_steps(
            values, level_source, operator_terms, inverse, spacing, recipe, False, pad_faces
        )
    return coarse


def solution(mesh):
    placed = (P("gx", "gy", "gz"), P("gx", "gy", "gz"))
    return jax.shard_map(
        per_device, mesh=mesh, in_specs=placed, out_specs=P("gx", "gy", "gz"), check_vma=False
    )
```

profile of v0, /device:TPU:7, one launch (start us, length us, event | category | flops | bytes accessed | tf_op | source)
XLA Modules:
  0.0 1159.0 jit_solution(10282231384721060054)
XLA Ops:
  7.2 5.0 collective-permute-start.3
  35.3 4.5 collective-permute-start.7
  67.9 4.7 collective-permute-start.13
  72.6 35.6 %reshape.32 = f32[16,2,16,2,64,2]{5,4,3,2,1,0:T(8,128)} reshape(f32[32,32,128]{2,1,0:T(8,128)} %param.3) | data formatting | bytes 1048576 | tf_op jit(solution)/shard_map/reshape | solution.py:96
  108.1 12.9 %reduce_sum.54 = f32[16,16,64]{2,1,0:T(8,128)} reduce(f32[16,2,16,2,64,2]{5,4,3,2,1,0:T(8,128)} %reshape.32, f32[]{:T(128)} %constant.46.clone.1), dimensions={1,3,5}, to_apply=%region_0.0 | reduce | flops 114688 | bytes 589828 | tf_op jit(solution)/shard_map/reduce_sum | solution.py:96
  147.4 5.3 fusion.132
  179.4 4.6 collective-permute-start.22
  200.0 4.7 collective-permute-start.29
  220.5 4.6 collective-permute-start.34
  230.3 4.9 fusion.71
  235.2 35.6 %reshape.33 = f32[16,2,16,2,64,2]{5,4,3,2,1,0:T(8,128)} reshape(f32[32,32,128]{2,1,0:T(8,128)} %fusion.71) | data formatting | bytes 1048576 | tf_op jit(solution)/shard_map/reshape | solution.py:96
  270.9 12.2 %reduce_sum.55 = f32[16,16,64]{2,1,0:T(8,128)S(1)} reduce(f32[16,2,16,2,64,2]{5,4,3,2,1,0:T(8,128)} %reshape.33, f32[]{:T(128)} %constant.46.clone.1), dimensions={1,3,5}, to_apply=%region_1.0 | reduce | flops 114688 | bytes 589828 | tf_op jit(solution)/shard_map/reduce_sum | solution.py:96
  313.0 4.5 collective-permute-start.43
  317.6 5.7 div.53
  414.0 6.6 reshape.34
  448.9 4.7 collective-permute-start.73
  471.9 4.8 collective-permute-start.84
  818.9 4.5 collective-permute-start.169
  864.7 4.5 collective-permute-start.181
  888.8 4.9 reshape.37
  895.9 4.5 collective-permute-start.187
  921.8 4.5 collective-permute-start.193
  948.0 4.5 collective-permute-start.199
  972.8 4.5 collective-permute-start.205
  996.2 11.4 broadcast_in_dim.8
  1007.6 24.5 %reshape.38 = f32[32,32,128]{2,1,0:T(8,128)} reshape(f32[16,2,16,2,64,2]{5,4,3,2,1,0:T(8,128)} %broadcast_in_dim.8) | data formatting | bytes 1048576 | tf_op jit(solution)/shard_map/reshape | solution.py:104
  1034.5 4.5 collective-permute-start.211
  1059.7 4.9 multiply_add_fusion
  1065.9 4.5 collective-permute-start.217
  1096.7 4.5 collective-permute-start.223
  1123.2 4.8 fusion.606
  1129.3 4.5 collective-permute-start.229
  (750 shorter events, 898.2 us)
Async XLA Ops:
  66.6 54.4 %collective-permute-start.12 = (f32[1,32,128]{2,1,0:T(8,128)S(1)}, f32[1,32,128]{2,1,0:T(8,128)S(1)}, u32[]{:S(2)}, u32[]{:S(2)}) collective-permute-start(f32[1,32,128]{2,1,0:T(8,128)S(1)} %get-tuple-element.111), channel_id=1, source_target_pairs={{0,32},{32,64},{64,96},{1,33},{33,65},{65,97},{2,34},{34,66},{66,9... | collective-permute-start | bytes 49160 | tf_op jit(solution)/shard_map/ppermute | solution.py:21
  67.9 53.1 %collective-permute-start.13 = (f32[1,32,128]{2,1,0:T(8,128)S(1)}, f32[1,32,128]{2,1,0:T(8,128)S(1)}, u32[]{:S(2)}, u32[]{:S(2)}) collective-permute-start(f32[1,32,128]{2,1,0:T(8,128)S(1)} %get-tuple-element.112), channel_id=1, source_target_pairs={{32,0},{64,32},{96,64},{33,1},{65,33},{97,65},{34,2},{66,34},{98,6... | collective-permute-start | bytes 49160 | tf_op jit(solution)/shard_map/ppermute | solution.py:24
  134.0 12.1 %collective-permute-start.17 = (f32[34,34,1]{1,2,0:T(1,128)S(1)}, f32[34,34,1]{1,2,0:T(1,128)S(1)}, u32[]{:S(2)}, u32[]{:S(2)}) collective-permute-start(f32[34,34,1]{1,2,0:T(1,128)S(1)} %copy.13), channel_id=1, source_target_pairs={{1,0},{2,1},{3,2},{5,4},{6,5},{7,6},{9,8},{10,9},{11,10},{13,12},{... | collective-permute-start | bytes 13880 | tf_op jit(solution)/shard_map/ppermute | solution.py:24
  139.3 18.9 %collective-permute-start.25 = (f32[1,16,64]{2,1,0:T(8,128)S(1)}, f32[1,16,64]{2,1,0:T(8,128)S(1)}, u32[]{:S(2)}, u32[]{:S(2)}) collective-permute-start(f32[1,16,64]{2,1,0:T(8,128)S(1)} %get-tuple-element.169), channel_id=1, source_target_pairs={{0,32},{32,64},{64,96},{1,33},{33,65},{65,97},{2,34},{34,66},{66,9... | collective-permute-start | bytes 12296 | tf_op jit(solution)/shard_map/ppermute | solution.py:21
  140.6 17.6 %collective-permute-start.24 = (f32[1,16,64]{2,1,0:T(8,128)S(1)}, f32[1,16,64]{2,1,0:T(8,128)S(1)}, u32[]{:S(2)}, u32[]{:S(2)}) collective-permute-start(f32[1,16,64]{2,1,0:T(8,128)S(1)} %get-tuple-element.170), channel_id=1, source_target_pairs={{32,0},{64,32},{96,64},{33,1},{65,33},{97,65},{34,2},{66,34},{98,6... | collective-permute-start | bytes 12296 | tf_op jit(solution)/shard_map/ppermute | solution.py:24
  152.7 11.2 collective-permute-start.18
  154.0 9.9 collective-permute-start.19
  158.9 25.1 %collective-permute-start.27 = (f32[18,1,64]{2,1,0:T(1,128)}, f32[18,1,64]{2,1,0:T(1,128)S(1)}, u32[]{:S(2)}, u32[]{:S(2)}) collective-permute-start(f32[18,1,64]{2,1,0:T(1,128)} %get-tuple-element.151), channel_id=1, source_target_pairs={{0,4},{4,8},{8,12},{12,16},{16,20},{20,24},{24,28},{1,5},{5,9},{9,... | collective-permute-start | bytes 13832 | tf_op jit(solution)/shard_map/ppermute | solution.py:21
  162.0 22.0 %collective-permute-start.26 = (f32[18,1,64]{2,1,0:T(1,128)}, f32[18,1,64]{2,1,0:T(1,128)S(1)}, u32[]{:S(2)}, u32[]{:S(2)}) collective-permute-start(f32[18,1,64]{2,1,0:T(1,128)} %get-tuple-element.152), channel_id=1, source_target_pairs={{4,0},{8,4},{12,8},{16,12},{20,16},{24,20},{28,24},{5,1},{9,5},{13... | collective-permute-start | bytes 13832 | tf_op jit(solution)/shard_map/ppermute | solution.py:24
  191.9 12.7 %collective-permute-start.30 = (f32[1,32,128]{2,1,0:T(8,128)S(1)}, f32[1,32,128]{2,1,0:T(8,128)S(1)}, u32[]{:S(2)}, u32[]{:S(2)}) collective-permute-start(f32[1,32,128]{2,1,0:T(8,128)S(1)} %get-tuple-element.107), channel_id=1, source_target_pairs={{0,32},{32,64},{64,96},{1,33},{33,65},{65,97},{2,34},{34,66},{66,9... | collective-permute-start | bytes 49160 | tf_op jit(solution)/shard_map/ppermute | solution.py:21
  193.2 11.4 collective-permute-start.31
  198.7 26.4 %collective-permute-start.28 = (f32[18,18,1]{2,1,0:T(8,128)S(1)}, f32[18,18,1]{2,1,0:T(8,128)}, u32[]{:S(2)}, u32[]{:S(2)}) collective-permute-start(f32[18,18,1]{2,1,0:T(8,128)S(1)} %get-tuple-element.133), channel_id=1, source_target_pairs={{1,0},{2,1},{3,2},{5,4},{6,5},{7,6},{9,8},{10,9},{11,10},{13,12},{... | collective-permute-start | bytes 3896 | tf_op jit(solution)/shard_map/ppermute | solution.py:24
  200.0 25.1 %collective-permute-start.29 = (f32[18,18,1]{2,1,0:T(8,128)S(1)}, f32[18,18,1]{2,1,0:T(8,128)}, u32[]{:S(2)}, u32[]{:S(2)}) collective-permute-start(f32[18,18,1]{2,1,0:T(8,128)S(1)} %get-tuple-element.134), channel_id=1, source_target_pairs={{0,1},{1,2},{2,3},{4,5},{5,6},{6,7},{8,9},{9,10},{10,11},{12,13},{... | collective-permute-start | bytes 3896 | tf_op jit(solution)/shard_map/ppermute | solution.py:21
  311.7 14.1 %collective-permute-start.42 = (f32[1,16,64]{2,1,0:T(8,128)S(1)}, f32[1,16,64]{2,1,0:T(8,128)S(1)}, u32[]{:S(2)}, u32[]{:S(2)}) collective-permute-start(f32[1,16,64]{2,1,0:T(8,128)S(1)} %get-tuple-element.165), channel_id=1, source_target_pairs={{0,32},{32,64},{64,96},{1,33},{33,65},{65,97},{2,34},{34,66},{66,9... | collective-permute-start | bytes 12296 | tf_op jit(solution)/shard_map/ppermute | solution.py:21
  313.0 12.9 %collective-permute-start.43 = (f32[1,16,64]{2,1,0:T(8,128)S(1)}, f32[1,16,64]{2,1,0:T(8,128)S(1)}, u32[]{:S(2)}, u32[]{:S(2)}) collective-permute-start(f32[1,16,64]{2,1,0:T(8,128)S(1)} %get-tuple-element.166), channel_id=1, source_target_pairs={{32,0},{64,32},{96,64},{33,1},{65,33},{97,65},{34,2},{66,34},{98,6... | collective-permute-start | bytes 12296 | tf_op jit(solution)/shard_map/ppermute | solution.py:24
  336.9 9.9 collective-permute-start.46
  341.2 14.6 %collective-permute-start.55 = (f32[1,8,32]{2,1,0:T(8,128)S(1)}, f32[1,8,32]{2,1,0:T(8,128)S(1)}, u32[]{:S(2)}, u32[]{:S(2)}) collective-permute-start(f32[1,8,32]{2,1,0:T(8,128)S(1)} %get-tuple-element.223), channel_id=1, source_target_pairs={{0,32},{32,64},{64,96},{1,33},{33,65},{65,97},{2,34},{34,66},{66,9... | collective-permute-start | bytes 3080 | tf_op jit(solution)/shard_map/ppermute | solution.py:21
  342.5 13.3 %collective-permute-start.54 = (f32[1,8,32]{2,1,0:T(8,128)S(1)}, f32[1,8,32]{2,1,0:T(8,128)S(1)}, u32[]{:S(2)}, u32[]{:S(2)}) collective-permute-start(f32[1,8,32]{2,1,0:T(8,128)S(1)} %get-tuple-element.224), channel_id=1, source_target_pairs={{32,0},{64,32},{96,64},{33,1},{65,33},{97,65},{34,2},{66,34},{98,6... | collective-permute-start | bytes 3080 | tf_op jit(solution)/shard_map/ppermute | solution.py:24
  350.2 11.1 collective-permute-start.48
  355.8 19.6 %collective-permute-start.57 = (f32[10,1,32]{2,1,0:T(1,128)S(1)}, f32[10,1,32]{2,1,0:T(1,128)S(1)}, u32[]{:S(2)}, u32[]{:S(2)}) collective-permute-start(f32[10,1,32]{2,1,0:T(1,128)S(1)} %get-tuple-element.205), channel_id=1, source_target_pairs={{0,4},{4,8},{8,12},{12,16},{16,20},{20,24},{24,28},{1,5},{5,9},{9,... | collective-permute-start | bytes 3848 | tf_op jit(solution)/shard_map/ppermute | solution.py:21
  359.3 16.1 %collective-permute-start.56 = (f32[10,1,32]{2,1,0:T(1,128)S(1)}, f32[10,1,32]{2,1,0:T(1,128)S(1)}, u32[]{:S(2)}, u32[]{:S(2)}) collective-permute-start(f32[10,1,32]{2,1,0:T(1,128)S(1)} %get-tuple-element.206), channel_id=1, source_target_pairs={{4,0},{8,4},{12,8},{16,12},{20,16},{24,20},{28,24},{5,1},{9,5},{13... | collective-permute-start | bytes 3848 | tf_op jit(solution)/shard_map/ppermute | solution.py:24
  382.3 11.0 collective-permute-start.60
  388.0 18.5 %collective-permute-start.58 = (f32[10,10,1]{2,1,0:T(8,128)S(1)}, f32[10,10,1]{2,1,0:T(8,128)S(1)}, u32[]{:S(2)}, u32[]{:S(2)}) collective-permute-start(f32[10,10,1]{2,1,0:T(8,128)S(1)} %get-tuple-element.187), channel_id=1, source_target_pairs={{1,0},{2,1},{3,2},{5,4},{6,5},{7,6},{9,8},{10,9},{11,10},{13,12},{... | collective-permute-start | bytes 1208 | tf_op jit(solution)/shard_map/ppermute | solution.py:24
  389.3 17.2 %collective-permute-start.59 = (f32[10,10,1]{2,1,0:T(8,128)S(1)}, f32[10,10,1]{2,1,0:T(8,128)S(1)}, u32[]{:S(2)}, u32[]{:S(2)}) collective-permute-start(f32[10,10,1]{2,1,0:T(8,128)S(1)} %get-tuple-element.188), channel_id=1, source_target_pairs={{0,1},{1,2},{2,3},{4,5},{5,6},{6,7},{8,9},{9,10},{10,11},{12,13},{... | collective-permute-start | bytes 1208 | tf_op jit(solution)/shard_map/ppermute | solution.py:21
  470.6 12.9 %collective-permute-start.85 = (f32[1,4,16]{2,1,0:T(4,128)S(1)}, f32[1,4,16]{2,1,0:T(4,128)S(1)}, u32[]{:S(2)}, u32[]{:S(2)}) collective-permute-start(f32[1,4,16]{2,1,0:T(4,128)S(1)} %get-tuple-element.295), channel_id=1, source_target_pairs={{0,32},{32,64},{64,96},{1,33},{33,65},{65,97},{2,34},{34,66},{66,9... | collective-permute-start | bytes 776 | tf_op jit(solution)/shard_map/ppermute | solution.py:21
  471.9 11.7 %collective-permute-start.84 = (f32[1,4,16]{2,1,0:T(4,128)S(1)}, f32[1,4,16]{2,1,0:T(4,128)S(1)}, u32[]{:S(2)}, u32[]{:S(2)}) collective-permute-start(f32[1,4,16]{2,1,0:T(4,128)S(1)} %get-tuple-element.296), channel_id=1, source_target_pairs={{32,0},{64,32},{96,64},{33,1},{65,33},{97,65},{34,2},{66,34},{98,6... | collective-permute-start | bytes 776 | tf_op jit(solution)/shard_map/ppermute | solution.py:24
  478.0 10.3 collective-permute-start.78
  483.6 19.1 %collective-permute-start.87 = (f32[6,1,16]{2,1,0:T(1,128)S(1)}, f32[6,1,16]{2,1,0:T(1,128)S(1)}, u32[]{:S(2)}, u32[]{:S(2)}) collective-permute-start(f32[6,1,16]{2,1,0:T(1,128)S(1)} %get-tuple-element.271), channel_id=1, source_target_pairs={{0,4},{4,8},{8,12},{12,16},{16,20},{20,24},{24,28},{1,5},{5,9},{9,... | collective-permute-start | bytes 1160 | tf_op jit(solution)/shard_map/ppermute | solution.py:21
  486.4 16.3 %collective-permute-start.86 = (f32[6,1,16]{2,1,0:T(1,128)S(1)}, f32[6,1,16]{2,1,0:T(1,128)S(1)}, u32[]{:S(2)}, u32[]{:S(2)}) collective-permute-start(f32[6,1,16]{2,1,0:T(1,128)S(1)} %get-tuple-element.272), channel_id=1, source_target_pairs={{4,0},{8,4},{12,8},{16,12},{20,16},{24,20},{28,24},{5,1},{9,5},{13... | collective-permute-start | bytes 1160 | tf_op jit(solution)/shard_map/ppermute | solution.py:24
  506.7 10.9 collective-permute-start.90
  512.3 17.6 %collective-permute-start.88 = (f32[6,6,1]{2,1,0:T(8,128)S(1)}, f32[6,6,1]{2,1,0:T(8,128)S(1)}, u32[]{:S(2)}, u32[]{:S(2)}) collective-permute-start(f32[6,6,1]{2,1,0:T(8,128)S(1)} %get-tuple-element.247), channel_id=1, source_target_pairs={{1,0},{2,1},{3,2},{5,4},{6,5},{7,6},{9,8},{10,9},{11,10},{13,12},{... | collective-permute-start | bytes 440 | tf_op jit(solution)/shard_map/ppermute | solution.py:24
  513.6 16.3 %collective-permute-start.89 = (f32[6,6,1]{2,1,0:T(8,128)S(1)}, f32[6,6,1]{2,1,0:T(8,128)S(1)}, u32[]{:S(2)}, u32[]{:S(2)}) collective-permute-start(f32[6,6,1]{2,1,0:T(8,128)S(1)} %get-tuple-element.248), channel_id=1, source_target_pairs={{0,1},{1,2},{2,3},{4,5},{5,6},{6,7},{8,9},{9,10},{10,11},{12,13},{... | collective-permute-start | bytes 440 | tf_op jit(solution)/shard_map/ppermute | solution.py:21
  (224 other events, 1731.8 us)
where the time goes:
time: 1180 us; the launch traced here: 1160 us
  starting transfers between devices  598 us (51%)
  waiting for transfers between devices  246 us (21%)
  local copies, waits for them, and re-layouts  205 us (17%)
  other arithmetic  106 us (9%)
    ppermute x117, starting transfers between devices, with_halo(): lax.ppermute(lax.slice_in_dim(block, 0, width, axis=dim), axis, backward)  300 us
    ppermute x117, starting transfers between devices, with_halo(): lax.ppermute(lax.slice_in_dim(block, block.shape[dim] - width, None, axis...  298 us
    ppermute x117, waiting for transfers between devices, with_halo(): lax.ppermute(lax.slice_in_dim(block, 0, width, axis=dim), axis, backward)  228 us
    reshape x4, local copies, waits for them, and re-layouts, restrict(): values.reshape(first // 2, 2, second // 2, 2, third // 2, 2)  79.6 us
    add x32, other arithmetic, run_steps(): values = values + update  44.3 us
    reduce_sum x6, other arithmetic, restrict(): values.reshape(first // 2, 2, second // 2, 2, third // 2, 2)  33.1 us
    reshape x3, local copies, waits for them, and re-layouts, prolong(): return spread_out.reshape(2 * first, 2 * second, 2 * third)  31.2 us
    slice x83, local copies, waits for them, and re-layouts, with_halo(): lax.slice_in_dim(block, block.shape[dim] - width, None, axis=dim)  26.6 us
  transfers between devices with their start and end apart: 234, of which 107 were waited for; matrix products, arithmetic and copies ran while one was open for 10% of the time, Pallas kernels for 0%

commit v1 on v0

v1 whole, which is shorter than its diff:
```python
import functools

import jax
import jax.numpy as jnp
from jax import lax
from jax.experimental import pallas as pl
from jax.experimental.pallas import tpu as pltpu
from jax.sharding import PartitionSpec as P

SMOOTH = 4
BOTTOM = 12
LOW_EIG = 0.3
HIGH_EIG = 2.0
BOTTOM_LOW = 0.02

AXES = ("gx", "gy", "gz")
F32 = jnp.float32
VMEM_LIMIT = 44 * 1024 * 1024


def cheb_plan(degree, lowest, highest):
    centre = 0.5 * (highest + lowest)
    radius = 0.5 * (highest - lowest)
    ratio_s = centre / radius
    rho_old = 1.0 / ratio_s
    recipe = [(0.0, 1.0 / centre)]
    for position in range(1, degree):
        rho_new = 1.0 / (2.0 * ratio_s - rho_old)
        recipe.append((rho_new * rho_old, 2.0 * rho_new / radius))
        rho_old = rho_new
    return recipe


RECIPE = cheb_plan(SMOOTH, LOW_EIG, HIGH_EIG)
BOTTOM_RECIPE = cheb_plan(BOTTOM, BOTTOM_LOW, HIGH_EIG)


def sds(*shape):
    return jax.ShapeDtypeStruct(shape, F32)


def vm(*shape):
    return pltpu.VMEM(shape, F32)


def call(body, outs, scratch=(), name=None):
    return pl.pallas_call(
        body,
        out_shape=outs,
        scratch_shapes=list(scratch),
        compiler_params=pltpu.CompilerParams(vmem_limit_bytes=VMEM_LIMIT),
        name=name,
    )


def lanes_of(rows):
    return lax.broadcasted_iota(jnp.int32, (rows, 128), 1)


def roll(value, shift):
    if isinstance(shift, int):
        shift = shift % 128
        if shift == 0:
            return value
    return pltpu.roll(value, shift, 1)


def flag(condition):
    return jnp.where(condition, 1.0, 0.0).astype(F32)


def dot(left, right):
    return lax.dot_general(
        left,
        right,
        (((1,), (0,)), ((), ())),
        precision=lax.Precision.HIGHEST,
        preferred_element_type=F32,
    )


def pick(match):
    row = lax.broadcasted_iota(jnp.int32, (128, 128), 0)
    col = lax.broadcasted_iota(jnp.int32, (128, 128), 1)
    return jnp.where(match(row, col), 1.0, 0.0).astype(F32)


def pack_x(src, beta, lo, hi):
    lo[0] = src[0:8]
    lo[1] = beta[0:8]
    hi[0] = src[24:32]
    hi[1] = beta[24:32]


def coarse_beta(beta, out, rows):
    total = []
    for x in range(8):
        s = beta[4 * x] + beta[4 * x + 1] + beta[4 * x + 2] + beta[4 * x + 3]
        rows[...] = s
        t = rows[pl.ds(0, 8, stride=4), :] + rows[pl.ds(1, 8, stride=4), :]
        t = t + rows[pl.ds(2, 8, stride=4), :] + rows[pl.ds(3, 8, stride=4), :]
        total.append(t * (1.0 / 64.0))
    for half in range(2):
        acc = jnp.zeros((8, 128), F32)
        for quarter in range(4):
            weight = pick(lambda r, c: (r // 4 + 32 * quarter) == c)
            acc = acc + dot(total[half * 4 + quarter], weight)
        out[half * 8 : half * 8 + 8, :] = acc


def pack_y(src, beta, from_lo, from_hi, lo, hi):
    index = lax.axis_index("gx")
    low = flag(index > 0)
    high = flag(index < lax.axis_size("gx") - 1)
    for field, ref in enumerate((src, beta)):
        for out, row in ((lo, 0), (hi, 24)):
            out[field, 0:8] = from_lo[field, :, row : row + 8, :] * low
            out[field, 8:40] = ref[:, row : row + 8, :]
            out[field, 40:48] = from_hi[field, :, row : row + 8, :] * high


def pack_z(src, beta, x_lo, x_hi, y_lo, y_hi, s_out, b_out, lo, hi):
    ix = lax.axis_index("gx")
    iy = lax.axis_index("gy")
    x_low = flag(ix > 0)
    x_high = flag(ix < lax.axis_size("gx") - 1)
    y_low = flag(iy > 0)
    y_high = flag(iy < lax.axis_size("gy") - 1)
    for field, (ref, out) in enumerate(((src, s_out), (beta, b_out))):
        out[0:8, 8:40, :] = x_lo[field] * x_low
        out[8:40, 8:40, :] = ref[...]
        out[40:48, 8:40, :] = x_hi[field] * x_high
        out[:, 0:8, :] = y_lo[field] * y_low
        out[:, 40:48, :] = y_hi[field] * y_high
    lane = lanes_of(48)

    def body(xx, carry):
        acc_lo = jnp.zeros((48, 128), F32)
        acc_hi = jnp.zeros((48, 128), F32)
        for g in range(8):
            s = s_out[g * 6 + xx]
            b = b_out[g * 6 + xx]
            first = (lane >= g * 16) & (lane < g * 16 + 8)
            second = (lane >= g * 16 + 8) & (lane < g * 16 + 16)
            acc_lo = jnp.where(first, roll(s, g * 16), acc_lo)
            acc_lo = jnp.where(second, roll(b, g * 16 + 8), acc_lo)
            acc_hi = jnp.where(first, roll(s, g * 16 + 8), acc_hi)
            acc_hi = jnp.where(second, roll(b, g * 16 + 16), acc_hi)
        lo[xx] = acc_lo
        hi[xx] = acc_hi
        return carry

    lax.fori_loop(0, 6, body, 0)


def strip_ghosts(values, ghost):
    lane = lanes_of(48)

    def body(xx, carry):
        acc = jnp.zeros((48, 128), F32)
        for g in range(8):
            acc = jnp.where(lane // 16 == g, roll(values[g * 6 + xx + 1, 8:56, :], g * 16 + 8), acc)
        ghost[xx] = acc
        return carry

    lax.fori_loop(0, 6, body, 0)


def strip_sides(strip, xx):
    after = strip[xx + 1, 8:56, :] if xx < 5 else roll(strip[0, 8:56, :], -16)
    before = strip[xx - 1, 8:56, :] if xx > 0 else roll(strip[5, 8:56, :], 16)
    return before, after


def strip_z(strip, ghost, xx, lane):
    here = strip[xx, 8:56, :]
    up = roll(jnp.where(lane % 16 == 8, ghost[xx], here), -1)
    down = roll(jnp.where(lane % 16 == 7, ghost[xx], here), 1)
    return down, up


def block_z(value, strip, x, lane):
    g = x // 6
    edge = roll(strip[x - g * 6, 8:56, :], 120 - g * 16)
    up = roll(jnp.where(lane == 0, edge, value), -1)
    down = roll(jnp.where(lane == 127, edge, value), 1)
    return down, up


def weights(here, sides):
    sums = [here + side for side in sides]
    total = sums[0] + sums[1] + sums[2] + sums[3] + sums[4] + sums[5]
    inverse = jnp.where(here > 0.0, 1.0 / total, 0.0)
    return [s * inverse for s in sums], inverse, total


def level0_setup(b_pad, bt_pad, ghost, src, src_t, g_main, g_strip, sp, sp_t, total):
    strip_ghosts(b_pad, ghost)
    lane = lanes_of(48)

    def body(x, carry):
        here = b_pad[x + 1, 8:56, :]
        down, up = block_z(here, bt_pad, x, lane)
        faces, inverse, tot = weights(
            here,
            (
                b_pad[x, 8:56, :],
                b_pad[x + 2, 8:56, :],
                b_pad[x + 1, 7:55, :],
                b_pad[x + 1, 9:57, :],
                down,
                up,
            ),
        )
        for i in range(6):
            g_main[i, x] = faces[i]
        sp[x] = src[x] * (2.0 * inverse)
        if total is not None:
            total[x] = tot
        return carry

    lax.fori_loop(0, 48, body, 0)
    for xx in range(6):
        before, after = strip_sides(bt_pad, xx)
        down, up = strip_z(bt_pad, ghost, xx, lane)
        faces, inverse, _ = weights(
            bt_pad[xx, 8:56, :],
            (before, after, bt_pad[xx, 7:55, :], bt_pad[xx, 9:57, :], down, up),
        )
        for i in range(6):
            g_strip[i, xx] = faces[i]
        sp_t[xx] = src_t[xx] * (2.0 * inverse)


def block_rest(v, t, g_main, sp, x, lane):
    here = v[x + 1, 8:56, :]
    down, up = block_z(here, t, x, lane)
    rest = sp[x] - here
    rest = rest + g_main[0, x] * v[x, 8:56, :] + g_main[1, x] * v[x + 2, 8:56, :]
    rest = rest + g_main[2, x] * v[x + 1, 7:55, :] + g_main[3, x] * v[x + 1, 9:57, :]
    rest = rest + g_main[4, x] * down + g_main[5, x] * up
    return here, rest


def level0_step(v, t, v_out, t_out, ghost, g_main, g_strip, sp, sp_t, u, u_t, low, high, retain, factor):
    strip_ghosts(v, ghost)
    lane = lanes_of(48)

    def body(x, carry):
        here, rest = block_rest(v, t, g_main, sp, x, lane)
        new = factor * rest
        if retain is not None:
            new = retain * u[x] + new
        u[x] = new
        v_out[x + 1, 8:56, :] = here + new
        return carry

    lax.fori_loop(low, high, body, 0)
    for xx in range(6):
        here = t[xx, 8:56, :]
        before, after = strip_sides(t, xx)
        down, up = strip_z(t, ghost, xx, lane)
        rest = sp_t[xx] - here
        rest = rest + g_strip[0, xx] * before + g_strip[1, xx] * after
        rest = rest + g_strip[2, xx] * t[xx, 7:55, :] + g_strip[3, xx] * t[xx, 9:57, :]
        rest = rest + g_strip[4, xx] * down + g_strip[5, xx] * up
        new = factor * rest
        if retain is not None:
            new = retain * u_t[xx] + new
        u_t[xx] = new
        t_out[xx, 8:56, :] = here + new


def clear_edges(ref, planes, rows):
    width = ref.shape[1]
    ref[0] = jnp.zeros((width, 128), F32)
    ref[planes + 1] = jnp.zeros((width, 128), F32)

    def body(x, carry):
        ref[x, 0:8, :] = jnp.zeros((8, 128), F32)
        ref[x, 8 + rows : width, :] = jnp.zeros((width - 8 - rows, 128), F32)
        return carry

    lax.fori_loop(0, planes + 2, body, 0)


def clear_strip(ref):
    for xx in range(6):
        ref[xx, 0:8, :] = jnp.zeros((8, 128), F32)
        ref[xx, 56:64, :] = jnp.zeros((8, 128), F32)


def unpack_strip(z_lo, z_hi, src_t, bt_pad):
    iz = lax.axis_index("gz")
    low = flag(iz > 0)
    high = flag(iz < lax.axis_size("gz") - 1)
    lower = lanes_of(48) % 16 < 8
    for xx in range(6):
        before = z_lo[xx] * low
        after = z_hi[xx] * high
        src_t[xx] = jnp.where(lower, before, roll(after, 8))
        bt_pad[xx, 8:56, :] = jnp.where(lower, roll(before, -8), after)


LEVEL0_SCRATCH = [
    vm(50, 64, 128),
    vm(6, 64, 128),
    vm(50, 64, 128),
    vm(50, 64, 128),
    vm(6, 64, 128),
    vm(6, 64, 128),
    vm(6, 48, 128),
    vm(6, 48, 48, 128),
    vm(6, 6, 48, 128),
    vm(48, 48, 128),
    vm(6, 48, 128),
    vm(48, 48, 128),
    vm(6, 48, 128),
    vm(6, 48, 128),
]


def level0_down(
    src, beta, z_lo, z_hi, iter_out, iter_t_out, c_out, c_lo, c_hi,
    b_pad, bt_pad, va, vb, ta, tb, ghost, g_main, g_strip, sp, sp_t, u, u_t, src_t, total, rows,
):
    for ref in (b_pad, va, vb):
        clear_edges(ref, 48, 48)
    for ref in (bt_pad, ta, tb):
        clear_strip(ref)
    b_pad[1:49, 8:56, :] = beta[...]
    unpack_strip(z_lo, z_hi, src_t, bt_pad)
    level0_setup(b_pad, bt_pad, ghost, src, src_t, g_main, g_strip, sp, sp_t, total)

    first = RECIPE[0][1]

    def start(x, carry):
        u[x] = first * sp[x]
        va[x + 1, 8:56, :] = u[x]
        return carry

    lax.fori_loop(0, 48, start, 0)
    for xx in range(6):
        u_t[xx] = first * sp_t[xx]
        ta[xx, 8:56, :] = u_t[xx]
    bufs = [(va, ta), (vb, tb)]
    for k in range(1, SMOOTH):
        (v, t), (w, s) = bufs
        retain, factor = RECIPE[k]
        level0_step(v, t, w, s, ghost, g_main, g_strip, sp, sp_t, u, u_t, k, 48 - k, retain, factor)
        for x in [*range(k), *range(48 - k, 48)]:
            w[x + 1, 8:56, :] = v[x + 1, 8:56, :]
        bufs = [(w, s), (v, t)]
    v, t = bufs[0]
    iter_out[...] = v[1:49, 8:56, :]
    for xx in range(6):
        iter_t_out[xx] = t[xx, 8:56, :]

    lane = lanes_of(48)
    to_low = pick(lambda r, c: r // 2 == c)
    to_high = pick(lambda r, c: r // 2 + 64 == c)

    def restrict(x2, carry):
        parts = []
        for half in range(2):
            x = 8 + 2 * x2 + half
            _, rest = block_rest(v, t, g_main, sp, x, lane)
            parts.append(rest * total[x])
        rows[0] = (parts[0] + parts[1]) * (0.5 / 8.0)
        rows[1] = (b_pad[9 + 2 * x2, 8:56, :] + b_pad[10 + 2 * x2, 8:56, :]) * (1.0 / 8.0)
        res = rows[0, pl.ds(8, 16, stride=2), :] + rows[0, pl.ds(9, 16, stride=2), :]
        bet = rows[1, pl.ds(8, 16, stride=2), :] + rows[1, pl.ds(9, 16, stride=2), :]
        c_out[x2] = dot(res, to_low) + dot(bet, to_high)
        return carry

    lax.fori_loop(0, 16, restrict, 0)
    c_lo[...] = c_out[0:10]
    c_hi[...] = c_out[6:16]


def pack1_y(c, from_lo, from_hi, lo, hi):
    index = lax.axis_index("gx")
    low = flag(index > 0)
    high = flag(index < lax.axis_size("gx") - 1)
    for x in range(36):
        if x < 10:
            plane = from_lo[x] * low
        elif x < 26:
            plane = c[x - 10]
        else:
            plane = from_hi[x - 26] * high
        lo[x * 10 : x * 10 + 10, :] = plane[0:10]
        hi[x * 10 : x * 10 + 10, :] = plane[6:16]


def pack1_z(c, x_lo, x_hi, y_lo, y_hi, ext, lo, hi):
    ix = lax.axis_index("gx")
    iy = lax.axis_index("gy")
    x_low = flag(ix > 0)
    x_high = flag(ix < lax.axis_size("gx") - 1)
    y_low = flag(iy > 0)
    y_high = flag(iy < lax.axis_size("gy") - 1)
    ext[0:10, 10:26, :] = x_lo[...] * x_low
    ext[10:26, 10:26, :] = c[...]
    ext[26:36, 10:26, :] = x_hi[...] * x_high
    for x in range(36):
        ext[x, 0:10, :] = y_lo[x * 10 : x * 10 + 10, :] * y_low
        ext[x, 26:36, :] = y_hi[x * 10 : x * 10 + 10, :] * y_high
        ext[x, 36:40, :] = jnp.zeros((4, 128), F32)
    lane = lanes_of(40)

    def body(xx, carry):
        acc_lo = jnp.zeros((40, 128), F32)
        acc_hi = jnp.zeros((40, 128), F32)
        for g in range(6):
            e = ext[g * 6 + xx]
            first = (lane >= g * 20) & (lane < g * 20 + 10)
            second = (lane >= g * 20 + 10) & (lane < g * 20 + 20)
            middle = roll(e, g * 20 - 54)
            acc_lo = jnp.where(first, roll(e, g * 20), acc_lo)
            acc_lo = jnp.where(second, middle, acc_lo)
            acc_hi = jnp.where(first, middle, acc_hi)
            acc_hi = jnp.where(second, roll(e, g * 20 + 20), acc_hi)
        lo[xx] = acc_lo
        hi[xx] = acc_hi
        return carry

    lax.fori_loop(0, 6, body, 0)


def ring_weights(b_pad, src, g, sp, total, planes, rows, scale, edges=None):
    lane = lanes_of(rows)

    def body(x, carry):
        here = b_pad[x + 1, 8 : 8 + rows, :]
        down = roll(here, 1)
        up = roll(here, -1)
        if edges is not None:
            down = jnp.where(lane == 0, 0.0, down)
            up = jnp.where(lane == 127, 0.0, up)
        faces, inverse, tot = weights(
            here,
            (
                b_pad[x, 8 : 8 + rows, :],
                b_pad[x + 2, 8 : 8 + rows, :],
                b_pad[x + 1, 7 : 7 + rows, :],
                b_pad[x + 1, 9 : 9 + rows, :],
                down,
                up,
            ),
        )
        if edges is not None:
            faces[4] = jnp.where(lane == 0, 0.0, faces[4])
            faces[5] = jnp.where(lane == 127, 0.0, faces[5])
        for i in range(6):
            g[i, x] = faces[i]
        sp[x] = src[x] * (scale * 2.0 * inverse)
        if total is not None:
            total[x] = tot
        return carry

    lax.fori_loop(0, planes, body, 0)


def ring_rest(v, g, sp, x, rows):
    here = v[x + 1, 8 : 8 + rows, :]
    rest = sp[x] - here
    rest = rest + g[0, x] * v[x, 8 : 8 + rows, :] + g[1, x] * v[x + 2, 8 : 8 + rows, :]
    rest = rest + g[2, x] * v[x + 1, 7 : 7 + rows, :] + g[3, x] * v[x + 1, 9 : 9 + rows, :]
    rest = rest + g[4, x] * roll(here, 1) + g[5, x] * roll(here, -1)
    return here, rest


def ring_step(v, v_out, g, sp, u, planes, rows, retain, factor):
    def body(x, carry):
        here, rest = ring_rest(v, g, sp, x, rows)
        new = factor * rest
        if retain is not None:
            new = retain * u[x] + new
        u[x] = new
        v_out[x + 1, 8 : 8 + rows, :] = here + new
        return carry

    lax.fori_loop(0, planes, body, 0)


def ring_zero_start(v, u, sp, planes, rows, factor):
    def body(x, carry):
        u[x] = factor * sp[x]
        v[x + 1, 8 : 8 + rows, :] = u[x]
        return carry

    lax.fori_loop(0, planes, body, 0)


def ring_cheb(va, vb, g, sp, u, planes, rows, recipe, from_zero):
    begin = 0
    if from_zero:
        ring_zero_start(va, u, sp, planes, rows, recipe[0][1])
        begin = 1
    for k in range(begin, len(recipe)):
        retain, factor = recipe[k]
        ring_step(va, vb, g, sp, u, planes, rows, None if k == 0 else retain, factor)
        va, vb = vb, va
    return va


LEVEL1_SCRATCH = [
    vm(38, 56, 128),
    vm(38, 56, 128),
    vm(38, 56, 128),
    vm(6, 36, 40, 128),
    vm(36, 40, 128),
    vm(36, 40, 128),
]


def level1_down(
    ext, z_lo, z_hi, src_out, beta_out, iter_out, chunk,
    b_pad, va, vb, g, sp, u, total, rows,
):
    iz = lax.axis_index("gz")
    low = flag(iz > 0)
    high = flag(iz < lax.axis_size("gz") - 1)
    lane = lanes_of(40)
    inner = lane < 64
    above = (lane >= 64) & (lane < 74)
    below = lane >= 118
    for ref in (b_pad, va, vb):
        clear_edges(ref, 36, 40)

    def unpack(xx, carry):
        before = z_lo[xx] * low
        after = z_hi[xx] * high
        for k in range(6):
            x = k * 6 + xx
            e = ext[x]
            s = jnp.where(inner, e, 0.0)
            s = jnp.where(above, roll(after, 64 - k * 20), s)
            s = jnp.where(below, roll(before, 118 - k * 20), s)
            b = jnp.where(inner, roll(e, 64), 0.0)
            b = jnp.where(above, roll(after, 54 - k * 20), b)
            b = jnp.where(below, roll(before, 108 - k * 20), b)
            src_out[x] = s
            beta_out[x] = b
            b_pad[x + 1, 8:48, :] = b
        return carry

    lax.fori_loop(0, 6, unpack, 0)
    ring_weights(b_pad, src_out, g, sp, total, 36, 40, 4.0)
    v = ring_cheb(va, vb, g, sp, u, 36, 40, RECIPE, True)
    iter_out[...] = v[1:37, 8:48, :]
    summed = []
    for x2 in range(8):
        parts = []
        for half in range(2):
            x = 10 + 2 * x2 + half
            _, rest = ring_rest(v, g, sp, x, 40)
            parts.append(rest * total[x])
        rows[...] = (parts[0] + parts[1]) * (0.25 * 0.5 / 8.0)
        summed.append(rows[pl.ds(10, 8, stride=2), :] + rows[pl.ds(11, 8, stride=2), :])
    packed = []
    for half in range(2):
        acc = jnp.zeros((8, 128), F32)
        for quarter in range(4):
            weight = pick(lambda r, c: (r < 64) & ((r // 2 + 32 * quarter) == c))
            acc = acc + dot(summed[half * 4 + quarter], weight)
        packed.append(acc)
    both = jnp.concatenate(packed, axis=0)

    def spread(d, carry):
        chunk[d] = both
        return carry

    lax.fori_loop(0, 128, spread, 0)


def whole_grid(parts, out, x_pad):
    lane = lanes_of(8)

    def body(i, carry):
        gx = i // 8
        gy = i - gx * 8
        for half in range(2):
            blocks = [parts[i * 4 + gz, half * 8 : half * 8 + 8, :] for gz in range(4)]
            for quarter in range(4):
                acc = roll(blocks[0], -quarter * 32)
                for gz in range(1, 4):
                    acc = jnp.where(lane // 32 == gz, roll(blocks[gz], (gz - quarter) * 32), acc)
                row = pl.multiple_of(8 + gy * 8, 8)
                out[gx * 8 + half * 4 + quarter + x_pad, pl.ds(row, 8), :] = acc
        return carry

    lax.fori_loop(0, 32, body, 0)


def bottom(
    s_parts, b_parts, out,
    s2, b2, va, vb, g, sp, u, total,
    b3, v3a, v3b, g3, sp3, u3, s3, rows, bw, wa, wb, gw, spw, uw, sw,
):
    def zero2(x, carry):
        for ref in (s2, b2, va, vb):
            ref[x] = jnp.zeros((80, 128), F32)
        return carry

    for ref in (s2, b2, va, vb):

        def clear(x, carry, ref=ref):
            ref[x, 0:8, :] = jnp.zeros((8, 128), F32)
            ref[x, 72:80, :] = jnp.zeros((8, 128), F32)
            return carry

        lax.fori_loop(0, 48, clear, 0)
        for x in [*range(8), *range(40, 48)]:
            ref[x, 8:72, :] = jnp.zeros((64, 128), F32)
    whole_grid(s_parts, s2, 8)
    whole_grid(b_parts, b2, 8)
    inner_b = b2.at[7:41]
    inner_s = s2.at[8:40, 8:72]
    ring_weights(inner_b, inner_s, g, sp, total, 32, 64, 16.0, edges=True)
    v = ring_cheb(va.at[7:41], vb.at[7:41], g, sp, u, 32, 64, RECIPE, True)
    iterate = vb if SMOOTH % 2 == 0 else va

    clear_edges(b3, 16, 32)
    clear_edges(v3a, 16, 32)
    clear_edges(v3b, 16, 32)
    half_z = pick(lambda r, c: r // 2 == c)

    def restrict(x2, carry):
        parts = []
        for half in range(2):
            x = 2 * x2 + half
            _, rest = ring_rest(v, g, sp, x, 64)
            parts.append(rest * total[x])
        rows[0] = (parts[0] + parts[1]) * (0.0625 * 0.5 / 8.0)
        rows[1] = (b2[8 + 2 * x2, 8:72, :] + b2[9 + 2 * x2, 8:72, :]) * (1.0 / 8.0)
        res = rows[0, pl.ds(0, 32, stride=2), :] + rows[0, pl.ds(1, 32, stride=2), :]
        bet = rows[1, pl.ds(0, 32, stride=2), :] + rows[1, pl.ds(1, 32, stride=2), :]
        s3[x2] = dot(res, half_z)
        b3[x2 + 1, 8:40, :] = dot(bet, half_z)
        return carry

    lax.fori_loop(0, 16, restrict, 0)
    ring_weights(b3, s3, g3, sp3, None, 16, 32, 64.0)
    c3 = ring_cheb(v3a, v3b, g3, sp3, u3, 16, 32, BOTTOM_RECIPE, True)

    other = va if iterate is vb else vb
    double_z = pick(lambda r, c: c // 2 == r)

    def prolong(x3, carry):
        wide = dot(c3[x3 + 1, 8:40, :], double_z)
        rows[0, pl.ds(0, 32, stride=2), :] = wide
        rows[0, pl.ds(1, 32, stride=2), :] = wide
        for half in range(2):
            x = 8 + 2 * x3 + half
            other[x, 8:72, :] = iterate[x, 8:72, :] + rows[0]
        return carry

    lax.fori_loop(0, 16, prolong, 0)
    ix = lax.axis_index("gx")
    iy = lax.axis_index("gy")
    iz = lax.axis_index("gz")
    clear_edges(bw, 22, 24)
    clear_edges(wa, 22, 24)
    clear_edges(wb, 22, 24)
    row = pl.multiple_of(iy * 8, 8)

    def window(x, carry):
        plane = ix * 8 + 1 + x
        bw[x + 1, 8:32, :] = b2[plane, pl.ds(row, 24), :]
        wa[x + 1, 8:32, :] = other[plane, pl.ds(row, 24), :]
        sw[x] = s2[plane, pl.ds(row, 24), :]
        return carry

    lax.fori_loop(0, 22, window, 0)
    ring_weights(bw, sw, gw, spw, None, 22, 24, 16.0, edges=True)
    c2 = ring_cheb(wa, wb, gw, spw, uw, 22, 24, RECIPE, False)
    shift = (128 - iz * 32) % 128
    for x in range(18):
        out[x] = roll(c2[x + 3, 8:32, :], shift)


BOTTOM_SCRATCH = [
    vm(48, 80, 128),
    vm(48, 80, 128),
    vm(48, 80, 128),
    vm(48, 80, 128),
    vm(6, 32, 64, 128),
    vm(32, 64, 128),
    vm(32, 64, 128),
    vm(32, 64, 128),
    vm(18, 48, 128),
    vm(18, 48, 128),
    vm(18, 48, 128),
    vm(6, 16, 32, 128),
    vm(16, 32, 128),
    vm(16, 32, 128),
    vm(16, 32, 128),
    vm(2, 64, 128),
    vm(24, 40, 128),
    vm(24, 40, 128),
    vm(24, 40, 128),
    vm(6, 22, 24, 128),
    vm(22, 24, 128),
    vm(22, 24, 128),
    vm(22, 24, 128),
]


def level1_up(c2, src, beta, iterate, out, b_pad, va, vb, g, sp, u, wide, rows):
    for ref in (b_pad, va, vb):
        clear_edges(ref, 36, 40)
    b_pad[1:37, 8:48, :] = beta[...]
    ring_weights(b_pad, src, g, sp, None, 36, 40, 4.0)
    spread = pick(lambda r, c: ((c < 74) & (c // 2 == r)) | ((c >= 118) & (c // 2 + 64 == r)))
    rows[...] = jnp.zeros((40, 128), F32)

    def prolong(x2, carry):
        wide[...] = dot(c2[x2], spread)
        part = wide[3:21, :]
        rows[pl.ds(0, 18, stride=2), :] = part
        rows[pl.ds(1, 18, stride=2), :] = part
        for half in range(2):
            x = 2 * x2 + half
            va[x + 1, 8:48, :] = jnp.where(beta[x] > 0.0, iterate[x] + rows[...], 0.0)
        return carry

    lax.fori_loop(0, 18, prolong, 0)
    v = ring_cheb(va, vb, g, sp, u, 36, 40, RECIPE, False)
    out[...] = v[7:31, 14:38, :]


def level0_up(
    c1, src, beta, z_lo, z_hi, iterate, iterate_t, out,
    b_pad, bt_pad, va, vb, ta, tb, ghost, g_main, g_strip, sp, sp_t, u, u_t, src_t, rows,
):
    for ref in (b_pad, va, vb):
        clear_edges(ref, 48, 48)
    for ref in (bt_pad, ta, tb):
        clear_strip(ref)
    b_pad[1:49, 8:56, :] = beta[...]
    unpack_strip(z_lo, z_hi, src_t, bt_pad)
    level0_setup(b_pad, bt_pad, ghost, src, src_t, g_main, g_strip, sp, sp_t, None)
    spread = pick(lambda r, c: c // 2 == r)

    def prolong(x1, carry):
        wide = dot(c1[x1], spread)
        rows[pl.ds(0, 24, stride=2), :] = wide
        rows[pl.ds(1, 24, stride=2), :] = wide
        for half in range(2):
            x = 2 * x1 + half
            va[x + 1, 8:56, :] = jnp.where(beta[x] > 0.0, iterate[x] + rows[...], 0.0)
        return carry

    lax.fori_loop(0, 24, prolong, 0)

    def prolong_strip(m, carry):
        acc = jnp.zeros((24, 128), F32)
        for k in range(8):
            to = pick(
                lambda r, c: (c // 16 == k)
                & (((c % 16 < 8) & (r == 124 + (c % 16) // 2)) | ((c % 16 >= 8) & (r == 64 + (c % 16 - 8) // 2)))
            )
            acc = acc + dot(c1[k * 3 + m], to)
        rows[pl.ds(0, 24, stride=2), :] = acc
        rows[pl.ds(1, 24, stride=2), :] = acc
        for half in range(2):
            xx = 2 * m + half
            ta[xx, 8:56, :] = jnp.where(bt_pad[xx, 8:56, :] > 0.0, iterate_t[xx] + rows[...], 0.0)
        return carry

    lax.fori_loop(0, 3, prolong_strip, 0)
    bufs = [(va, ta), (vb, tb)]
    for k in range(SMOOTH):
        (v, t), (w, s) = bufs
        retain, factor = RECIPE[k]
        if k == 0:
            retain = None
        if k < SMOOTH - 1:
            low, high = 4 + k, 44 - k
            level0_step(
                v, t, w, s, ghost, g_main, g_strip, sp, sp_t, u, u_t, low, high, retain, factor
            )
            for x in [*range(low), *range(high, 48)]:
                w[x + 1, 8:56, :] = v[x + 1, 8:56, :]
        else:
            lane = lanes_of(48)

            def last(x, carry):
                here, rest = block_rest(v, t, g_main, sp, x, lane)
                new = here + retain * u[x] + factor * rest
                rows[...] = new
                out[x - 8] = rows[8:40, :]
                return carry

            lax.fori_loop(8, 40, last, 0)
        bufs = [(w, s), (v, t)]


def ring(value, axis, step):
    count = lax.axis_size(axis)
    return lax.ppermute(value, axis, [(i, (i + step) % count) for i in range(count)])


def trade(lo, hi, axis):
    return ring(hi, axis, 1), ring(lo, axis, -1)


def per_device(source, beta):
    lo, hi = call(pack_x, (sds(2, 8, 32, 128), sds(2, 8, 32, 128)), name="pack_x")(source, beta)
    x_lo, x_hi = trade(lo, hi, "gx")
    beta2 = call(coarse_beta, sds(16, 128), [vm(32, 128)], name="coarse_beta")(beta)
    beta2_all = lax.all_gather(beta2, AXES)
    lo, hi = call(pack_y, (sds(2, 48, 8, 128), sds(2, 48, 8, 128)), name="pack_y")(
        source, beta, x_lo, x_hi
    )
    y_lo, y_hi = trade(lo, hi, "gy")
    src_ext, beta_ext, lo, hi = call(
        pack_z, (sds(48, 48, 128), sds(48, 48, 128), sds(6, 48, 128), sds(6, 48, 128)), name="pack_z"
    )(source, beta, x_lo, x_hi, y_lo, y_hi)
    z_lo, z_hi = trade(lo, hi, "gz")
    iter0, iter0_t, c, lo, hi = call(
        level0_down,
        (sds(48, 48, 128), sds(6, 48, 128), sds(16, 16, 128), sds(10, 16, 128), sds(10, 16, 128)),
        LEVEL0_SCRATCH + [vm(48, 48, 128), vm(2, 48, 128)],
        name="level0_down",
    )(src_ext, beta_ext, z_lo, z_hi)
    x_lo, x_hi = trade(lo, hi, "gx")
    lo, hi = call(pack1_y, (sds(360, 128), sds(360, 128)), name="pack1_y")(c, x_lo, x_hi)
    y_lo, y_hi = trade(lo, hi, "gy")
    ext, lo, hi = call(
        pack1_z, (sds(36, 40, 128), sds(6, 40, 128), sds(6, 40, 128)), name="pack1_z"
    )(c, x_lo, x_hi, y_lo, y_hi)
    z1_lo, z1_hi = trade(lo, hi, "gz")
    src1, beta1, iter1, chunk = call(
        level1_down,
        (sds(36, 40, 128), sds(36, 40, 128), sds(36, 40, 128), sds(128, 16, 128)),
        LEVEL1_SCRATCH + [vm(36, 40, 128), vm(40, 128)],
        name="level1_down",
    )(ext, z1_lo, z1_hi)
    source2_all = lax.all_to_all(chunk, AXES, 0, 0)
    c2 = call(bottom, sds(18, 24, 128), BOTTOM_SCRATCH, name="bottom")(source2_all, beta2_all)
    c1 = call(
        level1_up, sds(24, 24, 128), LEVEL1_SCRATCH + [vm(24, 128), vm(40, 128)], name="level1_up"
    )(c2, src1, beta1, iter1)
    return call(level0_up, sds(32, 32, 128), LEVEL0_SCRATCH + [vm(48, 128)], name="level0_up")(
        c1, src_ext, beta_ext, z_lo, z_hi, iter0, iter0_t
    )


def solution(mesh):
    placed = (P(*AXES), P(*AXES))
    return jax.shard_map(
        per_device, mesh=mesh, in_specs=placed, out_specs=P(*AXES), check_vma=False
    )
```

time: 1180 us -> 275 us (0.23); the launches traced: 1160 us -> 272 us
  starting transfers between devices: 598 us -> 24.1 us
  waiting for transfers between devices: 246 us -> 45.8 us
  local copies, waits for them, and re-layouts: 205 us -> 9.91 us
  Pallas kernels: 0 us -> 179 us
  other arithmetic: 106 us -> 0 us
    ppermute x234 -> x12, starting transfers between devices: 598 us -> 14.1 us  [ring(): lax.ppermute(value, axis, [(i, (i + step) % count) for i in range(count)])]
    ppermute x234 -> x12, waiting for transfers between devices: 246 us -> 27.7 us  [ring(): lax.ppermute(value, axis, [(i, (i + step) % count) for i in range(count)])]
    pallas_call x0 -> x11, Pallas kernels: none -> 179 us  [the longest x1 54.1 us: per_device(): call(bottom, sds(18, 24, 128), BOTTOM_SCRATCH, name='bottom')]
    reshape x7 -> x0, local copies, waits for them, and re-layouts: 111 us -> none  [the longest x4 79.6 us: restrict(): values.reshape(first // 2, 2, second // 2, 2, third // 2, 2)]
    add x35 -> x0, other arithmetic: 47.1 us -> none  [the longest x32 44.3 us: run_steps(): values = values + update]
    slice x97 -> x0, local copies, waits for them, and re-layouts: 43.8 us -> none  [the longest x83 26.6 us: with_halo(): lax.slice_in_dim(block, block.shape[dim] - width, None, axis=dim)]
    reduce_sum x6 -> x0, other arithmetic: 33.1 us -> none  [restrict(): values.reshape(first // 2, 2, second // 2, 2, third // 2, 2)]
    ppermute x18 -> x0, local copies, waits for them, and re-layouts: 24.7 us -> none  [the longest x9 12.4 us: with_halo(): lax.ppermute(lax.slice_in_dim(block, 0, width, axis=dim), axis, backward)]
  transfers between devices with their start and end apart: 234 -> 14, of which waited for: 107 -> 12; matrix products, arithmetic and copies ran while one was open for 10% -> 0% of each run, Pallas kernels for 0% -> 22%
where the time goes in v1:
time: 275 us; the launch traced here: 272 us
  Pallas kernels  179 us (65%)
  waiting for transfers between devices  45.8 us (17%)
  starting transfers between devices  24.1 us (9%)
  between operations  13.6 us (5%)
  local copies, waits for them, and re-layouts  9.91 us (4%)
    pallas_call x1, Pallas kernels, per_device(): call(bottom, sds(18, 24, 128), BOTTOM_SCRATCH, name='bottom')  54.1 us
    pallas_call x1, Pallas kernels, per_device(): call(level0_up, sds(32, 32, 128), LEVEL0_SCRATCH + [vm(48, 128)], name='l...  44 us
    pallas_call x1, Pallas kernels, per_device(): call(level0_down, (sds(48, 48, 128), sds(6, 48, 128), sds(16, 16, 128), s...  41.3 us
    ppermute x12, waiting for transfers between devices, ring(): lax.ppermute(value, axis, [(i, (i + step) % count) for i in range(count)])  27.7 us
    pallas_call x1, Pallas kernels, per_device(): call(level1_up, sds(24, 24, 128), LEVEL1_SCRATCH + [vm(24, 128), vm(40, 1...  19.7 us
    all_to_all x1, waiting for transfers between devices, per_device(): source2_all = lax.all_to_all(chunk, AXES, 0, 0)  18 us
    pallas_call x1, Pallas kernels, per_device(): call(level1_down, (sds(36, 40, 128), sds(36, 40, 128), sds(36, 40, 128),...  15.9 us
    ppermute x12, starting transfers between devices, ring(): lax.ppermute(value, axis, [(i, (i + step) % count) for i in range(count)])  14.1 us
  transfers between devices with their start and end apart: 14, of which 12 were waited for; matrix products, arithmetic and copies ran while one was open for 0% of the time, Pallas kernels for 22%

profile of v1, /device:TPU:7, one launch (start us, length us, event | category | flops | bytes accessed | tf_op | source)
XLA Modules:
  0.0 272.3 jit_solution(10262711693928697038)
XLA Ops:
  6.5 1.0 copy-done
  7.6 1.0 copy-done.2
  8.7 1.5 collective-permute-start.1
  10.2 1.2 coarse_beta.1
  11.4 4.5 %collective-permute-done.from_lo.x_lo = f32[2,8,32,128]{3,2,1,0:T(8,128)S(1)} collective-permute-done((f32[2,8,32,128]{3,2,1,0:T(8,128)S(1)}, f32[2,8,32,128]{3,2,1,0:T(8,128)S(1)}, u32[]{:S(2)}, u32[]{:S(2)}) %collective-permute-start) | collective-permute-done | bytes 262176 | tf_op jit(solution)/shard_map/ppermute | solution.py:803
  16.9 3.6 %collective-permute-start.2 = (f32[2,48,8,128]{3,2,1,0:T(8,128)S(1)}, f32[2,48,8,128]{3,2,1,0:T(8,128)S(1)}, u32[]{:S(2)}, u32[]{:S(2)}) collective-permute-start(f32[2,48,8,128]{3,2,1,0:T(8,128)S(1)} %get-tuple-element.29), channel_id=1, source_target_pairs={{0,4},{4,8},{8,12},{12,16},{16,20},{20,24},{24,28},{28,0},{1,5},{5... | collective-permute-start | bytes 1179656 | tf_op jit(solution)/shard_map/ppermute | solution.py:803
  20.5 4.7 %collective-permute-done.2.y_lo = f32[2,48,8,128]{3,2,1,0:T(8,128)S(1)} collective-permute-done((f32[2,48,8,128]{3,2,1,0:T(8,128)S(1)}, f32[2,48,8,128]{3,2,1,0:T(8,128)S(1)}, u32[]{:S(2)}, u32[]{:S(2)}) %collective-permute-start.2) | collective-permute-done | bytes 393248 | tf_op jit(solution)/shard_map/ppermute | solution.py:803
  25.2 2.5 collective-permute-done.3.y_hi
  29.6 1.7 pack_z.1
  31.3 1.4 collective-permute-start.4
  32.7 1.5 collective-permute-start.5
  34.2 4.3 %collective-permute-done.4.z_lo = f32[6,48,128]{2,1,0:T(8,128)S(1)} collective-permute-done((f32[6,48,128]{2,1,0:T(8,128)S(1)}, f32[6,48,128]{2,1,0:T(8,128)S(1)}, u32[]{:S(2)}, u32[]{:S(2)}) %collective-permute-start.4) | collective-permute-done | bytes 147488 | tf_op jit(solution)/shard_map/ppermute | solution.py:803
  38.5 41.3 %level0_down.1 = (f32[48,48,128]{2,1,0:T(8,128)S(1)}, f32[6,48,128]{2,1,0:T(8,128)S(1)}, f32[16,16,128]{2,1,0:T(8,128)S(1)}, f32[10,16,128]{2,1,0:T(8,128)S(1)}, f32[10,16,128]{2,1,0:T(8,128)S(1)}) custom-call(f32[48,48,128]{2,1,0:T(8,128)S(1)} %get-tuple-element.31.src, f32[48,48,128]{2,1,0:T(8,128)S(1)} %get-tuple-element.32.beta, ...), custom_call_target="tpu_custom_call" | custom-call | tf_op jit(solution)/shard_map/level0_down/pallas_call | solution.py:823
  79.8 1.0 copy-done.4
  81.1 1.2 collective-permute-start.7
  82.3 1.8 collective-permute-done.6.from_lo.x_lo
  84.1 1.4 collective-permute-done.7.from_hi.x_hi
  85.6 1.9 collective-permute-start.8
  87.6 2.4 collective-permute-done.8.y_lo
  90.0 2.8 %collective-permute-done.9.y_hi = f32[360,128]{1,0:T(8,128)S(1)} collective-permute-done((f32[360,128]{1,0:T(8,128)S(1)}, f32[360,128]{1,0:T(8,128)S(1)}, u32[]{:S(2)}, u32[]{:S(2)}) %collective-permute-start.9) | collective-permute-done | bytes 184352 | tf_op jit(solution)/shard_map/ppermute | solution.py:803
  92.8 1.0 pack1_z.1
  93.8 1.4 collective-permute-start.10
  95.2 1.4 collective-permute-start.11
  96.6 2.3 collective-permute-done.10.z_lo
  98.9 15.9 %level1_down.1 = (f32[36,40,128]{2,1,0:T(8,128)S(1)}, f32[36,40,128]{2,1,0:T(8,128)S(1)}, f32[36,40,128]{2,1,0:T(8,128)S(1)}, f32[128,16,128]{2,1,0:T(8,128)S(1)}) custom-call(f32[36,40,128]{2,1,0:T(8,128)S(1)} %get-tuple-element.40.ext, f32[6,40,128]{2,1,0:T(8,128)S(1)} %collective-permute-done.10.z_lo, f32[6,40,128]{2,1,0:T(8,128)S(1)} %collective-permute-done.11.z_hi), custom_call_target="tpu_custom_call" | custom-call | tf_op jit(solution)/shard_map/level1_down/pallas_call | solution.py:836
  114.8 1.0 copy-done.7
  118.5 9.9 %all-to-all-start = ((f32[128,16,128]{2,1,0:T(8,128)}), f32[128,16,128]{2,1,0:T(8,128)S(1)}, u32[]{:S(2)}, u32[]{:S(2)}) async-start(f32[128,16,128]{2,1,0:T(8,128)} %copy-done.7), calls=%async_computation | async-start | bytes 2097152 | tf_op jit(solution)/shard_map/all_to_all | solution.py:842
  128.4 18.0 %all-to-all-done.s_parts = f32[128,16,128]{2,1,0:T(8,128)S(1)} async-done(((f32[128,16,128]{2,1,0:T(8,128)}), f32[128,16,128]{2,1,0:T(8,128)S(1)}, u32[]{:S(2)}, u32[]{:S(2)}) %all-to-all-start) | async-done | bytes 1048608 | tf_op jit(solution)/shard_map/all_to_all | solution.py:842
  146.4 1.2 copy-done.6
  147.7 54.1 %bottom.1.c2 = f32[18,24,128]{2,1,0:T(8,128)S(1)} custom-call(f32[128,16,128]{2,1,0:T(8,128)S(1)} %all-to-all-done.s_parts, f32[128,16,128]{2,1,0:T(8,128)S(1)} %bitcast.1), custom_call_target="tpu_custom_call" | custom-call | tf_op jit(solution)/shard_map/bottom/pallas_call | solution.py:843
  201.8 19.7 %level1_up.1.c1 = f32[24,24,128]{2,1,0:T(8,128)S(1)} custom-call(f32[18,24,128]{2,1,0:T(8,128)S(1)} %bottom.1.c2, f32[36,40,128]{2,1,0:T(8,128)S(1)} %copy-done.13, f32[36,40,128]{2,1,0:T(8,128)S(1)} %copy-done.15, f32[36,40,128]{2,1,0:T(8,128)S(1)} %copy-done.17), custom_call_target="tpu_custom_call" | custom-call | tf_op jit(solution)/shard_map/level1_up/pallas_call | solution.py:844
  221.5 44.0 %level0_up.1 = f32[32,32,128]{2,1,0:T(8,128)} custom-call(f32[24,24,128]{2,1,0:T(8,128)S(1)} %level1_up.1.c1, f32[48,48,128]{2,1,0:T(8,128)S(1)} %get-tuple-element.31.src, f32[48,48,128]{2,1,0:T(8,128)S(1)} %get-tuple-element.32.beta, f32[6,48,128]{2,1,0:T(8,128)S(1)} %collective-permute-done.4.z_lo, f32[6,48,128]{2,1,0:T(8,128)S(1)} %copy-done.19, ...), custom_call_target="tpu_custom_call" | custom-call | tf_op jit(solution)/shard_map/level0_up/pallas_call | solution.py:847
  (52 shorter events, 6.2 us)
Async XLA Ops:
  6.5 121.9 %all-gather.3.cloned.1.call-start = ((), (), s32[]{:S(2)}) async-start(), calls=%async_computation.1 | async-start | bytes 1056768 | tf_op jit(solution)/shard_map/all_gather | solution.py:814
  6.5 1.0 copy-start
  7.6 1.0 copy-start.2
  8.6 1.6 copy-start.1
  8.6 8.2 %copy-start.3 = (f32[32,32,128]{2,1,0:T(8,128)S(1)}, f32[32,32,128]{2,1,0:T(8,128)}, u32[]{:S(2)}) copy-start(f32[32,32,128]{2,1,0:T(8,128)} %src.5) | copy-start | bytes 1572868
  8.7 7.2 %collective-permute-start = (f32[2,8,32,128]{3,2,1,0:T(8,128)S(1)}, f32[2,8,32,128]{3,2,1,0:T(8,128)S(1)}, u32[]{:S(2)}, u32[]{:S(2)}) collective-permute-start(f32[2,8,32,128]{3,2,1,0:T(8,128)S(1)} %get-tuple-element.27), channel_id=1, source_target_pairs={{0,32},{32,64},{64,96},{96,0},{1,33},{33,65},{65,97},{97,1},{2,34}... | collective-permute-start | bytes 786440 | tf_op jit(solution)/shard_map/ppermute | solution.py:803
  8.7 8.1 %collective-permute-start.1 = (f32[2,8,32,128]{3,2,1,0:T(8,128)S(1)}, f32[2,8,32,128]{3,2,1,0:T(8,128)S(1)}, u32[]{:S(2)}, u32[]{:S(2)}) collective-permute-start(f32[2,8,32,128]{3,2,1,0:T(8,128)S(1)} %get-tuple-element.28), channel_id=1, source_target_pairs={{0,96},{32,0},{64,32},{96,64},{1,97},{33,1},{65,33},{97,65},{2,98}... | collective-permute-start | bytes 786440 | tf_op jit(solution)/shard_map/ppermute | solution.py:803
  15.9 9.3 %copy-start.8 = (f32[2,8,32,128]{3,2,1,0:T(8,128)}, f32[2,8,32,128]{3,2,1,0:T(8,128)S(1)}, u32[]{:S(2)}) copy-start(f32[2,8,32,128]{3,2,1,0:T(8,128)S(1)} %collective-permute-done.from_lo.x_lo) | copy-start | bytes 786436
  16.8 8.3 %copy-start.10 = (f32[2,8,32,128]{3,2,1,0:T(8,128)}, f32[2,8,32,128]{3,2,1,0:T(8,128)S(1)}, u32[]{:S(2)}) copy-start(f32[2,8,32,128]{3,2,1,0:T(8,128)S(1)} %collective-permute-done.1.from_hi.x_hi) | copy-start | bytes 786436
  16.9 8.3 %collective-permute-start.2 = (f32[2,48,8,128]{3,2,1,0:T(8,128)S(1)}, f32[2,48,8,128]{3,2,1,0:T(8,128)S(1)}, u32[]{:S(2)}, u32[]{:S(2)}) collective-permute-start(f32[2,48,8,128]{3,2,1,0:T(8,128)S(1)} %get-tuple-element.29), channel_id=1, source_target_pairs={{0,4},{4,8},{8,12},{12,16},{16,20},{20,24},{24,28},{28,0},{1,5},{5... | collective-permute-start | bytes 1179656 | tf_op jit(solution)/shard_map/ppermute | solution.py:803
  20.5 7.2 %collective-permute-start.3 = (f32[2,48,8,128]{3,2,1,0:T(8,128)S(1)}, f32[2,48,8,128]{3,2,1,0:T(8,128)S(1)}, u32[]{:S(2)}, u32[]{:S(2)}) collective-permute-start(f32[2,48,8,128]{3,2,1,0:T(8,128)S(1)} %get-tuple-element.30), channel_id=1, source_target_pairs={{0,28},{4,0},{8,4},{12,8},{16,12},{20,16},{24,20},{28,24},{1,29},{... | collective-permute-start | bytes 1179656 | tf_op jit(solution)/shard_map/ppermute | solution.py:803
  27.7 1.0 copy-start.9
  31.3 7.2 %collective-permute-start.4 = (f32[6,48,128]{2,1,0:T(8,128)S(1)}, f32[6,48,128]{2,1,0:T(8,128)S(1)}, u32[]{:S(2)}, u32[]{:S(2)}) collective-permute-start(f32[6,48,128]{2,1,0:T(8,128)S(1)} %get-tuple-element.33), channel_id=1, source_target_pairs={{0,1},{1,2},{2,3},{3,0},{4,5},{5,6},{6,7},{7,4},{8,9},{9,10},{10,1... | collective-permute-start | bytes 442376 | tf_op jit(solution)/shard_map/ppermute | solution.py:803
  32.7 5.8 %collective-permute-start.5 = (f32[6,48,128]{2,1,0:T(8,128)S(1)}, f32[6,48,128]{2,1,0:T(8,128)S(1)}, u32[]{:S(2)}, u32[]{:S(2)}) collective-permute-start(f32[6,48,128]{2,1,0:T(8,128)S(1)} %get-tuple-element.34), channel_id=1, source_target_pairs={{0,3},{1,0},{2,1},{3,2},{4,7},{5,4},{6,5},{7,6},{8,11},{9,8},{10,9... | collective-permute-start | bytes 442376 | tf_op jit(solution)/shard_map/ppermute | solution.py:803
  38.5 41.3 %copy-start.18 = (f32[6,48,128]{2,1,0:T(8,128)}, f32[6,48,128]{2,1,0:T(8,128)S(1)}, u32[]{:S(2)}) copy-start(f32[6,48,128]{2,1,0:T(8,128)S(1)} %collective-permute-done.5.z_hi) | copy-start | bytes 442372
  79.8 1.0 copy-start.4
  80.9 9.2 %copy-start.20 = (f32[6,48,128]{2,1,0:T(8,128)}, f32[6,48,128]{2,1,0:T(8,128)S(1)}, u32[]{:S(2)}) copy-start(f32[6,48,128]{2,1,0:T(8,128)S(1)} %get-tuple-element.48.iterate_t) | copy-start | bytes 442372
  80.9 3.3 %collective-permute-start.6 = (f32[10,16,128]{2,1,0:T(8,128)S(1)}, f32[10,16,128]{2,1,0:T(8,128)S(1)}, u32[]{:S(2)}, u32[]{:S(2)}) collective-permute-start(f32[10,16,128]{2,1,0:T(8,128)S(1)} %get-tuple-element.36), channel_id=1, source_target_pairs={{0,32},{32,64},{64,96},{96,0},{1,33},{33,65},{65,97},{97,1},{2,34}... | collective-permute-start | bytes 245768 | tf_op jit(solution)/shard_map/ppermute | solution.py:803
  81.1 4.5 %collective-permute-start.7 = (f32[10,16,128]{2,1,0:T(8,128)S(1)}, f32[10,16,128]{2,1,0:T(8,128)S(1)}, u32[]{:S(2)}, u32[]{:S(2)}) collective-permute-start(f32[10,16,128]{2,1,0:T(8,128)S(1)} %get-tuple-element.37), channel_id=1, source_target_pairs={{0,96},{32,0},{64,32},{96,64},{1,97},{33,1},{65,33},{97,65},{2,98}... | collective-permute-start | bytes 245768 | tf_op jit(solution)/shard_map/ppermute | solution.py:803
  85.6 4.4 %collective-permute-start.8 = (f32[360,128]{1,0:T(8,128)S(1)}, f32[360,128]{1,0:T(8,128)S(1)}, u32[]{:S(2)}, u32[]{:S(2)}) collective-permute-start(f32[360,128]{1,0:T(8,128)S(1)} %get-tuple-element.38), channel_id=1, source_target_pairs={{0,4},{4,8},{8,12},{12,16},{16,20},{20,24},{24,28},{28,0},{1,5},{5... | collective-permute-start | bytes 552968 | tf_op jit(solution)/shard_map/ppermute | solution.py:803
  87.5 5.3 %collective-permute-start.9 = (f32[360,128]{1,0:T(8,128)S(1)}, f32[360,128]{1,0:T(8,128)S(1)}, u32[]{:S(2)}, u32[]{:S(2)}) collective-permute-start(f32[360,128]{1,0:T(8,128)S(1)} %get-tuple-element.39), channel_id=1, source_target_pairs={{0,28},{4,0},{8,4},{12,8},{16,12},{20,16},{24,20},{28,24},{1,29},{... | collective-permute-start | bytes 552968 | tf_op jit(solution)/shard_map/ppermute | solution.py:803
  93.8 5.0 %collective-permute-start.10 = (f32[6,40,128]{2,1,0:T(8,128)S(1)}, f32[6,40,128]{2,1,0:T(8,128)S(1)}, u32[]{:S(2)}, u32[]{:S(2)}) collective-permute-start(f32[6,40,128]{2,1,0:T(8,128)S(1)} %get-tuple-element.41), channel_id=1, source_target_pairs={{0,1},{1,2},{2,3},{3,0},{4,5},{5,6},{6,7},{7,4},{8,9},{9,10},{10,1... | collective-permute-start | bytes 368648 | tf_op jit(solution)/shard_map/ppermute | solution.py:803
  95.2 3.7 %collective-permute-start.11 = (f32[6,40,128]{2,1,0:T(8,128)S(1)}, f32[6,40,128]{2,1,0:T(8,128)S(1)}, u32[]{:S(2)}, u32[]{:S(2)}) collective-permute-start(f32[6,40,128]{2,1,0:T(8,128)S(1)} %get-tuple-element.42), channel_id=1, source_target_pairs={{0,3},{1,0},{2,1},{3,2},{4,7},{5,4},{6,5},{7,6},{8,11},{9,8},{10,9... | collective-permute-start | bytes 368648 | tf_op jit(solution)/shard_map/ppermute | solution.py:803
  114.8 1.0 copy-start.7
  118.5 28.0 %all-to-all-start = ((f32[128,16,128]{2,1,0:T(8,128)}), f32[128,16,128]{2,1,0:T(8,128)S(1)}, u32[]{:S(2)}, u32[]{:S(2)}) async-start(f32[128,16,128]{2,1,0:T(8,128)} %copy-done.7), calls=%async_computation | async-start | bytes 2097152 | tf_op jit(solution)/shard_map/all_to_all | solution.py:842
  146.4 1.2 copy-start.6
  147.7 54.1 %copy-start.13 = (f32[36,40,128]{2,1,0:T(8,128)S(1)}, f32[36,40,128]{2,1,0:T(8,128)}, u32[]{:S(2)}) copy-start(f32[36,40,128]{2,1,0:T(8,128)} %copy-done.12) | copy-start | bytes 2211844
  147.7 54.1 %copy-start.15 = (f32[36,40,128]{2,1,0:T(8,128)S(1)}, f32[36,40,128]{2,1,0:T(8,128)}, u32[]{:S(2)}) copy-start(f32[36,40,128]{2,1,0:T(8,128)} %copy-done.14) | copy-start | bytes 2211844
  147.7 54.1 %copy-start.17 = (f32[36,40,128]{2,1,0:T(8,128)S(1)}, f32[36,40,128]{2,1,0:T(8,128)}, u32[]{:S(2)}) copy-start(f32[36,40,128]{2,1,0:T(8,128)} %copy-done.16) | copy-start | bytes 2211844
  201.7 19.8 %copy-start.5 = (f32[48,48,128]{2,1,0:T(8,128)S(1)}, f32[48,48,128]{2,1,0:T(8,128)}, u32[]{:S(2)}) copy-start(f32[48,48,128]{2,1,0:T(8,128)} %copy-done.4) | copy-start | bytes 3538948
  201.8 19.8 %copy-start.19 = (f32[6,48,128]{2,1,0:T(8,128)S(1)}, f32[6,48,128]{2,1,0:T(8,128)}, u32[]{:S(2)}) copy-start(f32[6,48,128]{2,1,0:T(8,128)} %copy-done.18) | copy-start | bytes 442372
  201.8 19.8 %copy-start.21 = (f32[6,48,128]{2,1,0:T(8,128)S(1)}, f32[6,48,128]{2,1,0:T(8,128)}, u32[]{:S(2)}) copy-start(f32[6,48,128]{2,1,0:T(8,128)} %copy-done.20) | copy-start | bytes 442372
  (4 other events, 3.6 us)
Sparse Core Ops, SparseCore 0:
  11.5 65.3 all-gather.2

commit v2 on v1

--- a/solution.py
+++ b/solution.py
@@ -1,5 +1,3 @@
-import functools
-
 import jax
 import jax.numpy as jnp
 from jax import lax
@@ -15,7 +13,7 @@
 
 AXES = ("gx", "gy", "gz")
 F32 = jnp.float32
-VMEM_LIMIT = 44 * 1024 * 1024
+MIB = 1024 * 1024
 
 
 def cheb_plan(degree, lowest, highest):
@@ -43,14 +41,35 @@
     return pltpu.VMEM(shape, F32)
 
 
-def call(body, outs, scratch=(), name=None):
+def call(body, outs, scratch=(), name=None, mib=8):
     return pl.pallas_call(
         body,
         out_shape=outs,
         scratch_shapes=list(scratch),
-        compiler_params=pltpu.CompilerParams(vmem_limit_bytes=VMEM_LIMIT),
+        compiler_params=pltpu.CompilerParams(vmem_limit_bytes=mib * MIB),
         name=name,
     )
+
+
+def loop(low, high, vectors, body):
+    count = high - low
+    most = max(1, min(count, 72 // vectors))
+    width = max([w for w in range(1, most + 1) if count % w == 0])
+    if width * 2 < most:
+        width = most
+    rounds = count // width
+
+    def chunk(i, carry):
+        for k in range(width):
+            body(low + i * width + k)
+        return carry
+
+    if rounds > 1:
+        lax.fori_loop(0, rounds, chunk, 0)
+    else:
+        chunk(0, 0)
+    for x in range(low + rounds * width, high):
+        body(x)
 
 
 def lanes_of(rows):
@@ -134,7 +153,7 @@
         out[:, 40:48, :] = y_hi[field] * y_high
     lane = lanes_of(48)
 
-    def body(xx, carry):
+    def body(xx):
         acc_lo = jnp.zeros((48, 128), F32)
         acc_hi = jnp.zeros((48, 128), F32)
         for g in range(8):
@@ -148,22 +167,20 @@
             acc_hi = jnp.where(second, roll(b, g * 16 + 16), acc_hi)
         lo[xx] = acc_lo
         hi[xx] = acc_hi
-        return carry
-
-    lax.fori_loop(0, 6, body, 0)
+
+    loop(0, 6, 36, body)
 
 
 def strip_ghosts(values, ghost):
     lane = lanes_of(48)
 
-    def body(xx, carry):
+    def body(xx):
         acc = jnp.zeros((48, 128), F32)
         for g in range(8):
             acc = jnp.where(lane // 16 == g, roll(values[g * 6 + xx + 1, 8:56, :], g * 16 + 8), acc)
         ghost[xx] = acc
-        return carry
-
-    lax.fori_loop(0, 6, body, 0)
+
+    loop(0, 6, 36, body)
 
 
 def strip_sides(strip, xx):
@@ -179,9 +196,9 @@
     return down, up
 
 
-def block_z(value, strip, x, lane):
+def block_z(value, strip, x, lane, first=8, count=48):
     g = x // 6
-    edge = roll(strip[x - g * 6, 8:56, :], 120 - g * 16)
+    edge = roll(strip[x - g * 6, first : first + count, :], 120 - g * 16)
     up = roll(jnp.where(lane == 0, edge, value), -1)
     down = roll(jnp.where(lane == 127, edge, value), 1)
     return down, up
@@ -198,7 +215,7 @@
     strip_ghosts(b_pad, ghost)
     lane = lanes_of(48)
 
-    def body(x, carry):
+    def body(x):
         here = b_pad[x + 1, 8:56, :]
         down, up = block_z(here, bt_pad, x, lane)
         faces, inverse, tot = weights(
@@ -217,9 +234,8 @@
         sp[x] = src[x] * (2.0 * inverse)
         if total is not None:
             total[x] = tot
-        return carry
-
-    lax.fori_loop(0, 48, body, 0)
+
+    loop(0, 48, 12, body)
     for xx in range(6):
         before, after = strip_sides(bt_pad, xx)
         down, up = strip_z(bt_pad, ghost, xx, lane)
@@ -232,13 +248,18 @@
         sp_t[xx] = src_t[xx] * (2.0 * inverse)
 
 
-def block_rest(v, t, g_main, sp, x, lane):
-    here = v[x + 1, 8:56, :]
-    down, up = block_z(here, t, x, lane)
-    rest = sp[x] - here
-    rest = rest + g_main[0, x] * v[x, 8:56, :] + g_main[1, x] * v[x + 2, 8:56, :]
-    rest = rest + g_main[2, x] * v[x + 1, 7:55, :] + g_main[3, x] * v[x + 1, 9:57, :]
-    rest = rest + g_main[4, x] * down + g_main[5, x] * up
+def block_rest(v, t, g_main, sp, x, lane, skip=0):
+    count = 48 - 2 * skip
+    first = 8 + skip
+    keep = slice(skip, 48 - skip)
+    here = v[x + 1, first : first + count, :]
+    down, up = block_z(here, t, x, lane, first, count)
+    rest = sp[x, keep] - here
+    rest = rest + g_main[0, x, keep] * v[x, first : first + count, :]
+    rest = rest + g_main[1, x, keep] * v[x + 2, first : first + count, :]
+    rest = rest + g_main[2, x, keep] * v[x + 1, first - 1 : first - 1 + count, :]
+    rest = rest + g_main[3, x, keep] * v[x + 1, first + 1 : first + 1 + count, :]
+    rest = rest + g_main[4, x, keep] * down + g_main[5, x, keep] * up
     return here, rest
 
 
@@ -246,16 +267,15 @@
     strip_ghosts(v, ghost)
     lane = lanes_of(48)
 
-    def body(x, carry):
+    def body(x):
         here, rest = block_rest(v, t, g_main, sp, x, lane)
         new = factor * rest
         if retain is not None:
             new = retain * u[x] + new
         u[x] = new
         v_out[x + 1, 8:56, :] = here + new
-        return carry
-
-    lax.fori_loop(low, high, body, 0)
+
+    loop(low, high, 4, body)
     for xx in range(6):
         here = t[xx, 8:56, :]
         before, after = strip_sides(t, xx)
@@ -276,12 +296,11 @@
     ref[0] = jnp.zeros((width, 128), F32)
     ref[planes + 1] = jnp.zeros((width, 128), F32)
 
-    def body(x, carry):
+    def body(x):
         ref[x, 0:8, :] = jnp.zeros((8, 128), F32)
         ref[x, 8 + rows : width, :] = jnp.zeros((width - 8 - rows, 128), F32)
-        return carry
-
-    lax.fori_loop(0, planes + 2, body, 0)
+
+    loop(0, planes + 2, 4, body)
 
 
 def clear_strip(ref):
@@ -334,12 +353,11 @@
 
     first = RECIPE[0][1]
 
-    def start(x, carry):
+    def start(x):
         u[x] = first * sp[x]
         va[x + 1, 8:56, :] = u[x]
-        return carry
-
-    lax.fori_loop(0, 48, start, 0)
+
+    loop(0, 48, 8, start)
     for xx in range(6):
         u_t[xx] = first * sp_t[xx]
         ta[xx, 8:56, :] = u_t[xx]
@@ -356,24 +374,27 @@
     for xx in range(6):
         iter_t_out[xx] = t[xx, 8:56, :]
 
-    lane = lanes_of(48)
+    lane = lanes_of(32)
     to_low = pick(lambda r, c: r // 2 == c)
     to_high = pick(lambda r, c: r // 2 + 64 == c)
 
-    def restrict(x2, carry):
+    def restrict(x2):
         parts = []
         for half in range(2):
             x = 8 + 2 * x2 + half
-            _, rest = block_rest(v, t, g_main, sp, x, lane)
-            parts.append(rest * total[x])
-        rows[0] = (parts[0] + parts[1]) * (0.5 / 8.0)
-        rows[1] = (b_pad[9 + 2 * x2, 8:56, :] + b_pad[10 + 2 * x2, 8:56, :]) * (1.0 / 8.0)
-        res = rows[0, pl.ds(8, 16, stride=2), :] + rows[0, pl.ds(9, 16, stride=2), :]
-        bet = rows[1, pl.ds(8, 16, stride=2), :] + rows[1, pl.ds(9, 16, stride=2), :]
+            _, rest = block_rest(v, t, g_main, sp, x, lane, 8)
+            parts.append(rest * total[x, 8:40])
+        rows[0, x2] = (parts[0] + parts[1]) * (0.5 / 8.0)
+        rows[1, x2] = (b_pad[9 + 2 * x2, 16:48, :] + b_pad[10 + 2 * x2, 16:48, :]) * (1.0 / 8.0)
+
+    loop(0, 16, 8, restrict)
+
+    def compress(x2):
+        res = rows[0, x2, pl.ds(0, 16, stride=2), :] + rows[0, x2, pl.ds(1, 16, stride=2), :]
+        bet = rows[1, x2, pl.ds(0, 16, stride=2), :] + rows[1, x2, pl.ds(1, 16, stride=2), :]
         c_out[x2] = dot(res, to_low) + dot(bet, to_high)
-        return carry
-
-    lax.fori_loop(0, 16, restrict, 0)
+
+    loop(0, 16, 8, compress)
     c_lo[...] = c_out[0:10]
     c_hi[...] = c_out[6:16]
 
@@ -409,7 +430,7 @@
         ext[x, 36:40, :] = jnp.zeros((4, 128), F32)
     lane = lanes_of(40)
 
-    def body(xx, carry):
+    def body(xx):
         acc_lo = jnp.zeros((40, 128), F32)
         acc_hi = jnp.zeros((40, 128), F32)
         for g in range(6):
@@ -423,15 +444,14 @@
             acc_hi = jnp.where(second, roll(e, g * 20 + 20), acc_hi)
         lo[xx] = acc_lo
         hi[xx] = acc_hi
-        return carry
-
-    lax.fori_loop(0, 6, body, 0)
+
+    loop(0, 6, 36, body)
 
 
 def ring_weights(b_pad, src, g, sp, total, planes, rows, scale, edges=None):
     lane = lanes_of(rows)
 
-    def body(x, carry):
+    def body(x):
         here = b_pad[x + 1, 8 : 8 + rows, :]
         down = roll(here, 1)
         up = roll(here, -1)
@@ -457,9 +477,8 @@
         sp[x] = src[x] * (scale * 2.0 * inverse)
         if total is not None:
             total[x] = tot
-        return carry
-
-    lax.fori_loop(0, planes, body, 0)
+
+    loop(0, planes, rows // 4, body)
 
 
 def ring_rest(v, g, sp, x, rows):
@@ -472,25 +491,23 @@
 
 
 def ring_step(v, v_out, g, sp, u, planes, rows, retain, factor):
-    def body(x, carry):
+    def body(x):
         here, rest = ring_rest(v, g, sp, x, rows)
         new = factor * rest
         if retain is not None:
             new = retain * u[x] + new
         u[x] = new
         v_out[x + 1, 8 : 8 + rows, :] = here + new
-        return carry
-
-    lax.fori_loop(0, planes, body, 0)
+
+    loop(0, planes, rows // 16, body)
 
 
 def ring_zero_start(v, u, sp, planes, rows, factor):
-    def body(x, carry):
+    def body(x):
         u[x] = factor * sp[x]
         v[x + 1, 8 : 8 + rows, :] = u[x]
-        return carry
-
-    lax.fori_loop(0, planes, body, 0)
+
+    loop(0, planes, rows // 8, body)
 
 
 def ring_cheb(va, vb, g, sp, u, planes, rows, recipe, from_zero):
@@ -529,7 +546,7 @@
     for ref in (b_pad, va, vb):
         clear_edges(ref, 36, 40)
 
-    def unpack(xx, carry):
+    def unpack(xx):
         before = z_lo[xx] * low
         after = z_hi[xx] * high
         for k in range(6):
@@ -544,9 +561,8 @@
             src_out[x] = s
             beta_out[x] = b
             b_pad[x + 1, 8:48, :] = b
-        return carry
-
-    lax.fori_loop(0, 6, unpack, 0)
+
+    loop(0, 6, 36, unpack)
     ring_weights(b_pad, src_out, g, sp, total, 36, 40, 4.0)
     v = ring_cheb(va, vb, g, sp, u, 36, 40, RECIPE, True)
     iter_out[...] = v[1:37, 8:48, :]
@@ -557,8 +573,8 @@
             x = 10 + 2 * x2 + half
             _, rest = ring_rest(v, g, sp, x, 40)
             parts.append(rest * total[x])
-        rows[...] = (parts[0] + parts[1]) * (0.25 * 0.5 / 8.0)
-        summed.append(rows[pl.ds(10, 8, stride=2), :] + rows[pl.ds(11, 8, stride=2), :])
+        rows[x2] = (parts[0] + parts[1]) * (0.25 * 0.5 / 8.0)
+        summed.append(rows[x2, pl.ds(10, 8, stride=2), :] + rows[x2, pl.ds(11, 8, stride=2), :])
     packed = []
     for half in range(2):
         acc = jnp.zeros((8, 128), F32)
@@ -568,17 +584,16 @@
         packed.append(acc)
     both = jnp.concatenate(packed, axis=0)
 
-    def spread(d, carry):
+    def spread(d):
         chunk[d] = both
-        return carry
-
-    lax.fori_loop(0, 128, spread, 0)
+
+    loop(0, 128, 2, spread)
 
 
 def whole_grid(parts, out, x_pad):
     lane = lanes_of(8)
 
-    def body(i, carry):
+    def body(i):
         gx = i // 8
         gy = i - gx * 8
         for half in range(2):
@@ -589,9 +604,8 @@
                     acc = jnp.where(lane // 32 == gz, roll(blocks[gz], (gz - quarter) * 32), acc)
                 row = pl.multiple_of(8 + gy * 8, 8)
                 out[gx * 8 + half * 4 + quarter + x_pad, pl.ds(row, 8), :] = acc
-        return carry
-
-    lax.fori_loop(0, 32, body, 0)
+
+    loop(0, 32, 18, body)
 
 
 def bottom(
@@ -599,19 +613,13 @@
     s2, b2, va, vb, g, sp, u, total,
     b3, v3a, v3b, g3, sp3, u3, s3, rows, bw, wa, wb, gw, spw, uw, sw,
 ):
-    def zero2(x, carry):
-        for ref in (s2, b2, va, vb):
-            ref[x] = jnp.zeros((80, 128), F32)
-        return carry
-
     for ref in (s2, b2, va, vb):
 
-        def clear(x, carry, ref=ref):
+        def clear(x, ref=ref):
             ref[x, 0:8, :] = jnp.zeros((8, 128), F32)
             ref[x, 72:80, :] = jnp.zeros((8, 128), F32)
-            return carry
-
-        lax.fori_loop(0, 48, clear, 0)
+
+        loop(0, 48, 2, clear)
         for x in [*range(8), *range(40, 48)]:
             ref[x, 8:72, :] = jnp.zeros((64, 128), F32)
     whole_grid(s_parts, s2, 8)
@@ -627,37 +635,39 @@
     clear_edges(v3b, 16, 32)
     half_z = pick(lambda r, c: r // 2 == c)
 
-    def restrict(x2, carry):
+    def restrict(x2):
         parts = []
         for half in range(2):
             x = 2 * x2 + half
             _, rest = ring_rest(v, g, sp, x, 64)
             parts.append(rest * total[x])
-        rows[0] = (parts[0] + parts[1]) * (0.0625 * 0.5 / 8.0)
-        rows[1] = (b2[8 + 2 * x2, 8:72, :] + b2[9 + 2 * x2, 8:72, :]) * (1.0 / 8.0)
-        res = rows[0, pl.ds(0, 32, stride=2), :] + rows[0, pl.ds(1, 32, stride=2), :]
-        bet = rows[1, pl.ds(0, 32, stride=2), :] + rows[1, pl.ds(1, 32, stride=2), :]
+        rows[0, x2] = (parts[0] + parts[1]) * (0.0625 * 0.5 / 8.0)
+        rows[1, x2] = (b2[8 + 2 * x2, 8:72, :] + b2[9 + 2 * x2, 8:72, :]) * (1.0 / 8.0)
+
+    loop(0, 16, 16, restrict)
+
+    def compress(x2):
+        res = rows[0, x2, pl.ds(0, 32, stride=2), :] + rows[0, x2, pl.ds(1, 32, stride=2), :]
+        bet = rows[1, x2, pl.ds(0, 32, stride=2), :] + rows[1, x2, pl.ds(1, 32, stride=2), :]
         s3[x2] = dot(res, half_z)
         b3[x2 + 1, 8:40, :] = dot(bet, half_z)
-        return carry
-
-    lax.fori_loop(0, 16, restrict, 0)
+
+    loop(0, 16, 18, compress)
     ring_weights(b3, s3, g3, sp3, None, 16, 32, 64.0)
     c3 = ring_cheb(v3a, v3b, g3, sp3, u3, 16, 32, BOTTOM_RECIPE, True)
 
     other = va if iterate is vb else vb
     double_z = pick(lambda r, c: c // 2 == r)
 
-    def prolong(x3, carry):
+    def prolong(x3):
         wide = dot(c3[x3 + 1, 8:40, :], double_z)
-        rows[0, pl.ds(0, 32, stride=2), :] = wide
-        rows[0, pl.ds(1, 32, stride=2), :] = wide
+        rows[0, x3, pl.ds(0, 32, stride=2), :] = wide
+        rows[0, x3, pl.ds(1, 32, stride=2), :] = wide
         for half in range(2):
             x = 8 + 2 * x3 + half
-            other[x, 8:72, :] = iterate[x, 8:72, :] + rows[0]
-        return carry
-
-    lax.fori_loop(0, 16, prolong, 0)
+            other[x, 8:72, :] = iterate[x, 8:72, :] + rows[0, x3]
+
+    loop(0, 16, 18, prolong)
     ix = lax.axis_index("gx")
     iy = lax.axis_index("gy")
     iz = lax.axis_index("gz")
@@ -666,14 +676,13 @@
     clear_edges(wb, 22, 24)
     row = pl.multiple_of(iy * 8, 8)
 
-    def window(x, carry):
+    def window(x):
         plane = ix * 8 + 1 + x
         bw[x + 1, 8:32, :] = b2[plane, pl.ds(row, 24), :]
         wa[x + 1, 8:32, :] = other[plane, pl.ds(row, 24), :]
         sw[x] = s2[plane, pl.ds(row, 24), :]
-        return carry
-
-    lax.fori_loop(0, 22, window, 0)
+
+    loop(0, 22, 6, window)
     ring_weights(bw, sw, gw, spw, None, 22, 24, 16.0, edges=True)
     c2 = ring_cheb(wa, wb, gw, spw, uw, 22, 24, RECIPE, False)
     shift = (128 - iz * 32) % 128
@@ -697,7 +706,7 @@
     vm(16, 32, 128),
     vm(16, 32, 128),
     vm(16, 32, 128),
-    vm(2, 64, 128),
+    vm(2, 16, 64, 128),
     vm(24, 40, 128),
     vm(24, 40, 128),
     vm(24, 40, 128),
@@ -714,19 +723,19 @@
     b_pad[1:37, 8:48, :] = beta[...]
     ring_weights(b_pad, src, g, sp, None, 36, 40, 4.0)
     spread = pick(lambda r, c: ((c < 74) & (c // 2 == r)) | ((c >= 118) & (c // 2 + 64 == r)))
-    rows[...] = jnp.zeros((40, 128), F32)
-
-    def prolong(x2, carry):
-        wide[...] = dot(c2[x2], spread)
-        part = wide[3:21, :]
-        rows[pl.ds(0, 18, stride=2), :] = part
-        rows[pl.ds(1, 18, stride=2), :] = part
+    for x2 in range(18):
+        rows[x2, 32:40, :] = jnp.zeros((8, 128), F32)
+
+    def prolong(x2):
+        wide[x2] = dot(c2[x2], spread)
+        part = wide[x2, 3:21, :]
+        rows[x2, pl.ds(0, 18, stride=2), :] = part
+        rows[x2, pl.ds(1, 18, stride=2), :] = part
         for half in range(2):
             x = 2 * x2 + half
-            va[x + 1, 8:48, :] = jnp.where(beta[x] > 0.0, iterate[x] + rows[...], 0.0)
-        return carry
-
-    lax.fori_loop(0, 18, prolong, 0)
+            va[x + 1, 8:48, :] = jnp.where(beta[x] > 0.0, iterate[x] + rows[x2], 0.0)
+
+    loop(0, 18, 12, prolong)
     v = ring_cheb(va, vb, g, sp, u, 36, 40, RECIPE, False)
     out[...] = v[7:31, 14:38, :]
 
@@ -744,18 +753,17 @@
     level0_setup(b_pad, bt_pad, ghost, src, src_t, g_main, g_strip, sp, sp_t, None)
     spread = pick(lambda r, c: c // 2 == r)
 
-    def prolong(x1, carry):
+    def prolong(x1):
         wide = dot(c1[x1], spread)
-        rows[pl.ds(0, 24, stride=2), :] = wide
-        rows[pl.ds(1, 24, stride=2), :] = wide
+        rows[x1, pl.ds(0, 24, stride=2), :] = wide
+        rows[x1, pl.ds(1, 24, stride=2), :] = wide
         for half in range(2):
             x = 2 * x1 + half
-            va[x + 1, 8:56, :] = jnp.where(beta[x] > 0.0, iterate[x] + rows[...], 0.0)
-        return carry
-
-    lax.fori_loop(0, 24, prolong, 0)
-
-    def prolong_strip(m, carry):
+            va[x + 1, 8:56, :] = jnp.where(beta[x] > 0.0, iterate[x] + rows[x1], 0.0)
+
+    loop(0, 24, 12, prolong)
+
+    def prolong_strip(m):
         acc = jnp.zeros((24, 128), F32)
         for k in range(8):
             to = pick(
@@ -763,14 +771,13 @@
                 & (((c % 16 < 8) & (r == 124 + (c % 16) // 2)) | ((c % 16 >= 8) & (r == 64 + (c % 16 - 8) // 2)))
             )
             acc = acc + dot(c1[k * 3 + m], to)
-        rows[pl.ds(0, 24, stride=2), :] = acc
-        rows[pl.ds(1, 24, stride=2), :] = acc
+        rows[m, pl.ds(0, 24, stride=2), :] = acc
+        rows[m, pl.ds(1, 24, stride=2), :] = acc
         for half in range(2):
             xx = 2 * m + half
-            ta[xx, 8:56, :] = jnp.where(bt_pad[xx, 8:56, :] > 0.0, iterate_t[xx] + rows[...], 0.0)
-        return carry
-
-    lax.fori_loop(0, 3, prolong_strip, 0)
+            ta[xx, 8:56, :] = jnp.where(bt_pad[xx, 8:56, :] > 0.0, iterate_t[xx] + rows[m], 0.0)
+
+    loop(0, 3, 36, prolong_strip)
     bufs = [(va, ta), (vb, tb)]
     for k in range(SMOOTH):
         (v, t), (w, s) = bufs
@@ -785,16 +792,13 @@
             for x in [*range(low), *range(high, 48)]:
                 w[x + 1, 8:56, :] = v[x + 1, 8:56, :]
         else:
-            lane = lanes_of(48)
-
-            def last(x, carry):
-                here, rest = block_rest(v, t, g_main, sp, x, lane)
-                new = here + retain * u[x] + factor * rest
-                rows[...] = new
-                out[x - 8] = rows[8:40, :]
-                return carry
-
-            lax.fori_loop(8, 40, last, 0)
+            lane = lanes_of(32)
+
+            def last(x):
+                here, rest = block_rest(v, t, g_main, sp, x, lane, 8)
+                out[x - 8] = here + retain * u[x, 8:40] + factor * rest
+
+            loop(8, 40, 4, last)
         bufs = [(w, s), (v, t)]
 
 
@@ -817,14 +821,14 @@
     )
     y_lo, y_hi = trade(lo, hi, "gy")
     src_ext, beta_ext, lo, hi = call(
-        pack_z, (sds(48, 48, 128), sds(48, 48, 128), sds(6, 48, 128), sds(6, 48, 128)), name="pack_z"
+        pack_z, (sds(48, 48, 128), sds(48, 48, 128), sds(6, 48, 128), sds(6, 48, 128)), name="pack_z", mib=14
     )(source, beta, x_lo, x_hi, y_lo, y_hi)
     z_lo, z_hi = trade(lo, hi, "gz")
     iter0, iter0_t, c, lo, hi = call(
         level0_down,
         (sds(48, 48, 128), sds(6, 48, 128), sds(16, 16, 128), sds(10, 16, 128), sds(10, 16, 128)),
-        LEVEL0_SCRATCH + [vm(48, 48, 128), vm(2, 48, 128)],
-        name="level0_down",
+        LEVEL0_SCRATCH + [vm(48, 48, 128), vm(2, 16, 32, 128)],
+        name="level0_down", mib=30,
     )(src_ext, beta_ext, z_lo, z_hi)
     x_lo, x_hi = trade(lo, hi, "gx")
     lo, hi = call(pack1_y, (sds(360, 128), sds(360, 128)), name="pack1_y")(c, x_lo, x_hi)
@@ -836,15 +840,15 @@
     src1, beta1, iter1, chunk = call(
         level1_down,
         (sds(36, 40, 128), sds(36, 40, 128), sds(36, 40, 128), sds(128, 16, 128)),
-        LEVEL1_SCRATCH + [vm(36, 40, 128), vm(40, 128)],
-        name="level1_down",
+        LEVEL1_SCRATCH + [vm(36, 40, 128), vm(8, 40, 128)],
+        name="level1_down", mib=14,
     )(ext, z1_lo, z1_hi)
     source2_all = lax.all_to_all(chunk, AXES, 0, 0)
-    c2 = call(bottom, sds(18, 24, 128), BOTTOM_SCRATCH, name="bottom")(source2_all, beta2_all)
+    c2 = call(bottom, sds(18, 24, 128), BOTTOM_SCRATCH, name="bottom", mib=34)(source2_all, beta2_all)
     c1 = call(
-        level1_up, sds(24, 24, 128), LEVEL1_SCRATCH + [vm(24, 128), vm(40, 128)], name="level1_up"
+        level1_up, sds(24, 24, 128), LEVEL1_SCRATCH + [vm(18, 24, 128), vm(18, 40, 128)], name="level1_up", mib=14
     )(c2, src1, beta1, iter1)
-    return call(level0_up, sds(32, 32, 128), LEVEL0_SCRATCH + [vm(48, 128)], name="level0_up")(
+    return call(level0_up, sds(32, 32, 128), LEVEL0_SCRATCH + [vm(24, 48, 128)], name="level0_up", mib=32)(
         c1, src_ext, beta_ext, z_lo, z_hi, iter0, iter0_t
     )
 

time: 275 us -> 157 us (0.57)
  Pallas kernels: 179 us -> 59.7 us
    pallas_call x3, Pallas kernels: 118 us -> 36.3 us  [the longest x1 16.5 us: per_device(): call(level0_up, sds(32, 32, 128), LEVEL0_SCRATCH + [vm(24, 48, 128)], nam...]
    pallas_call x1, Pallas kernels: 41.3 us -> 15.4 us  [per_device(): call(level0_down, (sds(48, 48, 128), sds(6, 48, 128), sds(16, 16, 128), s...]
    pallas_call x1, Pallas kernels: 15.9 us -> 4.33 us  [per_device(): call(level1_down, (sds(36, 40, 128), sds(36, 40, 128), sds(36, 40, 128),...]
  transfers between devices with their start and end apart: 14 -> 14, of which waited for: 12 -> 12; matrix products, arithmetic and copies ran while one was open for 0% -> 0% of each run, Pallas kernels for 22% -> 15%
where the time goes in v2:
time: 157 us; the launch traced here: 154 us
  Pallas kernels  59.7 us (38%)
  waiting for transfers between devices  46.8 us (30%)
  starting transfers between devices  24 us (15%)
  between operations  13.6 us (9%)
  local copies, waits for them, and re-layouts  9.91 us (6%)
    ppermute x12, waiting for transfers between devices, ring(): lax.ppermute(value, axis, [(i, (i + step) % count) for i in range(count)])  28.7 us
    all_to_all x1, waiting for transfers between devices, per_device(): source2_all = lax.all_to_all(chunk, AXES, 0, 0)  18 us
    pallas_call x1, Pallas kernels, per_device(): call(level0_up, sds(32, 32, 128), LEVEL0_SCRATCH + [vm(24, 48, 128)], nam...  16.5 us
    pallas_call x1, Pallas kernels, per_device(): call(level0_down, (sds(48, 48, 128), sds(6, 48, 128), sds(16, 16, 128), s...  15.4 us
    pallas_call x1, Pallas kernels, per_device(): call(bottom, sds(18, 24, 128), BOTTOM_SCRATCH, name='bottom', mib=34)  15.1 us
    ppermute x12, starting transfers between devices, ring(): lax.ppermute(value, axis, [(i, (i + step) % count) for i in range(count)])  14.1 us
    unnamed x44, local copies, waits for them, and re-layouts  9.91 us
    all_to_all x1, starting transfers between devices, per_device(): source2_all = lax.all_to_all(chunk, AXES, 0, 0)  9.87 us
  transfers between devices with their start and end apart: 14, of which 12 were waited for; matrix products, arithmetic and copies ran while one was open for 0% of the time, Pallas kernels for 15%

profile of v2, /device:TPU:7, one launch (start us, length us, event | category | flops | bytes accessed | tf_op | source)
XLA Modules:
  0.0 154.0 jit_solution(7510838637999316863)
XLA Ops:
  6.5 1.0 copy-done
  7.6 1.0 copy-done.2
  8.7 1.5 collective-permute-start.1
  10.2 1.2 coarse_beta.1
  11.4 4.5 %collective-permute-done.from_lo.x_lo = f32[2,8,32,128]{3,2,1,0:T(8,128)S(1)} collective-permute-done((f32[2,8,32,128]{3,2,1,0:T(8,128)S(1)}, f32[2,8,32,128]{3,2,1,0:T(8,128)S(1)}, u32[]{:S(2)}, u32[]{:S(2)}) %collective-permute-start) | collective-permute-done | bytes 262176 | tf_op jit(solution)/shard_map/ppermute | solution.py:807
  16.9 3.6 %collective-permute-start.2 = (f32[2,48,8,128]{3,2,1,0:T(8,128)S(1)}, f32[2,48,8,128]{3,2,1,0:T(8,128)S(1)}, u32[]{:S(2)}, u32[]{:S(2)}) collective-permute-start(f32[2,48,8,128]{3,2,1,0:T(8,128)S(1)} %get-tuple-element.29), channel_id=1, source_target_pairs={{0,4},{4,8},{8,12},{12,16},{16,20},{20,24},{24,28},{28,0},{1,5},{5... | collective-permute-start | bytes 1179656 | tf_op jit(solution)/shard_map/ppermute | solution.py:807
  20.5 4.7 %collective-permute-done.2.y_lo = f32[2,48,8,128]{3,2,1,0:T(8,128)S(1)} collective-permute-done((f32[2,48,8,128]{3,2,1,0:T(8,128)S(1)}, f32[2,48,8,128]{3,2,1,0:T(8,128)S(1)}, u32[]{:S(2)}, u32[]{:S(2)}) %collective-permute-start.2) | collective-permute-done | bytes 393248 | tf_op jit(solution)/shard_map/ppermute | solution.py:807
  25.2 2.5 %collective-permute-done.3.y_hi = f32[2,48,8,128]{3,2,1,0:T(8,128)S(1)} collective-permute-done((f32[2,48,8,128]{3,2,1,0:T(8,128)S(1)}, f32[2,48,8,128]{3,2,1,0:T(8,128)S(1)}, u32[]{:S(2)}, u32[]{:S(2)}) %collective-permute-start.3) | collective-permute-done | bytes 393248 | tf_op jit(solution)/shard_map/ppermute | solution.py:807
  27.7 0.9 copy-done.9
  29.6 1.5 pack_z.1
  31.1 1.4 collective-permute-start.4
  32.5 1.5 collective-permute-start.5
  34.0 4.3 %collective-permute-done.4.z_lo = f32[6,48,128]{2,1,0:T(8,128)S(1)} collective-permute-done((f32[6,48,128]{2,1,0:T(8,128)S(1)}, f32[6,48,128]{2,1,0:T(8,128)S(1)}, u32[]{:S(2)}, u32[]{:S(2)}) %collective-permute-start.4) | collective-permute-done | bytes 147488 | tf_op jit(solution)/shard_map/ppermute | solution.py:807
  38.3 15.4 %level0_down.1 = (f32[48,48,128]{2,1,0:T(8,128)S(1)}, f32[6,48,128]{2,1,0:T(8,128)S(1)}, f32[16,16,128]{2,1,0:T(8,128)S(1)}, f32[10,16,128]{2,1,0:T(8,128)S(1)}, f32[10,16,128]{2,1,0:T(8,128)S(1)}) custom-call(f32[48,48,128]{2,1,0:T(8,128)S(1)} %get-tuple-element.31.src, f32[48,48,128]{2,1,0:T(8,128)S(1)} %get-tuple-element.32.beta, ...), custom_call_target="tpu_custom_call" | custom-call | tf_op jit(solution)/shard_map/level0_down/pallas_call | solution.py:827
  53.7 1.0 copy-done.4
  55.0 1.2 collective-permute-start.7
  56.2 1.8 %collective-permute-done.6.from_lo.x_lo = f32[10,16,128]{2,1,0:T(8,128)S(1)} collective-permute-done((f32[10,16,128]{2,1,0:T(8,128)S(1)}, f32[10,16,128]{2,1,0:T(8,128)S(1)}, u32[]{:S(2)}, u32[]{:S(2)}) %collective-permute-start.6) | collective-permute-done | bytes 81952 | tf_op jit(solution)/shard_map/ppermute | solution.py:807
  58.0 1.4 collective-permute-done.7.from_hi.x_hi
  59.5 1.9 %collective-permute-start.8 = (f32[360,128]{1,0:T(8,128)S(1)}, f32[360,128]{1,0:T(8,128)S(1)}, u32[]{:S(2)}, u32[]{:S(2)}) collective-permute-start(f32[360,128]{1,0:T(8,128)S(1)} %get-tuple-element.38), channel_id=1, source_target_pairs={{0,4},{4,8},{8,12},{12,16},{16,20},{20,24},{24,28},{28,0},{1,5},{5... | collective-permute-start | bytes 552968 | tf_op jit(solution)/shard_map/ppermute | solution.py:807
  61.5 2.9 %collective-permute-done.8.y_lo = f32[360,128]{1,0:T(8,128)S(1)} collective-permute-done((f32[360,128]{1,0:T(8,128)S(1)}, f32[360,128]{1,0:T(8,128)S(1)}, u32[]{:S(2)}, u32[]{:S(2)}) %collective-permute-start.8) | collective-permute-done | bytes 184352 | tf_op jit(solution)/shard_map/ppermute | solution.py:807
  64.4 2.9 %collective-permute-done.9.y_hi = f32[360,128]{1,0:T(8,128)S(1)} collective-permute-done((f32[360,128]{1,0:T(8,128)S(1)}, f32[360,128]{1,0:T(8,128)S(1)}, u32[]{:S(2)}, u32[]{:S(2)}) %collective-permute-start.9) | collective-permute-done | bytes 184352 | tf_op jit(solution)/shard_map/ppermute | solution.py:807
  68.1 1.3 collective-permute-start.10
  69.4 1.5 collective-permute-start.11
  70.9 2.3 %collective-permute-done.10.z_lo = f32[6,40,128]{2,1,0:T(8,128)S(1)} collective-permute-done((f32[6,40,128]{2,1,0:T(8,128)S(1)}, f32[6,40,128]{2,1,0:T(8,128)S(1)}, u32[]{:S(2)}, u32[]{:S(2)}) %collective-permute-start.10) | collective-permute-done | bytes 122912 | tf_op jit(solution)/shard_map/ppermute | solution.py:807
  73.6 4.3 %level1_down.1 = (f32[36,40,128]{2,1,0:T(8,128)S(1)}, f32[36,40,128]{2,1,0:T(8,128)S(1)}, f32[36,40,128]{2,1,0:T(8,128)S(1)}, f32[128,16,128]{2,1,0:T(8,128)S(1)}) custom-call(f32[36,40,128]{2,1,0:T(8,128)S(1)} %get-tuple-element.40.ext, f32[6,40,128]{2,1,0:T(8,128)S(1)} %collective-permute-done.10.z_lo, f32[6,40,128]{2,1,0:T(8,128)S(1)} %collective-permute-done.11.z_hi), custom_call_target="tpu_custom_call" | custom-call | tf_op jit(solution)/shard_map/level1_down/pallas_call | solution.py:840
  78.0 1.0 copy-done.7
  81.6 9.9 %all-to-all-start = ((f32[128,16,128]{2,1,0:T(8,128)}), f32[128,16,128]{2,1,0:T(8,128)S(1)}, u32[]{:S(2)}, u32[]{:S(2)}) async-start(f32[128,16,128]{2,1,0:T(8,128)} %copy-done.7), calls=%async_computation | async-start | bytes 2097152 | tf_op jit(solution)/shard_map/all_to_all | solution.py:846
  91.5 18.0 %all-to-all-done.s_parts = f32[128,16,128]{2,1,0:T(8,128)S(1)} async-done(((f32[128,16,128]{2,1,0:T(8,128)}), f32[128,16,128]{2,1,0:T(8,128)S(1)}, u32[]{:S(2)}, u32[]{:S(2)}) %all-to-all-start) | async-done | bytes 1048608 | tf_op jit(solution)/shard_map/all_to_all | solution.py:846
  109.5 1.2 copy-done.6
  110.7 15.1 %bottom.1.c2 = f32[18,24,128]{2,1,0:T(8,128)S(1)} custom-call(f32[128,16,128]{2,1,0:T(8,128)S(1)} %all-to-all-done.s_parts, f32[128,16,128]{2,1,0:T(8,128)S(1)} %bitcast.1), custom_call_target="tpu_custom_call" | custom-call | tf_op jit(solution)/shard_map/bottom/pallas_call | solution.py:847
  125.9 4.7 %level1_up.1.c1 = f32[24,24,128]{2,1,0:T(8,128)S(1)} custom-call(f32[18,24,128]{2,1,0:T(8,128)S(1)} %bottom.1.c2, f32[36,40,128]{2,1,0:T(8,128)S(1)} %copy-done.13, f32[36,40,128]{2,1,0:T(8,128)S(1)} %copy-done.15, f32[36,40,128]{2,1,0:T(8,128)S(1)} %copy-done.17), custom_call_target="tpu_custom_call" | custom-call | tf_op jit(solution)/shard_map/level1_up/pallas_call | solution.py:848
  130.7 16.5 %level0_up.1 = f32[32,32,128]{2,1,0:T(8,128)} custom-call(f32[24,24,128]{2,1,0:T(8,128)S(1)} %level1_up.1.c1, f32[48,48,128]{2,1,0:T(8,128)S(1)} %get-tuple-element.31.src, f32[48,48,128]{2,1,0:T(8,128)S(1)} %get-tuple-element.32.beta, f32[6,48,128]{2,1,0:T(8,128)S(1)} %collective-permute-done.4.z_lo, f32[6,48,128]{2,1,0:T(8,128)S(1)} %copy-done.19, ...), custom_call_target="tpu_custom_call" | custom-call | tf_op jit(solution)/shard_map/level0_up/pallas_call | solution.py:851
  (52 shorter events, 6.4 us)
Async XLA Ops:
  6.5 85.0 %all-gather.3.cloned.1.call-start = ((), (), s32[]{:S(2)}) async-start(), calls=%async_computation.1 | async-start | bytes 1056768 | tf_op jit(solution)/shard_map/all_gather | solution.py:818
  6.5 1.0 copy-start
  7.6 1.0 copy-start.2
  8.6 1.6 %copy-start.1 = (f32[32,32,128]{2,1,0:T(8,128)S(1)}, f32[32,32,128]{2,1,0:T(8,128)}, u32[]{:S(2)}) copy-start(f32[32,32,128]{2,1,0:T(8,128)} %beta.7) | copy-start | bytes 1572868
  8.6 8.2 %copy-start.3 = (f32[32,32,128]{2,1,0:T(8,128)S(1)}, f32[32,32,128]{2,1,0:T(8,128)}, u32[]{:S(2)}) copy-start(f32[32,32,128]{2,1,0:T(8,128)} %src.5) | copy-start | bytes 1572868
  8.7 7.2 %collective-permute-start = (f32[2,8,32,128]{3,2,1,0:T(8,128)S(1)}, f32[2,8,32,128]{3,2,1,0:T(8,128)S(1)}, u32[]{:S(2)}, u32[]{:S(2)}) collective-permute-start(f32[2,8,32,128]{3,2,1,0:T(8,128)S(1)} %get-tuple-element.27), channel_id=1, source_target_pairs={{0,32},{32,64},{64,96},{96,0},{1,33},{33,65},{65,97},{97,1},{2,34}... | collective-permute-start | bytes 786440 | tf_op jit(solution)/shard_map/ppermute | solution.py:807
  8.7 8.1 %collective-permute-start.1 = (f32[2,8,32,128]{3,2,1,0:T(8,128)S(1)}, f32[2,8,32,128]{3,2,1,0:T(8,128)S(1)}, u32[]{:S(2)}, u32[]{:S(2)}) collective-permute-start(f32[2,8,32,128]{3,2,1,0:T(8,128)S(1)} %get-tuple-element.28), channel_id=1, source_target_pairs={{0,96},{32,0},{64,32},{96,64},{1,97},{33,1},{65,33},{97,65},{2,98}... | collective-permute-start | bytes 786440 | tf_op jit(solution)/shard_map/ppermute | solution.py:807
  15.9 9.3 %copy-start.8 = (f32[2,8,32,128]{3,2,1,0:T(8,128)}, f32[2,8,32,128]{3,2,1,0:T(8,128)S(1)}, u32[]{:S(2)}) copy-start(f32[2,8,32,128]{3,2,1,0:T(8,128)S(1)} %collective-permute-done.from_lo.x_lo) | copy-start | bytes 786436
  16.8 8.3 %copy-start.10 = (f32[2,8,32,128]{3,2,1,0:T(8,128)}, f32[2,8,32,128]{3,2,1,0:T(8,128)S(1)}, u32[]{:S(2)}) copy-start(f32[2,8,32,128]{3,2,1,0:T(8,128)S(1)} %collective-permute-done.1.from_hi.x_hi) | copy-start | bytes 786436
  16.9 8.3 %collective-permute-start.2 = (f32[2,48,8,128]{3,2,1,0:T(8,128)S(1)}, f32[2,48,8,128]{3,2,1,0:T(8,128)S(1)}, u32[]{:S(2)}, u32[]{:S(2)}) collective-permute-start(f32[2,48,8,128]{3,2,1,0:T(8,128)S(1)} %get-tuple-element.29), channel_id=1, source_target_pairs={{0,4},{4,8},{8,12},{12,16},{16,20},{20,24},{24,28},{28,0},{1,5},{5... | collective-permute-start | bytes 1179656 | tf_op jit(solution)/shard_map/ppermute | solution.py:807
  20.5 7.2 %collective-permute-start.3 = (f32[2,48,8,128]{3,2,1,0:T(8,128)S(1)}, f32[2,48,8,128]{3,2,1,0:T(8,128)S(1)}, u32[]{:S(2)}, u32[]{:S(2)}) collective-permute-start(f32[2,48,8,128]{3,2,1,0:T(8,128)S(1)} %get-tuple-element.30), channel_id=1, source_target_pairs={{0,28},{4,0},{8,4},{12,8},{16,12},{20,16},{24,20},{28,24},{1,29},{... | collective-permute-start | bytes 1179656 | tf_op jit(solution)/shard_map/ppermute | solution.py:807
  27.7 1.0 copy-start.9
  31.1 7.2 %collective-permute-start.4 = (f32[6,48,128]{2,1,0:T(8,128)S(1)}, f32[6,48,128]{2,1,0:T(8,128)S(1)}, u32[]{:S(2)}, u32[]{:S(2)}) collective-permute-start(f32[6,48,128]{2,1,0:T(8,128)S(1)} %get-tuple-element.33), channel_id=1, source_target_pairs={{0,1},{1,2},{2,3},{3,0},{4,5},{5,6},{6,7},{7,4},{8,9},{9,10},{10,1... | collective-permute-start | bytes 442376 | tf_op jit(solution)/shard_map/ppermute | solution.py:807
  32.5 5.8 %collective-permute-start.5 = (f32[6,48,128]{2,1,0:T(8,128)S(1)}, f32[6,48,128]{2,1,0:T(8,128)S(1)}, u32[]{:S(2)}, u32[]{:S(2)}) collective-permute-start(f32[6,48,128]{2,1,0:T(8,128)S(1)} %get-tuple-element.34), channel_id=1, source_target_pairs={{0,3},{1,0},{2,1},{3,2},{4,7},{5,4},{6,5},{7,6},{8,11},{9,8},{10,9... | collective-permute-start | bytes 442376 | tf_op jit(solution)/shard_map/ppermute | solution.py:807
  38.3 15.4 %copy-start.18 = (f32[6,48,128]{2,1,0:T(8,128)}, f32[6,48,128]{2,1,0:T(8,128)S(1)}, u32[]{:S(2)}) copy-start(f32[6,48,128]{2,1,0:T(8,128)S(1)} %collective-permute-done.5.z_hi) | copy-start | bytes 442372
  53.7 1.0 copy-start.4
  54.7 23.2 %copy-start.20 = (f32[6,48,128]{2,1,0:T(8,128)}, f32[6,48,128]{2,1,0:T(8,128)S(1)}, u32[]{:S(2)}) copy-start(f32[6,48,128]{2,1,0:T(8,128)S(1)} %get-tuple-element.48.iterate_t) | copy-start | bytes 442372
  54.7 3.3 %collective-permute-start.6 = (f32[10,16,128]{2,1,0:T(8,128)S(1)}, f32[10,16,128]{2,1,0:T(8,128)S(1)}, u32[]{:S(2)}, u32[]{:S(2)}) collective-permute-start(f32[10,16,128]{2,1,0:T(8,128)S(1)} %get-tuple-element.36), channel_id=1, source_target_pairs={{0,32},{32,64},{64,96},{96,0},{1,33},{33,65},{65,97},{97,1},{2,34}... | collective-permute-start | bytes 245768 | tf_op jit(solution)/shard_map/ppermute | solution.py:807
  55.0 4.5 %collective-permute-start.7 = (f32[10,16,128]{2,1,0:T(8,128)S(1)}, f32[10,16,128]{2,1,0:T(8,128)S(1)}, u32[]{:S(2)}, u32[]{:S(2)}) collective-permute-start(f32[10,16,128]{2,1,0:T(8,128)S(1)} %get-tuple-element.37), channel_id=1, source_target_pairs={{0,96},{32,0},{64,32},{96,64},{1,97},{33,1},{65,33},{97,65},{2,98}... | collective-permute-start | bytes 245768 | tf_op jit(solution)/shard_map/ppermute | solution.py:807
  59.5 4.9 %collective-permute-start.8 = (f32[360,128]{1,0:T(8,128)S(1)}, f32[360,128]{1,0:T(8,128)S(1)}, u32[]{:S(2)}, u32[]{:S(2)}) collective-permute-start(f32[360,128]{1,0:T(8,128)S(1)} %get-tuple-element.38), channel_id=1, source_target_pairs={{0,4},{4,8},{8,12},{12,16},{16,20},{20,24},{24,28},{28,0},{1,5},{5... | collective-permute-start | bytes 552968 | tf_op jit(solution)/shard_map/ppermute | solution.py:807
  61.4 5.9 %collective-permute-start.9 = (f32[360,128]{1,0:T(8,128)S(1)}, f32[360,128]{1,0:T(8,128)S(1)}, u32[]{:S(2)}, u32[]{:S(2)}) collective-permute-start(f32[360,128]{1,0:T(8,128)S(1)} %get-tuple-element.39), channel_id=1, source_target_pairs={{0,28},{4,0},{8,4},{12,8},{16,12},{20,16},{24,20},{28,24},{1,29},{... | collective-permute-start | bytes 552968 | tf_op jit(solution)/shard_map/ppermute | solution.py:807
  68.1 5.0 %collective-permute-start.10 = (f32[6,40,128]{2,1,0:T(8,128)S(1)}, f32[6,40,128]{2,1,0:T(8,128)S(1)}, u32[]{:S(2)}, u32[]{:S(2)}) collective-permute-start(f32[6,40,128]{2,1,0:T(8,128)S(1)} %get-tuple-element.41), channel_id=1, source_target_pairs={{0,1},{1,2},{2,3},{3,0},{4,5},{5,6},{6,7},{7,4},{8,9},{9,10},{10,1... | collective-permute-start | bytes 368648 | tf_op jit(solution)/shard_map/ppermute | solution.py:807
  69.4 4.2 %collective-permute-start.11 = (f32[6,40,128]{2,1,0:T(8,128)S(1)}, f32[6,40,128]{2,1,0:T(8,128)S(1)}, u32[]{:S(2)}, u32[]{:S(2)}) collective-permute-start(f32[6,40,128]{2,1,0:T(8,128)S(1)} %get-tuple-element.42), channel_id=1, source_target_pairs={{0,3},{1,0},{2,1},{3,2},{4,7},{5,4},{6,5},{7,6},{8,11},{9,8},{10,9... | collective-permute-start | bytes 368648 | tf_op jit(solution)/shard_map/ppermute | solution.py:807
  77.9 1.0 copy-start.7
  81.6 27.9 %all-to-all-start = ((f32[128,16,128]{2,1,0:T(8,128)}), f32[128,16,128]{2,1,0:T(8,128)S(1)}, u32[]{:S(2)}, u32[]{:S(2)}) async-start(f32[128,16,128]{2,1,0:T(8,128)} %copy-done.7), calls=%async_computation | async-start | bytes 2097152 | tf_op jit(solution)/shard_map/all_to_all | solution.py:846
  109.5 1.2 copy-start.6
  110.7 15.1 %copy-start.13 = (f32[36,40,128]{2,1,0:T(8,128)S(1)}, f32[36,40,128]{2,1,0:T(8,128)}, u32[]{:S(2)}) copy-start(f32[36,40,128]{2,1,0:T(8,128)} %copy-done.12) | copy-start | bytes 2211844
  110.7 15.1 %copy-start.15 = (f32[36,40,128]{2,1,0:T(8,128)S(1)}, f32[36,40,128]{2,1,0:T(8,128)}, u32[]{:S(2)}) copy-start(f32[36,40,128]{2,1,0:T(8,128)} %copy-done.14) | copy-start | bytes 2211844
  110.7 15.1 %copy-start.17 = (f32[36,40,128]{2,1,0:T(8,128)S(1)}, f32[36,40,128]{2,1,0:T(8,128)}, u32[]{:S(2)}) copy-start(f32[36,40,128]{2,1,0:T(8,128)} %copy-done.16) | copy-start | bytes 2211844
  125.9 4.8 %copy-start.5 = (f32[48,48,128]{2,1,0:T(8,128)S(1)}, f32[48,48,128]{2,1,0:T(8,128)}, u32[]{:S(2)}) copy-start(f32[48,48,128]{2,1,0:T(8,128)} %copy-done.4) | copy-start | bytes 3538948
  125.9 4.8 %copy-start.19 = (f32[6,48,128]{2,1,0:T(8,128)S(1)}, f32[6,48,128]{2,1,0:T(8,128)}, u32[]{:S(2)}) copy-start(f32[6,48,128]{2,1,0:T(8,128)} %copy-done.18) | copy-start | bytes 442372
  125.9 4.8 %copy-start.21 = (f32[6,48,128]{2,1,0:T(8,128)S(1)}, f32[6,48,128]{2,1,0:T(8,128)}, u32[]{:S(2)}) copy-start(f32[6,48,128]{2,1,0:T(8,128)} %copy-done.20) | copy-start | bytes 442372
  (4 other events, 3.6 us)
Sparse Core Ops, SparseCore 0:
  11.5 65.2 all-gather.2

commit v3 on v2

--- a/solution.py
+++ b/solution.py
@@ -41,7 +41,7 @@
     return pltpu.VMEM(shape, F32)
 
 
-def call(body, outs, scratch=(), name=None, mib=8):
+def call(body, outs, scratch=(), name=None, mib=2):
     return pl.pallas_call(
         body,
         out_shape=outs,
@@ -102,13 +102,6 @@
     row = lax.broadcasted_iota(jnp.int32, (128, 128), 0)
     col = lax.broadcasted_iota(jnp.int32, (128, 128), 1)
     return jnp.where(match(row, col), 1.0, 0.0).astype(F32)
-
-
-def pack_x(src, beta, lo, hi):
-    lo[0] = src[0:8]
-    lo[1] = beta[0:8]
-    hi[0] = src[24:32]
-    hi[1] = beta[24:32]
 
 
 def coarse_beta(beta, out, rows):
@@ -127,28 +120,24 @@
         out[half * 8 : half * 8 + 8, :] = acc
 
 
-def pack_y(src, beta, from_lo, from_hi, lo, hi):
+def pack_y(src, beta, from_lo, from_hi, lo, hi, s_mid, b_mid):
     index = lax.axis_index("gx")
     low = flag(index > 0)
     high = flag(index < lax.axis_size("gx") - 1)
-    for field, ref in enumerate((src, beta)):
-        for out, row in ((lo, 0), (hi, 24)):
-            out[field, 0:8] = from_lo[field, :, row : row + 8, :] * low
-            out[field, 8:40] = ref[:, row : row + 8, :]
-            out[field, 40:48] = from_hi[field, :, row : row + 8, :] * high
-
-
-def pack_z(src, beta, x_lo, x_hi, y_lo, y_hi, s_out, b_out, lo, hi):
-    ix = lax.axis_index("gx")
+    for field, (ref, mid) in enumerate(((src, s_mid), (beta, b_mid))):
+        mid[0:8] = from_lo[field] * low
+        mid[8:40] = ref[...]
+        mid[40:48] = from_hi[field] * high
+        lo[field] = mid[:, 0:8, :]
+        hi[field] = mid[:, 24:32, :]
+
+
+def pack_z(s_mid, b_mid, y_lo, y_hi, s_out, b_out, lo, hi):
     iy = lax.axis_index("gy")
-    x_low = flag(ix > 0)
-    x_high = flag(ix < lax.axis_size("gx") - 1)
     y_low = flag(iy > 0)
     y_high = flag(iy < lax.axis_size("gy") - 1)
-    for field, (ref, out) in enumerate(((src, s_out), (beta, b_out))):
-        out[0:8, 8:40, :] = x_lo[field] * x_low
-        out[8:40, 8:40, :] = ref[...]
-        out[40:48, 8:40, :] = x_hi[field] * x_high
+    for field, (mid, out) in enumerate(((s_mid, s_out), (b_mid, b_out))):
+        out[:, 8:40, :] = mid[...]
         out[:, 0:8, :] = y_lo[field] * y_low
         out[:, 40:48, :] = y_hi[field] * y_high
     lane = lanes_of(48)
@@ -474,7 +463,7 @@
             faces[5] = jnp.where(lane == 127, 0.0, faces[5])
         for i in range(6):
             g[i, x] = faces[i]
-        sp[x] = src[x] * (scale * 2.0 * inverse)
+        sp[x] = scale * 2.0 * inverse if src is None else src[x] * (scale * 2.0 * inverse)
         if total is not None:
             total[x] = tot
 
@@ -532,10 +521,7 @@
 ]
 
 
-def level1_down(
-    ext, z_lo, z_hi, src_out, beta_out, iter_out, chunk,
-    b_pad, va, vb, g, sp, u, total, rows,
-):
+def level1_unpack(ext, z_lo, z_hi, source, b_pad, beta_out):
     iz = lax.axis_index("gz")
     low = flag(iz > 0)
     high = flag(iz < lax.axis_size("gz") - 1)
@@ -543,8 +529,6 @@
     inner = lane < 64
     above = (lane >= 64) & (lane < 74)
     below = lane >= 118
-    for ref in (b_pad, va, vb):
-        clear_edges(ref, 36, 40)
 
     def unpack(xx):
         before = z_lo[xx] * low
@@ -558,12 +542,22 @@
             b = jnp.where(inner, roll(e, 64), 0.0)
             b = jnp.where(above, roll(after, 54 - k * 20), b)
             b = jnp.where(below, roll(before, 108 - k * 20), b)
-            src_out[x] = s
-            beta_out[x] = b
+            source[x] = s
             b_pad[x + 1, 8:48, :] = b
+            if beta_out is not None:
+                beta_out[x] = b
 
     loop(0, 6, 36, unpack)
-    ring_weights(b_pad, src_out, g, sp, total, 36, 40, 4.0)
+
+
+def level1_down(
+    ext, z_lo, z_hi, iter_out, chunk,
+    b_pad, va, vb, g, sp, u, src, total, rows,
+):
+    for ref in (b_pad, va, vb):
+        clear_edges(ref, 36, 40)
+    level1_unpack(ext, z_lo, z_hi, src, b_pad, None)
+    ring_weights(b_pad, src, g, sp, total, 36, 40, 4.0)
     v = ring_cheb(va, vb, g, sp, u, 36, 40, RECIPE, True)
     iter_out[...] = v[1:37, 8:48, :]
     summed = []
@@ -575,19 +569,48 @@
             parts.append(rest * total[x])
         rows[x2] = (parts[0] + parts[1]) * (0.25 * 0.5 / 8.0)
         summed.append(rows[x2, pl.ds(10, 8, stride=2), :] + rows[x2, pl.ds(11, 8, stride=2), :])
-    packed = []
     for half in range(2):
         acc = jnp.zeros((8, 128), F32)
         for quarter in range(4):
             weight = pick(lambda r, c: (r < 64) & ((r // 2 + 32 * quarter) == c))
             acc = acc + dot(summed[half * 4 + quarter], weight)
-        packed.append(acc)
-    both = jnp.concatenate(packed, axis=0)
-
-    def spread(d):
-        chunk[d] = both
-
-    loop(0, 128, 2, spread)
+        chunk[half * 8 : half * 8 + 8, :] = acc
+
+
+def level1_prepare(ext, z_lo, z_hi, g, sp, beta_out, b_pad, src):
+    clear_edges(b_pad, 36, 40)
+    level1_unpack(ext, z_lo, z_hi, src, b_pad, beta_out)
+    ring_weights(b_pad, src, g, sp, None, 36, 40, 4.0)
+
+
+def sender(axis, step):
+    count = lax.axis_size(axis)
+    return lax.rem(lax.axis_index(axis) + count - step, count)
+
+
+def gather_z(*refs):
+    *parts, out = refs
+    lane = lanes_of(8)
+    for half in range(2):
+        for quarter in range(4):
+            acc = jnp.zeros((8, 128), F32)
+            for step, part in enumerate(parts):
+                owner = sender("gz", step)
+                moved = roll(part[half * 8 : half * 8 + 8, :], lax.rem(owner - quarter + 4, 4) * 32)
+                acc = jnp.where(lane // 32 == owner, moved, acc)
+            out[half * 4 + quarter] = acc
+
+
+def gather_x(*refs):
+    *parts, out = refs
+    for step, part in enumerate(parts):
+        out[pl.ds(sender("gx", step) * 8, 8)] = part[...]
+
+
+def gather_y(parts, out):
+    for step, part in enumerate(parts):
+        row = pl.multiple_of(8 + sender("gy", step) * 8, 8)
+        out[8:40, pl.ds(row, 8), :] = part[...]
 
 
 def whole_grid(parts, out, x_pad):
@@ -608,29 +631,71 @@
     loop(0, 32, 18, body)
 
 
+def clear_whole(ref):
+    def clear(x):
+        ref[x, 0:8, :] = jnp.zeros((8, 128), F32)
+        ref[x, 72:80, :] = jnp.zeros((8, 128), F32)
+
+    loop(0, 48, 2, clear)
+    for x in [*range(8), *range(40, 48)]:
+        ref[x, 8:72, :] = jnp.zeros((64, 128), F32)
+
+
+def coarse_prepare(b_parts, g, inv, total, g3, inv3, gw, invw, b2, b3, bw, rows):
+    clear_whole(b2)
+    clear_edges(b3, 16, 32)
+    clear_edges(bw, 22, 24)
+    whole_grid(b_parts, b2, 8)
+    ring_weights(b2.at[7:41], None, g, inv, total, 32, 64, 16.0, edges=True)
+    half_z = pick(lambda r, c: r // 2 == c)
+
+    def restrict(x2):
+        rows[x2] = (b2[8 + 2 * x2, 8:72, :] + b2[9 + 2 * x2, 8:72, :]) * (1.0 / 8.0)
+
+    loop(0, 16, 8, restrict)
+
+    def compress(x2):
+        bet = rows[x2, pl.ds(0, 32, stride=2), :] + rows[x2, pl.ds(1, 32, stride=2), :]
+        b3[x2 + 1, 8:40, :] = dot(bet, half_z)
+
+    loop(0, 16, 9, compress)
+    ring_weights(b3, None, g3, inv3, None, 16, 32, 64.0)
+    ix = lax.axis_index("gx")
+    row = pl.multiple_of(lax.axis_index("gy") * 8, 8)
+
+    def window(x):
+        bw[x + 1, 8:32, :] = b2[ix * 8 + 1 + x, pl.ds(row, 24), :]
+
+    loop(0, 22, 6, window)
+    ring_weights(bw, None, gw, invw, None, 22, 24, 16.0, edges=True)
+
+
+COARSE_SHAPES = [
+    (6, 32, 64, 128),
+    (32, 64, 128),
+    (32, 64, 128),
+    (6, 16, 32, 128),
+    (16, 32, 128),
+    (6, 22, 24, 128),
+    (22, 24, 128),
+]
+
+
 def bottom(
-    s_parts, b_parts, out,
-    s2, b2, va, vb, g, sp, u, total,
-    b3, v3a, v3b, g3, sp3, u3, s3, rows, bw, wa, wb, gw, spw, uw, sw,
+    p0, p1, p2, p3, p4, p5, p6, p7, g, inv, total, g3, inv3, gw, invw, out,
+    s2, va, vb, sp, u, v3a, v3b, sp3, u3, rows, wa, wb, spw, uw,
 ):
-    for ref in (s2, b2, va, vb):
-
-        def clear(x, ref=ref):
-            ref[x, 0:8, :] = jnp.zeros((8, 128), F32)
-            ref[x, 72:80, :] = jnp.zeros((8, 128), F32)
-
-        loop(0, 48, 2, clear)
-        for x in [*range(8), *range(40, 48)]:
-            ref[x, 8:72, :] = jnp.zeros((64, 128), F32)
-    whole_grid(s_parts, s2, 8)
-    whole_grid(b_parts, b2, 8)
-    inner_b = b2.at[7:41]
-    inner_s = s2.at[8:40, 8:72]
-    ring_weights(inner_b, inner_s, g, sp, total, 32, 64, 16.0, edges=True)
+    for ref in (s2, va, vb):
+        clear_whole(ref)
+    gather_y((p0, p1, p2, p3, p4, p5, p6, p7), s2)
+
+    def scale(x):
+        sp[x] = s2[x + 8, 8:72, :] * inv[x]
+
+    loop(0, 32, 8, scale)
     v = ring_cheb(va.at[7:41], vb.at[7:41], g, sp, u, 32, 64, RECIPE, True)
     iterate = vb if SMOOTH % 2 == 0 else va
 
-    clear_edges(b3, 16, 32)
     clear_edges(v3a, 16, 32)
     clear_edges(v3b, 16, 32)
     half_z = pick(lambda r, c: r // 2 == c)
@@ -641,19 +706,15 @@
             x = 2 * x2 + half
             _, rest = ring_rest(v, g, sp, x, 64)
             parts.append(rest * total[x])
-        rows[0, x2] = (parts[0] + parts[1]) * (0.0625 * 0.5 / 8.0)
-        rows[1, x2] = (b2[8 + 2 * x2, 8:72, :] + b2[9 + 2 * x2, 8:72, :]) * (1.0 / 8.0)
+        rows[x2] = (parts[0] + parts[1]) * (0.0625 * 0.5 / 8.0)
 
     loop(0, 16, 16, restrict)
 
     def compress(x2):
-        res = rows[0, x2, pl.ds(0, 32, stride=2), :] + rows[0, x2, pl.ds(1, 32, stride=2), :]
-        bet = rows[1, x2, pl.ds(0, 32, stride=2), :] + rows[1, x2, pl.ds(1, 32, stride=2), :]
-        s3[x2] = dot(res, half_z)
-        b3[x2 + 1, 8:40, :] = dot(bet, half_z)
-
-    loop(0, 16, 18, compress)
-    ring_weights(b3, s3, g3, sp3, None, 16, 32, 64.0)
+        res = rows[x2, pl.ds(0, 32, stride=2), :] + rows[x2, pl.ds(1, 32, stride=2), :]
+        sp3[x2] = dot(res, half_z) * inv3[x2]
+
+    loop(0, 16, 9, compress)
     c3 = ring_cheb(v3a, v3b, g3, sp3, u3, 16, 32, BOTTOM_RECIPE, True)
 
     other = va if iterate is vb else vb
@@ -661,67 +722,58 @@
 
     def prolong(x3):
         wide = dot(c3[x3 + 1, 8:40, :], double_z)
-        rows[0, x3, pl.ds(0, 32, stride=2), :] = wide
-        rows[0, x3, pl.ds(1, 32, stride=2), :] = wide
+        rows[x3, pl.ds(0, 32, stride=2), :] = wide
+        rows[x3, pl.ds(1, 32, stride=2), :] = wide
         for half in range(2):
             x = 8 + 2 * x3 + half
-            other[x, 8:72, :] = iterate[x, 8:72, :] + rows[0, x3]
+            other[x, 8:72, :] = iterate[x, 8:72, :] + rows[x3]
 
     loop(0, 16, 18, prolong)
     ix = lax.axis_index("gx")
-    iy = lax.axis_index("gy")
     iz = lax.axis_index("gz")
-    clear_edges(bw, 22, 24)
     clear_edges(wa, 22, 24)
     clear_edges(wb, 22, 24)
-    row = pl.multiple_of(iy * 8, 8)
+    row = pl.multiple_of(lax.axis_index("gy") * 8, 8)
 
     def window(x):
         plane = ix * 8 + 1 + x
-        bw[x + 1, 8:32, :] = b2[plane, pl.ds(row, 24), :]
         wa[x + 1, 8:32, :] = other[plane, pl.ds(row, 24), :]
-        sw[x] = s2[plane, pl.ds(row, 24), :]
+        spw[x] = s2[plane, pl.ds(row, 24), :] * invw[x]
 
     loop(0, 22, 6, window)
-    ring_weights(bw, sw, gw, spw, None, 22, 24, 16.0, edges=True)
     c2 = ring_cheb(wa, wb, gw, spw, uw, 22, 24, RECIPE, False)
     shift = (128 - iz * 32) % 128
     for x in range(18):
         out[x] = roll(c2[x + 3, 8:32, :], shift)
 
 
+COARSE_SCRATCH = [
+    vm(48, 80, 128),
+    vm(18, 48, 128),
+    vm(24, 40, 128),
+    vm(16, 64, 128),
+]
 BOTTOM_SCRATCH = [
     vm(48, 80, 128),
     vm(48, 80, 128),
     vm(48, 80, 128),
-    vm(48, 80, 128),
-    vm(6, 32, 64, 128),
-    vm(32, 64, 128),
     vm(32, 64, 128),
     vm(32, 64, 128),
     vm(18, 48, 128),
     vm(18, 48, 128),
-    vm(18, 48, 128),
-    vm(6, 16, 32, 128),
     vm(16, 32, 128),
     vm(16, 32, 128),
-    vm(16, 32, 128),
-    vm(2, 16, 64, 128),
+    vm(16, 64, 128),
     vm(24, 40, 128),
     vm(24, 40, 128),
-    vm(24, 40, 128),
-    vm(6, 22, 24, 128),
-    vm(22, 24, 128),
     vm(22, 24, 128),
     vm(22, 24, 128),
 ]
 
 
-def level1_up(c2, src, beta, iterate, out, b_pad, va, vb, g, sp, u, wide, rows):
-    for ref in (b_pad, va, vb):
+def level1_up(c2, g, sp, beta, iterate, out, va, vb, u, wide, rows):
+    for ref in (va, vb):
         clear_edges(ref, 36, 40)
-    b_pad[1:37, 8:48, :] = beta[...]
-    ring_weights(b_pad, src, g, sp, None, 36, 40, 4.0)
     spread = pick(lambda r, c: ((c < 74) & (c // 2 == r)) | ((c >= 118) & (c // 2 + 64 == r)))
     for x2 in range(18):
         rows[x2, 32:40, :] = jnp.zeros((8, 128), F32)
@@ -740,17 +792,24 @@
     out[...] = v[7:31, 14:38, :]
 
 
-def level0_up(
-    c1, src, beta, z_lo, z_hi, iterate, iterate_t, out,
-    b_pad, bt_pad, va, vb, ta, tb, ghost, g_main, g_strip, sp, sp_t, u, u_t, src_t, rows,
-):
-    for ref in (b_pad, va, vb):
-        clear_edges(ref, 48, 48)
-    for ref in (bt_pad, ta, tb):
-        clear_strip(ref)
+def level0_prepare(src, beta, z_lo, z_hi, g_main, g_strip, sp, sp_t, bt_out, b_pad, bt_pad, ghost, src_t):
+    clear_edges(b_pad, 48, 48)
+    clear_strip(bt_pad)
     b_pad[1:49, 8:56, :] = beta[...]
     unpack_strip(z_lo, z_hi, src_t, bt_pad)
+    for xx in range(6):
+        bt_out[xx] = bt_pad[xx, 8:56, :]
     level0_setup(b_pad, bt_pad, ghost, src, src_t, g_main, g_strip, sp, sp_t, None)
+
+
+def level0_up(
+    c1, beta, g_main, g_strip, sp, sp_t, beta_t, iterate, iterate_t, out,
+    va, vb, ta, tb, ghost, u, u_t, rows,
+):
+    for ref in (va, vb):
+        clear_edges(ref, 48, 48)
+    for ref in (ta, tb):
+        clear_strip(ref)
     spread = pick(lambda r, c: c // 2 == r)
 
     def prolong(x1):
@@ -775,7 +834,7 @@
         rows[m, pl.ds(1, 24, stride=2), :] = acc
         for half in range(2):
             xx = 2 * m + half
-            ta[xx, 8:56, :] = jnp.where(bt_pad[xx, 8:56, :] > 0.0, iterate_t[xx] + rows[m], 0.0)
+            ta[xx, 8:56, :] = jnp.where(beta_t[xx] > 0.0, iterate_t[xx] + rows[m], 0.0)
 
     loop(0, 3, 36, prolong_strip)
     bufs = [(va, ta), (vb, tb)]
@@ -811,24 +870,35 @@
     return ring(hi, axis, 1), ring(lo, axis, -1)
 
 
+def around(value, axis):
+    return [value] + [ring(value, axis, step) for step in range(1, lax.axis_size(axis))]
+
+
 def per_device(source, beta):
-    lo, hi = call(pack_x, (sds(2, 8, 32, 128), sds(2, 8, 32, 128)), name="pack_x")(source, beta)
+    lo = jnp.stack([source[0:8], beta[0:8]])
+    hi = jnp.stack([source[24:32], beta[24:32]])
+    lo, hi, source, beta = lax.optimization_barrier((lo, hi, source, beta))
     x_lo, x_hi = trade(lo, hi, "gx")
     beta2 = call(coarse_beta, sds(16, 128), [vm(32, 128)], name="coarse_beta")(beta)
     beta2_all = lax.all_gather(beta2, AXES)
-    lo, hi = call(pack_y, (sds(2, 48, 8, 128), sds(2, 48, 8, 128)), name="pack_y")(
+    slab = sds(2, 48, 8, 128)
+    mid = sds(48, 32, 128)
+    lo, hi, s_mid, b_mid = call(pack_y, (slab, slab, mid, mid), name="pack_y", mib=4)(
         source, beta, x_lo, x_hi
     )
     y_lo, y_hi = trade(lo, hi, "gy")
+    whole = sds(48, 48, 128)
+    strip = sds(6, 48, 128)
     src_ext, beta_ext, lo, hi = call(
-        pack_z, (sds(48, 48, 128), sds(48, 48, 128), sds(6, 48, 128), sds(6, 48, 128)), name="pack_z", mib=14
-    )(source, beta, x_lo, x_hi, y_lo, y_hi)
+        pack_z, (whole, whole, strip, strip), name="pack_z", mib=4
+    )(s_mid, b_mid, y_lo, y_hi)
     z_lo, z_hi = trade(lo, hi, "gz")
     iter0, iter0_t, c, lo, hi = call(
         level0_down,
-        (sds(48, 48, 128), sds(6, 48, 128), sds(16, 16, 128), sds(10, 16, 128), sds(10, 16, 128)),
+        (whole, strip, sds(16, 16, 128), sds(10, 16, 128), sds(10, 16, 128)),
         LEVEL0_SCRATCH + [vm(48, 48, 128), vm(2, 16, 32, 128)],
-        name="level0_down", mib=30,
+        name="level0_down",
+        mib=24,
     )(src_ext, beta_ext, z_lo, z_hi)
     x_lo, x_hi = trade(lo, hi, "gx")
     lo, hi = call(pack1_y, (sds(360, 128), sds(360, 128)), name="pack1_y")(c, x_lo, x_hi)
@@ -837,20 +907,60 @@
         pack1_z, (sds(36, 40, 128), sds(6, 40, 128), sds(6, 40, 128)), name="pack1_z"
     )(c, x_lo, x_hi, y_lo, y_hi)
     z1_lo, z1_hi = trade(lo, hi, "gz")
-    src1, beta1, iter1, chunk = call(
+    iter1, chunk = call(
         level1_down,
-        (sds(36, 40, 128), sds(36, 40, 128), sds(36, 40, 128), sds(128, 16, 128)),
-        LEVEL1_SCRATCH + [vm(36, 40, 128), vm(8, 40, 128)],
-        name="level1_down", mib=14,
+        (sds(36, 40, 128), sds(16, 128)),
+        LEVEL1_SCRATCH + [vm(36, 40, 128), vm(36, 40, 128), vm(8, 40, 128)],
+        name="level1_down",
+        mib=11,
     )(ext, z1_lo, z1_hi)
-    source2_all = lax.all_to_all(chunk, AXES, 0, 0)
-    c2 = call(bottom, sds(18, 24, 128), BOTTOM_SCRATCH, name="bottom", mib=34)(source2_all, beta2_all)
+    chunk, beta2_all = lax.optimization_barrier((chunk, beta2_all))
+    parts = around(chunk, "gz")
+    coarse = call(
+        coarse_prepare,
+        tuple(sds(*shape) for shape in COARSE_SHAPES),
+        COARSE_SCRATCH,
+        name="coarse_prepare",
+        mib=8,
+    )(beta2_all)
+    block = call(gather_z, sds(8, 8, 128), name="gather_z")(*parts)
+    block, ext, z1_lo, z1_hi = lax.optimization_barrier((block, ext, z1_lo, z1_hi))
+    parts = around(block, "gx")
+    g1, sp1, beta1 = call(
+        level1_prepare,
+        (sds(6, 36, 40, 128), sds(36, 40, 128), sds(36, 40, 128)),
+        [vm(38, 56, 128), vm(36, 40, 128)],
+        name="level1_prepare",
+        mib=4,
+    )(ext, z1_lo, z1_hi)
+    slab = call(gather_x, sds(32, 8, 128), name="gather_x")(*parts)
+    slab, src_ext, beta_ext, z_lo, z_hi = lax.optimization_barrier(
+        (slab, src_ext, beta_ext, z_lo, z_hi)
+    )
+    parts = around(slab, "gy")
+    ready = call(
+        level0_prepare,
+        (sds(6, 48, 48, 128), sds(6, 6, 48, 128), whole, strip, strip),
+        [vm(50, 64, 128), vm(6, 64, 128), vm(6, 48, 128), vm(6, 48, 128)],
+        name="level0_prepare",
+        mib=6,
+    )(src_ext, beta_ext, z_lo, z_hi)
+    c2 = call(bottom, sds(18, 24, 128), BOTTOM_SCRATCH, name="bottom", mib=18)(*parts, *coarse)
     c1 = call(
-        level1_up, sds(24, 24, 128), LEVEL1_SCRATCH + [vm(18, 24, 128), vm(18, 40, 128)], name="level1_up", mib=14
-    )(c2, src1, beta1, iter1)
-    return call(level0_up, sds(32, 32, 128), LEVEL0_SCRATCH + [vm(24, 48, 128)], name="level0_up", mib=32)(
-        c1, src_ext, beta_ext, z_lo, z_hi, iter0, iter0_t
-    )
+        level1_up,
+        sds(24, 24, 128),
+        [vm(38, 56, 128), vm(38, 56, 128), vm(36, 40, 128), vm(18, 24, 128), vm(18, 40, 128)],
+        name="level1_up",
+        mib=6,
+    )(c2, g1, sp1, beta1, iter1)
+    return call(
+        level0_up,
+        sds(32, 32, 128),
+        [vm(50, 64, 128), vm(50, 64, 128), vm(6, 64, 128), vm(6, 64, 128), vm(6, 48, 128)]
+        + [vm(48, 48, 128), vm(6, 48, 128), vm(24, 48, 128)],
+        name="level0_up",
+        mib=12,
+    )(c1, beta_ext, *ready, iter0, iter0_t)
 
 
 def solution(mesh):

time: 157 us -> 153 us (0.975)
  starting transfers between devices: 24 us -> 33.2 us
  waiting for transfers between devices: 46.8 us -> 37.7 us
  local copies, waits for them, and re-layouts: 9.91 us -> 6.78 us
    ppermute x12 -> x25, starting transfers between devices: 14.1 us -> 33.2 us  [ring(): lax.ppermute(value, axis, [(i, (i + step) % count) for i in range(count)])]
    all_to_all x1 -> x0, waiting for transfers between devices: 18 us -> none  [per_device(): source2_all = lax.all_to_all(chunk, AXES, 0, 0)]
    all_to_all x1 -> x0, starting transfers between devices: 9.87 us -> none  [per_device(): source2_all = lax.all_to_all(chunk, AXES, 0, 0)]
    ppermute x12 -> x25, waiting for transfers between devices: 28.7 us -> 37.7 us  [ring(): lax.ppermute(value, axis, [(i, (i + step) % count) for i in range(count)])]
    unnamed x44 -> x22, local copies, waits for them, and re-layouts: 9.91 us -> 4.72 us
    another operation x0 -> x2, local copies, waits for them, and re-layouts: none -> 2.06 us  [per_device(): hi = jnp.stack([source[24:32], beta[24:32]])]
    pallas_call x8 -> x12, Pallas kernels: 57.7 us -> 57.9 us  [the longest x1 15.4 us: per_device(): call(level0_down, (whole, strip, sds(16, 16, 128), sds(10, 16, 128), sds(...]
  transfers between devices with their start and end apart: 14 -> 26, of which waited for: 12 -> 18; matrix products, arithmetic and copies ran while one was open for 0% -> 0% of each run, Pallas kernels for 15% -> 21%
where the time goes in v3:
time: 153 us; the launch traced here: 151 us
  Pallas kernels  59.9 us (39%)
  waiting for transfers between devices  37.7 us (25%)
  starting transfers between devices  33.2 us (22%)
  between operations  13.7 us (9%)
  local copies, waits for them, and re-layouts  6.78 us (4%)
    ppermute x25, waiting for transfers between devices, ring(): lax.ppermute(value, axis, [(i, (i + step) % count) for i in range(count)])  37.7 us
    ppermute x25, starting transfers between devices, ring(): lax.ppermute(value, axis, [(i, (i + step) % count) for i in range(count)])  33.2 us
    pallas_call x1, Pallas kernels, per_device(): call(level0_down, (whole, strip, sds(16, 16, 128), sds(10, 16, 128), sds(...  15.4 us
    pallas_call x1, Pallas kernels, per_device(): call(level0_up, sds(32, 32, 128), [vm(50, 64, 128), vm(50, 64, 128), vm(6...  13.5 us
    pallas_call x1, Pallas kernels, per_device(): call(bottom, sds(18, 24, 128), BOTTOM_SCRATCH, name='bottom', mib=18)  9.26 us
    pallas_call x1, Pallas kernels, per_device(): call(coarse_prepare, tuple((sds(*shape) for shape in COARSE_SHAPES)), COA...  4.79 us
    unnamed x22, local copies, waits for them, and re-layouts  4.72 us
    pallas_call x1, Pallas kernels, per_device(): call(level1_down, (sds(36, 40, 128), sds(16, 128)), LEVEL1_SCRATCH + [vm(...  4.25 us
  transfers between devices with their start and end apart: 26, of which 18 were waited for; matrix products, arithmetic and copies ran while one was open for 0% of the time, Pallas kernels for 21%

profile of v3, /device:TPU:7, one launch (start us, length us, event | category | flops | bytes accessed | tf_op | source)
XLA Modules:
  0.0 151.2 jit_solution(15004988778910730503)
XLA Ops:
  9.9 1.5 collective-permute-start.1
  11.4 5.7 %collective-permute-done.from_lo = f32[2,8,32,128]{3,2,1,0:T(8,128)S(1)} collective-permute-done((f32[2,8,32,128]{3,2,1,0:T(8,128)S(1)}, f32[2,8,32,128]{3,2,1,0:T(8,128)S(1)}, u32[]{:S(2)}, u32[]{:S(2)}) %collective-permute-start) | collective-permute-done | bytes 262176 | tf_op jit(solution)/shard_map/ppermute | solution.py:866
  18.2 3.6 %collective-permute-start.2 = (f32[2,48,8,128]{3,2,1,0:T(8,128)S(1)}, f32[2,48,8,128]{3,2,1,0:T(8,128)S(1)}, u32[]{:S(2)}, u32[]{:S(2)}) collective-permute-start(f32[2,48,8,128]{3,2,1,0:T(8,128)S(1)} %get-tuple-element.61), channel_id=1, source_target_pairs={{0,4},{4,8},{8,12},{12,16},{16,20},{20,24},{24,28},{28,0},{1,5},{5... | collective-permute-start | bytes 1179656 | tf_op jit(solution)/shard_map/ppermute | solution.py:866
  21.7 4.7 %collective-permute-done.2.y_lo = f32[2,48,8,128]{3,2,1,0:T(8,128)S(1)} collective-permute-done((f32[2,48,8,128]{3,2,1,0:T(8,128)S(1)}, f32[2,48,8,128]{3,2,1,0:T(8,128)S(1)}, u32[]{:S(2)}, u32[]{:S(2)}) %collective-permute-start.2) | collective-permute-done | bytes 393248 | tf_op jit(solution)/shard_map/ppermute | solution.py:866
  26.5 2.9 %collective-permute-done.3.y_hi = f32[2,48,8,128]{3,2,1,0:T(8,128)S(1)} collective-permute-done((f32[2,48,8,128]{3,2,1,0:T(8,128)S(1)}, f32[2,48,8,128]{3,2,1,0:T(8,128)S(1)}, u32[]{:S(2)}, u32[]{:S(2)}) %collective-permute-start.3) | collective-permute-done | bytes 393248 | tf_op jit(solution)/shard_map/ppermute | solution.py:866
  29.4 1.5 pack_z.1
  30.9 1.4 collective-permute-start.4
  32.3 1.5 %collective-permute-start.5 = (f32[6,48,128]{2,1,0:T(8,128)S(1)}, f32[6,48,128]{2,1,0:T(8,128)S(1)}, u32[]{:S(2)}, u32[]{:S(2)}) collective-permute-start(f32[6,48,128]{2,1,0:T(8,128)S(1)} %get-tuple-element.66), channel_id=1, source_target_pairs={{0,3},{1,0},{2,1},{3,2},{4,7},{5,4},{6,5},{7,6},{8,11},{9,8},{10,9... | collective-permute-start | bytes 442376 | tf_op jit(solution)/shard_map/ppermute | solution.py:866
  33.8 3.6 %collective-permute-done.4.z_lo = f32[6,48,128]{2,1,0:T(8,128)S(1)} collective-permute-done((f32[6,48,128]{2,1,0:T(8,128)S(1)}, f32[6,48,128]{2,1,0:T(8,128)S(1)}, u32[]{:S(2)}, u32[]{:S(2)}) %collective-permute-start.4) | collective-permute-done | bytes 147488 | tf_op jit(solution)/shard_map/ppermute | solution.py:866
  38.1 15.4 %level0_down.1 = (f32[48,48,128]{2,1,0:T(8,128)S(1)}, f32[6,48,128]{2,1,0:T(8,128)S(1)}, f32[16,16,128]{2,1,0:T(8,128)S(1)}, f32[10,16,128]{2,1,0:T(8,128)S(1)}, f32[10,16,128]{2,1,0:T(8,128)S(1)}) custom-call(f32[48,48,128]{2,1,0:T(8,128)S(1)} %get-tuple-element.95.src, f32[48,48,128]{2,1,0:T(8,128)S(1)} %get-tuple-element.94.beta, ...), custom_call_target="tpu_custom_call" | custom-call | tf_op jit(solution)/shard_map/level0_down/pallas_call | solution.py:896
  54.6 1.5 collective-permute-start.7
  56.1 1.8 %collective-permute-done.6.from_lo.x_lo = f32[10,16,128]{2,1,0:T(8,128)S(1)} collective-permute-done((f32[10,16,128]{2,1,0:T(8,128)S(1)}, f32[10,16,128]{2,1,0:T(8,128)S(1)}, u32[]{:S(2)}, u32[]{:S(2)}) %collective-permute-start.6) | collective-permute-done | bytes 81952 | tf_op jit(solution)/shard_map/ppermute | solution.py:866
  59.2 1.6 %collective-permute-start.8 = (f32[360,128]{1,0:T(8,128)S(1)}, f32[360,128]{1,0:T(8,128)S(1)}, u32[]{:S(2)}, u32[]{:S(2)}) collective-permute-start(f32[360,128]{1,0:T(8,128)S(1)} %get-tuple-element.70), channel_id=1, source_target_pairs={{0,4},{4,8},{8,12},{12,16},{16,20},{20,24},{24,28},{28,0},{1,5},{5... | collective-permute-start | bytes 552968 | tf_op jit(solution)/shard_map/ppermute | solution.py:866
  60.8 2.7 %collective-permute-done.8.y_lo = f32[360,128]{1,0:T(8,128)S(1)} collective-permute-done((f32[360,128]{1,0:T(8,128)S(1)}, f32[360,128]{1,0:T(8,128)S(1)}, u32[]{:S(2)}, u32[]{:S(2)}) %collective-permute-start.8) | collective-permute-done | bytes 184352 | tf_op jit(solution)/shard_map/ppermute | solution.py:866
  63.5 2.5 %collective-permute-done.9.y_hi = f32[360,128]{1,0:T(8,128)S(1)} collective-permute-done((f32[360,128]{1,0:T(8,128)S(1)}, f32[360,128]{1,0:T(8,128)S(1)}, u32[]{:S(2)}, u32[]{:S(2)}) %collective-permute-start.9) | collective-permute-done | bytes 184352 | tf_op jit(solution)/shard_map/ppermute | solution.py:866
  68.2 1.4 collective-permute-start.11
  69.7 2.4 %collective-permute-done.10.z_lo = f32[6,40,128]{2,1,0:T(8,128)S(1)} collective-permute-done((f32[6,40,128]{2,1,0:T(8,128)S(1)}, f32[6,40,128]{2,1,0:T(8,128)S(1)}, u32[]{:S(2)}, u32[]{:S(2)}) %collective-permute-start.10) | collective-permute-done | bytes 122912 | tf_op jit(solution)/shard_map/ppermute | solution.py:866
  72.4 4.2 %level1_down.1 = (f32[36,40,128]{2,1,0:T(8,128)S(1)}, f32[16,128]{1,0:T(8,128)S(1)}) custom-call(f32[36,40,128]{2,1,0:T(8,128)S(1)} %get-tuple-element.87.ext, f32[6,40,128]{2,1,0:T(8,128)S(1)} %collective-permute-done.10.z_lo, f32[6,40,128]{2,1,0:T(8,128)S(1)} %collective-permute-done.11.z_hi), custom_call_target="tpu_custom_call" | custom-call | tf_op jit(solution)/shard_map/level1_down/pallas_call | solution.py:910
  79.1 2.6 %collective-permute-start.13 = (f32[16,128]{1,0:T(8,128)S(1)}, f32[16,128]{1,0:T(8,128)S(1)}, u32[]{:S(2)}, u32[]{:S(2)}) collective-permute-start(f32[16,128]{1,0:T(8,128)S(1)} %get-tuple-element.76.refs_0_), channel_id=1, source_target_pairs={{0,2},{1,3},{2,0},{3,1},{4,6},{5,7},{6,4},{7,5},{8,10},{9,11},{10,... | collective-permute-start | bytes 24584 | tf_op jit(solution)/shard_map/ppermute | solution.py:866
  84.6 1.8 %collective-permute-start.16 = (f32[8,8,128]{2,1,0:T(8,128)S(1)}, f32[8,8,128]{2,1,0:T(8,128)S(1)}, u32[]{:S(2)}, u32[]{:S(2)}) collective-permute-start(f32[8,8,128]{2,1,0:T(8,128)S(1)} %gather_z.1.refs_0_), channel_id=1, source_target_pairs={{0,64},{32,96},{64,0},{96,32},{1,65},{33,97},{65,1},{97,33},{2,66}... | collective-permute-start | bytes 98312 | tf_op jit(solution)/shard_map/ppermute | solution.py:866
  87.3 1.6 %collective-permute-done.16.refs_2_ = f32[8,8,128]{2,1,0:T(8,128)S(1)} collective-permute-done((f32[8,8,128]{2,1,0:T(8,128)S(1)}, f32[8,8,128]{2,1,0:T(8,128)S(1)}, u32[]{:S(2)}, u32[]{:S(2)}) %collective-permute-start.16) | collective-permute-done | bytes 32800 | tf_op jit(solution)/shard_map/ppermute | solution.py:866
  88.9 1.5 collective-permute-done.17.refs_3_
  90.4 5.7 %collective-permute-start.18 = (f32[32,8,128]{2,1,0:T(8,128)S(1)}, f32[32,8,128]{2,1,0:T(8,128)S(1)}, u32[]{:S(2)}, u32[]{:S(2)}) collective-permute-start(f32[32,8,128]{2,1,0:T(8,128)S(1)} %gather_x.1.p0), channel_id=1, source_target_pairs={{0,4},{4,8},{8,12},{12,16},{16,20},{20,24},{24,28},{28,0},{1,5},{5... | collective-permute-start | bytes 393224 | tf_op jit(solution)/shard_map/ppermute | solution.py:866
  97.4 2.1 %collective-permute-start.20 = (f32[32,8,128]{2,1,0:T(8,128)S(1)}, f32[32,8,128]{2,1,0:T(8,128)S(1)}, u32[]{:S(2)}, u32[]{:S(2)}) collective-permute-start(f32[32,8,128]{2,1,0:T(8,128)S(1)} %gather_x.1.p0), channel_id=1, source_target_pairs={{0,12},{4,16},{8,20},{12,24},{16,28},{20,0},{24,4},{28,8},{1,13},{... | collective-permute-start | bytes 393224 | tf_op jit(solution)/shard_map/ppermute | solution.py:866
  100.5 2.6 %collective-permute-start.22 = (f32[32,8,128]{2,1,0:T(8,128)S(1)}, f32[32,8,128]{2,1,0:T(8,128)S(1)}, u32[]{:S(2)}, u32[]{:S(2)}) collective-permute-start(f32[32,8,128]{2,1,0:T(8,128)S(1)} %gather_x.1.p0), channel_id=1, source_target_pairs={{0,20},{4,24},{8,28},{12,0},{16,4},{20,8},{24,12},{28,16},{1,21},{... | collective-permute-start | bytes 393224 | tf_op jit(solution)/shard_map/ppermute | solution.py:866
  103.1 2.6 %collective-permute-done.19.p2 = f32[32,8,128]{2,1,0:T(8,128)S(1)} collective-permute-done((f32[32,8,128]{2,1,0:T(8,128)S(1)}, f32[32,8,128]{2,1,0:T(8,128)S(1)}, u32[]{:S(2)}, u32[]{:S(2)}) %collective-permute-start.19) | collective-permute-done | bytes 131104 | tf_op jit(solution)/shard_map/ppermute | solution.py:866
  106.9 4.8 %coarse_prepare.1 = (f32[6,32,64,128]{3,2,1,0:T(8,128)S(1)}, f32[32,64,128]{2,1,0:T(8,128)S(1)}, f32[32,64,128]{2,1,0:T(8,128)S(1)}, f32[6,16,32,128]{3,2,1,0:T(...) custom-call(f32[128,16,128]{2,1,0:T(8,128)S(1)} %bitcast.9), custom_call_target="tpu_custom_call" | custom-call | tf_op jit(solution)/shard_map/coarse_prepare/pallas_call | solution.py:919
  112.6 2.2 %level1_prepare.1 = (f32[6,36,40,128]{3,2,1,0:T(8,128)S(1)}, f32[36,40,128]{2,1,0:T(8,128)S(1)}, f32[36,40,128]{2,1,0:T(8,128)S(1)}) custom-call(f32[36,40,128]{2,1,0:T(8,128)S(1)} %get-tuple-element.87.ext, f32[6,40,128]{2,1,0:T(8,128)S(1)} %collective-permute-done.10.z_lo, f32[6,40,128]{2,1,0:T(8,128)S(1)} %copy-done.8), custom_call_target="tpu_custom_call" | custom-call | tf_op jit(solution)/shard_map/level1_prepare/pallas_call | solution.py:929
  114.9 3.0 %level0_prepare.1 = (f32[6,48,48,128]{3,2,1,0:T(8,128)S(1)}, f32[6,6,48,128]{3,2,1,0:T(8,128)S(1)}, f32[48,48,128]{2,1,0:T(8,128)S(1)}, f32[6,48,128]{2,1,0:T(8,128)S(1)}, f32[6,48,128]{2,1,0:T(8,128)S(1)}) custom-call(f32[48,48,128]{2,1,0:T(8,128)S(1)} %get-tuple-element.95.src, f32[48,48,128]{2,1,0:T(8,128)S(1)} %get-tuple-element.94.beta, ...), custom_call_target="tpu_custom_call" | custom-call | tf_op jit(solution)/shard_map/level0_prepare/pallas_call | solution.py:941
  117.9 9.3 %bottom.1.c2 = f32[18,24,128]{2,1,0:T(8,128)S(1)} custom-call(f32[32,8,128]{2,1,0:T(8,128)S(1)} %gather_x.1.p0, f32[32,8,128]{2,1,0:T(8,128)S(1)} %collective-permute-done.18.p1, f32[32,8,128]{2,1,0:T(8,128)S(1)} %collective-permute-done.19.p2, f32[32,8,128]{2,1,0:T(8,128)S(1)} %collective-permute-done.20.p3, f32[32,8,128]{2,1,0:T(8,128)S(1)} %collective-permute-done.21.p4, ...), custom_call_target="tpu_custom_call" | custom-call | tf_op jit(solution)/shard_map/bottom/pallas_call | solution.py:948
  127.2 3.7 %level1_up.1.c1 = f32[24,24,128]{2,1,0:T(8,128)S(1)} custom-call(f32[18,24,128]{2,1,0:T(8,128)S(1)} %bottom.1.c2, f32[6,36,40,128]{3,2,1,0:T(8,128)S(1)} %get-tuple-element.90.g, f32[36,40,128]{2,1,0:T(8,128)S(1)} %get-tuple-element.91.sp, f32[36,40,128]{2,1,0:T(8,128)S(1)} %get-tuple-element.92.beta, f32[36,40,128]{2,1,0:T(8,128)S(1)} %copy-done.6), custom_call_target="tpu_custom_call" | custom-call | tf_op jit(solution)/shard_map/level1_up/pallas_call | solution.py:949
  130.9 13.5 %level0_up.1 = f32[32,32,128]{2,1,0:T(8,128)} custom-call(f32[24,24,128]{2,1,0:T(8,128)S(1)} %level1_up.1.c1, f32[48,48,128]{2,1,0:T(8,128)S(1)} %get-tuple-element.94.beta, f32[6,48,48,128]{3,2,1,0:T(8,128)S(1)} %get-tuple-element.98.g_main, f32[6,6,48,128]{3,2,1,0:T(8,128)S(1)} %get-tuple-element.99.g_strip, f32[48,48,128]{2,1,0:T(8,128)S(1)} %get-tuple-element.100.sp, ...), custom_call_target="tpu_custom_call" | custom-call | tf_op jit(solution)/shard_map/level0_up/pallas_call | solution.py:956
  (61 shorter events, 20.8 us)
Async XLA Ops:
  6.5 2.1 %copy-start = (f32[32,32,128]{2,1,0:T(8,128)S(1)}, f32[32,32,128]{2,1,0:T(8,128)}, u32[]{:S(2)}) copy-start(f32[32,32,128]{2,1,0:T(8,128)} %beta.1) | copy-start | bytes 1572868
  6.5 11.5 %copy-start.3 = (f32[32,32,128]{2,1,0:T(8,128)S(1)}, f32[32,32,128]{2,1,0:T(8,128)}, u32[]{:S(2)}) copy-start(f32[32,32,128]{2,1,0:T(8,128)} %src) | copy-start | bytes 1572868
  6.5 71.6 %all-gather.3.cloned.1.call-start = ((), (), s32[]{:S(2)}) async-start(), calls=%async_computation | async-start | bytes 1056768 | tf_op jit(solution)/shard_map/all_gather | solution.py:883
  9.8 7.2 %collective-permute-start = (f32[2,8,32,128]{3,2,1,0:T(8,128)S(1)}, f32[2,8,32,128]{3,2,1,0:T(8,128)S(1)}, u32[]{:S(2)}, u32[]{:S(2)}) collective-permute-start(f32[2,8,32,128]{3,2,1,0:T(8,128)S(1)} %get-tuple-element.57), channel_id=1, source_target_pairs={{0,32},{32,64},{64,96},{96,0},{1,33},{33,65},{65,97},{97,1},{2,34}... | collective-permute-start | bytes 786440 | tf_op jit(solution)/shard_map/ppermute | solution.py:866
  9.9 8.1 %collective-permute-start.1 = (f32[2,8,32,128]{3,2,1,0:T(8,128)S(1)}, f32[2,8,32,128]{3,2,1,0:T(8,128)S(1)}, u32[]{:S(2)}, u32[]{:S(2)}) collective-permute-start(f32[2,8,32,128]{3,2,1,0:T(8,128)S(1)} %get-tuple-element.58), channel_id=1, source_target_pairs={{0,96},{32,0},{64,32},{96,64},{1,97},{33,1},{65,33},{97,65},{2,98}... | collective-permute-start | bytes 786440 | tf_op jit(solution)/shard_map/ppermute | solution.py:866
  18.2 8.3 %collective-permute-start.2 = (f32[2,48,8,128]{3,2,1,0:T(8,128)S(1)}, f32[2,48,8,128]{3,2,1,0:T(8,128)S(1)}, u32[]{:S(2)}, u32[]{:S(2)}) collective-permute-start(f32[2,48,8,128]{3,2,1,0:T(8,128)S(1)} %get-tuple-element.61), channel_id=1, source_target_pairs={{0,4},{4,8},{8,12},{12,16},{16,20},{20,24},{24,28},{28,0},{1,5},{5... | collective-permute-start | bytes 1179656 | tf_op jit(solution)/shard_map/ppermute | solution.py:866
  21.7 7.6 %collective-permute-start.3 = (f32[2,48,8,128]{3,2,1,0:T(8,128)S(1)}, f32[2,48,8,128]{3,2,1,0:T(8,128)S(1)}, u32[]{:S(2)}, u32[]{:S(2)}) collective-permute-start(f32[2,48,8,128]{3,2,1,0:T(8,128)S(1)} %get-tuple-element.62), channel_id=1, source_target_pairs={{0,28},{4,0},{8,4},{12,8},{16,12},{20,16},{24,20},{28,24},{1,29},{... | collective-permute-start | bytes 1179656 | tf_op jit(solution)/shard_map/ppermute | solution.py:866
  30.9 6.5 %collective-permute-start.4 = (f32[6,48,128]{2,1,0:T(8,128)S(1)}, f32[6,48,128]{2,1,0:T(8,128)S(1)}, u32[]{:S(2)}, u32[]{:S(2)}) collective-permute-start(f32[6,48,128]{2,1,0:T(8,128)S(1)} %get-tuple-element.65), channel_id=1, source_target_pairs={{0,1},{1,2},{2,3},{3,0},{4,5},{5,6},{6,7},{7,4},{8,9},{9,10},{10,1... | collective-permute-start | bytes 442376 | tf_op jit(solution)/shard_map/ppermute | solution.py:866
  32.3 5.8 %collective-permute-start.5 = (f32[6,48,128]{2,1,0:T(8,128)S(1)}, f32[6,48,128]{2,1,0:T(8,128)S(1)}, u32[]{:S(2)}, u32[]{:S(2)}) collective-permute-start(f32[6,48,128]{2,1,0:T(8,128)S(1)} %get-tuple-element.66), channel_id=1, source_target_pairs={{0,3},{1,0},{2,1},{3,2},{4,7},{5,4},{6,5},{7,6},{8,11},{9,8},{10,9... | collective-permute-start | bytes 442376 | tf_op jit(solution)/shard_map/ppermute | solution.py:866
  54.6 17.8 %copy-start.9 = (f32[6,48,128]{2,1,0:T(8,128)}, f32[6,48,128]{2,1,0:T(8,128)S(1)}, u32[]{:S(2)}) copy-start(f32[6,48,128]{2,1,0:T(8,128)S(1)} %get-tuple-element.104.iterate_t) | copy-start | bytes 442372
  54.6 3.3 %collective-permute-start.6 = (f32[10,16,128]{2,1,0:T(8,128)S(1)}, f32[10,16,128]{2,1,0:T(8,128)S(1)}, u32[]{:S(2)}, u32[]{:S(2)}) collective-permute-start(f32[10,16,128]{2,1,0:T(8,128)S(1)} %get-tuple-element.68), channel_id=1, source_target_pairs={{0,32},{32,64},{64,96},{96,0},{1,33},{33,65},{65,97},{97,1},{2,34}... | collective-permute-start | bytes 245768 | tf_op jit(solution)/shard_map/ppermute | solution.py:866
  54.6 4.5 %collective-permute-start.7 = (f32[10,16,128]{2,1,0:T(8,128)S(1)}, f32[10,16,128]{2,1,0:T(8,128)S(1)}, u32[]{:S(2)}, u32[]{:S(2)}) collective-permute-start(f32[10,16,128]{2,1,0:T(8,128)S(1)} %get-tuple-element.69), channel_id=1, source_target_pairs={{0,96},{32,0},{64,32},{96,64},{1,97},{33,1},{65,33},{97,65},{2,98}... | collective-permute-start | bytes 245768 | tf_op jit(solution)/shard_map/ppermute | solution.py:866
  59.2 4.4 %collective-permute-start.8 = (f32[360,128]{1,0:T(8,128)S(1)}, f32[360,128]{1,0:T(8,128)S(1)}, u32[]{:S(2)}, u32[]{:S(2)}) collective-permute-start(f32[360,128]{1,0:T(8,128)S(1)} %get-tuple-element.70), channel_id=1, source_target_pairs={{0,4},{4,8},{8,12},{12,16},{16,20},{20,24},{24,28},{28,0},{1,5},{5... | collective-permute-start | bytes 552968 | tf_op jit(solution)/shard_map/ppermute | solution.py:866
  60.8 5.3 %collective-permute-start.9 = (f32[360,128]{1,0:T(8,128)S(1)}, f32[360,128]{1,0:T(8,128)S(1)}, u32[]{:S(2)}, u32[]{:S(2)}) collective-permute-start(f32[360,128]{1,0:T(8,128)S(1)} %get-tuple-element.71), channel_id=1, source_target_pairs={{0,28},{4,0},{8,4},{12,8},{16,12},{20,16},{24,20},{28,24},{1,29},{... | collective-permute-start | bytes 552968 | tf_op jit(solution)/shard_map/ppermute | solution.py:866
  66.9 5.2 %collective-permute-start.10 = (f32[6,40,128]{2,1,0:T(8,128)S(1)}, f32[6,40,128]{2,1,0:T(8,128)S(1)}, u32[]{:S(2)}, u32[]{:S(2)}) collective-permute-start(f32[6,40,128]{2,1,0:T(8,128)S(1)} %get-tuple-element.73), channel_id=1, source_target_pairs={{0,1},{1,2},{2,3},{3,0},{4,5},{5,6},{6,7},{7,4},{8,9},{9,10},{10,1... | collective-permute-start | bytes 368648 | tf_op jit(solution)/shard_map/ppermute | solution.py:866
  68.2 4.1 %collective-permute-start.11 = (f32[6,40,128]{2,1,0:T(8,128)S(1)}, f32[6,40,128]{2,1,0:T(8,128)S(1)}, u32[]{:S(2)}, u32[]{:S(2)}) collective-permute-start(f32[6,40,128]{2,1,0:T(8,128)S(1)} %get-tuple-element.74), channel_id=1, source_target_pairs={{0,3},{1,0},{2,1},{3,2},{4,7},{5,4},{6,5},{7,6},{8,11},{9,8},{10,9... | collective-permute-start | bytes 368648 | tf_op jit(solution)/shard_map/ppermute | solution.py:866
  78.2 4.7 %collective-permute-start.12 = (f32[16,128]{1,0:T(8,128)S(1)}, f32[16,128]{1,0:T(8,128)S(1)}, u32[]{:S(2)}, u32[]{:S(2)}) collective-permute-start(f32[16,128]{1,0:T(8,128)S(1)} %get-tuple-element.76.refs_0_), channel_id=1, source_target_pairs={{0,1},{1,2},{2,3},{3,0},{4,5},{5,6},{6,7},{7,4},{8,9},{9,10},{10,1... | collective-permute-start | bytes 24584 | tf_op jit(solution)/shard_map/ppermute | solution.py:866
  79.1 4.0 %collective-permute-start.13 = (f32[16,128]{1,0:T(8,128)S(1)}, f32[16,128]{1,0:T(8,128)S(1)}, u32[]{:S(2)}, u32[]{:S(2)}) collective-permute-start(f32[16,128]{1,0:T(8,128)S(1)} %get-tuple-element.76.refs_0_), channel_id=1, source_target_pairs={{0,2},{1,3},{2,0},{3,1},{4,6},{5,7},{6,4},{7,5},{8,10},{9,11},{10,... | collective-permute-start | bytes 24584 | tf_op jit(solution)/shard_map/ppermute | solution.py:866
  81.6 2.8 %collective-permute-start.14 = (f32[16,128]{1,0:T(8,128)S(1)}, f32[16,128]{1,0:T(8,128)S(1)}, u32[]{:S(2)}, u32[]{:S(2)}) collective-permute-start(f32[16,128]{1,0:T(8,128)S(1)} %get-tuple-element.76.refs_0_), channel_id=1, source_target_pairs={{0,3},{1,0},{2,1},{3,2},{4,7},{5,4},{6,5},{7,6},{8,11},{9,8},{10,9... | collective-permute-start | bytes 24584 | tf_op jit(solution)/shard_map/ppermute | solution.py:866
  84.5 2.8 %collective-permute-start.15 = (f32[8,8,128]{2,1,0:T(8,128)S(1)}, f32[8,8,128]{2,1,0:T(8,128)S(1)}, u32[]{:S(2)}, u32[]{:S(2)}) collective-permute-start(f32[8,8,128]{2,1,0:T(8,128)S(1)} %gather_z.1.refs_0_), channel_id=1, source_target_pairs={{0,32},{32,64},{64,96},{96,0},{1,33},{33,65},{65,97},{97,1},{2,34}... | collective-permute-start | bytes 98312 | tf_op jit(solution)/shard_map/ppermute | solution.py:866
  84.6 4.3 %collective-permute-start.16 = (f32[8,8,128]{2,1,0:T(8,128)S(1)}, f32[8,8,128]{2,1,0:T(8,128)S(1)}, u32[]{:S(2)}, u32[]{:S(2)}) collective-permute-start(f32[8,8,128]{2,1,0:T(8,128)S(1)} %gather_z.1.refs_0_), channel_id=1, source_target_pairs={{0,64},{32,96},{64,0},{96,32},{1,65},{33,97},{65,1},{97,33},{2,66}... | collective-permute-start | bytes 98312 | tf_op jit(solution)/shard_map/ppermute | solution.py:866
  86.4 4.0 %collective-permute-start.17 = (f32[8,8,128]{2,1,0:T(8,128)S(1)}, f32[8,8,128]{2,1,0:T(8,128)S(1)}, u32[]{:S(2)}, u32[]{:S(2)}) collective-permute-start(f32[8,8,128]{2,1,0:T(8,128)S(1)} %gather_z.1.refs_0_), channel_id=1, source_target_pairs={{0,96},{32,0},{64,32},{96,64},{1,97},{33,1},{65,33},{97,65},{2,98}... | collective-permute-start | bytes 98312 | tf_op jit(solution)/shard_map/ppermute | solution.py:866
  90.4 12.7 %collective-permute-start.18 = (f32[32,8,128]{2,1,0:T(8,128)S(1)}, f32[32,8,128]{2,1,0:T(8,128)S(1)}, u32[]{:S(2)}, u32[]{:S(2)}) collective-permute-start(f32[32,8,128]{2,1,0:T(8,128)S(1)} %gather_x.1.p0), channel_id=1, source_target_pairs={{0,4},{4,8},{8,12},{12,16},{16,20},{20,24},{24,28},{28,0},{1,5},{5... | collective-permute-start | bytes 393224 | tf_op jit(solution)/shard_map/ppermute | solution.py:866
  96.1 9.6 %collective-permute-start.19 = (f32[32,8,128]{2,1,0:T(8,128)S(1)}, f32[32,8,128]{2,1,0:T(8,128)S(1)}, u32[]{:S(2)}, u32[]{:S(2)}) collective-permute-start(f32[32,8,128]{2,1,0:T(8,128)S(1)} %gather_x.1.p0), channel_id=1, source_target_pairs={{0,8},{4,12},{8,16},{12,20},{16,24},{20,28},{24,0},{28,4},{1,9},{5... | collective-permute-start | bytes 393224 | tf_op jit(solution)/shard_map/ppermute | solution.py:866
  97.4 20.5 %collective-permute-start.20 = (f32[32,8,128]{2,1,0:T(8,128)S(1)}, f32[32,8,128]{2,1,0:T(8,128)S(1)}, u32[]{:S(2)}, u32[]{:S(2)}) collective-permute-start(f32[32,8,128]{2,1,0:T(8,128)S(1)} %gather_x.1.p0), channel_id=1, source_target_pairs={{0,12},{4,16},{8,20},{12,24},{16,28},{20,0},{24,4},{28,8},{1,13},{... | collective-permute-start | bytes 393224 | tf_op jit(solution)/shard_map/ppermute | solution.py:866
  99.5 18.4 %collective-permute-start.21 = (f32[32,8,128]{2,1,0:T(8,128)S(1)}, f32[32,8,128]{2,1,0:T(8,128)S(1)}, u32[]{:S(2)}, u32[]{:S(2)}) collective-permute-start(f32[32,8,128]{2,1,0:T(8,128)S(1)} %gather_x.1.p0), channel_id=1, source_target_pairs={{0,16},{4,20},{8,24},{12,28},{16,0},{20,4},{24,8},{28,12},{1,17},{... | collective-permute-start | bytes 393224 | tf_op jit(solution)/shard_map/ppermute | solution.py:866
  100.5 17.4 %collective-permute-start.22 = (f32[32,8,128]{2,1,0:T(8,128)S(1)}, f32[32,8,128]{2,1,0:T(8,128)S(1)}, u32[]{:S(2)}, u32[]{:S(2)}) collective-permute-start(f32[32,8,128]{2,1,0:T(8,128)S(1)} %gather_x.1.p0), channel_id=1, source_target_pairs={{0,20},{4,24},{8,28},{12,0},{16,4},{20,8},{24,12},{28,16},{1,21},{... | collective-permute-start | bytes 393224 | tf_op jit(solution)/shard_map/ppermute | solution.py:866
  103.1 14.8 %collective-permute-start.23 = (f32[32,8,128]{2,1,0:T(8,128)S(1)}, f32[32,8,128]{2,1,0:T(8,128)S(1)}, u32[]{:S(2)}, u32[]{:S(2)}) collective-permute-start(f32[32,8,128]{2,1,0:T(8,128)S(1)} %gather_x.1.p0), channel_id=1, source_target_pairs={{0,24},{4,28},{8,0},{12,4},{16,8},{20,12},{24,16},{28,20},{1,25},{... | collective-permute-start | bytes 393224 | tf_op jit(solution)/shard_map/ppermute | solution.py:866
  105.7 12.2 %collective-permute-start.24 = (f32[32,8,128]{2,1,0:T(8,128)S(1)}, f32[32,8,128]{2,1,0:T(8,128)S(1)}, u32[]{:S(2)}, u32[]{:S(2)}) collective-permute-start(f32[32,8,128]{2,1,0:T(8,128)S(1)} %gather_x.1.p0), channel_id=1, source_target_pairs={{0,28},{4,0},{8,4},{12,8},{16,12},{20,16},{24,20},{28,24},{1,29},{... | collective-permute-start | bytes 393224 | tf_op jit(solution)/shard_map/ppermute | solution.py:866
  117.9 9.3 %copy-start.6 = (f32[36,40,128]{2,1,0:T(8,128)S(1)}, f32[36,40,128]{2,1,0:T(8,128)}, u32[]{:S(2)}) copy-start(f32[36,40,128]{2,1,0:T(8,128)} %copy-done.5) | copy-start | bytes 2211844
  127.2 3.7 %copy-start.2 = (f32[48,48,128]{2,1,0:T(8,128)S(1)}, f32[48,48,128]{2,1,0:T(8,128)}, u32[]{:S(2)}) copy-start(f32[48,48,128]{2,1,0:T(8,128)} %copy-done.1) | copy-start | bytes 3538948
  127.2 3.7 %copy-start.10 = (f32[6,48,128]{2,1,0:T(8,128)S(1)}, f32[6,48,128]{2,1,0:T(8,128)}, u32[]{:S(2)}) copy-start(f32[6,48,128]{2,1,0:T(8,128)} %copy-done.9) | copy-start | bytes 442372
  (5 other events, 4.7 us)
Sparse Core Ops, SparseCore 0:
  10.1 64.8 all-gather.2

commit v4 on v3

--- a/solution.py
+++ b/solution.py
@@ -180,17 +180,14 @@
 
 def strip_z(strip, ghost, xx, lane):
     here = strip[xx, 8:56, :]
-    up = roll(jnp.where(lane % 16 == 8, ghost[xx], here), -1)
-    down = roll(jnp.where(lane % 16 == 7, ghost[xx], here), 1)
+    up = jnp.where(lane % 16 == 8, ghost[xx], roll(here, 1))
+    down = jnp.where(lane % 16 == 7, ghost[xx], roll(here, -1))
     return down, up
 
 
-def block_z(value, strip, x, lane, first=8, count=48):
+def block_edge(strip, x, first=8, count=48):
     g = x // 6
-    edge = roll(strip[x - g * 6, first : first + count, :], 120 - g * 16)
-    up = roll(jnp.where(lane == 0, edge, value), -1)
-    down = roll(jnp.where(lane == 127, edge, value), 1)
-    return down, up
+    return roll(strip[x - g * 6, first : first + count, :], 120 - g * 16)
 
 
 def weights(here, sides):
@@ -206,7 +203,9 @@
 
     def body(x):
         here = b_pad[x + 1, 8:56, :]
-        down, up = block_z(here, bt_pad, x, lane)
+        edge = block_edge(bt_pad, x)
+        down = jnp.where(lane == 0, edge, roll(here, 1))
+        up = jnp.where(lane == 127, edge, roll(here, -1))
         faces, inverse, tot = weights(
             here,
             (
@@ -218,8 +217,11 @@
                 up,
             ),
         )
-        for i in range(6):
+        for i in range(4):
             g_main[i, x] = faces[i]
+        g_main[4, x] = jnp.where(lane == 0, 0.0, faces[4])
+        g_main[5, x] = jnp.where(lane == 127, 0.0, faces[5])
+        g_main[6, x] = jnp.where(lane == 0, faces[4], jnp.where(lane == 127, faces[5], 0.0))
         sp[x] = src[x] * (2.0 * inverse)
         if total is not None:
             total[x] = tot
@@ -237,18 +239,18 @@
         sp_t[xx] = src_t[xx] * (2.0 * inverse)
 
 
-def block_rest(v, t, g_main, sp, x, lane, skip=0):
+def block_rest(v, t, g_main, sp, x, skip=0):
     count = 48 - 2 * skip
     first = 8 + skip
     keep = slice(skip, 48 - skip)
     here = v[x + 1, first : first + count, :]
-    down, up = block_z(here, t, x, lane, first, count)
     rest = sp[x, keep] - here
     rest = rest + g_main[0, x, keep] * v[x, first : first + count, :]
     rest = rest + g_main[1, x, keep] * v[x + 2, first : first + count, :]
     rest = rest + g_main[2, x, keep] * v[x + 1, first - 1 : first - 1 + count, :]
     rest = rest + g_main[3, x, keep] * v[x + 1, first + 1 : first + 1 + count, :]
-    rest = rest + g_main[4, x, keep] * down + g_main[5, x, keep] * up
+    rest = rest + g_main[4, x, keep] * roll(here, 1) + g_main[5, x, keep] * roll(here, -1)
+    rest = rest + g_main[6, x, keep] * block_edge(t, x, first, count)
     return here, rest
 
 
@@ -257,14 +259,14 @@
     lane = lanes_of(48)
 
     def body(x):
-        here, rest = block_rest(v, t, g_main, sp, x, lane)
+        here, rest = block_rest(v, t, g_main, sp, x)
         new = factor * rest
         if retain is not None:
             new = retain * u[x] + new
         u[x] = new
         v_out[x + 1, 8:56, :] = here + new
 
-    loop(low, high, 4, body)
+    loop(low, high, 6, body)
     for xx in range(6):
         here = t[xx, 8:56, :]
         before, after = strip_sides(t, xx)
@@ -302,12 +304,17 @@
     iz = lax.axis_index("gz")
     low = flag(iz > 0)
     high = flag(iz < lax.axis_size("gz") - 1)
-    lower = lanes_of(48) % 16 < 8
+
+    def mirror(first, last):
+        return pick(lambda r, c: (r // 16 == c // 16) & ((r % 16 < 8) == first) & (r % 16 + c % 16 == last))
+
+    s_lo, s_hi = mirror(True, 15), mirror(True, 7)
+    b_lo, b_hi = mirror(False, 23), mirror(False, 15)
     for xx in range(6):
         before = z_lo[xx] * low
         after = z_hi[xx] * high
-        src_t[xx] = jnp.where(lower, before, roll(after, 8))
-        bt_pad[xx, 8:56, :] = jnp.where(lower, roll(before, -8), after)
+        src_t[xx] = dot(before, s_lo) + dot(after, s_hi)
+        bt_pad[xx, 8:56, :] = dot(before, b_lo) + dot(after, b_hi)
 
 
 LEVEL0_SCRATCH = [
@@ -318,7 +325,7 @@
     vm(6, 64, 128),
     vm(6, 64, 128),
     vm(6, 48, 128),
-    vm(6, 48, 48, 128),
+    vm(7, 48, 48, 128),
     vm(6, 6, 48, 128),
     vm(48, 48, 128),
     vm(6, 48, 128),
@@ -354,16 +361,13 @@
     for k in range(1, SMOOTH):
         (v, t), (w, s) = bufs
         retain, factor = RECIPE[k]
-        level0_step(v, t, w, s, ghost, g_main, g_strip, sp, sp_t, u, u_t, k, 48 - k, retain, factor)
-        for x in [*range(k), *range(48 - k, 48)]:
-            w[x + 1, 8:56, :] = v[x + 1, 8:56, :]
+        level0_step(v, t, w, s, ghost, g_main, g_strip, sp, sp_t, u, u_t, 0, 48, retain, factor)
         bufs = [(w, s), (v, t)]
     v, t = bufs[0]
     iter_out[...] = v[1:49, 8:56, :]
     for xx in range(6):
         iter_t_out[xx] = t[xx, 8:56, :]
 
-    lane = lanes_of(32)
     to_low = pick(lambda r, c: r // 2 == c)
     to_high = pick(lambda r, c: r // 2 + 64 == c)
 
@@ -371,7 +375,7 @@
         parts = []
         for half in range(2):
             x = 8 + 2 * x2 + half
-            _, rest = block_rest(v, t, g_main, sp, x, lane, 8)
+            _, rest = block_rest(v, t, g_main, sp, x, 8)
             parts.append(rest * total[x, 8:40])
         rows[0, x2] = (parts[0] + parts[1]) * (0.5 / 8.0)
         rows[1, x2] = (b_pad[9 + 2 * x2, 16:48, :] + b_pad[10 + 2 * x2, 16:48, :]) * (1.0 / 8.0)
@@ -827,7 +831,10 @@
         for k in range(8):
             to = pick(
                 lambda r, c: (c // 16 == k)
-                & (((c % 16 < 8) & (r == 124 + (c % 16) // 2)) | ((c % 16 >= 8) & (r == 64 + (c % 16 - 8) // 2)))
+                & (
+                    ((c % 16 < 8) & (r == 64 + (7 - c % 16) // 2))
+                    | ((c % 16 >= 8) & (r == 124 + (15 - c % 16) // 2))
+                )
             )
             acc = acc + dot(c1[k * 3 + m], to)
         rows[m, pl.ds(0, 24, stride=2), :] = acc
@@ -837,6 +844,8 @@
             ta[xx, 8:56, :] = jnp.where(beta_t[xx] > 0.0, iterate_t[xx] + rows[m], 0.0)
 
     loop(0, 3, 36, prolong_strip)
+    for x in [*range(6), *range(42, 48)]:
+        vb[x + 1, 8:56, :] = jnp.zeros((48, 128), F32)
     bufs = [(va, ta), (vb, tb)]
     for k in range(SMOOTH):
         (v, t), (w, s) = bufs
@@ -844,17 +853,14 @@
         if k == 0:
             retain = None
         if k < SMOOTH - 1:
-            low, high = 4 + k, 44 - k
+            low, high = (4, 44) if k < 2 else (6, 42)
             level0_step(
                 v, t, w, s, ghost, g_main, g_strip, sp, sp_t, u, u_t, low, high, retain, factor
             )
-            for x in [*range(low), *range(high, 48)]:
-                w[x + 1, 8:56, :] = v[x + 1, 8:56, :]
         else:
-            lane = lanes_of(32)
 
             def last(x):
-                here, rest = block_rest(v, t, g_main, sp, x, lane, 8)
+                here, rest = block_rest(v, t, g_main, sp, x, 8)
                 out[x - 8] = here + retain * u[x, 8:40] + factor * rest
 
             loop(8, 40, 4, last)
@@ -898,7 +904,7 @@
         (whole, strip, sds(16, 16, 128), sds(10, 16, 128), sds(10, 16, 128)),
         LEVEL0_SCRATCH + [vm(48, 48, 128), vm(2, 16, 32, 128)],
         name="level0_down",
-        mib=24,
+        mib=26,
     )(src_ext, beta_ext, z_lo, z_hi)
     x_lo, x_hi = trade(lo, hi, "gx")
     lo, hi = call(pack1_y, (sds(360, 128), sds(360, 128)), name="pack1_y")(c, x_lo, x_hi)
@@ -940,7 +946,7 @@
     parts = around(slab, "gy")
     ready = call(
         level0_prepare,
-        (sds(6, 48, 48, 128), sds(6, 6, 48, 128), whole, strip, strip),
+        (sds(7, 48, 48, 128), sds(6, 6, 48, 128), whole, strip, strip),
         [vm(50, 64, 128), vm(6, 64, 128), vm(6, 48, 128), vm(6, 48, 128)],
         name="level0_prepare",
         mib=6,

time: 153 us -> 151 us (0.987)
  Pallas kernels: 59.9 us -> 54.2 us
  waiting for transfers between devices: 37.7 us -> 43.2 us
    ppermute x25, waiting for transfers between devices: 37.7 us -> 43.2 us  [ring(): lax.ppermute(value, axis, [(i, (i + step) % count) for i in range(count)])]
    pallas_call x1, Pallas kernels: 13.5 us -> 9.9 us  [per_device(): call(level0_up, sds(32, 32, 128), [vm(50, 64, 128), vm(50, 64, 128), vm(6...]
    pallas_call x1, Pallas kernels: 15.4 us -> 12.4 us  [per_device(): call(level0_down, (whole, strip, sds(16, 16, 128), sds(10, 16, 128), sds(...]
  transfers between devices with their start and end apart: 26 -> 26, of which waited for: 18 -> 18; matrix products, arithmetic and copies ran while one was open for 0% -> 0% of each run, Pallas kernels for 21% -> 20%
where the time goes in v4:
time: 151 us
  Pallas kernels  54.2 us (36%)
  waiting for transfers between devices  43.2 us (29%)
  starting transfers between devices  32.7 us (22%)
  between operations  13.6 us (9%)
  local copies, waits for them, and re-layouts  6.78 us (4%)
    ppermute x25, waiting for transfers between devices, ring(): lax.ppermute(value, axis, [(i, (i + step) % count) for i in range(count)])  43.2 us
    ppermute x25, starting transfers between devices, ring(): lax.ppermute(value, axis, [(i, (i + step) % count) for i in range(count)])  32.7 us
    pallas_call x1, Pallas kernels, per_device(): call(level0_down, (whole, strip, sds(16, 16, 128), sds(10, 16, 128), sds(...  12.4 us
    pallas_call x1, Pallas kernels, per_device(): call(level0_up, sds(32, 32, 128), [vm(50, 64, 128), vm(50, 64, 128), vm(6...  9.9 us
    pallas_call x1, Pallas kernels, per_device(): call(bottom, sds(18, 24, 128), BOTTOM_SCRATCH, name='bottom', mib=18)  9.26 us
    pallas_call x1, Pallas kernels, per_device(): call(coarse_prepare, tuple((sds(*shape) for shape in COARSE_SHAPES)), COA...  4.8 us
    unnamed x22, local copies, waits for them, and re-layouts  4.72 us
    pallas_call x1, Pallas kernels, per_device(): call(level1_down, (sds(36, 40, 128), sds(16, 128)), LEVEL1_SCRATCH + [vm(...  4.25 us
  transfers between devices with their start and end apart: 26, of which 18 were waited for; matrix products, arithmetic and copies ran while one was open for 0% of the time, Pallas kernels for 20%

profile of v4, /device:TPU:7, one launch (start us, length us, event | category | flops | bytes accessed | tf_op | source)
XLA Modules:
  0.0 150.6 jit_solution(9113050625756495979)
XLA Ops:
  9.9 1.5 collective-permute-start.1
  11.4 5.7 %collective-permute-done.from_lo = f32[2,8,32,128]{3,2,1,0:T(8,128)S(1)} collective-permute-done((f32[2,8,32,128]{3,2,1,0:T(8,128)S(1)}, f32[2,8,32,128]{3,2,1,0:T(8,128)S(1)}, u32[]{:S(2)}, u32[]{:S(2)}) %collective-permute-start) | collective-permute-done | bytes 262176 | tf_op jit(solution)/shard_map/ppermute | solution.py:872
  18.2 3.6 %collective-permute-start.2 = (f32[2,48,8,128]{3,2,1,0:T(8,128)S(1)}, f32[2,48,8,128]{3,2,1,0:T(8,128)S(1)}, u32[]{:S(2)}, u32[]{:S(2)}) collective-permute-start(f32[2,48,8,128]{3,2,1,0:T(8,128)S(1)} %get-tuple-element.61), channel_id=1, source_target_pairs={{0,4},{4,8},{8,12},{12,16},{16,20},{20,24},{24,28},{28,0},{1,5},{5... | collective-permute-start | bytes 1179656 | tf_op jit(solution)/shard_map/ppermute | solution.py:872
  21.7 4.7 %collective-permute-done.2.y_lo = f32[2,48,8,128]{3,2,1,0:T(8,128)S(1)} collective-permute-done((f32[2,48,8,128]{3,2,1,0:T(8,128)S(1)}, f32[2,48,8,128]{3,2,1,0:T(8,128)S(1)}, u32[]{:S(2)}, u32[]{:S(2)}) %collective-permute-start.2) | collective-permute-done | bytes 393248 | tf_op jit(solution)/shard_map/ppermute | solution.py:872
  26.5 2.9 %collective-permute-done.3.y_hi = f32[2,48,8,128]{3,2,1,0:T(8,128)S(1)} collective-permute-done((f32[2,48,8,128]{3,2,1,0:T(8,128)S(1)}, f32[2,48,8,128]{3,2,1,0:T(8,128)S(1)}, u32[]{:S(2)}, u32[]{:S(2)}) %collective-permute-start.3) | collective-permute-done | bytes 393248 | tf_op jit(solution)/shard_map/ppermute | solution.py:872
  29.4 1.5 pack_z.1
  30.9 1.4 collective-permute-start.4
  32.3 1.5 %collective-permute-start.5 = (f32[6,48,128]{2,1,0:T(8,128)S(1)}, f32[6,48,128]{2,1,0:T(8,128)S(1)}, u32[]{:S(2)}, u32[]{:S(2)}) collective-permute-start(f32[6,48,128]{2,1,0:T(8,128)S(1)} %get-tuple-element.66), channel_id=1, source_target_pairs={{0,3},{1,0},{2,1},{3,2},{4,7},{5,4},{6,5},{7,6},{8,11},{9,8},{10,9... | collective-permute-start | bytes 442376 | tf_op jit(solution)/shard_map/ppermute | solution.py:872
  33.8 3.6 %collective-permute-done.4.z_lo = f32[6,48,128]{2,1,0:T(8,128)S(1)} collective-permute-done((f32[6,48,128]{2,1,0:T(8,128)S(1)}, f32[6,48,128]{2,1,0:T(8,128)S(1)}, u32[]{:S(2)}, u32[]{:S(2)}) %collective-permute-start.4) | collective-permute-done | bytes 147488 | tf_op jit(solution)/shard_map/ppermute | solution.py:872
  38.1 12.4 %level0_down.1 = (f32[48,48,128]{2,1,0:T(8,128)S(1)}, f32[6,48,128]{2,1,0:T(8,128)S(1)}, f32[16,16,128]{2,1,0:T(8,128)S(1)}, f32[10,16,128]{2,1,0:T(8,128)S(1)}, f32[10,16,128]{2,1,0:T(8,128)S(1)}) custom-call(f32[48,48,128]{2,1,0:T(8,128)S(1)} %get-tuple-element.95.src, f32[48,48,128]{2,1,0:T(8,128)S(1)} %get-tuple-element.94.beta, ...), custom_call_target="tpu_custom_call" | custom-call | tf_op jit(solution)/shard_map/level0_down/pallas_call | solution.py:902
  51.6 1.5 collective-permute-start.7
  53.0 1.8 %collective-permute-done.6.from_lo.x_lo = f32[10,16,128]{2,1,0:T(8,128)S(1)} collective-permute-done((f32[10,16,128]{2,1,0:T(8,128)S(1)}, f32[10,16,128]{2,1,0:T(8,128)S(1)}, u32[]{:S(2)}, u32[]{:S(2)}) %collective-permute-start.6) | collective-permute-done | bytes 81952 | tf_op jit(solution)/shard_map/ppermute | solution.py:872
  56.1 1.6 %collective-permute-start.8 = (f32[360,128]{1,0:T(8,128)S(1)}, f32[360,128]{1,0:T(8,128)S(1)}, u32[]{:S(2)}, u32[]{:S(2)}) collective-permute-start(f32[360,128]{1,0:T(8,128)S(1)} %get-tuple-element.70), channel_id=1, source_target_pairs={{0,4},{4,8},{8,12},{12,16},{16,20},{20,24},{24,28},{28,0},{1,5},{5... | collective-permute-start | bytes 552968 | tf_op jit(solution)/shard_map/ppermute | solution.py:872
  57.8 2.5 %collective-permute-done.8.y_lo = f32[360,128]{1,0:T(8,128)S(1)} collective-permute-done((f32[360,128]{1,0:T(8,128)S(1)}, f32[360,128]{1,0:T(8,128)S(1)}, u32[]{:S(2)}, u32[]{:S(2)}) %collective-permute-start.8) | collective-permute-done | bytes 184352 | tf_op jit(solution)/shard_map/ppermute | solution.py:872
  60.2 2.9 %collective-permute-done.9.y_hi = f32[360,128]{1,0:T(8,128)S(1)} collective-permute-done((f32[360,128]{1,0:T(8,128)S(1)}, f32[360,128]{1,0:T(8,128)S(1)}, u32[]{:S(2)}, u32[]{:S(2)}) %collective-permute-start.9) | collective-permute-done | bytes 184352 | tf_op jit(solution)/shard_map/ppermute | solution.py:872
  65.3 1.4 collective-permute-start.11
  66.7 2.9 %collective-permute-done.10.z_lo = f32[6,40,128]{2,1,0:T(8,128)S(1)} collective-permute-done((f32[6,40,128]{2,1,0:T(8,128)S(1)}, f32[6,40,128]{2,1,0:T(8,128)S(1)}, u32[]{:S(2)}, u32[]{:S(2)}) %collective-permute-start.10) | collective-permute-done | bytes 122912 | tf_op jit(solution)/shard_map/ppermute | solution.py:872
  69.6 4.2 %level1_down.1 = (f32[36,40,128]{2,1,0:T(8,128)S(1)}, f32[16,128]{1,0:T(8,128)S(1)}) custom-call(f32[36,40,128]{2,1,0:T(8,128)S(1)} %get-tuple-element.87.ext, f32[6,40,128]{2,1,0:T(8,128)S(1)} %collective-permute-done.10.z_lo, f32[6,40,128]{2,1,0:T(8,128)S(1)} %collective-permute-done.11.z_hi), custom_call_target="tpu_custom_call" | custom-call | tf_op jit(solution)/shard_map/level1_down/pallas_call | solution.py:916
  76.3 2.3 %collective-permute-start.13 = (f32[16,128]{1,0:T(8,128)S(1)}, f32[16,128]{1,0:T(8,128)S(1)}, u32[]{:S(2)}, u32[]{:S(2)}) collective-permute-start(f32[16,128]{1,0:T(8,128)S(1)} %get-tuple-element.76.refs_0_), channel_id=1, source_target_pairs={{0,2},{1,3},{2,0},{3,1},{4,6},{5,7},{6,4},{7,5},{8,10},{9,11},{10,... | collective-permute-start | bytes 24584 | tf_op jit(solution)/shard_map/ppermute | solution.py:872
  81.7 1.6 %collective-permute-start.16 = (f32[8,8,128]{2,1,0:T(8,128)S(1)}, f32[8,8,128]{2,1,0:T(8,128)S(1)}, u32[]{:S(2)}, u32[]{:S(2)}) collective-permute-start(f32[8,8,128]{2,1,0:T(8,128)S(1)} %gather_z.1.refs_0_), channel_id=1, source_target_pairs={{0,64},{32,96},{64,0},{96,32},{1,65},{33,97},{65,1},{97,33},{2,66}... | collective-permute-start | bytes 98312 | tf_op jit(solution)/shard_map/ppermute | solution.py:872
  84.3 1.6 %collective-permute-done.16.refs_2_ = f32[8,8,128]{2,1,0:T(8,128)S(1)} collective-permute-done((f32[8,8,128]{2,1,0:T(8,128)S(1)}, f32[8,8,128]{2,1,0:T(8,128)S(1)}, u32[]{:S(2)}, u32[]{:S(2)}) %collective-permute-start.16) | collective-permute-done | bytes 32800 | tf_op jit(solution)/shard_map/ppermute | solution.py:872
  87.3 4.8 %collective-permute-start.18 = (f32[32,8,128]{2,1,0:T(8,128)S(1)}, f32[32,8,128]{2,1,0:T(8,128)S(1)}, u32[]{:S(2)}, u32[]{:S(2)}) collective-permute-start(f32[32,8,128]{2,1,0:T(8,128)S(1)} %gather_x.1.p0), channel_id=1, source_target_pairs={{0,4},{4,8},{8,12},{12,16},{16,20},{20,24},{24,28},{28,0},{1,5},{5... | collective-permute-start | bytes 393224 | tf_op jit(solution)/shard_map/ppermute | solution.py:872
  93.5 2.1 %collective-permute-start.20 = (f32[32,8,128]{2,1,0:T(8,128)S(1)}, f32[32,8,128]{2,1,0:T(8,128)S(1)}, u32[]{:S(2)}, u32[]{:S(2)}) collective-permute-start(f32[32,8,128]{2,1,0:T(8,128)S(1)} %gather_x.1.p0), channel_id=1, source_target_pairs={{0,12},{4,16},{8,20},{12,24},{16,28},{20,0},{24,4},{28,8},{1,13},{... | collective-permute-start | bytes 393224 | tf_op jit(solution)/shard_map/ppermute | solution.py:872
  95.5 1.7 %collective-permute-start.21 = (f32[32,8,128]{2,1,0:T(8,128)S(1)}, f32[32,8,128]{2,1,0:T(8,128)S(1)}, u32[]{:S(2)}, u32[]{:S(2)}) collective-permute-start(f32[32,8,128]{2,1,0:T(8,128)S(1)} %gather_x.1.p0), channel_id=1, source_target_pairs={{0,16},{4,20},{8,24},{12,28},{16,0},{20,4},{24,8},{28,12},{1,17},{... | collective-permute-start | bytes 393224 | tf_op jit(solution)/shard_map/ppermute | solution.py:872
  97.3 2.6 %collective-permute-start.22 = (f32[32,8,128]{2,1,0:T(8,128)S(1)}, f32[32,8,128]{2,1,0:T(8,128)S(1)}, u32[]{:S(2)}, u32[]{:S(2)}) collective-permute-start(f32[32,8,128]{2,1,0:T(8,128)S(1)} %gather_x.1.p0), channel_id=1, source_target_pairs={{0,20},{4,24},{8,28},{12,0},{16,4},{20,8},{24,12},{28,16},{1,21},{... | collective-permute-start | bytes 393224 | tf_op jit(solution)/shard_map/ppermute | solution.py:872
  99.9 7.7 %collective-permute-done.19.p2 = f32[32,8,128]{2,1,0:T(8,128)S(1)} collective-permute-done((f32[32,8,128]{2,1,0:T(8,128)S(1)}, f32[32,8,128]{2,1,0:T(8,128)S(1)}, u32[]{:S(2)}, u32[]{:S(2)}) %collective-permute-start.19) | collective-permute-done | bytes 131104 | tf_op jit(solution)/shard_map/ppermute | solution.py:872
  108.8 4.8 %coarse_prepare.1 = (f32[6,32,64,128]{3,2,1,0:T(8,128)S(1)}, f32[32,64,128]{2,1,0:T(8,128)S(1)}, f32[32,64,128]{2,1,0:T(8,128)S(1)}, f32[6,16,32,128]{3,2,1,0:T(...) custom-call(f32[128,16,128]{2,1,0:T(8,128)S(1)} %bitcast.9), custom_call_target="tpu_custom_call" | custom-call | tf_op jit(solution)/shard_map/coarse_prepare/pallas_call | solution.py:925
  114.6 2.2 %level1_prepare.1 = (f32[6,36,40,128]{3,2,1,0:T(8,128)S(1)}, f32[36,40,128]{2,1,0:T(8,128)S(1)}, f32[36,40,128]{2,1,0:T(8,128)S(1)}) custom-call(f32[36,40,128]{2,1,0:T(8,128)S(1)} %get-tuple-element.87.ext, f32[6,40,128]{2,1,0:T(8,128)S(1)} %collective-permute-done.10.z_lo, f32[6,40,128]{2,1,0:T(8,128)S(1)} %copy-done.8), custom_call_target="tpu_custom_call" | custom-call | tf_op jit(solution)/shard_map/level1_prepare/pallas_call | solution.py:935
  116.8 4.0 %level0_prepare.1 = (f32[7,48,48,128]{3,2,1,0:T(8,128)S(1)}, f32[6,6,48,128]{3,2,1,0:T(8,128)S(1)}, f32[48,48,128]{2,1,0:T(8,128)S(1)}, f32[6,48,128]{2,1,0:T(8,128)S(1)}, f32[6,48,128]{2,1,0:T(8,128)S(1)}) custom-call(f32[48,48,128]{2,1,0:T(8,128)S(1)} %get-tuple-element.95.src, f32[48,48,128]{2,1,0:T(8,128)S(1)} %get-tuple-element.94.beta, ...), custom_call_target="tpu_custom_call" | custom-call | tf_op jit(solution)/shard_map/level0_prepare/pallas_call | solution.py:947
  120.9 9.3 %bottom.1.c2 = f32[18,24,128]{2,1,0:T(8,128)S(1)} custom-call(f32[32,8,128]{2,1,0:T(8,128)S(1)} %gather_x.1.p0, f32[32,8,128]{2,1,0:T(8,128)S(1)} %collective-permute-done.18.p1, f32[32,8,128]{2,1,0:T(8,128)S(1)} %collective-permute-done.19.p2, f32[32,8,128]{2,1,0:T(8,128)S(1)} %collective-permute-done.20.p3, f32[32,8,128]{2,1,0:T(8,128)S(1)} %collective-permute-done.21.p4, ...), custom_call_target="tpu_custom_call" | custom-call | tf_op jit(solution)/shard_map/bottom/pallas_call | solution.py:954
  130.2 3.7 %level1_up.1.c1 = f32[24,24,128]{2,1,0:T(8,128)S(1)} custom-call(f32[18,24,128]{2,1,0:T(8,128)S(1)} %bottom.1.c2, f32[6,36,40,128]{3,2,1,0:T(8,128)S(1)} %get-tuple-element.90.g, f32[36,40,128]{2,1,0:T(8,128)S(1)} %get-tuple-element.91.sp, f32[36,40,128]{2,1,0:T(8,128)S(1)} %get-tuple-element.92.beta, f32[36,40,128]{2,1,0:T(8,128)S(1)} %copy-done.6), custom_call_target="tpu_custom_call" | custom-call | tf_op jit(solution)/shard_map/level1_up/pallas_call | solution.py:955
  133.8 9.9 %level0_up.1 = f32[32,32,128]{2,1,0:T(8,128)} custom-call(f32[24,24,128]{2,1,0:T(8,128)S(1)} %level1_up.1.c1, f32[48,48,128]{2,1,0:T(8,128)S(1)} %get-tuple-element.94.beta, f32[7,48,48,128]{3,2,1,0:T(8,128)S(1)} %get-tuple-element.98.g_main, f32[6,6,48,128]{3,2,1,0:T(8,128)S(1)} %get-tuple-element.99.g_strip, f32[48,48,128]{2,1,0:T(8,128)S(1)} %get-tuple-element.100.sp, ...), custom_call_target="tpu_custom_call" | custom-call | tf_op jit(solution)/shard_map/level0_up/pallas_call | solution.py:962
  (61 shorter events, 21.1 us)
Async XLA Ops:
  6.5 2.1 %copy-start = (f32[32,32,128]{2,1,0:T(8,128)S(1)}, f32[32,32,128]{2,1,0:T(8,128)}, u32[]{:S(2)}) copy-start(f32[32,32,128]{2,1,0:T(8,128)} %beta.1) | copy-start | bytes 1572868
  6.5 11.5 %copy-start.1 = (f32[32,32,128]{2,1,0:T(8,128)S(1)}, f32[32,32,128]{2,1,0:T(8,128)}, u32[]{:S(2)}) copy-start(f32[32,32,128]{2,1,0:T(8,128)} %src) | copy-start | bytes 1572868
  6.5 68.9 %all-gather.3.cloned.1.call-start = ((), (), s32[]{:S(2)}) async-start(), calls=%async_computation | async-start | bytes 1056768 | tf_op jit(solution)/shard_map/all_gather | solution.py:889
  9.8 7.2 %collective-permute-start = (f32[2,8,32,128]{3,2,1,0:T(8,128)S(1)}, f32[2,8,32,128]{3,2,1,0:T(8,128)S(1)}, u32[]{:S(2)}, u32[]{:S(2)}) collective-permute-start(f32[2,8,32,128]{3,2,1,0:T(8,128)S(1)} %get-tuple-element.57), channel_id=1, source_target_pairs={{0,32},{32,64},{64,96},{96,0},{1,33},{33,65},{65,97},{97,1},{2,34}... | collective-permute-start | bytes 786440 | tf_op jit(solution)/shard_map/ppermute | solution.py:872
  9.9 8.1 %collective-permute-start.1 = (f32[2,8,32,128]{3,2,1,0:T(8,128)S(1)}, f32[2,8,32,128]{3,2,1,0:T(8,128)S(1)}, u32[]{:S(2)}, u32[]{:S(2)}) collective-permute-start(f32[2,8,32,128]{3,2,1,0:T(8,128)S(1)} %get-tuple-element.58), channel_id=1, source_target_pairs={{0,96},{32,0},{64,32},{96,64},{1,97},{33,1},{65,33},{97,65},{2,98}... | collective-permute-start | bytes 786440 | tf_op jit(solution)/shard_map/ppermute | solution.py:872
  18.2 8.3 %collective-permute-start.2 = (f32[2,48,8,128]{3,2,1,0:T(8,128)S(1)}, f32[2,48,8,128]{3,2,1,0:T(8,128)S(1)}, u32[]{:S(2)}, u32[]{:S(2)}) collective-permute-start(f32[2,48,8,128]{3,2,1,0:T(8,128)S(1)} %get-tuple-element.61), channel_id=1, source_target_pairs={{0,4},{4,8},{8,12},{12,16},{16,20},{20,24},{24,28},{28,0},{1,5},{5... | collective-permute-start | bytes 1179656 | tf_op jit(solution)/shard_map/ppermute | solution.py:872
  21.7 7.6 %collective-permute-start.3 = (f32[2,48,8,128]{3,2,1,0:T(8,128)S(1)}, f32[2,48,8,128]{3,2,1,0:T(8,128)S(1)}, u32[]{:S(2)}, u32[]{:S(2)}) collective-permute-start(f32[2,48,8,128]{3,2,1,0:T(8,128)S(1)} %get-tuple-element.62), channel_id=1, source_target_pairs={{0,28},{4,0},{8,4},{12,8},{16,12},{20,16},{24,20},{28,24},{1,29},{... | collective-permute-start | bytes 1179656 | tf_op jit(solution)/shard_map/ppermute | solution.py:872
  30.9 6.5 %collective-permute-start.4 = (f32[6,48,128]{2,1,0:T(8,128)S(1)}, f32[6,48,128]{2,1,0:T(8,128)S(1)}, u32[]{:S(2)}, u32[]{:S(2)}) collective-permute-start(f32[6,48,128]{2,1,0:T(8,128)S(1)} %get-tuple-element.65), channel_id=1, source_target_pairs={{0,1},{1,2},{2,3},{3,0},{4,5},{5,6},{6,7},{7,4},{8,9},{9,10},{10,1... | collective-permute-start | bytes 442376 | tf_op jit(solution)/shard_map/ppermute | solution.py:872
  32.3 5.8 %collective-permute-start.5 = (f32[6,48,128]{2,1,0:T(8,128)S(1)}, f32[6,48,128]{2,1,0:T(8,128)S(1)}, u32[]{:S(2)}, u32[]{:S(2)}) collective-permute-start(f32[6,48,128]{2,1,0:T(8,128)S(1)} %get-tuple-element.66), channel_id=1, source_target_pairs={{0,3},{1,0},{2,1},{3,2},{4,7},{5,4},{6,5},{7,6},{8,11},{9,8},{10,9... | collective-permute-start | bytes 442376 | tf_op jit(solution)/shard_map/ppermute | solution.py:872
  51.6 18.1 %copy-start.9 = (f32[6,48,128]{2,1,0:T(8,128)}, f32[6,48,128]{2,1,0:T(8,128)S(1)}, u32[]{:S(2)}) copy-start(f32[6,48,128]{2,1,0:T(8,128)S(1)} %get-tuple-element.104.iterate_t) | copy-start | bytes 442372
  51.6 3.3 %collective-permute-start.6 = (f32[10,16,128]{2,1,0:T(8,128)S(1)}, f32[10,16,128]{2,1,0:T(8,128)S(1)}, u32[]{:S(2)}, u32[]{:S(2)}) collective-permute-start(f32[10,16,128]{2,1,0:T(8,128)S(1)} %get-tuple-element.68), channel_id=1, source_target_pairs={{0,32},{32,64},{64,96},{96,0},{1,33},{33,65},{65,97},{97,1},{2,34}... | collective-permute-start | bytes 245768 | tf_op jit(solution)/shard_map/ppermute | solution.py:872
  51.6 4.5 %collective-permute-start.7 = (f32[10,16,128]{2,1,0:T(8,128)S(1)}, f32[10,16,128]{2,1,0:T(8,128)S(1)}, u32[]{:S(2)}, u32[]{:S(2)}) collective-permute-start(f32[10,16,128]{2,1,0:T(8,128)S(1)} %get-tuple-element.69), channel_id=1, source_target_pairs={{0,96},{32,0},{64,32},{96,64},{1,97},{33,1},{65,33},{97,65},{2,98}... | collective-permute-start | bytes 245768 | tf_op jit(solution)/shard_map/ppermute | solution.py:872
  56.1 4.1 %collective-permute-start.8 = (f32[360,128]{1,0:T(8,128)S(1)}, f32[360,128]{1,0:T(8,128)S(1)}, u32[]{:S(2)}, u32[]{:S(2)}) collective-permute-start(f32[360,128]{1,0:T(8,128)S(1)} %get-tuple-element.70), channel_id=1, source_target_pairs={{0,4},{4,8},{8,12},{12,16},{16,20},{20,24},{24,28},{28,0},{1,5},{5... | collective-permute-start | bytes 552968 | tf_op jit(solution)/shard_map/ppermute | solution.py:872
  57.8 5.4 %collective-permute-start.9 = (f32[360,128]{1,0:T(8,128)S(1)}, f32[360,128]{1,0:T(8,128)S(1)}, u32[]{:S(2)}, u32[]{:S(2)}) collective-permute-start(f32[360,128]{1,0:T(8,128)S(1)} %get-tuple-element.71), channel_id=1, source_target_pairs={{0,28},{4,0},{8,4},{12,8},{16,12},{20,16},{24,20},{28,24},{1,29},{... | collective-permute-start | bytes 552968 | tf_op jit(solution)/shard_map/ppermute | solution.py:872
  63.9 5.6 %collective-permute-start.10 = (f32[6,40,128]{2,1,0:T(8,128)S(1)}, f32[6,40,128]{2,1,0:T(8,128)S(1)}, u32[]{:S(2)}, u32[]{:S(2)}) collective-permute-start(f32[6,40,128]{2,1,0:T(8,128)S(1)} %get-tuple-element.73), channel_id=1, source_target_pairs={{0,1},{1,2},{2,3},{3,0},{4,5},{5,6},{6,7},{7,4},{8,9},{9,10},{10,1... | collective-permute-start | bytes 368648 | tf_op jit(solution)/shard_map/ppermute | solution.py:872
  65.3 4.3 %collective-permute-start.11 = (f32[6,40,128]{2,1,0:T(8,128)S(1)}, f32[6,40,128]{2,1,0:T(8,128)S(1)}, u32[]{:S(2)}, u32[]{:S(2)}) collective-permute-start(f32[6,40,128]{2,1,0:T(8,128)S(1)} %get-tuple-element.74), channel_id=1, source_target_pairs={{0,3},{1,0},{2,1},{3,2},{4,7},{5,4},{6,5},{7,6},{8,11},{9,8},{10,9... | collective-permute-start | bytes 368648 | tf_op jit(solution)/shard_map/ppermute | solution.py:872
  75.4 4.4 %collective-permute-start.12 = (f32[16,128]{1,0:T(8,128)S(1)}, f32[16,128]{1,0:T(8,128)S(1)}, u32[]{:S(2)}, u32[]{:S(2)}) collective-permute-start(f32[16,128]{1,0:T(8,128)S(1)} %get-tuple-element.76.refs_0_), channel_id=1, source_target_pairs={{0,1},{1,2},{2,3},{3,0},{4,5},{5,6},{6,7},{7,4},{8,9},{9,10},{10,1... | collective-permute-start | bytes 24584 | tf_op jit(solution)/shard_map/ppermute | solution.py:872
  76.3 4.0 %collective-permute-start.13 = (f32[16,128]{1,0:T(8,128)S(1)}, f32[16,128]{1,0:T(8,128)S(1)}, u32[]{:S(2)}, u32[]{:S(2)}) collective-permute-start(f32[16,128]{1,0:T(8,128)S(1)} %get-tuple-element.76.refs_0_), channel_id=1, source_target_pairs={{0,2},{1,3},{2,0},{3,1},{4,6},{5,7},{6,4},{7,5},{8,10},{9,11},{10,... | collective-permute-start | bytes 24584 | tf_op jit(solution)/shard_map/ppermute | solution.py:872
  78.6 2.8 %collective-permute-start.14 = (f32[16,128]{1,0:T(8,128)S(1)}, f32[16,128]{1,0:T(8,128)S(1)}, u32[]{:S(2)}, u32[]{:S(2)}) collective-permute-start(f32[16,128]{1,0:T(8,128)S(1)} %get-tuple-element.76.refs_0_), channel_id=1, source_target_pairs={{0,3},{1,0},{2,1},{3,2},{4,7},{5,4},{6,5},{7,6},{8,11},{9,8},{10,9... | collective-permute-start | bytes 24584 | tf_op jit(solution)/shard_map/ppermute | solution.py:872
  81.5 2.8 %collective-permute-start.15 = (f32[8,8,128]{2,1,0:T(8,128)S(1)}, f32[8,8,128]{2,1,0:T(8,128)S(1)}, u32[]{:S(2)}, u32[]{:S(2)}) collective-permute-start(f32[8,8,128]{2,1,0:T(8,128)S(1)} %gather_z.1.refs_0_), channel_id=1, source_target_pairs={{0,32},{32,64},{64,96},{96,0},{1,33},{33,65},{65,97},{97,1},{2,34}... | collective-permute-start | bytes 98312 | tf_op jit(solution)/shard_map/ppermute | solution.py:872
  81.7 4.3 %collective-permute-start.16 = (f32[8,8,128]{2,1,0:T(8,128)S(1)}, f32[8,8,128]{2,1,0:T(8,128)S(1)}, u32[]{:S(2)}, u32[]{:S(2)}) collective-permute-start(f32[8,8,128]{2,1,0:T(8,128)S(1)} %gather_z.1.refs_0_), channel_id=1, source_target_pairs={{0,64},{32,96},{64,0},{96,32},{1,65},{33,97},{65,1},{97,33},{2,66}... | collective-permute-start | bytes 98312 | tf_op jit(solution)/shard_map/ppermute | solution.py:872
  83.3 4.0 %collective-permute-start.17 = (f32[8,8,128]{2,1,0:T(8,128)S(1)}, f32[8,8,128]{2,1,0:T(8,128)S(1)}, u32[]{:S(2)}, u32[]{:S(2)}) collective-permute-start(f32[8,8,128]{2,1,0:T(8,128)S(1)} %gather_z.1.refs_0_), channel_id=1, source_target_pairs={{0,96},{32,0},{64,32},{96,64},{1,97},{33,1},{65,33},{97,65},{2,98}... | collective-permute-start | bytes 98312 | tf_op jit(solution)/shard_map/ppermute | solution.py:872
  87.3 12.6 %collective-permute-start.18 = (f32[32,8,128]{2,1,0:T(8,128)S(1)}, f32[32,8,128]{2,1,0:T(8,128)S(1)}, u32[]{:S(2)}, u32[]{:S(2)}) collective-permute-start(f32[32,8,128]{2,1,0:T(8,128)S(1)} %gather_x.1.p0), channel_id=1, source_target_pairs={{0,4},{4,8},{8,12},{12,16},{16,20},{20,24},{24,28},{28,0},{1,5},{5... | collective-permute-start | bytes 393224 | tf_op jit(solution)/shard_map/ppermute | solution.py:872
  92.2 15.5 %collective-permute-start.19 = (f32[32,8,128]{2,1,0:T(8,128)S(1)}, f32[32,8,128]{2,1,0:T(8,128)S(1)}, u32[]{:S(2)}, u32[]{:S(2)}) collective-permute-start(f32[32,8,128]{2,1,0:T(8,128)S(1)} %gather_x.1.p0), channel_id=1, source_target_pairs={{0,8},{4,12},{8,16},{12,20},{16,24},{20,28},{24,0},{28,4},{1,9},{5... | collective-permute-start | bytes 393224 | tf_op jit(solution)/shard_map/ppermute | solution.py:872
  93.5 27.3 %collective-permute-start.20 = (f32[32,8,128]{2,1,0:T(8,128)S(1)}, f32[32,8,128]{2,1,0:T(8,128)S(1)}, u32[]{:S(2)}, u32[]{:S(2)}) collective-permute-start(f32[32,8,128]{2,1,0:T(8,128)S(1)} %gather_x.1.p0), channel_id=1, source_target_pairs={{0,12},{4,16},{8,20},{12,24},{16,28},{20,0},{24,4},{28,8},{1,13},{... | collective-permute-start | bytes 393224 | tf_op jit(solution)/shard_map/ppermute | solution.py:872
  95.5 25.3 %collective-permute-start.21 = (f32[32,8,128]{2,1,0:T(8,128)S(1)}, f32[32,8,128]{2,1,0:T(8,128)S(1)}, u32[]{:S(2)}, u32[]{:S(2)}) collective-permute-start(f32[32,8,128]{2,1,0:T(8,128)S(1)} %gather_x.1.p0), channel_id=1, source_target_pairs={{0,16},{4,20},{8,24},{12,28},{16,0},{20,4},{24,8},{28,12},{1,17},{... | collective-permute-start | bytes 393224 | tf_op jit(solution)/shard_map/ppermute | solution.py:872
  97.3 23.6 %collective-permute-start.22 = (f32[32,8,128]{2,1,0:T(8,128)S(1)}, f32[32,8,128]{2,1,0:T(8,128)S(1)}, u32[]{:S(2)}, u32[]{:S(2)}) collective-permute-start(f32[32,8,128]{2,1,0:T(8,128)S(1)} %gather_x.1.p0), channel_id=1, source_target_pairs={{0,20},{4,24},{8,28},{12,0},{16,4},{20,8},{24,12},{28,16},{1,21},{... | collective-permute-start | bytes 393224 | tf_op jit(solution)/shard_map/ppermute | solution.py:872
  99.9 20.9 %collective-permute-start.23 = (f32[32,8,128]{2,1,0:T(8,128)S(1)}, f32[32,8,128]{2,1,0:T(8,128)S(1)}, u32[]{:S(2)}, u32[]{:S(2)}) collective-permute-start(f32[32,8,128]{2,1,0:T(8,128)S(1)} %gather_x.1.p0), channel_id=1, source_target_pairs={{0,24},{4,28},{8,0},{12,4},{16,8},{20,12},{24,16},{28,20},{1,25},{... | collective-permute-start | bytes 393224 | tf_op jit(solution)/shard_map/ppermute | solution.py:872
  107.6 13.2 %collective-permute-start.24 = (f32[32,8,128]{2,1,0:T(8,128)S(1)}, f32[32,8,128]{2,1,0:T(8,128)S(1)}, u32[]{:S(2)}, u32[]{:S(2)}) collective-permute-start(f32[32,8,128]{2,1,0:T(8,128)S(1)} %gather_x.1.p0), channel_id=1, source_target_pairs={{0,28},{4,0},{8,4},{12,8},{16,12},{20,16},{24,20},{28,24},{1,29},{... | collective-permute-start | bytes 393224 | tf_op jit(solution)/shard_map/ppermute | solution.py:872
  120.8 9.3 %copy-start.6 = (f32[36,40,128]{2,1,0:T(8,128)S(1)}, f32[36,40,128]{2,1,0:T(8,128)}, u32[]{:S(2)}) copy-start(f32[36,40,128]{2,1,0:T(8,128)} %copy-done.5) | copy-start | bytes 2211844
  130.1 3.7 %copy-start.3 = (f32[48,48,128]{2,1,0:T(8,128)S(1)}, f32[48,48,128]{2,1,0:T(8,128)}, u32[]{:S(2)}) copy-start(f32[48,48,128]{2,1,0:T(8,128)} %copy-done.2) | copy-start | bytes 3538948
  130.1 3.7 %copy-start.10 = (f32[6,48,128]{2,1,0:T(8,128)S(1)}, f32[6,48,128]{2,1,0:T(8,128)}, u32[]{:S(2)}) copy-start(f32[6,48,128]{2,1,0:T(8,128)} %copy-done.9) | copy-start | bytes 442372
  (5 other events, 4.7 us)
Sparse Core Ops, SparseCore 0:
  10.1 64.5 all-gather.2

commit v5 on v4

--- a/solution.py
+++ b/solution.py
@@ -41,10 +41,15 @@
     return pltpu.VMEM(shape, F32)
 
 
-def call(body, outs, scratch=(), name=None, mib=2):
+def call(body, outs, scratch=(), name=None, mib=2, last_unread=None):
+    specs = {}
+    if last_unread:
+        whole = pl.BlockSpec(memory_space=pltpu.VMEM)
+        specs["in_specs"] = [whole] * (last_unread - 1) + [pl.BlockSpec(memory_space=pl.ANY)]
     return pl.pallas_call(
         body,
         out_shape=outs,
+        **specs,
         scratch_shapes=list(scratch),
         compiler_params=pltpu.CompilerParams(vmem_limit_bytes=mib * MIB),
         name=name,
@@ -325,19 +330,17 @@
     vm(6, 64, 128),
     vm(6, 64, 128),
     vm(6, 48, 128),
-    vm(7, 48, 48, 128),
-    vm(6, 6, 48, 128),
-    vm(48, 48, 128),
-    vm(6, 48, 128),
     vm(48, 48, 128),
     vm(6, 48, 128),
     vm(6, 48, 128),
+    vm(48, 48, 128),
+    vm(2, 16, 32, 128),
 ]
 
 
 def level0_down(
-    src, beta, z_lo, z_hi, iter_out, iter_t_out, c_out, c_lo, c_hi,
-    b_pad, bt_pad, va, vb, ta, tb, ghost, g_main, g_strip, sp, sp_t, u, u_t, src_t, total, rows,
+    src, beta, z_lo, z_hi, iter_out, iter_t_out, c_out, c_lo, c_hi, g_main, g_strip, sp, sp_t, bt_out,
+    b_pad, bt_pad, va, vb, ta, tb, ghost, u, u_t, src_t, total, rows,
 ):
     for ref in (b_pad, va, vb):
         clear_edges(ref, 48, 48)
@@ -345,6 +348,8 @@
         clear_strip(ref)
     b_pad[1:49, 8:56, :] = beta[...]
     unpack_strip(z_lo, z_hi, src_t, bt_pad)
+    for xx in range(6):
+        bt_out[xx] = bt_pad[xx, 8:56, :]
     level0_setup(b_pad, bt_pad, ghost, src, src_t, g_main, g_strip, sp, sp_t, total)
 
     first = RECIPE[0][1]
@@ -519,9 +524,10 @@
     vm(38, 56, 128),
     vm(38, 56, 128),
     vm(38, 56, 128),
-    vm(6, 36, 40, 128),
     vm(36, 40, 128),
     vm(36, 40, 128),
+    vm(36, 40, 128),
+    vm(8, 40, 128),
 ]
 
 
@@ -548,19 +554,18 @@
             b = jnp.where(below, roll(before, 108 - k * 20), b)
             source[x] = s
             b_pad[x + 1, 8:48, :] = b
-            if beta_out is not None:
-                beta_out[x] = b
+            beta_out[x] = b
 
     loop(0, 6, 36, unpack)
 
 
 def level1_down(
-    ext, z_lo, z_hi, iter_out, chunk,
-    b_pad, va, vb, g, sp, u, src, total, rows,
+    ext, z_lo, z_hi, iter_out, chunk, g, sp, beta_out,
+    b_pad, va, vb, u, src, total, rows,
 ):
     for ref in (b_pad, va, vb):
         clear_edges(ref, 36, 40)
-    level1_unpack(ext, z_lo, z_hi, src, b_pad, None)
+    level1_unpack(ext, z_lo, z_hi, src, b_pad, beta_out)
     ring_weights(b_pad, src, g, sp, total, 36, 40, 4.0)
     v = ring_cheb(va, vb, g, sp, u, 36, 40, RECIPE, True)
     iter_out[...] = v[1:37, 8:48, :]
@@ -581,19 +586,13 @@
         chunk[half * 8 : half * 8 + 8, :] = acc
 
 
-def level1_prepare(ext, z_lo, z_hi, g, sp, beta_out, b_pad, src):
-    clear_edges(b_pad, 36, 40)
-    level1_unpack(ext, z_lo, z_hi, src, b_pad, beta_out)
-    ring_weights(b_pad, src, g, sp, None, 36, 40, 4.0)
-
-
 def sender(axis, step):
     count = lax.axis_size(axis)
     return lax.rem(lax.axis_index(axis) + count - step, count)
 
 
 def gather_z(*refs):
-    *parts, out = refs
+    *parts, _, out = refs
     lane = lanes_of(8)
     for half in range(2):
         for quarter in range(4):
@@ -606,7 +605,7 @@
 
 
 def gather_x(*refs):
-    *parts, out = refs
+    *parts, _, out = refs
     for step, part in enumerate(parts):
         out[pl.ds(sender("gx", step) * 8, 8)] = part[...]
 
@@ -617,24 +616,6 @@
         out[8:40, pl.ds(row, 8), :] = part[...]
 
 
-def whole_grid(parts, out, x_pad):
-    lane = lanes_of(8)
-
-    def body(i):
-        gx = i // 8
-        gy = i - gx * 8
-        for half in range(2):
-            blocks = [parts[i * 4 + gz, half * 8 : half * 8 + 8, :] for gz in range(4)]
-            for quarter in range(4):
-                acc = roll(blocks[0], -quarter * 32)
-                for gz in range(1, 4):
-                    acc = jnp.where(lane // 32 == gz, roll(blocks[gz], (gz - quarter) * 32), acc)
-                row = pl.multiple_of(8 + gy * 8, 8)
-                out[gx * 8 + half * 4 + quarter + x_pad, pl.ds(row, 8), :] = acc
-
-    loop(0, 32, 18, body)
-
-
 def clear_whole(ref):
     def clear(x):
         ref[x, 0:8, :] = jnp.zeros((8, 128), F32)
@@ -645,11 +626,11 @@
         ref[x, 8:72, :] = jnp.zeros((64, 128), F32)
 
 
-def coarse_prepare(b_parts, g, inv, total, g3, inv3, gw, invw, b2, b3, bw, rows):
+def coarse_prepare(p0, p1, p2, p3, p4, p5, p6, p7, g, inv, total, g3, inv3, gw, invw, b2, b3, bw, rows):
     clear_whole(b2)
     clear_edges(b3, 16, 32)
     clear_edges(bw, 22, 24)
-    whole_grid(b_parts, b2, 8)
+    gather_y((p0, p1, p2, p3, p4, p5, p6, p7), b2)
     ring_weights(b2.at[7:41], None, g, inv, total, 32, 64, 16.0, edges=True)
     half_z = pick(lambda r, c: r // 2 == c)
 
@@ -796,16 +777,6 @@
     out[...] = v[7:31, 14:38, :]
 
 
-def level0_prepare(src, beta, z_lo, z_hi, g_main, g_strip, sp, sp_t, bt_out, b_pad, bt_pad, ghost, src_t):
-    clear_edges(b_pad, 48, 48)
-    clear_strip(bt_pad)
-    b_pad[1:49, 8:56, :] = beta[...]
-    unpack_strip(z_lo, z_hi, src_t, bt_pad)
-    for xx in range(6):
-        bt_out[xx] = bt_pad[xx, 8:56, :]
-    level0_setup(b_pad, bt_pad, ghost, src, src_t, g_main, g_strip, sp, sp_t, None)
-
-
 def level0_up(
     c1, beta, g_main, g_strip, sp, sp_t, beta_t, iterate, iterate_t, out,
     va, vb, ta, tb, ghost, u, u_t, rows,
@@ -876,8 +847,20 @@
     return ring(hi, axis, 1), ring(lo, axis, -1)
 
 
+def gather(kernel, parts, after, *shape):
+    return call(kernel, sds(*shape), name=kernel.__name__, last_unread=len(parts) + 1)(*parts, after)
+
+
 def around(value, axis):
     return [value] + [ring(value, axis, step) for step in range(1, lax.axis_size(axis))]
+
+
+def carry(parts, steps, after, *values):
+    slab, _ = lax.optimization_barrier((parts[0], after))
+    moved = [ring(slab, "gy", step) for step in steps]
+    *values, last = lax.optimization_barrier((*values, tuple(moved)))
+    parts.extend(last)
+    return values
 
 
 def per_device(source, beta):
@@ -886,78 +869,78 @@
     lo, hi, source, beta = lax.optimization_barrier((lo, hi, source, beta))
     x_lo, x_hi = trade(lo, hi, "gx")
     beta2 = call(coarse_beta, sds(16, 128), [vm(32, 128)], name="coarse_beta")(beta)
-    beta2_all = lax.all_gather(beta2, AXES)
+    x_lo, x_hi, beta2 = lax.optimization_barrier((x_lo, x_hi, beta2))
     slab = sds(2, 48, 8, 128)
     mid = sds(48, 32, 128)
     lo, hi, s_mid, b_mid = call(pack_y, (slab, slab, mid, mid), name="pack_y", mib=4)(
         source, beta, x_lo, x_hi
     )
     y_lo, y_hi = trade(lo, hi, "gy")
+    beta2_block = gather(gather_z, around(beta2, "gz"), lo, 8, 8, 128)
+    y_lo, y_hi, beta2_block = lax.optimization_barrier((y_lo, y_hi, beta2_block))
     whole = sds(48, 48, 128)
     strip = sds(6, 48, 128)
     src_ext, beta_ext, lo, hi = call(
         pack_z, (whole, whole, strip, strip), name="pack_z", mib=4
     )(s_mid, b_mid, y_lo, y_hi)
     z_lo, z_hi = trade(lo, hi, "gz")
-    iter0, iter0_t, c, lo, hi = call(
+    beta2_slab = gather(gather_x, around(beta2_block, "gx"), lo, 32, 8, 128)
+    z_lo, z_hi, beta2_slab = lax.optimization_barrier((z_lo, z_hi, beta2_slab))
+    beta2_y = [beta2_slab]
+    iter0, iter0_t, c, lo, hi, *ready = call(
         level0_down,
-        (whole, strip, sds(16, 16, 128), sds(10, 16, 128), sds(10, 16, 128)),
-        LEVEL0_SCRATCH + [vm(48, 48, 128), vm(2, 16, 32, 128)],
+        (
+            whole,
+            strip,
+            sds(16, 16, 128),
+            sds(10, 16, 128),
+            sds(10, 16, 128),
+            sds(7, 48, 48, 128),
+            sds(6, 6, 48, 128),
+            whole,
+            strip,
+            strip,
+        ),
+        LEVEL0_SCRATCH,
         name="level0_down",
-        mib=26,
+        mib=16,
     )(src_ext, beta_ext, z_lo, z_hi)
     x_lo, x_hi = trade(lo, hi, "gx")
+    x_lo, x_hi = carry(beta2_y, (1, 2, 3), lo, x_lo, x_hi)
     lo, hi = call(pack1_y, (sds(360, 128), sds(360, 128)), name="pack1_y")(c, x_lo, x_hi)
     y_lo, y_hi = trade(lo, hi, "gy")
+    y_lo, y_hi = carry(beta2_y, (4,), lo, y_lo, y_hi)
     ext, lo, hi = call(
         pack1_z, (sds(36, 40, 128), sds(6, 40, 128), sds(6, 40, 128)), name="pack1_z"
     )(c, x_lo, x_hi, y_lo, y_hi)
     z1_lo, z1_hi = trade(lo, hi, "gz")
-    iter1, chunk = call(
+    z1_lo, z1_hi = carry(beta2_y, (5, 6, 7), lo, z1_lo, z1_hi)
+    level1 = sds(36, 40, 128)
+    iter1, chunk, g1, sp1, beta1 = call(
         level1_down,
-        (sds(36, 40, 128), sds(16, 128)),
-        LEVEL1_SCRATCH + [vm(36, 40, 128), vm(36, 40, 128), vm(8, 40, 128)],
+        (level1, sds(16, 128), sds(6, 36, 40, 128), level1, level1),
+        LEVEL1_SCRATCH,
         name="level1_down",
-        mib=11,
+        mib=8,
     )(ext, z1_lo, z1_hi)
-    chunk, beta2_all = lax.optimization_barrier((chunk, beta2_all))
     parts = around(chunk, "gz")
+    parts = around(gather(gather_z, parts, chunk, 8, 8, 128), "gx")
+    slab = gather(gather_x, parts, chunk, 32, 8, 128)
+    parts = around(slab, "gy")
     coarse = call(
         coarse_prepare,
         tuple(sds(*shape) for shape in COARSE_SHAPES),
         COARSE_SCRATCH,
         name="coarse_prepare",
         mib=8,
-    )(beta2_all)
-    block = call(gather_z, sds(8, 8, 128), name="gather_z")(*parts)
-    block, ext, z1_lo, z1_hi = lax.optimization_barrier((block, ext, z1_lo, z1_hi))
-    parts = around(block, "gx")
-    g1, sp1, beta1 = call(
-        level1_prepare,
-        (sds(6, 36, 40, 128), sds(36, 40, 128), sds(36, 40, 128)),
-        [vm(38, 56, 128), vm(36, 40, 128)],
-        name="level1_prepare",
-        mib=4,
-    )(ext, z1_lo, z1_hi)
-    slab = call(gather_x, sds(32, 8, 128), name="gather_x")(*parts)
-    slab, src_ext, beta_ext, z_lo, z_hi = lax.optimization_barrier(
-        (slab, src_ext, beta_ext, z_lo, z_hi)
-    )
-    parts = around(slab, "gy")
-    ready = call(
-        level0_prepare,
-        (sds(7, 48, 48, 128), sds(6, 6, 48, 128), whole, strip, strip),
-        [vm(50, 64, 128), vm(6, 64, 128), vm(6, 48, 128), vm(6, 48, 128)],
-        name="level0_prepare",
-        mib=6,
-    )(src_ext, beta_ext, z_lo, z_hi)
+    )(*beta2_y)
     c2 = call(bottom, sds(18, 24, 128), BOTTOM_SCRATCH, name="bottom", mib=18)(*parts, *coarse)
     c1 = call(
         level1_up,
         sds(24, 24, 128),
         [vm(38, 56, 128), vm(38, 56, 128), vm(36, 40, 128), vm(18, 24, 128), vm(18, 40, 128)],
         name="level1_up",
-        mib=6,
+        mib=8,
     )(c2, g1, sp1, beta1, iter1)
     return call(
         level0_up,
@@ -965,7 +948,7 @@
         [vm(50, 64, 128), vm(50, 64, 128), vm(6, 64, 128), vm(6, 64, 128), vm(6, 48, 128)]
         + [vm(48, 48, 128), vm(6, 48, 128), vm(24, 48, 128)],
         name="level0_up",
-        mib=12,
+        mib=14,
     )(c1, beta_ext, *ready, iter0, iter0_t)
 
 

time: 151 us -> 140 us (0.927)
  starting transfers between devices: 32.7 us -> 52.4 us
  between operations: 13.6 us -> 0.21 us
  Pallas kernels: 54.2 us -> 46.7 us
  waiting for transfers between devices: 43.2 us -> 36.7 us
  local copies, waits for them, and re-layouts: 6.78 us -> 2.07 us
    ppermute x25 -> x38, starting transfers between devices: 32.7 us -> 52.4 us  [ring(): lax.ppermute(value, axis, [(i, (i + step) % count) for i in range(count)])]
    ppermute x25 -> x38, waiting for transfers between devices: 43.2 us -> 36.7 us  [ring(): lax.ppermute(value, axis, [(i, (i + step) % count) for i in range(count)])]
    pallas_call x5, Pallas kernels: 10.6 us -> 4.49 us  [the longest x1 4.25 us: per_device(): call(level1_down, (level1, sds(16, 128), sds(6, 36, 40, 128), level1, lev...]
    unnamed x22 -> x4, local copies, waits for them, and re-layouts: 4.72 us -> 0.01 us
  transfers between devices with their start and end apart: 26 -> 38, of which waited for: 18 -> 22; matrix products, arithmetic and copies ran while one was open for 0% -> 0% of each run, Pallas kernels for 20% -> 3%
where the time goes in v5:
time: 140 us; the launch traced here: 138 us
  starting transfers between devices  52.4 us (37%)
  Pallas kernels  46.7 us (33%)
  waiting for transfers between devices  36.7 us (26%)
  local copies, waits for them, and re-layouts  2.07 us (1%)
    ppermute x38, starting transfers between devices, ring(): lax.ppermute(value, axis, [(i, (i + step) % count) for i in range(count)])  52.4 us
    ppermute x38, waiting for transfers between devices, ring(): lax.ppermute(value, axis, [(i, (i + step) % count) for i in range(count)])  36.7 us
    pallas_call x1, Pallas kernels, per_device(): call(level0_down, (whole, strip, sds(16, 16, 128), sds(10, 16, 128), sds(...  12.6 us
    pallas_call x1, Pallas kernels, per_device(): call(level0_up, sds(32, 32, 128), [vm(50, 64, 128), vm(50, 64, 128), vm(6...  10 us
    pallas_call x1, Pallas kernels, per_device(): call(bottom, sds(18, 24, 128), BOTTOM_SCRATCH, name='bottom', mib=18)  9.34 us
    pallas_call x1, Pallas kernels, per_device(): call(level1_down, (level1, sds(16, 128), sds(6, 36, 40, 128), level1, lev...  4.25 us
    pallas_call x1, Pallas kernels, per_device(): call(level1_up, sds(24, 24, 128), [vm(38, 56, 128), vm(38, 56, 128), vm(3...  3.66 us
    pallas_call x1, Pallas kernels, per_device(): call(coarse_prepare, tuple((sds(*shape) for shape in COARSE_SHAPES)), COA...  3.52 us
  transfers between devices with their start and end apart: 38, of which 22 were waited for; matrix products, arithmetic and copies ran while one was open for 0% of the time, Pallas kernels for 3%

profile of v5, /device:TPU:7, one launch (start us, length us, event | category | flops | bytes accessed | tf_op | source)
XLA Modules:
  0.0 138.1 jit_solution(7502101633186091791)
XLA Ops:
  2.2 1.5 %collective-permute-start.1 = (f32[2,8,32,128]{3,2,1,0:T(8,128)S(1)}, f32[2,8,32,128]{3,2,1,0:T(8,128)S(1)}, u32[]{:S(2)}, u32[]{:S(2)}) collective-permute-start(f32[2,8,32,128]{3,2,1,0:T(8,128)S(1)} %get-tuple-element.72), channel_id=1, source_target_pairs={{0,96},{32,0},{64,32},{96,64},{1,97},{33,1},{65,33},{97,65},{2,98}... | collective-permute-start | bytes 786440 | tf_op jit(solution)/shard_map/ppermute | solution.py:843
  4.2 5.2 %collective-permute-done.from_lo = f32[2,8,32,128]{3,2,1,0:T(8,128)S(1)} collective-permute-done((f32[2,8,32,128]{3,2,1,0:T(8,128)S(1)}, f32[2,8,32,128]{3,2,1,0:T(8,128)S(1)}, u32[]{:S(2)}, u32[]{:S(2)}) %collective-permute-start) | collective-permute-done | bytes 262176 | tf_op jit(solution)/shard_map/ppermute | solution.py:843
  10.5 1.9 %collective-permute-start.3 = (f32[2,48,8,128]{3,2,1,0:T(8,128)S(1)}, f32[2,48,8,128]{3,2,1,0:T(8,128)S(1)}, u32[]{:S(2)}, u32[]{:S(2)}) collective-permute-start(f32[2,48,8,128]{3,2,1,0:T(8,128)S(1)} %get-tuple-element.78.refs_4_), channel_id=1, source_target_pairs={{0,28},{4,0},{8,4},{12,8},{16,12},{20,16},{24,20},{28,24},{1,29},{... | collective-permute-start | bytes 1179656 | tf_op jit(solution)/shard_map/ppermute | solution.py:843
  12.4 1.7 %collective-permute-start.2 = (f32[2,48,8,128]{3,2,1,0:T(8,128)S(1)}, f32[2,48,8,128]{3,2,1,0:T(8,128)S(1)}, u32[]{:S(2)}, u32[]{:S(2)}) collective-permute-start(f32[2,48,8,128]{3,2,1,0:T(8,128)S(1)} %get-tuple-element.77), channel_id=1, source_target_pairs={{0,4},{4,8},{8,12},{12,16},{16,20},{20,24},{24,28},{28,0},{1,5},{5... | collective-permute-start | bytes 1179656 | tf_op jit(solution)/shard_map/ppermute | solution.py:843
  15.3 2.6 %collective-permute-start.5 = (f32[16,128]{1,0:T(8,128)S(1)}, f32[16,128]{1,0:T(8,128)S(1)}, u32[]{:S(2)}, u32[]{:S(2)}) collective-permute-start(f32[16,128]{1,0:T(8,128)S(1)} %coarse_beta.1.refs_0_), channel_id=1, source_target_pairs={{0,2},{1,3},{2,0},{3,1},{4,6},{5,7},{6,4},{7,5},{8,10},{9,11},{10,... | collective-permute-start | bytes 24584 | tf_op jit(solution)/shard_map/ppermute | solution.py:843
  19.3 1.4 %collective-permute-done.6.refs_3_ = f32[16,128]{1,0:T(8,128)S(1)} collective-permute-done((f32[16,128]{1,0:T(8,128)S(1)}, f32[16,128]{1,0:T(8,128)S(1)}, u32[]{:S(2)}, u32[]{:S(2)}) %collective-permute-start.6) | collective-permute-done | bytes 8224 | tf_op jit(solution)/shard_map/ppermute | solution.py:843
  20.9 1.5 %pack_z.1 = (f32[48,48,128]{2,1,0:T(8,128)S(1)}, f32[48,48,128]{2,1,0:T(8,128)S(1)}, f32[6,48,128]{2,1,0:T(8,128)S(1)}, f32[6,48,128]{2,1,0:T(8,128)S(1)}) custom-call(f32[48,32,128]{2,1,0:T(8,128)S(1)} %get-tuple-element.75.s_mid, f32[48,32,128]{2,1,0:T(8,128)S(1)} %get-tuple-element.76.b_mid, f32[2,48,8,128]{3,2,1,0:T(8,128)S(1)} %collective-permute-done.2.y_lo, ...), custom_call_target="tpu_custom_call" | custom-call | tf_op jit(solution)/shard_map/pack_z/pallas_call | solution.py:883
  22.7 2.5 %collective-permute-start.8 = (f32[6,48,128]{2,1,0:T(8,128)S(1)}, f32[6,48,128]{2,1,0:T(8,128)S(1)}, u32[]{:S(2)}, u32[]{:S(2)}) collective-permute-start(f32[6,48,128]{2,1,0:T(8,128)S(1)} %get-tuple-element.85.refs_4_), channel_id=1, source_target_pairs={{0,3},{1,0},{2,1},{3,2},{4,7},{5,4},{6,5},{7,6},{8,11},{9,8},{10,9... | collective-permute-start | bytes 442376 | tf_op jit(solution)/shard_map/ppermute | solution.py:843
  26.1 2.7 %collective-permute-start.9 = (f32[8,8,128]{2,1,0:T(8,128)S(1)}, f32[8,8,128]{2,1,0:T(8,128)S(1)}, u32[]{:S(2)}, u32[]{:S(2)}) collective-permute-start(f32[8,8,128]{2,1,0:T(8,128)S(1)} %gather_z.2.refs_0_), channel_id=1, source_target_pairs={{0,32},{32,64},{64,96},{96,0},{1,33},{33,65},{65,97},{97,1},{2,34}... | collective-permute-start | bytes 98312 | tf_op jit(solution)/shard_map/ppermute | solution.py:843
  30.4 12.6 %level0_down.1 = (f32[48,48,128]{2,1,0:T(8,128)S(1)}, f32[6,48,128]{2,1,0:T(8,128)S(1)}, f32[16,16,128]{2,1,0:T(8,128)S(1)}, f32[10,16,128]{2,1,0:T(8,128)S(1)},...) custom-call(f32[48,48,128]{2,1,0:T(8,128)S(1)} %get-tuple-element.82, ...), custom_call_target="tpu_custom_call" | custom-call | tf_op jit(solution)/shard_map/level0_down/pallas_call | solution.py:890
  43.0 3.7 %collective-permute-start.14 = (f32[32,8,128]{2,1,0:T(8,128)S(1)}, f32[32,8,128]{2,1,0:T(8,128)S(1)}, u32[]{:S(2)}, u32[]{:S(2)}) collective-permute-start(f32[32,8,128]{2,1,0:T(8,128)S(1)} %gather_x.2.p0), channel_id=1, source_target_pairs={{0,4},{4,8},{8,12},{12,16},{16,20},{20,24},{24,28},{28,0},{1,5},{5... | collective-permute-start | bytes 393224 | tf_op jit(solution)/shard_map/ppermute | solution.py:843
  46.7 1.6 %collective-permute-start.15 = (f32[32,8,128]{2,1,0:T(8,128)S(1)}, f32[32,8,128]{2,1,0:T(8,128)S(1)}, u32[]{:S(2)}, u32[]{:S(2)}) collective-permute-start(f32[32,8,128]{2,1,0:T(8,128)S(1)} %gather_x.2.p0), channel_id=1, source_target_pairs={{0,8},{4,12},{8,16},{12,20},{16,24},{20,28},{24,0},{28,4},{1,9},{5... | collective-permute-start | bytes 393224 | tf_op jit(solution)/shard_map/ppermute | solution.py:843
  48.2 2.0 %collective-permute-start.16 = (f32[32,8,128]{2,1,0:T(8,128)S(1)}, f32[32,8,128]{2,1,0:T(8,128)S(1)}, u32[]{:S(2)}, u32[]{:S(2)}) collective-permute-start(f32[32,8,128]{2,1,0:T(8,128)S(1)} %gather_x.2.p0), channel_id=1, source_target_pairs={{0,12},{4,16},{8,20},{12,24},{16,28},{20,0},{24,4},{28,8},{1,13},{... | collective-permute-start | bytes 393224 | tf_op jit(solution)/shard_map/ppermute | solution.py:843
  50.3 2.9 %collective-permute-start.12 = (f32[10,16,128]{2,1,0:T(8,128)S(1)}, f32[10,16,128]{2,1,0:T(8,128)S(1)}, u32[]{:S(2)}, u32[]{:S(2)}) collective-permute-start(f32[10,16,128]{2,1,0:T(8,128)S(1)} %get-tuple-element.90), channel_id=1, source_target_pairs={{0,32},{32,64},{64,96},{96,0},{1,33},{33,65},{65,97},{97,1},{2,34}... | collective-permute-start | bytes 245768 | tf_op jit(solution)/shard_map/ppermute | solution.py:843
  53.2 2.1 %collective-permute-done.12.from_lo.x_lo = f32[10,16,128]{2,1,0:T(8,128)S(1)} collective-permute-done((f32[10,16,128]{2,1,0:T(8,128)S(1)}, f32[10,16,128]{2,1,0:T(8,128)S(1)}, u32[]{:S(2)}, u32[]{:S(2)}) %collective-permute-start.12) | collective-permute-done | bytes 81952 | tf_op jit(solution)/shard_map/ppermute | solution.py:843
  55.3 3.2 %collective-permute-done.13.from_hi.x_hi = f32[10,16,128]{2,1,0:T(8,128)S(1)} collective-permute-done((f32[10,16,128]{2,1,0:T(8,128)S(1)}, f32[10,16,128]{2,1,0:T(8,128)S(1)}, u32[]{:S(2)}, u32[]{:S(2)}) %collective-permute-start.13) | collective-permute-done | bytes 81952 | tf_op jit(solution)/shard_map/ppermute | solution.py:843
  59.7 1.7 %collective-permute-start.19 = (f32[32,8,128]{2,1,0:T(8,128)S(1)}, f32[32,8,128]{2,1,0:T(8,128)S(1)}, u32[]{:S(2)}, u32[]{:S(2)}) collective-permute-start(f32[32,8,128]{2,1,0:T(8,128)S(1)} %gather_x.2.p0), channel_id=1, source_target_pairs={{0,16},{4,20},{8,24},{12,28},{16,0},{20,4},{24,8},{28,12},{1,17},{... | collective-permute-start | bytes 393224 | tf_op jit(solution)/shard_map/ppermute | solution.py:843
  61.3 4.4 %collective-permute-done.19.p4 = f32[32,8,128]{2,1,0:T(8,128)S(1)} collective-permute-done((f32[32,8,128]{2,1,0:T(8,128)S(1)}, f32[32,8,128]{2,1,0:T(8,128)S(1)}, u32[]{:S(2)}, u32[]{:S(2)}) %collective-permute-start.19) | collective-permute-done | bytes 131104 | tf_op jit(solution)/shard_map/ppermute | solution.py:843
  66.9 4.5 %collective-permute-start.22 = (f32[32,8,128]{2,1,0:T(8,128)S(1)}, f32[32,8,128]{2,1,0:T(8,128)S(1)}, u32[]{:S(2)}, u32[]{:S(2)}) collective-permute-start(f32[32,8,128]{2,1,0:T(8,128)S(1)} %gather_x.2.p0), channel_id=1, source_target_pairs={{0,20},{4,24},{8,28},{12,0},{16,4},{20,8},{24,12},{28,16},{1,21},{... | collective-permute-start | bytes 393224 | tf_op jit(solution)/shard_map/ppermute | solution.py:843
  72.1 2.7 %collective-permute-start.21 = (f32[6,40,128]{2,1,0:T(8,128)S(1)}, f32[6,40,128]{2,1,0:T(8,128)S(1)}, u32[]{:S(2)}, u32[]{:S(2)}) collective-permute-start(f32[6,40,128]{2,1,0:T(8,128)S(1)} %get-tuple-element.103), channel_id=1, source_target_pairs={{0,3},{1,0},{2,1},{3,2},{4,7},{5,4},{6,5},{7,6},{8,11},{9,8},{10,9... | collective-permute-start | bytes 368648 | tf_op jit(solution)/shard_map/ppermute | solution.py:843
  74.7 3.1 %collective-permute-done.20.z_lo = f32[6,40,128]{2,1,0:T(8,128)S(1)} collective-permute-done((f32[6,40,128]{2,1,0:T(8,128)S(1)}, f32[6,40,128]{2,1,0:T(8,128)S(1)}, u32[]{:S(2)}, u32[]{:S(2)}) %collective-permute-start.20) | collective-permute-done | bytes 122912 | tf_op jit(solution)/shard_map/ppermute | solution.py:843
  79.4 4.2 %level1_down.1 = (f32[36,40,128]{2,1,0:T(8,128)S(1)}, f32[16,128]{1,0:T(8,128)S(1)}, f32[6,36,40,128]{3,2,1,0:T(8,128)S(1)}, f32[36,40,128]{2,1,0:T(8,128)S(1)}, f32[36,40,128]{2,1,0:T(8,128)S(1)}) custom-call(f32[36,40,128]{2,1,0:T(8,128)S(1)} %get-tuple-element.101.ext, f32[6,40,128]{2,1,0:T(8,128)S(1)} %collective-permute-done.20.z_lo, ...), custom_call_target="tpu_custom_call" | custom-call | tf_op jit(solution)/shard_map/level1_down/pallas_call | solution.py:919
  83.7 2.5 %collective-permute-start.26 = (f32[16,128]{1,0:T(8,128)S(1)}, f32[16,128]{1,0:T(8,128)S(1)}, u32[]{:S(2)}, u32[]{:S(2)}) collective-permute-start(f32[16,128]{1,0:T(8,128)S(1)} %get-tuple-element.107.refs_0_.refs_4_), channel_id=1, source_target_pairs={{0,2},{1,3},{2,0},{3,1},{4,6},{5,7},{6,4},{7,5},{8,10},{9,11},{10,... | collective-permute-start | bytes 24584 | tf_op jit(solution)/shard_map/ppermute | solution.py:843
  92.0 2.9 %collective-permute-done.29.refs_2_ = f32[8,8,128]{2,1,0:T(8,128)S(1)} collective-permute-done((f32[8,8,128]{2,1,0:T(8,128)S(1)}, f32[8,8,128]{2,1,0:T(8,128)S(1)}, u32[]{:S(2)}, u32[]{:S(2)}) %collective-permute-start.29) | collective-permute-done | bytes 32800 | tf_op jit(solution)/shard_map/ppermute | solution.py:843
  94.9 4.9 %collective-permute-start.31 = (f32[32,8,128]{2,1,0:T(8,128)S(1)}, f32[32,8,128]{2,1,0:T(8,128)S(1)}, u32[]{:S(2)}, u32[]{:S(2)}) collective-permute-start(f32[32,8,128]{2,1,0:T(8,128)S(1)} %gather_x.3.p0), channel_id=1, source_target_pairs={{0,4},{4,8},{8,12},{12,16},{16,20},{20,24},{24,28},{28,0},{1,5},{5... | collective-permute-start | bytes 393224 | tf_op jit(solution)/shard_map/ppermute | solution.py:843
  103.1 1.9 %collective-permute-start.35 = (f32[32,8,128]{2,1,0:T(8,128)S(1)}, f32[32,8,128]{2,1,0:T(8,128)S(1)}, u32[]{:S(2)}, u32[]{:S(2)}) collective-permute-start(f32[32,8,128]{2,1,0:T(8,128)S(1)} %gather_x.3.p0), channel_id=1, source_target_pairs={{0,20},{4,24},{8,28},{12,0},{16,4},{20,8},{24,12},{28,16},{1,21},{... | collective-permute-start | bytes 393224 | tf_op jit(solution)/shard_map/ppermute | solution.py:843
  105.1 2.1 %collective-permute-done.32.p2 = f32[32,8,128]{2,1,0:T(8,128)S(1)} collective-permute-done((f32[32,8,128]{2,1,0:T(8,128)S(1)}, f32[32,8,128]{2,1,0:T(8,128)S(1)}, u32[]{:S(2)}, u32[]{:S(2)}) %collective-permute-start.32) | collective-permute-done | bytes 131104 | tf_op jit(solution)/shard_map/ppermute | solution.py:843
  107.4 3.5 %coarse_prepare.1 = (f32[6,32,64,128]{3,2,1,0:T(8,128)S(1)}, f32[32,64,128]{2,1,0:T(8,128)S(1)}, f32[32,64,128]{2,1,0:T(8,128)S(1)}, f32[6,16,32,128]{3,2,1,0:T(...) custom-call(f32[32,8,128]{2,1,0:T(8,128)S(1)} %gather_x.2.p0, ...), custom_call_target="tpu_custom_call" | custom-call | tf_op jit(solution)/shard_map/coarse_prepare/pallas_call | solution.py:930
  110.9 2.2 %collective-permute-done.34.p4 = f32[32,8,128]{2,1,0:T(8,128)S(1)} collective-permute-done((f32[32,8,128]{2,1,0:T(8,128)S(1)}, f32[32,8,128]{2,1,0:T(8,128)S(1)}, u32[]{:S(2)}, u32[]{:S(2)}) %collective-permute-start.34) | collective-permute-done | bytes 131104 | tf_op jit(solution)/shard_map/ppermute | solution.py:843
  115.1 9.3 %bottom.1.c2 = f32[18,24,128]{2,1,0:T(8,128)S(1)} custom-call(f32[32,8,128]{2,1,0:T(8,128)S(1)} %gather_x.3.p0, f32[32,8,128]{2,1,0:T(8,128)S(1)} %collective-permute-done.31.p1, f32[32,8,128]{2,1,0:T(8,128)S(1)} %collective-permute-done.32.p2, f32[32,8,128]{2,1,0:T(8,128)S(1)} %collective-permute-done.33.p3, f32[32,8,128]{2,1,0:T(8,128)S(1)} %collective-permute-done.34.p4, ...), custom_call_target="tpu_custom_call" | custom-call | tf_op jit(solution)/shard_map/bottom/pallas_call | solution.py:937
  124.4 3.7 %level1_up.1.c1 = f32[24,24,128]{2,1,0:T(8,128)S(1)} custom-call(f32[18,24,128]{2,1,0:T(8,128)S(1)} %bottom.1.c2, f32[6,36,40,128]{3,2,1,0:T(8,128)S(1)} %get-tuple-element.122.g, f32[36,40,128]{2,1,0:T(8,128)S(1)} %get-tuple-element.123.sp, f32[36,40,128]{2,1,0:T(8,128)S(1)} %get-tuple-element.124.beta, f32[36,40,128]{2,1,0:T(8,128)S(1)} %get-tuple-element.125.iterate), custom_call_target="tpu_custom_call" | custom-call | tf_op jit(solution)/shard_map/level1_up/pallas_call | solution.py:938
  128.1 10.0 %level0_up.1 = f32[32,32,128]{2,1,0:T(8,128)} custom-call(f32[24,24,128]{2,1,0:T(8,128)S(1)} %level1_up.1.c1, f32[48,48,128]{2,1,0:T(8,128)S(1)} %get-tuple-element.83.beta, f32[7,48,48,128]{3,2,1,0:T(8,128)S(1)} %get-tuple-element.126.g_main, f32[6,6,48,128]{3,2,1,0:T(8,128)S(1)} %get-tuple-element.127.g_strip, f32[48,48,128]{2,1,0:T(8,128)S(1)} %get-tuple-element.128.sp, ...), custom_call_target="tpu_custom_call" | custom-call | tf_op jit(solution)/shard_map/level0_up/pallas_call | solution.py:945
  (66 shorter events, 25.4 us)
Async XLA Ops:
  2.1 7.2 %collective-permute-start = (f32[2,8,32,128]{3,2,1,0:T(8,128)S(1)}, f32[2,8,32,128]{3,2,1,0:T(8,128)S(1)}, u32[]{:S(2)}, u32[]{:S(2)}) collective-permute-start(f32[2,8,32,128]{3,2,1,0:T(8,128)S(1)} %get-tuple-element.71), channel_id=1, source_target_pairs={{0,32},{32,64},{64,96},{96,0},{1,33},{33,65},{65,97},{97,1},{2,34}... | collective-permute-start | bytes 786440 | tf_op jit(solution)/shard_map/ppermute | solution.py:843
  2.2 8.1 %collective-permute-start.1 = (f32[2,8,32,128]{3,2,1,0:T(8,128)S(1)}, f32[2,8,32,128]{3,2,1,0:T(8,128)S(1)}, u32[]{:S(2)}, u32[]{:S(2)}) collective-permute-start(f32[2,8,32,128]{3,2,1,0:T(8,128)S(1)} %get-tuple-element.72), channel_id=1, source_target_pairs={{0,96},{32,0},{64,32},{96,64},{1,97},{33,1},{65,33},{97,65},{2,98}... | collective-permute-start | bytes 786440 | tf_op jit(solution)/shard_map/ppermute | solution.py:843
  10.5 10.4 %collective-permute-start.3 = (f32[2,48,8,128]{3,2,1,0:T(8,128)S(1)}, f32[2,48,8,128]{3,2,1,0:T(8,128)S(1)}, u32[]{:S(2)}, u32[]{:S(2)}) collective-permute-start(f32[2,48,8,128]{3,2,1,0:T(8,128)S(1)} %get-tuple-element.78.refs_4_), channel_id=1, source_target_pairs={{0,28},{4,0},{8,4},{12,8},{16,12},{20,16},{24,20},{28,24},{1,29},{... | collective-permute-start | bytes 1179656 | tf_op jit(solution)/shard_map/ppermute | solution.py:843
  12.4 8.5 %collective-permute-start.2 = (f32[2,48,8,128]{3,2,1,0:T(8,128)S(1)}, f32[2,48,8,128]{3,2,1,0:T(8,128)S(1)}, u32[]{:S(2)}, u32[]{:S(2)}) collective-permute-start(f32[2,48,8,128]{3,2,1,0:T(8,128)S(1)} %get-tuple-element.77), channel_id=1, source_target_pairs={{0,4},{4,8},{8,12},{12,16},{16,20},{20,24},{24,28},{28,0},{1,5},{5... | collective-permute-start | bytes 1179656 | tf_op jit(solution)/shard_map/ppermute | solution.py:843
  14.0 5.0 %collective-permute-start.4 = (f32[16,128]{1,0:T(8,128)S(1)}, f32[16,128]{1,0:T(8,128)S(1)}, u32[]{:S(2)}, u32[]{:S(2)}) collective-permute-start(f32[16,128]{1,0:T(8,128)S(1)} %coarse_beta.1.refs_0_), channel_id=1, source_target_pairs={{0,1},{1,2},{2,3},{3,0},{4,5},{5,6},{6,7},{7,4},{8,9},{9,10},{10,1... | collective-permute-start | bytes 24584 | tf_op jit(solution)/shard_map/ppermute | solution.py:843
  22.4 8.0 %collective-permute-start.7 = (f32[6,48,128]{2,1,0:T(8,128)S(1)}, f32[6,48,128]{2,1,0:T(8,128)S(1)}, u32[]{:S(2)}, u32[]{:S(2)}) collective-permute-start(f32[6,48,128]{2,1,0:T(8,128)S(1)} %get-tuple-element.84), channel_id=1, source_target_pairs={{0,1},{1,2},{2,3},{3,0},{4,5},{5,6},{6,7},{7,4},{8,9},{9,10},{10,1... | collective-permute-start | bytes 442376 | tf_op jit(solution)/shard_map/ppermute | solution.py:843
  22.7 7.7 %collective-permute-start.8 = (f32[6,48,128]{2,1,0:T(8,128)S(1)}, f32[6,48,128]{2,1,0:T(8,128)S(1)}, u32[]{:S(2)}, u32[]{:S(2)}) collective-permute-start(f32[6,48,128]{2,1,0:T(8,128)S(1)} %get-tuple-element.85.refs_4_), channel_id=1, source_target_pairs={{0,3},{1,0},{2,1},{3,2},{4,7},{5,4},{6,5},{7,6},{8,11},{9,8},{10,9... | collective-permute-start | bytes 442376 | tf_op jit(solution)/shard_map/ppermute | solution.py:843
  25.2 4.3 %collective-permute-start.10 = (f32[8,8,128]{2,1,0:T(8,128)S(1)}, f32[8,8,128]{2,1,0:T(8,128)S(1)}, u32[]{:S(2)}, u32[]{:S(2)}) collective-permute-start(f32[8,8,128]{2,1,0:T(8,128)S(1)} %gather_z.2.refs_0_), channel_id=1, source_target_pairs={{0,64},{32,96},{64,0},{96,32},{1,65},{33,97},{65,1},{97,33},{2,66}... | collective-permute-start | bytes 98312 | tf_op jit(solution)/shard_map/ppermute | solution.py:843
  26.1 4.3 %collective-permute-start.11 = (f32[8,8,128]{2,1,0:T(8,128)S(1)}, f32[8,8,128]{2,1,0:T(8,128)S(1)}, u32[]{:S(2)}, u32[]{:S(2)}) collective-permute-start(f32[8,8,128]{2,1,0:T(8,128)S(1)} %gather_z.2.refs_0_), channel_id=1, source_target_pairs={{0,96},{32,0},{64,32},{96,64},{1,97},{33,1},{65,33},{97,65},{2,98}... | collective-permute-start | bytes 98312 | tf_op jit(solution)/shard_map/ppermute | solution.py:843
  26.1 4.3 %collective-permute-start.9 = (f32[8,8,128]{2,1,0:T(8,128)S(1)}, f32[8,8,128]{2,1,0:T(8,128)S(1)}, u32[]{:S(2)}, u32[]{:S(2)}) collective-permute-start(f32[8,8,128]{2,1,0:T(8,128)S(1)} %gather_z.2.refs_0_), channel_id=1, source_target_pairs={{0,32},{32,64},{64,96},{96,0},{1,33},{33,65},{65,97},{97,1},{2,34}... | collective-permute-start | bytes 98312 | tf_op jit(solution)/shard_map/ppermute | solution.py:843
  43.0 15.5 %collective-permute-start.14 = (f32[32,8,128]{2,1,0:T(8,128)S(1)}, f32[32,8,128]{2,1,0:T(8,128)S(1)}, u32[]{:S(2)}, u32[]{:S(2)}) collective-permute-start(f32[32,8,128]{2,1,0:T(8,128)S(1)} %gather_x.2.p0), channel_id=1, source_target_pairs={{0,4},{4,8},{8,12},{12,16},{16,20},{20,24},{24,28},{28,0},{1,5},{5... | collective-permute-start | bytes 393224 | tf_op jit(solution)/shard_map/ppermute | solution.py:843
  46.7 11.8 %collective-permute-start.15 = (f32[32,8,128]{2,1,0:T(8,128)S(1)}, f32[32,8,128]{2,1,0:T(8,128)S(1)}, u32[]{:S(2)}, u32[]{:S(2)}) collective-permute-start(f32[32,8,128]{2,1,0:T(8,128)S(1)} %gather_x.2.p0), channel_id=1, source_target_pairs={{0,8},{4,12},{8,16},{12,20},{16,24},{20,28},{24,0},{28,4},{1,9},{5... | collective-permute-start | bytes 393224 | tf_op jit(solution)/shard_map/ppermute | solution.py:843
  48.2 10.3 %collective-permute-start.16 = (f32[32,8,128]{2,1,0:T(8,128)S(1)}, f32[32,8,128]{2,1,0:T(8,128)S(1)}, u32[]{:S(2)}, u32[]{:S(2)}) collective-permute-start(f32[32,8,128]{2,1,0:T(8,128)S(1)} %gather_x.2.p0), channel_id=1, source_target_pairs={{0,12},{4,16},{8,20},{12,24},{16,28},{20,0},{24,4},{28,8},{1,13},{... | collective-permute-start | bytes 393224 | tf_op jit(solution)/shard_map/ppermute | solution.py:843
  50.3 5.0 %collective-permute-start.12 = (f32[10,16,128]{2,1,0:T(8,128)S(1)}, f32[10,16,128]{2,1,0:T(8,128)S(1)}, u32[]{:S(2)}, u32[]{:S(2)}) collective-permute-start(f32[10,16,128]{2,1,0:T(8,128)S(1)} %get-tuple-element.90), channel_id=1, source_target_pairs={{0,32},{32,64},{64,96},{96,0},{1,33},{33,65},{65,97},{97,1},{2,34}... | collective-permute-start | bytes 245768 | tf_op jit(solution)/shard_map/ppermute | solution.py:843
  53.2 5.3 %collective-permute-start.13 = (f32[10,16,128]{2,1,0:T(8,128)S(1)}, f32[10,16,128]{2,1,0:T(8,128)S(1)}, u32[]{:S(2)}, u32[]{:S(2)}) collective-permute-start(f32[10,16,128]{2,1,0:T(8,128)S(1)} %get-tuple-element.91), channel_id=1, source_target_pairs={{0,96},{32,0},{64,32},{96,64},{1,97},{33,1},{65,33},{97,65},{2,98}... | collective-permute-start | bytes 245768 | tf_op jit(solution)/shard_map/ppermute | solution.py:843
  58.6 7.2 %collective-permute-start.17 = (f32[360,128]{1,0:T(8,128)S(1)}, f32[360,128]{1,0:T(8,128)S(1)}, u32[]{:S(2)}, u32[]{:S(2)}) collective-permute-start(f32[360,128]{1,0:T(8,128)S(1)} %get-tuple-element.96), channel_id=1, source_target_pairs={{0,4},{4,8},{8,12},{12,16},{16,20},{20,24},{24,28},{28,0},{1,5},{5... | collective-permute-start | bytes 552968 | tf_op jit(solution)/shard_map/ppermute | solution.py:843
  59.7 6.4 %collective-permute-start.18 = (f32[360,128]{1,0:T(8,128)S(1)}, f32[360,128]{1,0:T(8,128)S(1)}, u32[]{:S(2)}, u32[]{:S(2)}) collective-permute-start(f32[360,128]{1,0:T(8,128)S(1)} %get-tuple-element.97), channel_id=1, source_target_pairs={{0,28},{4,0},{8,4},{12,8},{16,12},{20,16},{24,20},{28,24},{1,29},{... | collective-permute-start | bytes 552968 | tf_op jit(solution)/shard_map/ppermute | solution.py:843
  59.7 6.1 %collective-permute-start.19 = (f32[32,8,128]{2,1,0:T(8,128)S(1)}, f32[32,8,128]{2,1,0:T(8,128)S(1)}, u32[]{:S(2)}, u32[]{:S(2)}) collective-permute-start(f32[32,8,128]{2,1,0:T(8,128)S(1)} %gather_x.2.p0), channel_id=1, source_target_pairs={{0,16},{4,20},{8,24},{12,28},{16,0},{20,4},{24,8},{28,12},{1,17},{... | collective-permute-start | bytes 393224 | tf_op jit(solution)/shard_map/ppermute | solution.py:843
  66.9 10.9 %collective-permute-start.22 = (f32[32,8,128]{2,1,0:T(8,128)S(1)}, f32[32,8,128]{2,1,0:T(8,128)S(1)}, u32[]{:S(2)}, u32[]{:S(2)}) collective-permute-start(f32[32,8,128]{2,1,0:T(8,128)S(1)} %gather_x.2.p0), channel_id=1, source_target_pairs={{0,20},{4,24},{8,28},{12,0},{16,4},{20,8},{24,12},{28,16},{1,21},{... | collective-permute-start | bytes 393224 | tf_op jit(solution)/shard_map/ppermute | solution.py:843
  71.4 6.7 %collective-permute-start.23 = (f32[32,8,128]{2,1,0:T(8,128)S(1)}, f32[32,8,128]{2,1,0:T(8,128)S(1)}, u32[]{:S(2)}, u32[]{:S(2)}) collective-permute-start(f32[32,8,128]{2,1,0:T(8,128)S(1)} %gather_x.2.p0), channel_id=1, source_target_pairs={{0,24},{4,28},{8,0},{12,4},{16,8},{20,12},{24,16},{28,20},{1,25},{... | collective-permute-start | bytes 393224 | tf_op jit(solution)/shard_map/ppermute | solution.py:843
  71.9 7.5 %collective-permute-start.24 = (f32[32,8,128]{2,1,0:T(8,128)S(1)}, f32[32,8,128]{2,1,0:T(8,128)S(1)}, u32[]{:S(2)}, u32[]{:S(2)}) collective-permute-start(f32[32,8,128]{2,1,0:T(8,128)S(1)} %gather_x.2.p0), channel_id=1, source_target_pairs={{0,28},{4,0},{8,4},{12,8},{16,12},{20,16},{24,20},{28,24},{1,29},{... | collective-permute-start | bytes 393224 | tf_op jit(solution)/shard_map/ppermute | solution.py:843
  72.1 5.7 %collective-permute-start.20 = (f32[6,40,128]{2,1,0:T(8,128)S(1)}, f32[6,40,128]{2,1,0:T(8,128)S(1)}, u32[]{:S(2)}, u32[]{:S(2)}) collective-permute-start(f32[6,40,128]{2,1,0:T(8,128)S(1)} %get-tuple-element.102), channel_id=1, source_target_pairs={{0,1},{1,2},{2,3},{3,0},{4,5},{5,6},{6,7},{7,4},{8,9},{9,10},{10,1... | collective-permute-start | bytes 368648 | tf_op jit(solution)/shard_map/ppermute | solution.py:843
  72.1 5.7 %collective-permute-start.21 = (f32[6,40,128]{2,1,0:T(8,128)S(1)}, f32[6,40,128]{2,1,0:T(8,128)S(1)}, u32[]{:S(2)}, u32[]{:S(2)}) collective-permute-start(f32[6,40,128]{2,1,0:T(8,128)S(1)} %get-tuple-element.103), channel_id=1, source_target_pairs={{0,3},{1,0},{2,1},{3,2},{4,7},{5,4},{6,5},{7,6},{8,11},{9,8},{10,9... | collective-permute-start | bytes 368648 | tf_op jit(solution)/shard_map/ppermute | solution.py:843
  90.6 4.3 %collective-permute-start.29 = (f32[8,8,128]{2,1,0:T(8,128)S(1)}, f32[8,8,128]{2,1,0:T(8,128)S(1)}, u32[]{:S(2)}, u32[]{:S(2)}) collective-permute-start(f32[8,8,128]{2,1,0:T(8,128)S(1)} %gather_z.3.refs_0_), channel_id=1, source_target_pairs={{0,64},{32,96},{64,0},{96,32},{1,65},{33,97},{65,1},{97,33},{2,66}... | collective-permute-start | bytes 98312 | tf_op jit(solution)/shard_map/ppermute | solution.py:843
  90.6 4.3 %collective-permute-start.30 = (f32[8,8,128]{2,1,0:T(8,128)S(1)}, f32[8,8,128]{2,1,0:T(8,128)S(1)}, u32[]{:S(2)}, u32[]{:S(2)}) collective-permute-start(f32[8,8,128]{2,1,0:T(8,128)S(1)} %gather_z.3.refs_0_), channel_id=1, source_target_pairs={{0,96},{32,0},{64,32},{96,64},{1,97},{33,1},{65,33},{97,65},{2,98}... | collective-permute-start | bytes 98312 | tf_op jit(solution)/shard_map/ppermute | solution.py:843
  94.9 10.1 %collective-permute-start.31 = (f32[32,8,128]{2,1,0:T(8,128)S(1)}, f32[32,8,128]{2,1,0:T(8,128)S(1)}, u32[]{:S(2)}, u32[]{:S(2)}) collective-permute-start(f32[32,8,128]{2,1,0:T(8,128)S(1)} %gather_x.3.p0), channel_id=1, source_target_pairs={{0,4},{4,8},{8,12},{12,16},{16,20},{20,24},{24,28},{28,0},{1,5},{5... | collective-permute-start | bytes 393224 | tf_op jit(solution)/shard_map/ppermute | solution.py:843
  99.8 7.4 %collective-permute-start.32 = (f32[32,8,128]{2,1,0:T(8,128)S(1)}, f32[32,8,128]{2,1,0:T(8,128)S(1)}, u32[]{:S(2)}, u32[]{:S(2)}) collective-permute-start(f32[32,8,128]{2,1,0:T(8,128)S(1)} %gather_x.3.p0), channel_id=1, source_target_pairs={{0,8},{4,12},{8,16},{12,20},{16,24},{20,28},{24,0},{28,4},{1,9},{5... | collective-permute-start | bytes 393224 | tf_op jit(solution)/shard_map/ppermute | solution.py:843
  101.0 9.9 %collective-permute-start.33 = (f32[32,8,128]{2,1,0:T(8,128)S(1)}, f32[32,8,128]{2,1,0:T(8,128)S(1)}, u32[]{:S(2)}, u32[]{:S(2)}) collective-permute-start(f32[32,8,128]{2,1,0:T(8,128)S(1)} %gather_x.3.p0), channel_id=1, source_target_pairs={{0,12},{4,16},{8,20},{12,24},{16,28},{20,0},{24,4},{28,8},{1,13},{... | collective-permute-start | bytes 393224 | tf_op jit(solution)/shard_map/ppermute | solution.py:843
  101.9 11.2 %collective-permute-start.34 = (f32[32,8,128]{2,1,0:T(8,128)S(1)}, f32[32,8,128]{2,1,0:T(8,128)S(1)}, u32[]{:S(2)}, u32[]{:S(2)}) collective-permute-start(f32[32,8,128]{2,1,0:T(8,128)S(1)} %gather_x.3.p0), channel_id=1, source_target_pairs={{0,16},{4,20},{8,24},{12,28},{16,0},{20,4},{24,8},{28,12},{1,17},{... | collective-permute-start | bytes 393224 | tf_op jit(solution)/shard_map/ppermute | solution.py:843
  103.1 10.6 %collective-permute-start.35 = (f32[32,8,128]{2,1,0:T(8,128)S(1)}, f32[32,8,128]{2,1,0:T(8,128)S(1)}, u32[]{:S(2)}, u32[]{:S(2)}) collective-permute-start(f32[32,8,128]{2,1,0:T(8,128)S(1)} %gather_x.3.p0), channel_id=1, source_target_pairs={{0,20},{4,24},{8,28},{12,0},{16,4},{20,8},{24,12},{28,16},{1,21},{... | collective-permute-start | bytes 393224 | tf_op jit(solution)/shard_map/ppermute | solution.py:843
  105.0 8.7 %collective-permute-start.36 = (f32[32,8,128]{2,1,0:T(8,128)S(1)}, f32[32,8,128]{2,1,0:T(8,128)S(1)}, u32[]{:S(2)}, u32[]{:S(2)}) collective-permute-start(f32[32,8,128]{2,1,0:T(8,128)S(1)} %gather_x.3.p0), channel_id=1, source_target_pairs={{0,24},{4,28},{8,0},{12,4},{16,8},{20,12},{24,16},{28,20},{1,25},{... | collective-permute-start | bytes 393224 | tf_op jit(solution)/shard_map/ppermute | solution.py:843
  107.1 7.9 %collective-permute-start.37 = (f32[32,8,128]{2,1,0:T(8,128)S(1)}, f32[32,8,128]{2,1,0:T(8,128)S(1)}, u32[]{:S(2)}, u32[]{:S(2)}) collective-permute-start(f32[32,8,128]{2,1,0:T(8,128)S(1)} %gather_x.3.p0), channel_id=1, source_target_pairs={{0,28},{4,0},{8,4},{12,8},{16,12},{20,16},{24,20},{28,24},{1,29},{... | collective-permute-start | bytes 393224 | tf_op jit(solution)/shard_map/ppermute | solution.py:843
  (8 other events, 34.3 us)

commit v6 on v5

--- a/solution.py
+++ b/solution.py
@@ -610,10 +610,21 @@
         out[pl.ds(sender("gx", step) * 8, 8)] = part[...]
 
 
-def gather_y(parts, out):
+def stack_y(*refs):
+    *parts, _, out = refs
     for step, part in enumerate(parts):
-        row = pl.multiple_of(8 + sender("gy", step) * 8, 8)
-        out[8:40, pl.ds(row, 8), :] = part[...]
+        out[step] = part[...]
+
+
+def gather_y(same, other, out):
+    count = lax.axis_size("gy")
+    index = lax.axis_index("gy")
+    sibling = index + 1 - 2 * lax.rem(index, 2)
+    for stack, first in ((same, index), (other, sibling)):
+        for step in range(4):
+            owner = lax.rem(first + count - 2 * step, count)
+            row = pl.multiple_of(8 + owner * 8, 8)
+            out[8:40, pl.ds(row, 8), :] = stack[step]
 
 
 def clear_whole(ref):
@@ -626,11 +637,11 @@
         ref[x, 8:72, :] = jnp.zeros((64, 128), F32)
 
 
-def coarse_prepare(p0, p1, p2, p3, p4, p5, p6, p7, g, inv, total, g3, inv3, gw, invw, b2, b3, bw, rows):
+def coarse_prepare(same, sibling, g, inv, total, g3, inv3, gw, invw, b2, b3, bw, rows):
     clear_whole(b2)
     clear_edges(b3, 16, 32)
     clear_edges(bw, 22, 24)
-    gather_y((p0, p1, p2, p3, p4, p5, p6, p7), b2)
+    gather_y(same, sibling, b2)
     ring_weights(b2.at[7:41], None, g, inv, total, 32, 64, 16.0, edges=True)
     half_z = pick(lambda r, c: r // 2 == c)
 
@@ -667,12 +678,12 @@
 
 
 def bottom(
-    p0, p1, p2, p3, p4, p5, p6, p7, g, inv, total, g3, inv3, gw, invw, out,
+    same, sibling, g, inv, total, g3, inv3, gw, invw, out,
     s2, va, vb, sp, u, v3a, v3b, sp3, u3, rows, wa, wb, spw, uw,
 ):
     for ref in (s2, va, vb):
         clear_whole(ref)
-    gather_y((p0, p1, p2, p3, p4, p5, p6, p7), s2)
+    gather_y(same, sibling, s2)
 
     def scale(x):
         sp[x] = s2[x + 8, 8:72, :] * inv[x]
@@ -855,12 +866,13 @@
     return [value] + [ring(value, axis, step) for step in range(1, lax.axis_size(axis))]
 
 
-def carry(parts, steps, after, *values):
-    slab, _ = lax.optimization_barrier((parts[0], after))
-    moved = [ring(slab, "gy", step) for step in steps]
-    *values, last = lax.optimization_barrier((*values, tuple(moved)))
-    parts.extend(last)
-    return values
+def chips(value):
+    return [value] + [ring(value, "gy", 2 * step) for step in (1, 2, 3)]
+
+
+def across(value):
+    count = lax.axis_size("gy")
+    return lax.ppermute(value, "gy", [(i, i + 1 - 2 * (i % 2)) for i in range(count)])
 
 
 def per_device(source, beta):
@@ -869,24 +881,24 @@
     lo, hi, source, beta = lax.optimization_barrier((lo, hi, source, beta))
     x_lo, x_hi = trade(lo, hi, "gx")
     beta2 = call(coarse_beta, sds(16, 128), [vm(32, 128)], name="coarse_beta")(beta)
-    x_lo, x_hi, beta2 = lax.optimization_barrier((x_lo, x_hi, beta2))
+    beta2_block = gather(gather_z, around(beta2, "gz"), lo, 8, 8, 128)
+    x_lo, x_hi, beta2_block = lax.optimization_barrier((x_lo, x_hi, beta2_block))
     slab = sds(2, 48, 8, 128)
     mid = sds(48, 32, 128)
     lo, hi, s_mid, b_mid = call(pack_y, (slab, slab, mid, mid), name="pack_y", mib=4)(
         source, beta, x_lo, x_hi
     )
     y_lo, y_hi = trade(lo, hi, "gy")
-    beta2_block = gather(gather_z, around(beta2, "gz"), lo, 8, 8, 128)
-    y_lo, y_hi, beta2_block = lax.optimization_barrier((y_lo, y_hi, beta2_block))
+    beta2_slab = gather(gather_x, around(beta2_block, "gx"), lo, 32, 8, 128)
+    y_lo, y_hi, beta2_slab = lax.optimization_barrier((y_lo, y_hi, beta2_slab))
     whole = sds(48, 48, 128)
     strip = sds(6, 48, 128)
     src_ext, beta_ext, lo, hi = call(
         pack_z, (whole, whole, strip, strip), name="pack_z", mib=4
     )(s_mid, b_mid, y_lo, y_hi)
     z_lo, z_hi = trade(lo, hi, "gz")
-    beta2_slab = gather(gather_x, around(beta2_block, "gx"), lo, 32, 8, 128)
-    z_lo, z_hi, beta2_slab = lax.optimization_barrier((z_lo, z_hi, beta2_slab))
-    beta2_y = [beta2_slab]
+    beta2_stack = gather(stack_y, chips(beta2_slab), lo, 4, 32, 8, 128)
+    z_lo, z_hi, beta2_stack = lax.optimization_barrier((z_lo, z_hi, beta2_stack))
     iter0, iter0_t, c, lo, hi, *ready = call(
         level0_down,
         (
@@ -906,15 +918,15 @@
         mib=16,
     )(src_ext, beta_ext, z_lo, z_hi)
     x_lo, x_hi = trade(lo, hi, "gx")
-    x_lo, x_hi = carry(beta2_y, (1, 2, 3), lo, x_lo, x_hi)
     lo, hi = call(pack1_y, (sds(360, 128), sds(360, 128)), name="pack1_y")(c, x_lo, x_hi)
     y_lo, y_hi = trade(lo, hi, "gy")
-    y_lo, y_hi = carry(beta2_y, (4,), lo, y_lo, y_hi)
     ext, lo, hi = call(
         pack1_z, (sds(36, 40, 128), sds(6, 40, 128), sds(6, 40, 128)), name="pack1_z"
     )(c, x_lo, x_hi, y_lo, y_hi)
     z1_lo, z1_hi = trade(lo, hi, "gz")
-    z1_lo, z1_hi = carry(beta2_y, (5, 6, 7), lo, z1_lo, z1_hi)
+    beta2_stack, _ = lax.optimization_barrier((beta2_stack, lo))
+    beta2_other = across(beta2_stack)
+    z1_lo, z1_hi, beta2_other = lax.optimization_barrier((z1_lo, z1_hi, beta2_other))
     level1 = sds(36, 40, 128)
     iter1, chunk, g1, sp1, beta1 = call(
         level1_down,
@@ -926,15 +938,18 @@
     parts = around(chunk, "gz")
     parts = around(gather(gather_z, parts, chunk, 8, 8, 128), "gx")
     slab = gather(gather_x, parts, chunk, 32, 8, 128)
-    parts = around(slab, "gy")
+    stack = gather(stack_y, chips(slab), slab, 4, 32, 8, 128)
+    stack_other = across(stack)
     coarse = call(
         coarse_prepare,
         tuple(sds(*shape) for shape in COARSE_SHAPES),
         COARSE_SCRATCH,
         name="coarse_prepare",
         mib=8,
-    )(*beta2_y)
-    c2 = call(bottom, sds(18, 24, 128), BOTTOM_SCRATCH, name="bottom", mib=18)(*parts, *coarse)
+    )(beta2_stack, beta2_other)
+    c2 = call(bottom, sds(18, 24, 128), BOTTOM_SCRATCH, name="bottom", mib=18)(
+        stack, stack_other, *coarse
+    )
     c1 = call(
         level1_up,
         sds(24, 24, 128),

time: 140 us -> 131 us (0.936)
  starting transfers between devices: 52.4 us -> 47.4 us
  waiting for transfers between devices: 36.7 us -> 32.5 us
    ppermute x38 -> x30, starting transfers between devices: 52.4 us -> 40.7 us  [ring(): lax.ppermute(value, axis, [(i, (i + step) % count) for i in range(count)])]
    ppermute x0 -> x2, starting transfers between devices: none -> 6.68 us  [across(): lax.ppermute(value, 'gy', [(i, i + 1 - 2 * (i % 2)) for i in range(count)])]
    ppermute x38 -> x30, waiting for transfers between devices: 36.7 us -> 32.5 us  [ring(): lax.ppermute(value, axis, [(i, (i + step) % count) for i in range(count)])]
  transfers between devices with their start and end apart: 38 -> 32, of which waited for: 22 -> 22; matrix products, arithmetic and copies ran while one was open for 0% -> 0% of each run, Pallas kernels for 3% -> 3%
where the time goes in v6:
time: 131 us; the launch traced here: 129 us
  starting transfers between devices  47.4 us (36%)
  Pallas kernels  46.7 us (36%)
  waiting for transfers between devices  32.5 us (25%)
  local copies, waits for them, and re-layouts  2.07 us (2%)
    ppermute x30, starting transfers between devices, ring(): lax.ppermute(value, axis, [(i, (i + step) % count) for i in range(count)])  40.7 us
    ppermute x30, waiting for transfers between devices, ring(): lax.ppermute(value, axis, [(i, (i + step) % count) for i in range(count)])  32.5 us
    pallas_call x1, Pallas kernels, per_device(): call(level0_down, (whole, strip, sds(16, 16, 128), sds(10, 16, 128), sds(...  12.5 us
    pallas_call x1, Pallas kernels, per_device(): call(level0_up, sds(32, 32, 128), [vm(50, 64, 128), vm(50, 64, 128), vm(6...  10 us
    pallas_call x1, Pallas kernels, per_device(): call(bottom, sds(18, 24, 128), BOTTOM_SCRATCH, name='bottom', mib=18)  9.31 us
    ppermute x2, starting transfers between devices, across(): lax.ppermute(value, 'gy', [(i, i + 1 - 2 * (i % 2)) for i in range(count)])  6.68 us
    pallas_call x1, Pallas kernels, per_device(): call(level1_down, (level1, sds(16, 128), sds(6, 36, 40, 128), level1, lev...  4.25 us
    pallas_call x1, Pallas kernels, per_device(): call(level1_up, sds(24, 24, 128), [vm(38, 56, 128), vm(38, 56, 128), vm(3...  3.65 us
  transfers between devices with their start and end apart: 32, of which 22 were waited for; matrix products, arithmetic and copies ran while one was open for 0% of the time, Pallas kernels for 3%

profile of v6, /device:TPU:7, one launch (start us, length us, event | category | flops | bytes accessed | tf_op | source)
XLA Modules:
  0.0 128.9 jit_solution(13243289535981319687)
XLA Ops:
  2.7 2.1 %collective-permute-start = (f32[2,8,32,128]{3,2,1,0:T(8,128)S(1)}, f32[2,8,32,128]{3,2,1,0:T(8,128)S(1)}, u32[]{:S(2)}, u32[]{:S(2)}) collective-permute-start(f32[2,8,32,128]{3,2,1,0:T(8,128)S(1)} %get-tuple-element.59), channel_id=1, source_target_pairs={{0,32},{32,64},{64,96},{96,0},{1,33},{33,65},{65,97},{97,1},{2,34}... | collective-permute-start | bytes 786440 | tf_op jit(solution)/shard_map/ppermute | solution.py:854
  6.7 2.6 %collective-permute-start.3 = (f32[16,128]{1,0:T(8,128)S(1)}, f32[16,128]{1,0:T(8,128)S(1)}, u32[]{:S(2)}, u32[]{:S(2)}) collective-permute-start(f32[16,128]{1,0:T(8,128)S(1)} %coarse_beta.1.refs_0_), channel_id=1, source_target_pairs={{0,2},{1,3},{2,0},{3,1},{4,6},{5,7},{6,4},{7,5},{8,10},{9,11},{10,... | collective-permute-start | bytes 24584 | tf_op jit(solution)/shard_map/ppermute | solution.py:854
  10.7 1.4 %collective-permute-done.4.refs_3_ = f32[16,128]{1,0:T(8,128)S(1)} collective-permute-done((f32[16,128]{1,0:T(8,128)S(1)}, f32[16,128]{1,0:T(8,128)S(1)}, u32[]{:S(2)}, u32[]{:S(2)}) %collective-permute-start.4) | collective-permute-done | bytes 8224 | tf_op jit(solution)/shard_map/ppermute | solution.py:854
  12.5 4.2 %collective-permute-start.5 = (f32[2,48,8,128]{3,2,1,0:T(8,128)S(1)}, f32[2,48,8,128]{3,2,1,0:T(8,128)S(1)}, u32[]{:S(2)}, u32[]{:S(2)}) collective-permute-start(f32[2,48,8,128]{3,2,1,0:T(8,128)S(1)} %get-tuple-element.65), channel_id=1, source_target_pairs={{0,4},{4,8},{8,12},{12,16},{16,20},{20,24},{24,28},{28,0},{1,5},{5... | collective-permute-start | bytes 1179656 | tf_op jit(solution)/shard_map/ppermute | solution.py:854
  18.1 1.6 %collective-permute-done.7.refs_1_ = f32[8,8,128]{2,1,0:T(8,128)S(1)} collective-permute-done((f32[8,8,128]{2,1,0:T(8,128)S(1)}, f32[8,8,128]{2,1,0:T(8,128)S(1)}, u32[]{:S(2)}, u32[]{:S(2)}) %collective-permute-start.7) | collective-permute-done | bytes 32800 | tf_op jit(solution)/shard_map/ppermute | solution.py:854
  22.1 2.0 %collective-permute-done.6.y_hi = f32[2,48,8,128]{3,2,1,0:T(8,128)S(1)} collective-permute-done((f32[2,48,8,128]{3,2,1,0:T(8,128)S(1)}, f32[2,48,8,128]{3,2,1,0:T(8,128)S(1)}, u32[]{:S(2)}, u32[]{:S(2)}) %collective-permute-start.6) | collective-permute-done | bytes 393248 | tf_op jit(solution)/shard_map/ppermute | solution.py:854
  24.1 1.5 %pack_z.1 = (f32[48,48,128]{2,1,0:T(8,128)S(1)}, f32[48,48,128]{2,1,0:T(8,128)S(1)}, f32[6,48,128]{2,1,0:T(8,128)S(1)}, f32[6,48,128]{2,1,0:T(8,128)S(1)}) custom-call(f32[48,32,128]{2,1,0:T(8,128)S(1)} %get-tuple-element.63.s_mid, f32[48,32,128]{2,1,0:T(8,128)S(1)} %get-tuple-element.64.b_mid, f32[2,48,8,128]{3,2,1,0:T(8,128)S(1)} %collective-permute-done.5.y_lo, ...), custom_call_target="tpu_custom_call" | custom-call | tf_op jit(solution)/shard_map/pack_z/pallas_call | solution.py:896
  25.8 2.7 %collective-permute-start.11 = (f32[6,48,128]{2,1,0:T(8,128)S(1)}, f32[6,48,128]{2,1,0:T(8,128)S(1)}, u32[]{:S(2)}, u32[]{:S(2)}) collective-permute-start(f32[6,48,128]{2,1,0:T(8,128)S(1)} %get-tuple-element.73.refs_4_), channel_id=1, source_target_pairs={{0,3},{1,0},{2,1},{3,2},{4,7},{5,4},{6,5},{7,6},{8,11},{9,8},{10,9... | collective-permute-start | bytes 442376 | tf_op jit(solution)/shard_map/ppermute | solution.py:854
  28.4 1.3 %collective-permute-start.12 = (f32[32,8,128]{2,1,0:T(8,128)S(1)}, f32[32,8,128]{2,1,0:T(8,128)S(1)}, u32[]{:S(2)}, u32[]{:S(2)}) collective-permute-start(f32[32,8,128]{2,1,0:T(8,128)S(1)} %gather_x.2.refs_0_), channel_id=1, source_target_pairs={{0,8},{4,12},{8,16},{12,20},{16,24},{20,28},{24,0},{28,4},{1,9},{5... | collective-permute-start | bytes 393224 | tf_op jit(solution)/shard_map/ppermute | solution.py:854
  29.8 1.8 %collective-permute-start.13 = (f32[32,8,128]{2,1,0:T(8,128)S(1)}, f32[32,8,128]{2,1,0:T(8,128)S(1)}, u32[]{:S(2)}, u32[]{:S(2)}) collective-permute-start(f32[32,8,128]{2,1,0:T(8,128)S(1)} %gather_x.2.refs_0_), channel_id=1, source_target_pairs={{0,16},{4,20},{8,24},{12,28},{16,0},{20,4},{24,8},{28,12},{1,17},{... | collective-permute-start | bytes 393224 | tf_op jit(solution)/shard_map/ppermute | solution.py:854
  31.6 1.9 %collective-permute-start.14 = (f32[32,8,128]{2,1,0:T(8,128)S(1)}, f32[32,8,128]{2,1,0:T(8,128)S(1)}, u32[]{:S(2)}, u32[]{:S(2)}) collective-permute-start(f32[32,8,128]{2,1,0:T(8,128)S(1)} %gather_x.2.refs_0_), channel_id=1, source_target_pairs={{0,24},{4,28},{8,0},{12,4},{16,8},{20,12},{24,16},{28,20},{1,25},{... | collective-permute-start | bytes 393224 | tf_op jit(solution)/shard_map/ppermute | solution.py:854
  33.5 2.2 %collective-permute-done.13.refs_2_ = f32[32,8,128]{2,1,0:T(8,128)S(1)} collective-permute-done((f32[32,8,128]{2,1,0:T(8,128)S(1)}, f32[32,8,128]{2,1,0:T(8,128)S(1)}, u32[]{:S(2)}, u32[]{:S(2)}) %collective-permute-start.13) | collective-permute-done | bytes 131104 | tf_op jit(solution)/shard_map/ppermute | solution.py:854
  35.7 1.5 %collective-permute-done.14.refs_3_ = f32[32,8,128]{2,1,0:T(8,128)S(1)} collective-permute-done((f32[32,8,128]{2,1,0:T(8,128)S(1)}, f32[32,8,128]{2,1,0:T(8,128)S(1)}, u32[]{:S(2)}, u32[]{:S(2)}) %collective-permute-start.14) | collective-permute-done | bytes 131104 | tf_op jit(solution)/shard_map/ppermute | solution.py:854
  37.3 12.5 %level0_down.1 = (f32[48,48,128]{2,1,0:T(8,128)S(1)}, f32[6,48,128]{2,1,0:T(8,128)S(1)}, f32[16,16,128]{2,1,0:T(8,128)S(1)}, f32[10,16,128]{2,1,0:T(8,128)S(1)},...) custom-call(f32[48,48,128]{2,1,0:T(8,128)S(1)} %get-tuple-element.70, ...), custom_call_target="tpu_custom_call" | custom-call | tf_op jit(solution)/shard_map/level0_down/pallas_call | solution.py:902
  49.9 1.5 %collective-permute-start.16 = (f32[10,16,128]{2,1,0:T(8,128)S(1)}, f32[10,16,128]{2,1,0:T(8,128)S(1)}, u32[]{:S(2)}, u32[]{:S(2)}) collective-permute-start(f32[10,16,128]{2,1,0:T(8,128)S(1)} %get-tuple-element.79), channel_id=1, source_target_pairs={{0,96},{32,0},{64,32},{96,64},{1,97},{33,1},{65,33},{97,65},{2,98}... | collective-permute-start | bytes 245768 | tf_op jit(solution)/shard_map/ppermute | solution.py:854
  51.3 1.8 %collective-permute-done.15.from_lo.x_lo = f32[10,16,128]{2,1,0:T(8,128)S(1)} collective-permute-done((f32[10,16,128]{2,1,0:T(8,128)S(1)}, f32[10,16,128]{2,1,0:T(8,128)S(1)}, u32[]{:S(2)}, u32[]{:S(2)}) %collective-permute-start.15) | collective-permute-done | bytes 81952 | tf_op jit(solution)/shard_map/ppermute | solution.py:854
  54.5 5.5 %collective-permute-start.17 = (f32[360,128]{1,0:T(8,128)S(1)}, f32[360,128]{1,0:T(8,128)S(1)}, u32[]{:S(2)}, u32[]{:S(2)}) collective-permute-start(f32[360,128]{1,0:T(8,128)S(1)} %get-tuple-element.80), channel_id=1, source_target_pairs={{0,4},{4,8},{8,12},{12,16},{16,20},{20,24},{24,28},{28,0},{1,5},{5... | collective-permute-start | bytes 552968 | tf_op jit(solution)/shard_map/ppermute | solution.py:854
  60.0 2.5 %collective-permute-done.17.y_lo = f32[360,128]{1,0:T(8,128)S(1)} collective-permute-done((f32[360,128]{1,0:T(8,128)S(1)}, f32[360,128]{1,0:T(8,128)S(1)}, u32[]{:S(2)}, u32[]{:S(2)}) %collective-permute-start.17) | collective-permute-done | bytes 184352 | tf_op jit(solution)/shard_map/ppermute | solution.py:854
  62.5 2.5 %collective-permute-done.18.y_hi = f32[360,128]{1,0:T(8,128)S(1)} collective-permute-done((f32[360,128]{1,0:T(8,128)S(1)}, f32[360,128]{1,0:T(8,128)S(1)}, u32[]{:S(2)}, u32[]{:S(2)}) %collective-permute-start.18) | collective-permute-done | bytes 184352 | tf_op jit(solution)/shard_map/ppermute | solution.py:854
  66.3 2.7 %collective-permute-start.20 = (f32[6,40,128]{2,1,0:T(8,128)S(1)}, f32[6,40,128]{2,1,0:T(8,128)S(1)}, u32[]{:S(2)}, u32[]{:S(2)}) collective-permute-start(f32[6,40,128]{2,1,0:T(8,128)S(1)} %get-tuple-element.84), channel_id=1, source_target_pairs={{0,3},{1,0},{2,1},{3,2},{4,7},{5,4},{6,5},{7,6},{8,11},{9,8},{10,9... | collective-permute-start | bytes 368648 | tf_op jit(solution)/shard_map/ppermute | solution.py:854
  69.0 3.2 %collective-permute-done.19.z_lo = f32[6,40,128]{2,1,0:T(8,128)S(1)} collective-permute-done((f32[6,40,128]{2,1,0:T(8,128)S(1)}, f32[6,40,128]{2,1,0:T(8,128)S(1)}, u32[]{:S(2)}, u32[]{:S(2)}) %collective-permute-start.19) | collective-permute-done | bytes 122912 | tf_op jit(solution)/shard_map/ppermute | solution.py:854
  72.2 4.2 %level1_down.1 = (f32[36,40,128]{2,1,0:T(8,128)S(1)}, f32[16,128]{1,0:T(8,128)S(1)}, f32[6,36,40,128]{3,2,1,0:T(8,128)S(1)}, f32[36,40,128]{2,1,0:T(8,128)S(1)}, f32[36,40,128]{2,1,0:T(8,128)S(1)}) custom-call(f32[36,40,128]{2,1,0:T(8,128)S(1)} %get-tuple-element.82.ext, f32[6,40,128]{2,1,0:T(8,128)S(1)} %collective-permute-done.19.z_lo, ...), custom_call_target="tpu_custom_call" | custom-call | tf_op jit(solution)/shard_map/level1_down/pallas_call | solution.py:931
  76.5 3.5 %collective-permute-start.23 = (f32[16,128]{1,0:T(8,128)S(1)}, f32[16,128]{1,0:T(8,128)S(1)}, u32[]{:S(2)}, u32[]{:S(2)}) collective-permute-start(f32[16,128]{1,0:T(8,128)S(1)} %get-tuple-element.89.refs_0_.refs_4_), channel_id=1, source_target_pairs={{0,2},{1,3},{2,0},{3,1},{4,6},{5,7},{6,4},{7,5},{8,10},{9,11},{10,... | collective-permute-start | bytes 24584 | tf_op jit(solution)/shard_map/ppermute | solution.py:854
  81.1 1.7 %collective-permute-done.24.refs_3_ = f32[16,128]{1,0:T(8,128)S(1)} collective-permute-done((f32[16,128]{1,0:T(8,128)S(1)}, f32[16,128]{1,0:T(8,128)S(1)}, u32[]{:S(2)}, u32[]{:S(2)}) %collective-permute-start.24) | collective-permute-done | bytes 8224 | tf_op jit(solution)/shard_map/ppermute | solution.py:854
  85.8 1.6 %collective-permute-done.26.refs_2_ = f32[8,8,128]{2,1,0:T(8,128)S(1)} collective-permute-done((f32[8,8,128]{2,1,0:T(8,128)S(1)}, f32[8,8,128]{2,1,0:T(8,128)S(1)}, u32[]{:S(2)}, u32[]{:S(2)}) %collective-permute-start.26) | collective-permute-done | bytes 32800 | tf_op jit(solution)/shard_map/ppermute | solution.py:854
  89.2 3.1 %collective-permute-start.29 = (f32[32,8,128]{2,1,0:T(8,128)S(1)}, f32[32,8,128]{2,1,0:T(8,128)S(1)}, u32[]{:S(2)}, u32[]{:S(2)}) collective-permute-start(f32[32,8,128]{2,1,0:T(8,128)S(1)} %gather_x.3.refs_0_.refs_4_), channel_id=1, source_target_pairs={{0,16},{4,20},{8,24},{12,28},{16,0},{20,4},{24,8},{28,12},{1,17},{... | collective-permute-start | bytes 393224 | tf_op jit(solution)/shard_map/ppermute | solution.py:854
  93.5 2.6 %collective-permute-done.29.refs_2_ = f32[32,8,128]{2,1,0:T(8,128)S(1)} collective-permute-done((f32[32,8,128]{2,1,0:T(8,128)S(1)}, f32[32,8,128]{2,1,0:T(8,128)S(1)}, u32[]{:S(2)}, u32[]{:S(2)}) %collective-permute-start.29) | collective-permute-done | bytes 131104 | tf_op jit(solution)/shard_map/ppermute | solution.py:854
  96.2 6.2 %collective-permute-start.31 = (f32[4,32,8,128]{3,2,1,0:T(8,128)S(1)}, f32[4,32,8,128]{3,2,1,0:T(8,128)S(1)}, u32[]{:S(2)}, u32[]{:S(2)}) collective-permute-start(f32[4,32,8,128]{3,2,1,0:T(8,128)S(1)} %stack_y.3.same), channel_id=1, source_target_pairs={{0,4},{4,0},{8,12},{12,8},{16,20},{20,16},{24,28},{28,24},{1,5},{5... | collective-permute-start | bytes 1572872 | tf_op jit(solution)/shard_map/ppermute | solution.py:875
  102.4 3.6 %coarse_prepare.1 = (f32[6,32,64,128]{3,2,1,0:T(8,128)S(1)}, f32[32,64,128]{2,1,0:T(8,128)S(1)}, f32[32,64,128]{2,1,0:T(8,128)S(1)}, f32[6,16,32,128]{3,2,1,0:T(...) custom-call(f32[4,32,8,128]{3,2,1,0:T(8,128)S(1)} %stack_y.2.same, ...), custom_call_target="tpu_custom_call" | custom-call | tf_op jit(solution)/shard_map/coarse_prepare/pallas_call | solution.py:943
  105.9 9.3 %bottom.1.c2 = f32[18,24,128]{2,1,0:T(8,128)S(1)} custom-call(f32[4,32,8,128]{3,2,1,0:T(8,128)S(1)} %stack_y.3.same, f32[4,32,8,128]{3,2,1,0:T(8,128)S(1)} %collective-permute-done.31.sibling, f32[6,32,64,128]{3,2,1,0:T(8,128)S(1)} %get-tuple-element.91.g, f32[32,64,128]{2,1,0:T(8,128)S(1)} %get-tuple-element.92.inv, ...), custom_call_target="tpu_custom_call" | custom-call | tf_op jit(solution)/shard_map/bottom/pallas_call | solution.py:950
  115.3 3.7 %level1_up.1.c1 = f32[24,24,128]{2,1,0:T(8,128)S(1)} custom-call(f32[18,24,128]{2,1,0:T(8,128)S(1)} %bottom.1.c2, f32[6,36,40,128]{3,2,1,0:T(8,128)S(1)} %get-tuple-element.98.g, f32[36,40,128]{2,1,0:T(8,128)S(1)} %get-tuple-element.99.sp, f32[36,40,128]{2,1,0:T(8,128)S(1)} %get-tuple-element.100.beta, f32[36,40,128]{2,1,0:T(8,128)S(1)} %get-tuple-element.101.iterate), custom_call_target="tpu_custom_call" | custom-call | tf_op jit(solution)/shard_map/level1_up/pallas_call | solution.py:953
  118.9 10.0 %level0_up.1 = f32[32,32,128]{2,1,0:T(8,128)} custom-call(f32[24,24,128]{2,1,0:T(8,128)S(1)} %level1_up.1.c1, f32[48,48,128]{2,1,0:T(8,128)S(1)} %get-tuple-element.71.beta, f32[7,48,48,128]{3,2,1,0:T(8,128)S(1)} %get-tuple-element.102.g_main, f32[6,6,48,128]{3,2,1,0:T(8,128)S(1)} %get-tuple-element.103.g_strip, f32[48,48,128]{2,1,0:T(8,128)S(1)} %get-tuple-element.104.sp, ...), custom_call_target="tpu_custom_call" | custom-call | tf_op jit(solution)/shard_map/level0_up/pallas_call | solution.py:960
  (56 shorter events, 20.2 us)
Async XLA Ops:
  2.1 10.1 %collective-permute-start.1 = (f32[2,8,32,128]{3,2,1,0:T(8,128)S(1)}, f32[2,8,32,128]{3,2,1,0:T(8,128)S(1)}, u32[]{:S(2)}, u32[]{:S(2)}) collective-permute-start(f32[2,8,32,128]{3,2,1,0:T(8,128)S(1)} %get-tuple-element.60.refs_4_), channel_id=1, source_target_pairs={{0,96},{32,0},{64,32},{96,64},{1,97},{33,1},{65,33},{97,65},{2,98}... | collective-permute-start | bytes 786440 | tf_op jit(solution)/shard_map/ppermute | solution.py:854
  2.7 9.5 %collective-permute-start = (f32[2,8,32,128]{3,2,1,0:T(8,128)S(1)}, f32[2,8,32,128]{3,2,1,0:T(8,128)S(1)}, u32[]{:S(2)}, u32[]{:S(2)}) collective-permute-start(f32[2,8,32,128]{3,2,1,0:T(8,128)S(1)} %get-tuple-element.59), channel_id=1, source_target_pairs={{0,32},{32,64},{64,96},{96,0},{1,33},{33,65},{65,97},{97,1},{2,34}... | collective-permute-start | bytes 786440 | tf_op jit(solution)/shard_map/ppermute | solution.py:854
  5.4 5.0 %collective-permute-start.2 = (f32[16,128]{1,0:T(8,128)S(1)}, f32[16,128]{1,0:T(8,128)S(1)}, u32[]{:S(2)}, u32[]{:S(2)}) collective-permute-start(f32[16,128]{1,0:T(8,128)S(1)} %coarse_beta.1.refs_0_), channel_id=1, source_target_pairs={{0,1},{1,2},{2,3},{3,0},{4,5},{5,6},{6,7},{7,4},{8,9},{9,10},{10,1... | collective-permute-start | bytes 24584 | tf_op jit(solution)/shard_map/ppermute | solution.py:854
  6.7 4.0 %collective-permute-start.3 = (f32[16,128]{1,0:T(8,128)S(1)}, f32[16,128]{1,0:T(8,128)S(1)}, u32[]{:S(2)}, u32[]{:S(2)}) collective-permute-start(f32[16,128]{1,0:T(8,128)S(1)} %coarse_beta.1.refs_0_), channel_id=1, source_target_pairs={{0,2},{1,3},{2,0},{3,1},{4,6},{5,7},{6,4},{7,5},{8,10},{9,11},{10,... | collective-permute-start | bytes 24584 | tf_op jit(solution)/shard_map/ppermute | solution.py:854
  9.4 2.8 %collective-permute-start.4 = (f32[16,128]{1,0:T(8,128)S(1)}, f32[16,128]{1,0:T(8,128)S(1)}, u32[]{:S(2)}, u32[]{:S(2)}) collective-permute-start(f32[16,128]{1,0:T(8,128)S(1)} %coarse_beta.1.refs_0_), channel_id=1, source_target_pairs={{0,3},{1,0},{2,1},{3,2},{4,7},{5,4},{6,5},{7,6},{8,11},{9,8},{10,9... | collective-permute-start | bytes 24584 | tf_op jit(solution)/shard_map/ppermute | solution.py:854
  12.5 9.7 %collective-permute-start.5 = (f32[2,48,8,128]{3,2,1,0:T(8,128)S(1)}, f32[2,48,8,128]{3,2,1,0:T(8,128)S(1)}, u32[]{:S(2)}, u32[]{:S(2)}) collective-permute-start(f32[2,48,8,128]{3,2,1,0:T(8,128)S(1)} %get-tuple-element.65), channel_id=1, source_target_pairs={{0,4},{4,8},{8,12},{12,16},{16,20},{20,24},{24,28},{28,0},{1,5},{5... | collective-permute-start | bytes 1179656 | tf_op jit(solution)/shard_map/ppermute | solution.py:854
  16.6 7.5 %collective-permute-start.6 = (f32[2,48,8,128]{3,2,1,0:T(8,128)S(1)}, f32[2,48,8,128]{3,2,1,0:T(8,128)S(1)}, u32[]{:S(2)}, u32[]{:S(2)}) collective-permute-start(f32[2,48,8,128]{3,2,1,0:T(8,128)S(1)} %get-tuple-element.66.refs_4_), channel_id=1, source_target_pairs={{0,28},{4,0},{8,4},{12,8},{16,12},{20,16},{24,20},{28,24},{1,29},{... | collective-permute-start | bytes 1179656 | tf_op jit(solution)/shard_map/ppermute | solution.py:854
  16.6 3.1 %collective-permute-start.7 = (f32[8,8,128]{2,1,0:T(8,128)S(1)}, f32[8,8,128]{2,1,0:T(8,128)S(1)}, u32[]{:S(2)}, u32[]{:S(2)}) collective-permute-start(f32[8,8,128]{2,1,0:T(8,128)S(1)} %gather_z.2.refs_0_), channel_id=1, source_target_pairs={{0,32},{32,64},{64,96},{96,0},{1,33},{33,65},{65,97},{97,1},{2,34}... | collective-permute-start | bytes 98312 | tf_op jit(solution)/shard_map/ppermute | solution.py:854
  16.7 4.3 %collective-permute-start.8 = (f32[8,8,128]{2,1,0:T(8,128)S(1)}, f32[8,8,128]{2,1,0:T(8,128)S(1)}, u32[]{:S(2)}, u32[]{:S(2)}) collective-permute-start(f32[8,8,128]{2,1,0:T(8,128)S(1)} %gather_z.2.refs_0_), channel_id=1, source_target_pairs={{0,64},{32,96},{64,0},{96,32},{1,65},{33,97},{65,1},{97,33},{2,66}... | collective-permute-start | bytes 98312 | tf_op jit(solution)/shard_map/ppermute | solution.py:854
  17.8 4.3 %collective-permute-start.9 = (f32[8,8,128]{2,1,0:T(8,128)S(1)}, f32[8,8,128]{2,1,0:T(8,128)S(1)}, u32[]{:S(2)}, u32[]{:S(2)}) collective-permute-start(f32[8,8,128]{2,1,0:T(8,128)S(1)} %gather_z.2.refs_0_), channel_id=1, source_target_pairs={{0,96},{32,0},{64,32},{96,64},{1,97},{33,1},{65,33},{97,65},{2,98}... | collective-permute-start | bytes 98312 | tf_op jit(solution)/shard_map/ppermute | solution.py:854
  25.7 11.6 %collective-permute-start.10 = (f32[6,48,128]{2,1,0:T(8,128)S(1)}, f32[6,48,128]{2,1,0:T(8,128)S(1)}, u32[]{:S(2)}, u32[]{:S(2)}) collective-permute-start(f32[6,48,128]{2,1,0:T(8,128)S(1)} %get-tuple-element.72), channel_id=1, source_target_pairs={{0,1},{1,2},{2,3},{3,0},{4,5},{5,6},{6,7},{7,4},{8,9},{9,10},{10,1... | collective-permute-start | bytes 442376 | tf_op jit(solution)/shard_map/ppermute | solution.py:854
  25.8 11.5 %collective-permute-start.11 = (f32[6,48,128]{2,1,0:T(8,128)S(1)}, f32[6,48,128]{2,1,0:T(8,128)S(1)}, u32[]{:S(2)}, u32[]{:S(2)}) collective-permute-start(f32[6,48,128]{2,1,0:T(8,128)S(1)} %get-tuple-element.73.refs_4_), channel_id=1, source_target_pairs={{0,3},{1,0},{2,1},{3,2},{4,7},{5,4},{6,5},{7,6},{8,11},{9,8},{10,9... | collective-permute-start | bytes 442376 | tf_op jit(solution)/shard_map/ppermute | solution.py:854
  28.4 5.1 %collective-permute-start.12 = (f32[32,8,128]{2,1,0:T(8,128)S(1)}, f32[32,8,128]{2,1,0:T(8,128)S(1)}, u32[]{:S(2)}, u32[]{:S(2)}) collective-permute-start(f32[32,8,128]{2,1,0:T(8,128)S(1)} %gather_x.2.refs_0_), channel_id=1, source_target_pairs={{0,8},{4,12},{8,16},{12,20},{16,24},{20,28},{24,0},{28,4},{1,9},{5... | collective-permute-start | bytes 393224 | tf_op jit(solution)/shard_map/ppermute | solution.py:854
  29.8 6.0 %collective-permute-start.13 = (f32[32,8,128]{2,1,0:T(8,128)S(1)}, f32[32,8,128]{2,1,0:T(8,128)S(1)}, u32[]{:S(2)}, u32[]{:S(2)}) collective-permute-start(f32[32,8,128]{2,1,0:T(8,128)S(1)} %gather_x.2.refs_0_), channel_id=1, source_target_pairs={{0,16},{4,20},{8,24},{12,28},{16,0},{20,4},{24,8},{28,12},{1,17},{... | collective-permute-start | bytes 393224 | tf_op jit(solution)/shard_map/ppermute | solution.py:854
  31.6 5.7 %collective-permute-start.14 = (f32[32,8,128]{2,1,0:T(8,128)S(1)}, f32[32,8,128]{2,1,0:T(8,128)S(1)}, u32[]{:S(2)}, u32[]{:S(2)}) collective-permute-start(f32[32,8,128]{2,1,0:T(8,128)S(1)} %gather_x.2.refs_0_), channel_id=1, source_target_pairs={{0,24},{4,28},{8,0},{12,4},{16,8},{20,12},{24,16},{28,20},{1,25},{... | collective-permute-start | bytes 393224 | tf_op jit(solution)/shard_map/ppermute | solution.py:854
  49.8 3.4 %collective-permute-start.15 = (f32[10,16,128]{2,1,0:T(8,128)S(1)}, f32[10,16,128]{2,1,0:T(8,128)S(1)}, u32[]{:S(2)}, u32[]{:S(2)}) collective-permute-start(f32[10,16,128]{2,1,0:T(8,128)S(1)} %get-tuple-element.78), channel_id=1, source_target_pairs={{0,32},{32,64},{64,96},{96,0},{1,33},{33,65},{65,97},{97,1},{2,34}... | collective-permute-start | bytes 245768 | tf_op jit(solution)/shard_map/ppermute | solution.py:854
  49.9 4.6 %collective-permute-start.16 = (f32[10,16,128]{2,1,0:T(8,128)S(1)}, f32[10,16,128]{2,1,0:T(8,128)S(1)}, u32[]{:S(2)}, u32[]{:S(2)}) collective-permute-start(f32[10,16,128]{2,1,0:T(8,128)S(1)} %get-tuple-element.79), channel_id=1, source_target_pairs={{0,96},{32,0},{64,32},{96,64},{1,97},{33,1},{65,33},{97,65},{2,98}... | collective-permute-start | bytes 245768 | tf_op jit(solution)/shard_map/ppermute | solution.py:854
  54.5 8.0 %collective-permute-start.17 = (f32[360,128]{1,0:T(8,128)S(1)}, f32[360,128]{1,0:T(8,128)S(1)}, u32[]{:S(2)}, u32[]{:S(2)}) collective-permute-start(f32[360,128]{1,0:T(8,128)S(1)} %get-tuple-element.80), channel_id=1, source_target_pairs={{0,4},{4,8},{8,12},{12,16},{16,20},{20,24},{24,28},{28,0},{1,5},{5... | collective-permute-start | bytes 552968 | tf_op jit(solution)/shard_map/ppermute | solution.py:854
  60.0 5.0 %collective-permute-start.18 = (f32[360,128]{1,0:T(8,128)S(1)}, f32[360,128]{1,0:T(8,128)S(1)}, u32[]{:S(2)}, u32[]{:S(2)}) collective-permute-start(f32[360,128]{1,0:T(8,128)S(1)} %get-tuple-element.81), channel_id=1, source_target_pairs={{0,28},{4,0},{8,4},{12,8},{16,12},{20,16},{24,20},{28,24},{1,29},{... | collective-permute-start | bytes 552968 | tf_op jit(solution)/shard_map/ppermute | solution.py:854
  65.8 6.4 %collective-permute-start.21 = (f32[4,32,8,128]{3,2,1,0:T(8,128)S(1)}, f32[4,32,8,128]{3,2,1,0:T(8,128)S(1)}, u32[]{:S(2)}, u32[]{:S(2)}) collective-permute-start(f32[4,32,8,128]{3,2,1,0:T(8,128)S(1)} %stack_y.2.same), channel_id=1, source_target_pairs={{0,4},{4,0},{8,12},{12,8},{16,20},{20,16},{24,28},{28,24},{1,5},{5... | collective-permute-start | bytes 1572872 | tf_op jit(solution)/shard_map/ppermute | solution.py:875
  66.3 5.9 %collective-permute-start.19 = (f32[6,40,128]{2,1,0:T(8,128)S(1)}, f32[6,40,128]{2,1,0:T(8,128)S(1)}, u32[]{:S(2)}, u32[]{:S(2)}) collective-permute-start(f32[6,40,128]{2,1,0:T(8,128)S(1)} %get-tuple-element.83), channel_id=1, source_target_pairs={{0,1},{1,2},{2,3},{3,0},{4,5},{5,6},{6,7},{7,4},{8,9},{9,10},{10,1... | collective-permute-start | bytes 368648 | tf_op jit(solution)/shard_map/ppermute | solution.py:854
  66.3 5.9 %collective-permute-start.20 = (f32[6,40,128]{2,1,0:T(8,128)S(1)}, f32[6,40,128]{2,1,0:T(8,128)S(1)}, u32[]{:S(2)}, u32[]{:S(2)}) collective-permute-start(f32[6,40,128]{2,1,0:T(8,128)S(1)} %get-tuple-element.84), channel_id=1, source_target_pairs={{0,3},{1,0},{2,1},{3,2},{4,7},{5,4},{6,5},{7,6},{8,11},{9,8},{10,9... | collective-permute-start | bytes 368648 | tf_op jit(solution)/shard_map/ppermute | solution.py:854
  76.4 3.8 %collective-permute-start.22 = (f32[16,128]{1,0:T(8,128)S(1)}, f32[16,128]{1,0:T(8,128)S(1)}, u32[]{:S(2)}, u32[]{:S(2)}) collective-permute-start(f32[16,128]{1,0:T(8,128)S(1)} %get-tuple-element.89.refs_0_.refs_4_), channel_id=1, source_target_pairs={{0,1},{1,2},{2,3},{3,0},{4,5},{5,6},{6,7},{7,4},{8,9},{9,10},{10,1... | collective-permute-start | bytes 24584 | tf_op jit(solution)/shard_map/ppermute | solution.py:854
  76.5 4.6 %collective-permute-start.23 = (f32[16,128]{1,0:T(8,128)S(1)}, f32[16,128]{1,0:T(8,128)S(1)}, u32[]{:S(2)}, u32[]{:S(2)}) collective-permute-start(f32[16,128]{1,0:T(8,128)S(1)} %get-tuple-element.89.refs_0_.refs_4_), channel_id=1, source_target_pairs={{0,2},{1,3},{2,0},{3,1},{4,6},{5,7},{6,4},{7,5},{8,10},{9,11},{10,... | collective-permute-start | bytes 24584 | tf_op jit(solution)/shard_map/ppermute | solution.py:854
  80.0 2.8 %collective-permute-start.24 = (f32[16,128]{1,0:T(8,128)S(1)}, f32[16,128]{1,0:T(8,128)S(1)}, u32[]{:S(2)}, u32[]{:S(2)}) collective-permute-start(f32[16,128]{1,0:T(8,128)S(1)} %get-tuple-element.89.refs_0_.refs_4_), channel_id=1, source_target_pairs={{0,3},{1,0},{2,1},{3,2},{4,7},{5,4},{6,5},{7,6},{8,11},{9,8},{10,9... | collective-permute-start | bytes 24584 | tf_op jit(solution)/shard_map/ppermute | solution.py:854
  83.0 2.8 %collective-permute-start.25 = (f32[8,8,128]{2,1,0:T(8,128)S(1)}, f32[8,8,128]{2,1,0:T(8,128)S(1)}, u32[]{:S(2)}, u32[]{:S(2)}) collective-permute-start(f32[8,8,128]{2,1,0:T(8,128)S(1)} %gather_z.3.refs_0_), channel_id=1, source_target_pairs={{0,32},{32,64},{64,96},{96,0},{1,33},{33,65},{65,97},{97,1},{2,34}... | collective-permute-start | bytes 98312 | tf_op jit(solution)/shard_map/ppermute | solution.py:854
  83.0 4.3 %collective-permute-start.26 = (f32[8,8,128]{2,1,0:T(8,128)S(1)}, f32[8,8,128]{2,1,0:T(8,128)S(1)}, u32[]{:S(2)}, u32[]{:S(2)}) collective-permute-start(f32[8,8,128]{2,1,0:T(8,128)S(1)} %gather_z.3.refs_0_), channel_id=1, source_target_pairs={{0,64},{32,96},{64,0},{96,32},{1,65},{33,97},{65,1},{97,33},{2,66}... | collective-permute-start | bytes 98312 | tf_op jit(solution)/shard_map/ppermute | solution.py:854
  83.9 4.3 %collective-permute-start.27 = (f32[8,8,128]{2,1,0:T(8,128)S(1)}, f32[8,8,128]{2,1,0:T(8,128)S(1)}, u32[]{:S(2)}, u32[]{:S(2)}) collective-permute-start(f32[8,8,128]{2,1,0:T(8,128)S(1)} %gather_z.3.refs_0_), channel_id=1, source_target_pairs={{0,96},{32,0},{64,32},{96,64},{1,97},{33,1},{65,33},{97,65},{2,98}... | collective-permute-start | bytes 98312 | tf_op jit(solution)/shard_map/ppermute | solution.py:854
  88.2 5.3 %collective-permute-start.28 = (f32[32,8,128]{2,1,0:T(8,128)S(1)}, f32[32,8,128]{2,1,0:T(8,128)S(1)}, u32[]{:S(2)}, u32[]{:S(2)}) collective-permute-start(f32[32,8,128]{2,1,0:T(8,128)S(1)} %gather_x.3.refs_0_.refs_4_), channel_id=1, source_target_pairs={{0,8},{4,12},{8,16},{12,20},{16,24},{20,28},{24,0},{28,4},{1,9},{5... | collective-permute-start | bytes 393224 | tf_op jit(solution)/shard_map/ppermute | solution.py:854
  89.2 6.9 %collective-permute-start.29 = (f32[32,8,128]{2,1,0:T(8,128)S(1)}, f32[32,8,128]{2,1,0:T(8,128)S(1)}, u32[]{:S(2)}, u32[]{:S(2)}) collective-permute-start(f32[32,8,128]{2,1,0:T(8,128)S(1)} %gather_x.3.refs_0_.refs_4_), channel_id=1, source_target_pairs={{0,16},{4,20},{8,24},{12,28},{16,0},{20,4},{24,8},{28,12},{1,17},{... | collective-permute-start | bytes 393224 | tf_op jit(solution)/shard_map/ppermute | solution.py:854
  92.3 3.8 %collective-permute-start.30 = (f32[32,8,128]{2,1,0:T(8,128)S(1)}, f32[32,8,128]{2,1,0:T(8,128)S(1)}, u32[]{:S(2)}, u32[]{:S(2)}) collective-permute-start(f32[32,8,128]{2,1,0:T(8,128)S(1)} %gather_x.3.refs_0_.refs_4_), channel_id=1, source_target_pairs={{0,24},{4,28},{8,0},{12,4},{16,8},{20,12},{24,16},{28,20},{1,25},{... | collective-permute-start | bytes 393224 | tf_op jit(solution)/shard_map/ppermute | solution.py:854
  96.2 9.8 %collective-permute-start.31 = (f32[4,32,8,128]{3,2,1,0:T(8,128)S(1)}, f32[4,32,8,128]{3,2,1,0:T(8,128)S(1)}, u32[]{:S(2)}, u32[]{:S(2)}) collective-permute-start(f32[4,32,8,128]{3,2,1,0:T(8,128)S(1)} %stack_y.3.same), channel_id=1, source_target_pairs={{0,4},{4,0},{8,12},{12,8},{16,20},{20,16},{24,28},{28,24},{1,5},{5... | collective-permute-start | bytes 1572872 | tf_op jit(solution)/shard_map/ppermute | solution.py:875
  (2 other events, 17.2 us)

commit v7 on v6

--- a/solution.py
+++ b/solution.py
@@ -231,7 +231,7 @@
         if total is not None:
             total[x] = tot
 
-    loop(0, 48, 12, body)
+    loop(0, 48, 6, body)
     for xx in range(6):
         before, after = strip_sides(bt_pad, xx)
         down, up = strip_z(bt_pad, ghost, xx, lane)
@@ -476,7 +476,7 @@
         if total is not None:
             total[x] = tot
 
-    loop(0, planes, rows // 4, body)
+    loop(0, planes, rows // 5, body)
 
 
 def ring_rest(v, g, sp, x, rows):
@@ -591,8 +591,13 @@
     return lax.rem(lax.axis_index(axis) + count - step, count)
 
 
+def singles(parts):
+    return [part.at[i] for part in parts for i in range(2)] if len(parts) == 2 else parts
+
+
 def gather_z(*refs):
     *parts, _, out = refs
+    parts = singles(parts)
     lane = lanes_of(8)
     for half in range(2):
         for quarter in range(4):
@@ -606,14 +611,20 @@
 
 def gather_x(*refs):
     *parts, _, out = refs
+    parts = singles(parts)
     for step, part in enumerate(parts):
         out[pl.ds(sender("gx", step) * 8, 8)] = part[...]
 
 
 def stack_y(*refs):
     *parts, _, out = refs
-    for step, part in enumerate(parts):
+    for step, part in enumerate(singles(parts)):
         out[step] = part[...]
+
+
+def pair(mine, other, _, out):
+    out[0] = mine[...]
+    out[1] = other[...]
 
 
 def gather_y(same, other, out):
@@ -881,24 +892,24 @@
     lo, hi, source, beta = lax.optimization_barrier((lo, hi, source, beta))
     x_lo, x_hi = trade(lo, hi, "gx")
     beta2 = call(coarse_beta, sds(16, 128), [vm(32, 128)], name="coarse_beta")(beta)
-    beta2_block = gather(gather_z, around(beta2, "gz"), lo, 8, 8, 128)
-    x_lo, x_hi, beta2_block = lax.optimization_barrier((x_lo, x_hi, beta2_block))
+    beta2_pair = gather(pair, [beta2, ring(beta2, "gz", 1)], lo, 2, 16, 128)
+    x_lo, x_hi, beta2_pair = lax.optimization_barrier((x_lo, x_hi, beta2_pair))
     slab = sds(2, 48, 8, 128)
     mid = sds(48, 32, 128)
     lo, hi, s_mid, b_mid = call(pack_y, (slab, slab, mid, mid), name="pack_y", mib=4)(
         source, beta, x_lo, x_hi
     )
     y_lo, y_hi = trade(lo, hi, "gy")
-    beta2_slab = gather(gather_x, around(beta2_block, "gx"), lo, 32, 8, 128)
-    y_lo, y_hi, beta2_slab = lax.optimization_barrier((y_lo, y_hi, beta2_slab))
+    beta2_block = gather(gather_z, [beta2_pair, ring(beta2_pair, "gz", 2)], lo, 8, 8, 128)
+    y_lo, y_hi, beta2_block = lax.optimization_barrier((y_lo, y_hi, beta2_block))
     whole = sds(48, 48, 128)
     strip = sds(6, 48, 128)
     src_ext, beta_ext, lo, hi = call(
         pack_z, (whole, whole, strip, strip), name="pack_z", mib=4
     )(s_mid, b_mid, y_lo, y_hi)
     z_lo, z_hi = trade(lo, hi, "gz")
-    beta2_stack = gather(stack_y, chips(beta2_slab), lo, 4, 32, 8, 128)
-    z_lo, z_hi, beta2_stack = lax.optimization_barrier((z_lo, z_hi, beta2_stack))
+    beta2_pair = gather(pair, [beta2_block, ring(beta2_block, "gx", 1)], lo, 2, 8, 8, 128)
+    z_lo, z_hi, beta2_pair = lax.optimization_barrier((z_lo, z_hi, beta2_pair))
     iter0, iter0_t, c, lo, hi, *ready = call(
         level0_down,
         (
@@ -918,15 +929,20 @@
         mib=16,
     )(src_ext, beta_ext, z_lo, z_hi)
     x_lo, x_hi = trade(lo, hi, "gx")
+    beta2_pair, _ = lax.optimization_barrier((beta2_pair, lo))
+    beta2_slab = gather(gather_x, [beta2_pair, ring(beta2_pair, "gx", 2)], lo, 32, 8, 128)
+    x_lo, x_hi, beta2_slab = lax.optimization_barrier((x_lo, x_hi, beta2_slab))
     lo, hi = call(pack1_y, (sds(360, 128), sds(360, 128)), name="pack1_y")(c, x_lo, x_hi)
     y_lo, y_hi = trade(lo, hi, "gy")
+    beta2_pair = gather(pair, [beta2_slab, ring(beta2_slab, "gy", 2)], lo, 2, 32, 8, 128)
+    y_lo, y_hi, beta2_pair = lax.optimization_barrier((y_lo, y_hi, beta2_pair))
     ext, lo, hi = call(
         pack1_z, (sds(36, 40, 128), sds(6, 40, 128), sds(6, 40, 128)), name="pack1_z"
     )(c, x_lo, x_hi, y_lo, y_hi)
     z1_lo, z1_hi = trade(lo, hi, "gz")
-    beta2_stack, _ = lax.optimization_barrier((beta2_stack, lo))
-    beta2_other = across(beta2_stack)
-    z1_lo, z1_hi, beta2_other = lax.optimization_barrier((z1_lo, z1_hi, beta2_other))
+    beta2_pair, _ = lax.optimization_barrier((beta2_pair, lo))
+    beta2_stack = gather(stack_y, [beta2_pair, ring(beta2_pair, "gy", 4)], lo, 4, 32, 8, 128)
+    z1_lo, z1_hi, beta2_stack = lax.optimization_barrier((z1_lo, z1_hi, beta2_stack))
     level1 = sds(36, 40, 128)
     iter1, chunk, g1, sp1, beta1 = call(
         level1_down,
@@ -936,6 +952,8 @@
         mib=8,
     )(ext, z1_lo, z1_hi)
     parts = around(chunk, "gz")
+    beta2_stack, _ = lax.optimization_barrier((beta2_stack, chunk))
+    *parts, beta2_other = lax.optimization_barrier((*parts, across(beta2_stack)))
     parts = around(gather(gather_z, parts, chunk, 8, 8, 128), "gx")
     slab = gather(gather_x, parts, chunk, 32, 8, 128)
     stack = gather(stack_y, chips(slab), slab, 4, 32, 8, 128)

time: 131 us -> 127 us (0.969)
  waiting for transfers between devices: 32.5 us -> 29.2 us
    ppermute x30 -> x27, waiting for transfers between devices: 32.5 us -> 29.2 us  [ring(): lax.ppermute(value, axis, [(i, (i + step) % count) for i in range(count)])]
    ppermute x30 -> x27, starting transfers between devices: 40.7 us -> 40 us  [ring(): lax.ppermute(value, axis, [(i, (i + step) % count) for i in range(count)])]
  transfers between devices with their start and end apart: 32 -> 29, of which waited for: 22 -> 19; matrix products, arithmetic and copies ran while one was open for 0% -> 0% of each run, Pallas kernels for 3% -> 3%
where the time goes in v7:
time: 127 us; the launch traced here: 126 us
  starting transfers between devices  47.8 us (38%)
  Pallas kernels  46.3 us (36%)
  waiting for transfers between devices  29.2 us (23%)
  local copies, waits for them, and re-layouts  2.07 us (2%)
    ppermute x27, starting transfers between devices, ring(): lax.ppermute(value, axis, [(i, (i + step) % count) for i in range(count)])  40 us
    ppermute x27, waiting for transfers between devices, ring(): lax.ppermute(value, axis, [(i, (i + step) % count) for i in range(count)])  29.2 us
    pallas_call x1, Pallas kernels, per_device(): call(level0_down, (whole, strip, sds(16, 16, 128), sds(10, 16, 128), sds(...  12.2 us
    pallas_call x1, Pallas kernels, per_device(): call(level0_up, sds(32, 32, 128), [vm(50, 64, 128), vm(50, 64, 128), vm(6...  10 us
    pallas_call x1, Pallas kernels, per_device(): call(bottom, sds(18, 24, 128), BOTTOM_SCRATCH, name='bottom', mib=18)  9.31 us
    ppermute x2, starting transfers between devices, across(): lax.ppermute(value, 'gy', [(i, i + 1 - 2 * (i % 2)) for i in range(count)])  7.84 us
    pallas_call x1, Pallas kernels, per_device(): call(level1_down, (level1, sds(16, 128), sds(6, 36, 40, 128), level1, lev...  4.14 us
    pallas_call x1, Pallas kernels, per_device(): call(level1_up, sds(24, 24, 128), [vm(38, 56, 128), vm(38, 56, 128), vm(3...  3.65 us
  transfers between devices with their start and end apart: 29, of which 19 were waited for; matrix products, arithmetic and copies ran while one was open for 0% of the time, Pallas kernels for 3%

profile of v7, /device:TPU:7, one launch (start us, length us, event | category | flops | bytes accessed | tf_op | source)
XLA Modules:
  0.0 125.6 jit_solution(7339038115496549146)
XLA Ops:
  2.7 2.1 %collective-permute-start = (f32[2,8,32,128]{3,2,1,0:T(8,128)S(1)}, f32[2,8,32,128]{3,2,1,0:T(8,128)S(1)}, u32[]{:S(2)}, u32[]{:S(2)}) collective-permute-start(f32[2,8,32,128]{3,2,1,0:T(8,128)S(1)} %get-tuple-element.72), channel_id=1, source_target_pairs={{0,32},{32,64},{64,96},{96,0},{1,33},{33,65},{65,97},{97,1},{2,34}... | collective-permute-start | bytes 786440 | tf_op jit(solution)/shard_map/ppermute | solution.py:865
  5.4 1.3 %collective-permute-start.2 = (f32[16,128]{1,0:T(8,128)S(1)}, f32[16,128]{1,0:T(8,128)S(1)}, u32[]{:S(2)}, u32[]{:S(2)}) collective-permute-start(f32[16,128]{1,0:T(8,128)S(1)} %coarse_beta.1.mine), channel_id=1, source_target_pairs={{0,1},{1,2},{2,3},{3,0},{4,5},{5,6},{6,7},{7,4},{8,9},{9,10},{10,1... | collective-permute-start | bytes 24584 | tf_op jit(solution)/shard_map/ppermute | solution.py:865
  6.7 2.8 %collective-permute-done.2.other = f32[16,128]{1,0:T(8,128)S(1)} collective-permute-done((f32[16,128]{1,0:T(8,128)S(1)}, f32[16,128]{1,0:T(8,128)S(1)}, u32[]{:S(2)}, u32[]{:S(2)}) %collective-permute-start.2) | collective-permute-done | bytes 8224 | tf_op jit(solution)/shard_map/ppermute | solution.py:865
  10.7 3.1 %collective-permute-start.3 = (f32[2,48,8,128]{3,2,1,0:T(8,128)S(1)}, f32[2,48,8,128]{3,2,1,0:T(8,128)S(1)}, u32[]{:S(2)}, u32[]{:S(2)}) collective-permute-start(f32[2,48,8,128]{3,2,1,0:T(8,128)S(1)} %get-tuple-element.78), channel_id=1, source_target_pairs={{0,4},{4,8},{8,12},{12,16},{16,20},{20,24},{24,28},{28,0},{1,5},{5... | collective-permute-start | bytes 1179656 | tf_op jit(solution)/shard_map/ppermute | solution.py:865
  13.8 2.9 %collective-permute-start.5 = (f32[2,16,128]{2,1,0:T(8,128)S(1)}, f32[2,16,128]{2,1,0:T(8,128)S(1)}, u32[]{:S(2)}, u32[]{:S(2)}) collective-permute-start(f32[2,16,128]{2,1,0:T(8,128)S(1)} %pair.3.refs_0_), channel_id=1, source_target_pairs={{0,2},{1,3},{2,0},{3,1},{4,6},{5,7},{6,4},{7,5},{8,10},{9,11},{10,... | collective-permute-start | bytes 49160 | tf_op jit(solution)/shard_map/ppermute | solution.py:865
  18.5 2.5 %collective-permute-done.4.y_hi = f32[2,48,8,128]{3,2,1,0:T(8,128)S(1)} collective-permute-done((f32[2,48,8,128]{3,2,1,0:T(8,128)S(1)}, f32[2,48,8,128]{3,2,1,0:T(8,128)S(1)}, u32[]{:S(2)}, u32[]{:S(2)}) %collective-permute-start.4) | collective-permute-done | bytes 393248 | tf_op jit(solution)/shard_map/ppermute | solution.py:865
  21.0 1.5 %pack_z.1 = (f32[48,48,128]{2,1,0:T(8,128)S(1)}, f32[48,48,128]{2,1,0:T(8,128)S(1)}, f32[6,48,128]{2,1,0:T(8,128)S(1)}, f32[6,48,128]{2,1,0:T(8,128)S(1)}) custom-call(f32[48,32,128]{2,1,0:T(8,128)S(1)} %get-tuple-element.76.s_mid, f32[48,32,128]{2,1,0:T(8,128)S(1)} %get-tuple-element.77.b_mid, f32[2,48,8,128]{3,2,1,0:T(8,128)S(1)} %collective-permute-done.3.y_lo, ...), custom_call_target="tpu_custom_call" | custom-call | tf_op jit(solution)/shard_map/pack_z/pallas_call | solution.py:907
  22.6 1.4 %collective-permute-start.6 = (f32[6,48,128]{2,1,0:T(8,128)S(1)}, f32[6,48,128]{2,1,0:T(8,128)S(1)}, u32[]{:S(2)}, u32[]{:S(2)}) collective-permute-start(f32[6,48,128]{2,1,0:T(8,128)S(1)} %get-tuple-element.85), channel_id=1, source_target_pairs={{0,1},{1,2},{2,3},{3,0},{4,5},{5,6},{6,7},{7,4},{8,9},{9,10},{10,1... | collective-permute-start | bytes 442376 | tf_op jit(solution)/shard_map/ppermute | solution.py:865
  23.9 1.5 %collective-permute-start.7 = (f32[6,48,128]{2,1,0:T(8,128)S(1)}, f32[6,48,128]{2,1,0:T(8,128)S(1)}, u32[]{:S(2)}, u32[]{:S(2)}) collective-permute-start(f32[6,48,128]{2,1,0:T(8,128)S(1)} %get-tuple-element.86._), channel_id=1, source_target_pairs={{0,3},{1,0},{2,1},{3,2},{4,7},{5,4},{6,5},{7,6},{8,11},{9,8},{10,9... | collective-permute-start | bytes 442376 | tf_op jit(solution)/shard_map/ppermute | solution.py:865
  25.4 2.7 %collective-permute-start.8 = (f32[8,8,128]{2,1,0:T(8,128)S(1)}, f32[8,8,128]{2,1,0:T(8,128)S(1)}, u32[]{:S(2)}, u32[]{:S(2)}) collective-permute-start(f32[8,8,128]{2,1,0:T(8,128)S(1)} %gather_z.2.mine), channel_id=1, source_target_pairs={{0,32},{32,64},{64,96},{96,0},{1,33},{33,65},{65,97},{97,1},{2,34}... | collective-permute-start | bytes 98312 | tf_op jit(solution)/shard_map/ppermute | solution.py:865
  29.7 12.2 %level0_down.1 = (f32[48,48,128]{2,1,0:T(8,128)S(1)}, f32[6,48,128]{2,1,0:T(8,128)S(1)}, f32[16,16,128]{2,1,0:T(8,128)S(1)}, f32[10,16,128]{2,1,0:T(8,128)S(1)},...) custom-call(f32[48,48,128]{2,1,0:T(8,128)S(1)} %get-tuple-element.83, ...), custom_call_target="tpu_custom_call" | custom-call | tf_op jit(solution)/shard_map/level0_down/pallas_call | solution.py:913
  41.9 2.8 %collective-permute-start.9 = (f32[10,16,128]{2,1,0:T(8,128)S(1)}, f32[10,16,128]{2,1,0:T(8,128)S(1)}, u32[]{:S(2)}, u32[]{:S(2)}) collective-permute-start(f32[10,16,128]{2,1,0:T(8,128)S(1)} %get-tuple-element.91), channel_id=1, source_target_pairs={{0,32},{32,64},{64,96},{96,0},{1,33},{33,65},{65,97},{97,1},{2,34}... | collective-permute-start | bytes 245768 | tf_op jit(solution)/shard_map/ppermute | solution.py:865
  45.9 3.9 %collective-permute-done.11.refs_1_ = f32[2,8,8,128]{3,2,1,0:T(8,128)S(1)} collective-permute-done((f32[2,8,8,128]{3,2,1,0:T(8,128)S(1)}, f32[2,8,8,128]{3,2,1,0:T(8,128)S(1)}, u32[]{:S(2)}, u32[]{:S(2)}) %collective-permute-start.11) | collective-permute-done | bytes 65568 | tf_op jit(solution)/shard_map/ppermute | solution.py:865
  49.9 2.3 %collective-permute-start.12 = (f32[360,128]{1,0:T(8,128)S(1)}, f32[360,128]{1,0:T(8,128)S(1)}, u32[]{:S(2)}, u32[]{:S(2)}) collective-permute-start(f32[360,128]{1,0:T(8,128)S(1)} %get-tuple-element.97), channel_id=1, source_target_pairs={{0,4},{4,8},{8,12},{12,16},{16,20},{20,24},{24,28},{28,0},{1,5},{5... | collective-permute-start | bytes 552968 | tf_op jit(solution)/shard_map/ppermute | solution.py:865
  52.2 1.6 %collective-permute-start.14 = (f32[32,8,128]{2,1,0:T(8,128)S(1)}, f32[32,8,128]{2,1,0:T(8,128)S(1)}, u32[]{:S(2)}, u32[]{:S(2)}) collective-permute-start(f32[32,8,128]{2,1,0:T(8,128)S(1)} %gather_x.2.mine), channel_id=1, source_target_pairs={{0,8},{4,12},{8,16},{12,20},{16,24},{20,28},{24,0},{28,4},{1,9},{5... | collective-permute-start | bytes 393224 | tf_op jit(solution)/shard_map/ppermute | solution.py:865
  53.8 4.9 %collective-permute-done.14.other = f32[32,8,128]{2,1,0:T(8,128)S(1)} collective-permute-done((f32[32,8,128]{2,1,0:T(8,128)S(1)}, f32[32,8,128]{2,1,0:T(8,128)S(1)}, u32[]{:S(2)}, u32[]{:S(2)}) %collective-permute-start.14) | collective-permute-done | bytes 131104 | tf_op jit(solution)/shard_map/ppermute | solution.py:865
  59.6 2.5 %collective-permute-start.17 = (f32[2,32,8,128]{3,2,1,0:T(8,128)S(1)}, f32[2,32,8,128]{3,2,1,0:T(8,128)S(1)}, u32[]{:S(2)}, u32[]{:S(2)}) collective-permute-start(f32[2,32,8,128]{3,2,1,0:T(8,128)S(1)} %pair.5.refs_0_), channel_id=1, source_target_pairs={{0,16},{4,20},{8,24},{12,28},{16,0},{20,4},{24,8},{28,12},{1,17},{... | collective-permute-start | bytes 786440 | tf_op jit(solution)/shard_map/ppermute | solution.py:865
  63.2 1.7 %collective-permute-start.16 = (f32[6,40,128]{2,1,0:T(8,128)S(1)}, f32[6,40,128]{2,1,0:T(8,128)S(1)}, u32[]{:S(2)}, u32[]{:S(2)}) collective-permute-start(f32[6,40,128]{2,1,0:T(8,128)S(1)} %get-tuple-element.104.refs_2_), channel_id=1, source_target_pairs={{0,3},{1,0},{2,1},{3,2},{4,7},{5,4},{6,5},{7,6},{8,11},{9,8},{10,9... | collective-permute-start | bytes 368648 | tf_op jit(solution)/shard_map/ppermute | solution.py:865
  64.8 2.1 %collective-permute-done.17.refs_1_ = f32[2,32,8,128]{3,2,1,0:T(8,128)S(1)} collective-permute-done((f32[2,32,8,128]{3,2,1,0:T(8,128)S(1)}, f32[2,32,8,128]{3,2,1,0:T(8,128)S(1)}, u32[]{:S(2)}, u32[]{:S(2)}) %collective-permute-start.17) | collective-permute-done | bytes 262176 | tf_op jit(solution)/shard_map/ppermute | solution.py:865
  67.4 4.1 %level1_down.1 = (f32[36,40,128]{2,1,0:T(8,128)S(1)}, f32[16,128]{1,0:T(8,128)S(1)}, f32[6,36,40,128]{3,2,1,0:T(8,128)S(1)}, f32[36,40,128]{2,1,0:T(8,128)S(1)}, f32[36,40,128]{2,1,0:T(8,128)S(1)}) custom-call(f32[36,40,128]{2,1,0:T(8,128)S(1)} %get-tuple-element.102.ext, f32[6,40,128]{2,1,0:T(8,128)S(1)} %collective-permute-done.15.z_lo, ...), custom_call_target="tpu_custom_call" | custom-call | tf_op jit(solution)/shard_map/level1_down/pallas_call | solution.py:947
  71.5 2.7 %collective-permute-start.21 = (f32[4,32,8,128]{3,2,1,0:T(8,128)S(1)}, f32[4,32,8,128]{3,2,1,0:T(8,128)S(1)}, u32[]{:S(2)}, u32[]{:S(2)}) collective-permute-start(f32[4,32,8,128]{3,2,1,0:T(8,128)S(1)} %stack_y.2.same), channel_id=1, source_target_pairs={{0,4},{4,0},{8,12},{12,8},{16,20},{20,16},{24,28},{28,24},{1,5},{5... | collective-permute-start | bytes 1572872 | tf_op jit(solution)/shard_map/ppermute | solution.py:886
  75.2 2.6 %collective-permute-start.19 = (f32[16,128]{1,0:T(8,128)S(1)}, f32[16,128]{1,0:T(8,128)S(1)}, u32[]{:S(2)}, u32[]{:S(2)}) collective-permute-start(f32[16,128]{1,0:T(8,128)S(1)} %get-tuple-element.112.refs_0_.refs_4_), channel_id=1, source_target_pairs={{0,2},{1,3},{2,0},{3,1},{4,6},{5,7},{6,4},{7,5},{8,10},{9,11},{10,... | collective-permute-start | bytes 24584 | tf_op jit(solution)/shard_map/ppermute | solution.py:865
  80.4 1.6 %collective-permute-start.22 = (f32[8,8,128]{2,1,0:T(8,128)S(1)}, f32[8,8,128]{2,1,0:T(8,128)S(1)}, u32[]{:S(2)}, u32[]{:S(2)}) collective-permute-start(f32[8,8,128]{2,1,0:T(8,128)S(1)} %gather_z.3.refs_0_), channel_id=1, source_target_pairs={{0,32},{32,64},{64,96},{96,0},{1,33},{33,65},{65,97},{97,1},{2,34}... | collective-permute-start | bytes 98312 | tf_op jit(solution)/shard_map/ppermute | solution.py:865
  83.3 3.1 %collective-permute-done.23.refs_2_ = f32[8,8,128]{2,1,0:T(8,128)S(1)} collective-permute-done((f32[8,8,128]{2,1,0:T(8,128)S(1)}, f32[8,8,128]{2,1,0:T(8,128)S(1)}, u32[]{:S(2)}, u32[]{:S(2)}) %collective-permute-start.23) | collective-permute-done | bytes 32800 | tf_op jit(solution)/shard_map/ppermute | solution.py:865
  87.4 2.5 %collective-permute-start.26 = (f32[32,8,128]{2,1,0:T(8,128)S(1)}, f32[32,8,128]{2,1,0:T(8,128)S(1)}, u32[]{:S(2)}, u32[]{:S(2)}) collective-permute-start(f32[32,8,128]{2,1,0:T(8,128)S(1)} %gather_x.3.refs_0_.refs_4_), channel_id=1, source_target_pairs={{0,16},{4,20},{8,24},{12,28},{16,0},{20,4},{24,8},{28,12},{1,17},{... | collective-permute-start | bytes 393224 | tf_op jit(solution)/shard_map/ppermute | solution.py:865
  89.9 1.3 %collective-permute-start.27 = (f32[32,8,128]{2,1,0:T(8,128)S(1)}, f32[32,8,128]{2,1,0:T(8,128)S(1)}, u32[]{:S(2)}, u32[]{:S(2)}) collective-permute-start(f32[32,8,128]{2,1,0:T(8,128)S(1)} %gather_x.3.refs_0_.refs_4_), channel_id=1, source_target_pairs={{0,24},{4,28},{8,0},{12,4},{16,8},{20,12},{24,16},{28,20},{1,25},{... | collective-permute-start | bytes 393224 | tf_op jit(solution)/shard_map/ppermute | solution.py:865
  91.8 1.8 %collective-permute-done.26.refs_2_ = f32[32,8,128]{2,1,0:T(8,128)S(1)} collective-permute-done((f32[32,8,128]{2,1,0:T(8,128)S(1)}, f32[32,8,128]{2,1,0:T(8,128)S(1)}, u32[]{:S(2)}, u32[]{:S(2)}) %collective-permute-start.26) | collective-permute-done | bytes 131104 | tf_op jit(solution)/shard_map/ppermute | solution.py:865
  93.8 5.2 %collective-permute-start.28 = (f32[4,32,8,128]{3,2,1,0:T(8,128)S(1)}, f32[4,32,8,128]{3,2,1,0:T(8,128)S(1)}, u32[]{:S(2)}, u32[]{:S(2)}) collective-permute-start(f32[4,32,8,128]{3,2,1,0:T(8,128)S(1)} %stack_y.3.same), channel_id=1, source_target_pairs={{0,4},{4,0},{8,12},{12,8},{16,20},{20,16},{24,28},{28,24},{1,5},{5... | collective-permute-start | bytes 1572872 | tf_op jit(solution)/shard_map/ppermute | solution.py:886
  99.0 3.6 %coarse_prepare.1 = (f32[6,32,64,128]{3,2,1,0:T(8,128)S(1)}, f32[32,64,128]{2,1,0:T(8,128)S(1)}, f32[32,64,128]{2,1,0:T(8,128)S(1)}, f32[6,16,32,128]{3,2,1,0:T(...) custom-call(f32[4,32,8,128]{3,2,1,0:T(8,128)S(1)} %stack_y.2.same, ...), custom_call_target="tpu_custom_call" | custom-call | tf_op jit(solution)/shard_map/coarse_prepare/pallas_call | solution.py:961
  102.6 9.3 %bottom.1.c2 = f32[18,24,128]{2,1,0:T(8,128)S(1)} custom-call(f32[4,32,8,128]{3,2,1,0:T(8,128)S(1)} %stack_y.3.same, f32[4,32,8,128]{3,2,1,0:T(8,128)S(1)} %collective-permute-done.28.sibling, f32[6,32,64,128]{3,2,1,0:T(8,128)S(1)} %get-tuple-element.117.g, f32[32,64,128]{2,1,0:T(8,128)S(1)} %get-tuple-element.118.inv, ...), custom_call_target="tpu_custom_call" | custom-call | tf_op jit(solution)/shard_map/bottom/pallas_call | solution.py:968
  111.9 3.7 %level1_up.1.c1 = f32[24,24,128]{2,1,0:T(8,128)S(1)} custom-call(f32[18,24,128]{2,1,0:T(8,128)S(1)} %bottom.1.c2, f32[6,36,40,128]{3,2,1,0:T(8,128)S(1)} %get-tuple-element.124.g, f32[36,40,128]{2,1,0:T(8,128)S(1)} %get-tuple-element.125.sp, f32[36,40,128]{2,1,0:T(8,128)S(1)} %get-tuple-element.126.beta, f32[36,40,128]{2,1,0:T(8,128)S(1)} %get-tuple-element.127.iterate), custom_call_target="tpu_custom_call" | custom-call | tf_op jit(solution)/shard_map/level1_up/pallas_call | solution.py:971
  115.6 10.0 %level0_up.1 = f32[32,32,128]{2,1,0:T(8,128)} custom-call(f32[24,24,128]{2,1,0:T(8,128)S(1)} %level1_up.1.c1, f32[48,48,128]{2,1,0:T(8,128)S(1)} %get-tuple-element.84.beta, f32[7,48,48,128]{3,2,1,0:T(8,128)S(1)} %get-tuple-element.128.g_main, f32[6,6,48,128]{3,2,1,0:T(8,128)S(1)} %get-tuple-element.129.g_strip, f32[48,48,128]{2,1,0:T(8,128)S(1)} %get-tuple-element.130.sp, ...), custom_call_target="tpu_custom_call" | custom-call | tf_op jit(solution)/shard_map/level0_up/pallas_call | solution.py:978
  (53 shorter events, 18.0 us)
Async XLA Ops:
  0.0 10.6 %copy-start.1 = (f32[32,32,128]{2,1,0:T(8,128)S(1)}, f32[32,32,128]{2,1,0:T(8,128)}, u32[]{:S(2)}) copy-start(f32[32,32,128]{2,1,0:T(8,128)} %src) | copy-start | bytes 1572868
  0.0 4.9 %copy-start = (f32[32,32,128]{2,1,0:T(8,128)S(1)}, f32[32,32,128]{2,1,0:T(8,128)}, u32[]{:S(2)}) copy-start(f32[32,32,128]{2,1,0:T(8,128)} %beta.1) | copy-start | bytes 1572868
  2.1 8.5 %collective-permute-start.1 = (f32[2,8,32,128]{3,2,1,0:T(8,128)S(1)}, f32[2,8,32,128]{3,2,1,0:T(8,128)S(1)}, u32[]{:S(2)}, u32[]{:S(2)}) collective-permute-start(f32[2,8,32,128]{3,2,1,0:T(8,128)S(1)} %get-tuple-element.73._), channel_id=1, source_target_pairs={{0,96},{32,0},{64,32},{96,64},{1,97},{33,1},{65,33},{97,65},{2,98}... | collective-permute-start | bytes 786440 | tf_op jit(solution)/shard_map/ppermute | solution.py:865
  2.7 7.8 %collective-permute-start = (f32[2,8,32,128]{3,2,1,0:T(8,128)S(1)}, f32[2,8,32,128]{3,2,1,0:T(8,128)S(1)}, u32[]{:S(2)}, u32[]{:S(2)}) collective-permute-start(f32[2,8,32,128]{3,2,1,0:T(8,128)S(1)} %get-tuple-element.72), channel_id=1, source_target_pairs={{0,32},{32,64},{64,96},{96,0},{1,33},{33,65},{65,97},{97,1},{2,34}... | collective-permute-start | bytes 786440 | tf_op jit(solution)/shard_map/ppermute | solution.py:865
  5.4 4.1 %collective-permute-start.2 = (f32[16,128]{1,0:T(8,128)S(1)}, f32[16,128]{1,0:T(8,128)S(1)}, u32[]{:S(2)}, u32[]{:S(2)}) collective-permute-start(f32[16,128]{1,0:T(8,128)S(1)} %coarse_beta.1.mine), channel_id=1, source_target_pairs={{0,1},{1,2},{2,3},{3,0},{4,5},{5,6},{6,7},{7,4},{8,9},{9,10},{10,1... | collective-permute-start | bytes 24584 | tf_op jit(solution)/shard_map/ppermute | solution.py:865
  10.7 7.8 %collective-permute-start.3 = (f32[2,48,8,128]{3,2,1,0:T(8,128)S(1)}, f32[2,48,8,128]{3,2,1,0:T(8,128)S(1)}, u32[]{:S(2)}, u32[]{:S(2)}) collective-permute-start(f32[2,48,8,128]{3,2,1,0:T(8,128)S(1)} %get-tuple-element.78), channel_id=1, source_target_pairs={{0,4},{4,8},{8,12},{12,16},{16,20},{20,24},{24,28},{28,0},{1,5},{5... | collective-permute-start | bytes 1179656 | tf_op jit(solution)/shard_map/ppermute | solution.py:865
  13.8 7.2 %collective-permute-start.4 = (f32[2,48,8,128]{3,2,1,0:T(8,128)S(1)}, f32[2,48,8,128]{3,2,1,0:T(8,128)S(1)}, u32[]{:S(2)}, u32[]{:S(2)}) collective-permute-start(f32[2,48,8,128]{3,2,1,0:T(8,128)S(1)} %get-tuple-element.79.refs_2_), channel_id=1, source_target_pairs={{0,28},{4,0},{8,4},{12,8},{16,12},{20,16},{24,20},{28,24},{1,29},{... | collective-permute-start | bytes 1179656 | tf_op jit(solution)/shard_map/ppermute | solution.py:865
  13.8 4.1 %collective-permute-start.5 = (f32[2,16,128]{2,1,0:T(8,128)S(1)}, f32[2,16,128]{2,1,0:T(8,128)S(1)}, u32[]{:S(2)}, u32[]{:S(2)}) collective-permute-start(f32[2,16,128]{2,1,0:T(8,128)S(1)} %pair.3.refs_0_), channel_id=1, source_target_pairs={{0,2},{1,3},{2,0},{3,1},{4,6},{5,7},{6,4},{7,5},{8,10},{9,11},{10,... | collective-permute-start | bytes 49160 | tf_op jit(solution)/shard_map/ppermute | solution.py:865
  22.6 7.1 %collective-permute-start.6 = (f32[6,48,128]{2,1,0:T(8,128)S(1)}, f32[6,48,128]{2,1,0:T(8,128)S(1)}, u32[]{:S(2)}, u32[]{:S(2)}) collective-permute-start(f32[6,48,128]{2,1,0:T(8,128)S(1)} %get-tuple-element.85), channel_id=1, source_target_pairs={{0,1},{1,2},{2,3},{3,0},{4,5},{5,6},{6,7},{7,4},{8,9},{9,10},{10,1... | collective-permute-start | bytes 442376 | tf_op jit(solution)/shard_map/ppermute | solution.py:865
  23.9 5.8 %collective-permute-start.7 = (f32[6,48,128]{2,1,0:T(8,128)S(1)}, f32[6,48,128]{2,1,0:T(8,128)S(1)}, u32[]{:S(2)}, u32[]{:S(2)}) collective-permute-start(f32[6,48,128]{2,1,0:T(8,128)S(1)} %get-tuple-element.86._), channel_id=1, source_target_pairs={{0,3},{1,0},{2,1},{3,2},{4,7},{5,4},{6,5},{7,6},{8,11},{9,8},{10,9... | collective-permute-start | bytes 442376 | tf_op jit(solution)/shard_map/ppermute | solution.py:865
  25.4 3.7 %collective-permute-start.8 = (f32[8,8,128]{2,1,0:T(8,128)S(1)}, f32[8,8,128]{2,1,0:T(8,128)S(1)}, u32[]{:S(2)}, u32[]{:S(2)}) collective-permute-start(f32[8,8,128]{2,1,0:T(8,128)S(1)} %gather_z.2.mine), channel_id=1, source_target_pairs={{0,32},{32,64},{64,96},{96,0},{1,33},{33,65},{65,97},{97,1},{2,34}... | collective-permute-start | bytes 98312 | tf_op jit(solution)/shard_map/ppermute | solution.py:865
  41.9 8.0 %collective-permute-start.10 = (f32[10,16,128]{2,1,0:T(8,128)S(1)}, f32[10,16,128]{2,1,0:T(8,128)S(1)}, u32[]{:S(2)}, u32[]{:S(2)}) collective-permute-start(f32[10,16,128]{2,1,0:T(8,128)S(1)} %get-tuple-element.92.refs_2_), channel_id=1, source_target_pairs={{0,96},{32,0},{64,32},{96,64},{1,97},{33,1},{65,33},{97,65},{2,98}... | collective-permute-start | bytes 245768 | tf_op jit(solution)/shard_map/ppermute | solution.py:865
  41.9 7.9 %collective-permute-start.9 = (f32[10,16,128]{2,1,0:T(8,128)S(1)}, f32[10,16,128]{2,1,0:T(8,128)S(1)}, u32[]{:S(2)}, u32[]{:S(2)}) collective-permute-start(f32[10,16,128]{2,1,0:T(8,128)S(1)} %get-tuple-element.91), channel_id=1, source_target_pairs={{0,32},{32,64},{64,96},{96,0},{1,33},{33,65},{65,97},{97,1},{2,34}... | collective-permute-start | bytes 245768 | tf_op jit(solution)/shard_map/ppermute | solution.py:865
  44.8 5.0 %collective-permute-start.11 = (f32[2,8,8,128]{3,2,1,0:T(8,128)S(1)}, f32[2,8,8,128]{3,2,1,0:T(8,128)S(1)}, u32[]{:S(2)}, u32[]{:S(2)}) collective-permute-start(f32[2,8,8,128]{3,2,1,0:T(8,128)S(1)} %pair.4.refs_0_), channel_id=1, source_target_pairs={{0,64},{32,96},{64,0},{96,32},{1,65},{33,97},{65,1},{97,33},{2,66}... | collective-permute-start | bytes 196616 | tf_op jit(solution)/shard_map/ppermute | solution.py:865
  49.9 8.9 %collective-permute-start.12 = (f32[360,128]{1,0:T(8,128)S(1)}, f32[360,128]{1,0:T(8,128)S(1)}, u32[]{:S(2)}, u32[]{:S(2)}) collective-permute-start(f32[360,128]{1,0:T(8,128)S(1)} %get-tuple-element.97), channel_id=1, source_target_pairs={{0,4},{4,8},{8,12},{12,16},{16,20},{20,24},{24,28},{28,0},{1,5},{5... | collective-permute-start | bytes 552968 | tf_op jit(solution)/shard_map/ppermute | solution.py:865
  52.2 6.6 %collective-permute-start.13 = (f32[360,128]{1,0:T(8,128)S(1)}, f32[360,128]{1,0:T(8,128)S(1)}, u32[]{:S(2)}, u32[]{:S(2)}) collective-permute-start(f32[360,128]{1,0:T(8,128)S(1)} %get-tuple-element.98._), channel_id=1, source_target_pairs={{0,28},{4,0},{8,4},{12,8},{16,12},{20,16},{24,20},{28,24},{1,29},{... | collective-permute-start | bytes 552968 | tf_op jit(solution)/shard_map/ppermute | solution.py:865
  52.2 6.6 %collective-permute-start.14 = (f32[32,8,128]{2,1,0:T(8,128)S(1)}, f32[32,8,128]{2,1,0:T(8,128)S(1)}, u32[]{:S(2)}, u32[]{:S(2)}) collective-permute-start(f32[32,8,128]{2,1,0:T(8,128)S(1)} %gather_x.2.mine), channel_id=1, source_target_pairs={{0,8},{4,12},{8,16},{12,20},{16,24},{20,28},{24,0},{28,4},{1,9},{5... | collective-permute-start | bytes 393224 | tf_op jit(solution)/shard_map/ppermute | solution.py:865
  59.6 7.4 %collective-permute-start.17 = (f32[2,32,8,128]{3,2,1,0:T(8,128)S(1)}, f32[2,32,8,128]{3,2,1,0:T(8,128)S(1)}, u32[]{:S(2)}, u32[]{:S(2)}) collective-permute-start(f32[2,32,8,128]{3,2,1,0:T(8,128)S(1)} %pair.5.refs_0_), channel_id=1, source_target_pairs={{0,16},{4,20},{8,24},{12,28},{16,0},{20,4},{24,8},{28,12},{1,17},{... | collective-permute-start | bytes 786440 | tf_op jit(solution)/shard_map/ppermute | solution.py:865
  62.2 5.2 %collective-permute-start.15 = (f32[6,40,128]{2,1,0:T(8,128)S(1)}, f32[6,40,128]{2,1,0:T(8,128)S(1)}, u32[]{:S(2)}, u32[]{:S(2)}) collective-permute-start(f32[6,40,128]{2,1,0:T(8,128)S(1)} %get-tuple-element.103), channel_id=1, source_target_pairs={{0,1},{1,2},{2,3},{3,0},{4,5},{5,6},{6,7},{7,4},{8,9},{9,10},{10,1... | collective-permute-start | bytes 368648 | tf_op jit(solution)/shard_map/ppermute | solution.py:865
  63.2 4.3 %collective-permute-start.16 = (f32[6,40,128]{2,1,0:T(8,128)S(1)}, f32[6,40,128]{2,1,0:T(8,128)S(1)}, u32[]{:S(2)}, u32[]{:S(2)}) collective-permute-start(f32[6,40,128]{2,1,0:T(8,128)S(1)} %get-tuple-element.104.refs_2_), channel_id=1, source_target_pairs={{0,3},{1,0},{2,1},{3,2},{4,7},{5,4},{6,5},{7,6},{8,11},{9,8},{10,9... | collective-permute-start | bytes 368648 | tf_op jit(solution)/shard_map/ppermute | solution.py:865
  71.5 8.8 %collective-permute-start.21 = (f32[4,32,8,128]{3,2,1,0:T(8,128)S(1)}, f32[4,32,8,128]{3,2,1,0:T(8,128)S(1)}, u32[]{:S(2)}, u32[]{:S(2)}) collective-permute-start(f32[4,32,8,128]{3,2,1,0:T(8,128)S(1)} %stack_y.2.same), channel_id=1, source_target_pairs={{0,4},{4,0},{8,12},{12,8},{16,20},{20,16},{24,28},{28,24},{1,5},{5... | collective-permute-start | bytes 1572872 | tf_op jit(solution)/shard_map/ppermute | solution.py:886
  74.2 4.4 %collective-permute-start.18 = (f32[16,128]{1,0:T(8,128)S(1)}, f32[16,128]{1,0:T(8,128)S(1)}, u32[]{:S(2)}, u32[]{:S(2)}) collective-permute-start(f32[16,128]{1,0:T(8,128)S(1)} %get-tuple-element.112.refs_0_.refs_4_), channel_id=1, source_target_pairs={{0,1},{1,2},{2,3},{3,0},{4,5},{5,6},{6,7},{7,4},{8,9},{9,10},{10,1... | collective-permute-start | bytes 24584 | tf_op jit(solution)/shard_map/ppermute | solution.py:865
  75.2 4.0 %collective-permute-start.19 = (f32[16,128]{1,0:T(8,128)S(1)}, f32[16,128]{1,0:T(8,128)S(1)}, u32[]{:S(2)}, u32[]{:S(2)}) collective-permute-start(f32[16,128]{1,0:T(8,128)S(1)} %get-tuple-element.112.refs_0_.refs_4_), channel_id=1, source_target_pairs={{0,2},{1,3},{2,0},{3,1},{4,6},{5,7},{6,4},{7,5},{8,10},{9,11},{10,... | collective-permute-start | bytes 24584 | tf_op jit(solution)/shard_map/ppermute | solution.py:865
  77.8 2.5 %collective-permute-start.20 = (f32[16,128]{1,0:T(8,128)S(1)}, f32[16,128]{1,0:T(8,128)S(1)}, u32[]{:S(2)}, u32[]{:S(2)}) collective-permute-start(f32[16,128]{1,0:T(8,128)S(1)} %get-tuple-element.112.refs_0_.refs_4_), channel_id=1, source_target_pairs={{0,3},{1,0},{2,1},{3,2},{4,7},{5,4},{6,5},{7,6},{8,11},{9,8},{10,9... | collective-permute-start | bytes 24584 | tf_op jit(solution)/shard_map/ppermute | solution.py:865
  80.4 2.8 %collective-permute-start.22 = (f32[8,8,128]{2,1,0:T(8,128)S(1)}, f32[8,8,128]{2,1,0:T(8,128)S(1)}, u32[]{:S(2)}, u32[]{:S(2)}) collective-permute-start(f32[8,8,128]{2,1,0:T(8,128)S(1)} %gather_z.3.refs_0_), channel_id=1, source_target_pairs={{0,32},{32,64},{64,96},{96,0},{1,33},{33,65},{65,97},{97,1},{2,34}... | collective-permute-start | bytes 98312 | tf_op jit(solution)/shard_map/ppermute | solution.py:865
  82.1 4.3 %collective-permute-start.23 = (f32[8,8,128]{2,1,0:T(8,128)S(1)}, f32[8,8,128]{2,1,0:T(8,128)S(1)}, u32[]{:S(2)}, u32[]{:S(2)}) collective-permute-start(f32[8,8,128]{2,1,0:T(8,128)S(1)} %gather_z.3.refs_0_), channel_id=1, source_target_pairs={{0,64},{32,96},{64,0},{96,32},{1,65},{33,97},{65,1},{97,33},{2,66}... | collective-permute-start | bytes 98312 | tf_op jit(solution)/shard_map/ppermute | solution.py:865
  82.6 4.1 %collective-permute-start.24 = (f32[8,8,128]{2,1,0:T(8,128)S(1)}, f32[8,8,128]{2,1,0:T(8,128)S(1)}, u32[]{:S(2)}, u32[]{:S(2)}) collective-permute-start(f32[8,8,128]{2,1,0:T(8,128)S(1)} %gather_z.3.refs_0_), channel_id=1, source_target_pairs={{0,96},{32,0},{64,32},{96,64},{1,97},{33,1},{65,33},{97,65},{2,98}... | collective-permute-start | bytes 98312 | tf_op jit(solution)/shard_map/ppermute | solution.py:865
  86.7 5.1 %collective-permute-start.25 = (f32[32,8,128]{2,1,0:T(8,128)S(1)}, f32[32,8,128]{2,1,0:T(8,128)S(1)}, u32[]{:S(2)}, u32[]{:S(2)}) collective-permute-start(f32[32,8,128]{2,1,0:T(8,128)S(1)} %gather_x.3.refs_0_.refs_4_), channel_id=1, source_target_pairs={{0,8},{4,12},{8,16},{12,20},{16,24},{20,28},{24,0},{28,4},{1,9},{5... | collective-permute-start | bytes 393224 | tf_op jit(solution)/shard_map/ppermute | solution.py:865
  87.4 6.2 %collective-permute-start.26 = (f32[32,8,128]{2,1,0:T(8,128)S(1)}, f32[32,8,128]{2,1,0:T(8,128)S(1)}, u32[]{:S(2)}, u32[]{:S(2)}) collective-permute-start(f32[32,8,128]{2,1,0:T(8,128)S(1)} %gather_x.3.refs_0_.refs_4_), channel_id=1, source_target_pairs={{0,16},{4,20},{8,24},{12,28},{16,0},{20,4},{24,8},{28,12},{1,17},{... | collective-permute-start | bytes 393224 | tf_op jit(solution)/shard_map/ppermute | solution.py:865
  89.9 3.9 %collective-permute-start.27 = (f32[32,8,128]{2,1,0:T(8,128)S(1)}, f32[32,8,128]{2,1,0:T(8,128)S(1)}, u32[]{:S(2)}, u32[]{:S(2)}) collective-permute-start(f32[32,8,128]{2,1,0:T(8,128)S(1)} %gather_x.3.refs_0_.refs_4_), channel_id=1, source_target_pairs={{0,24},{4,28},{8,0},{12,4},{16,8},{20,12},{24,16},{28,20},{1,25},{... | collective-permute-start | bytes 393224 | tf_op jit(solution)/shard_map/ppermute | solution.py:865
  93.8 8.7 %collective-permute-start.28 = (f32[4,32,8,128]{3,2,1,0:T(8,128)S(1)}, f32[4,32,8,128]{3,2,1,0:T(8,128)S(1)}, u32[]{:S(2)}, u32[]{:S(2)}) collective-permute-start(f32[4,32,8,128]{3,2,1,0:T(8,128)S(1)} %stack_y.3.same), channel_id=1, source_target_pairs={{0,4},{4,0},{8,12},{12,8},{16,20},{20,16},{24,28},{28,24},{1,5},{5... | collective-permute-start | bytes 1572872 | tf_op jit(solution)/shard_map/ppermute | solution.py:886

commit v8 on v7

--- a/solution.py
+++ b/solution.py
@@ -929,20 +929,18 @@
         mib=16,
     )(src_ext, beta_ext, z_lo, z_hi)
     x_lo, x_hi = trade(lo, hi, "gx")
+    lo, hi = call(pack1_y, (sds(360, 128), sds(360, 128)), name="pack1_y")(c, x_lo, x_hi)
+    y_lo, y_hi = trade(lo, hi, "gy")
     beta2_pair, _ = lax.optimization_barrier((beta2_pair, lo))
     beta2_slab = gather(gather_x, [beta2_pair, ring(beta2_pair, "gx", 2)], lo, 32, 8, 128)
-    x_lo, x_hi, beta2_slab = lax.optimization_barrier((x_lo, x_hi, beta2_slab))
-    lo, hi = call(pack1_y, (sds(360, 128), sds(360, 128)), name="pack1_y")(c, x_lo, x_hi)
-    y_lo, y_hi = trade(lo, hi, "gy")
-    beta2_pair = gather(pair, [beta2_slab, ring(beta2_slab, "gy", 2)], lo, 2, 32, 8, 128)
-    y_lo, y_hi, beta2_pair = lax.optimization_barrier((y_lo, y_hi, beta2_pair))
+    y_lo, y_hi, beta2_slab = lax.optimization_barrier((y_lo, y_hi, beta2_slab))
     ext, lo, hi = call(
         pack1_z, (sds(36, 40, 128), sds(6, 40, 128), sds(6, 40, 128)), name="pack1_z"
     )(c, x_lo, x_hi, y_lo, y_hi)
     z1_lo, z1_hi = trade(lo, hi, "gz")
-    beta2_pair, _ = lax.optimization_barrier((beta2_pair, lo))
-    beta2_stack = gather(stack_y, [beta2_pair, ring(beta2_pair, "gy", 4)], lo, 4, 32, 8, 128)
-    z1_lo, z1_hi, beta2_stack = lax.optimization_barrier((z1_lo, z1_hi, beta2_stack))
+    beta2_slab, _ = lax.optimization_barrier((beta2_slab, lo))
+    beta2_pair = gather(pair, [beta2_slab, ring(beta2_slab, "gy", 2)], lo, 2, 32, 8, 128)
+    z1_lo, z1_hi, beta2_pair = lax.optimization_barrier((z1_lo, z1_hi, beta2_pair))
     level1 = sds(36, 40, 128)
     iter1, chunk, g1, sp1, beta1 = call(
         level1_down,
@@ -952,9 +950,13 @@
         mib=8,
     )(ext, z1_lo, z1_hi)
     parts = around(chunk, "gz")
-    beta2_stack, _ = lax.optimization_barrier((beta2_stack, chunk))
-    *parts, beta2_other = lax.optimization_barrier((*parts, across(beta2_stack)))
-    parts = around(gather(gather_z, parts, chunk, 8, 8, 128), "gx")
+    beta2_pair, _ = lax.optimization_barrier((beta2_pair, chunk))
+    beta2_stack = gather(stack_y, [beta2_pair, ring(beta2_pair, "gy", 4)], chunk, 4, 32, 8, 128)
+    *parts, beta2_stack = lax.optimization_barrier((*parts, beta2_stack))
+    block = gather(gather_z, parts, chunk, 8, 8, 128)
+    parts = around(block, "gx")
+    beta2_sent, _ = lax.optimization_barrier((beta2_stack, block))
+    *parts, beta2_other = lax.optimization_barrier((*parts, across(beta2_sent)))
     slab = gather(gather_x, parts, chunk, 32, 8, 128)
     stack = gather(stack_y, chips(slab), slab, 4, 32, 8, 128)
     stack_other = across(stack)

time: 127 us -> 128 us (level)
  starting transfers between devices: 47.8 us -> 53.6 us
  waiting for transfers between devices: 29.2 us -> 24.2 us
    ppermute x27, starting transfers between devices: 40 us -> 48.1 us  [ring(): lax.ppermute(value, axis, [(i, (i + step) % count) for i in range(count)])]
    ppermute x27, waiting for transfers between devices: 29.2 us -> 24.2 us  [ring(): lax.ppermute(value, axis, [(i, (i + step) % count) for i in range(count)])]
    ppermute x2, starting transfers between devices: 7.84 us -> 5.44 us  [across(): lax.ppermute(value, 'gy', [(i, i + 1 - 2 * (i % 2)) for i in range(count)])]
  transfers between devices with their start and end apart: 29 -> 29, of which waited for: 19 -> 14; matrix products, arithmetic and copies ran while one was open for 0% -> 0% of each run, Pallas kernels for 3% -> 3%
where the time goes in v8:
time: 128 us; the launch traced here: 126 us
  starting transfers between devices  53.6 us (42%)
  Pallas kernels  46.3 us (36%)
  waiting for transfers between devices  24.2 us (19%)
  local copies, waits for them, and re-layouts  2.07 us (2%)
    ppermute x27, starting transfers between devices, ring(): lax.ppermute(value, axis, [(i, (i + step) % count) for i in range(count)])  48.1 us
    ppermute x27, waiting for transfers between devices, ring(): lax.ppermute(value, axis, [(i, (i + step) % count) for i in range(count)])  24.2 us
    pallas_call x1, Pallas kernels, per_device(): call(level0_down, (whole, strip, sds(16, 16, 128), sds(10, 16, 128), sds(...  12.2 us
    pallas_call x1, Pallas kernels, per_device(): call(level0_up, sds(32, 32, 128), [vm(50, 64, 128), vm(50, 64, 128), vm(6...  10 us
    pallas_call x1, Pallas kernels, per_device(): call(bottom, sds(18, 24, 128), BOTTOM_SCRATCH, name='bottom', mib=18)  9.31 us
    ppermute x2, starting transfers between devices, across(): lax.ppermute(value, 'gy', [(i, i + 1 - 2 * (i % 2)) for i in range(count)])  5.44 us
    pallas_call x1, Pallas kernels, per_device(): call(level1_down, (level1, sds(16, 128), sds(6, 36, 40, 128), level1, lev...  4.14 us
    pallas_call x1, Pallas kernels, per_device(): call(level1_up, sds(24, 24, 128), [vm(38, 56, 128), vm(38, 56, 128), vm(3...  3.65 us
  transfers between devices with their start and end apart: 29, of which 14 were waited for; matrix products, arithmetic and copies ran while one was open for 0% of the time, Pallas kernels for 3%

profile of v8, /device:TPU:7, one launch (start us, length us, event | category | flops | bytes accessed | tf_op | source)
XLA Modules:
  0.0 126.3 jit_solution(13258428410974430006)
XLA Ops:
  2.7 2.1 %collective-permute-start = (f32[2,8,32,128]{3,2,1,0:T(8,128)S(1)}, f32[2,8,32,128]{3,2,1,0:T(8,128)S(1)}, u32[]{:S(2)}, u32[]{:S(2)}) collective-permute-start(f32[2,8,32,128]{3,2,1,0:T(8,128)S(1)} %get-tuple-element.75), channel_id=1, source_target_pairs={{0,32},{32,64},{64,96},{96,0},{1,33},{33,65},{65,97},{97,1},{2,34}... | collective-permute-start | bytes 786440 | tf_op jit(solution)/shard_map/ppermute | solution.py:865
  6.7 2.8 %collective-permute-done.2.other = f32[16,128]{1,0:T(8,128)S(1)} collective-permute-done((f32[16,128]{1,0:T(8,128)S(1)}, f32[16,128]{1,0:T(8,128)S(1)}, u32[]{:S(2)}, u32[]{:S(2)}) %collective-permute-start.2) | collective-permute-done | bytes 8224 | tf_op jit(solution)/shard_map/ppermute | solution.py:865
  10.7 1.6 %collective-permute-start.4 = (f32[2,48,8,128]{3,2,1,0:T(8,128)S(1)}, f32[2,48,8,128]{3,2,1,0:T(8,128)S(1)}, u32[]{:S(2)}, u32[]{:S(2)}) collective-permute-start(f32[2,48,8,128]{3,2,1,0:T(8,128)S(1)} %get-tuple-element.82.refs_2_), channel_id=1, source_target_pairs={{0,28},{4,0},{8,4},{12,8},{16,12},{20,16},{24,20},{28,24},{1,29},{... | collective-permute-start | bytes 1179656 | tf_op jit(solution)/shard_map/ppermute | solution.py:865
  12.3 1.5 %collective-permute-start.3 = (f32[2,48,8,128]{3,2,1,0:T(8,128)S(1)}, f32[2,48,8,128]{3,2,1,0:T(8,128)S(1)}, u32[]{:S(2)}, u32[]{:S(2)}) collective-permute-start(f32[2,48,8,128]{3,2,1,0:T(8,128)S(1)} %get-tuple-element.81), channel_id=1, source_target_pairs={{0,4},{4,8},{8,12},{12,16},{16,20},{20,24},{24,28},{28,0},{1,5},{5... | collective-permute-start | bytes 1179656 | tf_op jit(solution)/shard_map/ppermute | solution.py:865
  13.9 2.9 %collective-permute-start.5 = (f32[2,16,128]{2,1,0:T(8,128)S(1)}, f32[2,16,128]{2,1,0:T(8,128)S(1)}, u32[]{:S(2)}, u32[]{:S(2)}) collective-permute-start(f32[2,16,128]{2,1,0:T(8,128)S(1)} %pair.3.refs_0_), channel_id=1, source_target_pairs={{0,2},{1,3},{2,0},{3,1},{4,6},{5,7},{6,4},{7,5},{8,10},{9,11},{10,... | collective-permute-start | bytes 49160 | tf_op jit(solution)/shard_map/ppermute | solution.py:865
  18.1 1.5 %collective-permute-done.4.y_hi = f32[2,48,8,128]{3,2,1,0:T(8,128)S(1)} collective-permute-done((f32[2,48,8,128]{3,2,1,0:T(8,128)S(1)}, f32[2,48,8,128]{3,2,1,0:T(8,128)S(1)}, u32[]{:S(2)}, u32[]{:S(2)}) %collective-permute-start.4) | collective-permute-done | bytes 393248 | tf_op jit(solution)/shard_map/ppermute | solution.py:865
  19.6 1.5 %pack_z.1 = (f32[48,48,128]{2,1,0:T(8,128)S(1)}, f32[48,48,128]{2,1,0:T(8,128)S(1)}, f32[6,48,128]{2,1,0:T(8,128)S(1)}, f32[6,48,128]{2,1,0:T(8,128)S(1)}) custom-call(f32[48,32,128]{2,1,0:T(8,128)S(1)} %get-tuple-element.79.s_mid, f32[48,32,128]{2,1,0:T(8,128)S(1)} %get-tuple-element.80.b_mid, f32[2,48,8,128]{3,2,1,0:T(8,128)S(1)} %collective-permute-done.3.y_lo, ...), custom_call_target="tpu_custom_call" | custom-call | tf_op jit(solution)/shard_map/pack_z/pallas_call | solution.py:907
  22.5 1.5 %collective-permute-start.7 = (f32[6,48,128]{2,1,0:T(8,128)S(1)}, f32[6,48,128]{2,1,0:T(8,128)S(1)}, u32[]{:S(2)}, u32[]{:S(2)}) collective-permute-start(f32[6,48,128]{2,1,0:T(8,128)S(1)} %get-tuple-element.89._), channel_id=1, source_target_pairs={{0,3},{1,0},{2,1},{3,2},{4,7},{5,4},{6,5},{7,6},{8,11},{9,8},{10,9... | collective-permute-start | bytes 442376 | tf_op jit(solution)/shard_map/ppermute | solution.py:865
  24.0 2.7 %collective-permute-start.8 = (f32[8,8,128]{2,1,0:T(8,128)S(1)}, f32[8,8,128]{2,1,0:T(8,128)S(1)}, u32[]{:S(2)}, u32[]{:S(2)}) collective-permute-start(f32[8,8,128]{2,1,0:T(8,128)S(1)} %gather_z.2.mine), channel_id=1, source_target_pairs={{0,32},{32,64},{64,96},{96,0},{1,33},{33,65},{65,97},{97,1},{2,34}... | collective-permute-start | bytes 98312 | tf_op jit(solution)/shard_map/ppermute | solution.py:865
  27.7 12.2 %level0_down.1 = (f32[48,48,128]{2,1,0:T(8,128)S(1)}, f32[6,48,128]{2,1,0:T(8,128)S(1)}, f32[16,16,128]{2,1,0:T(8,128)S(1)}, f32[10,16,128]{2,1,0:T(8,128)S(1)},...) custom-call(f32[48,48,128]{2,1,0:T(8,128)S(1)} %get-tuple-element.86, ...), custom_call_target="tpu_custom_call" | custom-call | tf_op jit(solution)/shard_map/level0_down/pallas_call | solution.py:913
  40.0 3.0 %collective-permute-start.9 = (f32[10,16,128]{2,1,0:T(8,128)S(1)}, f32[10,16,128]{2,1,0:T(8,128)S(1)}, u32[]{:S(2)}, u32[]{:S(2)}) collective-permute-start(f32[10,16,128]{2,1,0:T(8,128)S(1)} %get-tuple-element.94), channel_id=1, source_target_pairs={{0,32},{32,64},{64,96},{96,0},{1,33},{33,65},{65,97},{97,1},{2,34}... | collective-permute-start | bytes 245768 | tf_op jit(solution)/shard_map/ppermute | solution.py:865
  43.0 1.7 %collective-permute-done.10.from_hi.x_hi = f32[10,16,128]{2,1,0:T(8,128)S(1)} collective-permute-done((f32[10,16,128]{2,1,0:T(8,128)S(1)}, f32[10,16,128]{2,1,0:T(8,128)S(1)}, u32[]{:S(2)}, u32[]{:S(2)}) %collective-permute-start.10) | collective-permute-done | bytes 81952 | tf_op jit(solution)/shard_map/ppermute | solution.py:865
  44.8 3.9 %collective-permute-start.11 = (f32[360,128]{1,0:T(8,128)S(1)}, f32[360,128]{1,0:T(8,128)S(1)}, u32[]{:S(2)}, u32[]{:S(2)}) collective-permute-start(f32[360,128]{1,0:T(8,128)S(1)} %get-tuple-element.96), channel_id=1, source_target_pairs={{0,4},{4,8},{8,12},{12,16},{16,20},{20,24},{24,28},{28,0},{1,5},{5... | collective-permute-start | bytes 552968 | tf_op jit(solution)/shard_map/ppermute | solution.py:865
  48.7 2.0 %collective-permute-start.12 = (f32[360,128]{1,0:T(8,128)S(1)}, f32[360,128]{1,0:T(8,128)S(1)}, u32[]{:S(2)}, u32[]{:S(2)}) collective-permute-start(f32[360,128]{1,0:T(8,128)S(1)} %get-tuple-element.97.refs_2_), channel_id=1, source_target_pairs={{0,28},{4,0},{8,4},{12,8},{16,12},{20,16},{24,20},{28,24},{1,29},{... | collective-permute-start | bytes 552968 | tf_op jit(solution)/shard_map/ppermute | solution.py:865
  50.7 3.2 %collective-permute-start.13 = (f32[2,8,8,128]{3,2,1,0:T(8,128)S(1)}, f32[2,8,8,128]{3,2,1,0:T(8,128)S(1)}, u32[]{:S(2)}, u32[]{:S(2)}) collective-permute-start(f32[2,8,8,128]{3,2,1,0:T(8,128)S(1)} %pair.4.refs_0_), channel_id=1, source_target_pairs={{0,64},{32,96},{64,0},{96,32},{1,65},{33,97},{65,1},{97,33},{2,66}... | collective-permute-start | bytes 196616 | tf_op jit(solution)/shard_map/ppermute | solution.py:865
  53.9 1.7 %collective-permute-done.13.refs_1_ = f32[2,8,8,128]{3,2,1,0:T(8,128)S(1)} collective-permute-done((f32[2,8,8,128]{3,2,1,0:T(8,128)S(1)}, f32[2,8,8,128]{3,2,1,0:T(8,128)S(1)}, u32[]{:S(2)}, u32[]{:S(2)}) %collective-permute-start.13) | collective-permute-done | bytes 65568 | tf_op jit(solution)/shard_map/ppermute | solution.py:865
  56.9 2.6 %collective-permute-start.15 = (f32[6,40,128]{2,1,0:T(8,128)S(1)}, f32[6,40,128]{2,1,0:T(8,128)S(1)}, u32[]{:S(2)}, u32[]{:S(2)}) collective-permute-start(f32[6,40,128]{2,1,0:T(8,128)S(1)} %get-tuple-element.104._), channel_id=1, source_target_pairs={{0,3},{1,0},{2,1},{3,2},{4,7},{5,4},{6,5},{7,6},{8,11},{9,8},{10,9... | collective-permute-start | bytes 368648 | tf_op jit(solution)/shard_map/ppermute | solution.py:865
  59.5 3.2 %collective-permute-done.16.other = f32[32,8,128]{2,1,0:T(8,128)S(1)} collective-permute-done((f32[32,8,128]{2,1,0:T(8,128)S(1)}, f32[32,8,128]{2,1,0:T(8,128)S(1)}, u32[]{:S(2)}, u32[]{:S(2)}) %collective-permute-start.16) | collective-permute-done | bytes 131104 | tf_op jit(solution)/shard_map/ppermute | solution.py:865
  62.7 4.1 %level1_down.1 = (f32[36,40,128]{2,1,0:T(8,128)S(1)}, f32[16,128]{1,0:T(8,128)S(1)}, f32[6,36,40,128]{3,2,1,0:T(8,128)S(1)}, f32[36,40,128]{2,1,0:T(8,128)S(1)}, f32[36,40,128]{2,1,0:T(8,128)S(1)}) custom-call(f32[36,40,128]{2,1,0:T(8,128)S(1)} %get-tuple-element.102.ext, f32[6,40,128]{2,1,0:T(8,128)S(1)} %collective-permute-done.14.z_lo, ...), custom_call_target="tpu_custom_call" | custom-call | tf_op jit(solution)/shard_map/level1_down/pallas_call | solution.py:945
  66.9 5.2 %collective-permute-start.20 = (f32[2,32,8,128]{3,2,1,0:T(8,128)S(1)}, f32[2,32,8,128]{3,2,1,0:T(8,128)S(1)}, u32[]{:S(2)}, u32[]{:S(2)}) collective-permute-start(f32[2,32,8,128]{3,2,1,0:T(8,128)S(1)} %pair.5.refs_0_), channel_id=1, source_target_pairs={{0,16},{4,20},{8,24},{12,28},{16,0},{20,4},{24,8},{28,12},{1,17},{... | collective-permute-start | bytes 786440 | tf_op jit(solution)/shard_map/ppermute | solution.py:865
  72.0 3.6 %collective-permute-start.18 = (f32[16,128]{1,0:T(8,128)S(1)}, f32[16,128]{1,0:T(8,128)S(1)}, u32[]{:S(2)}, u32[]{:S(2)}) collective-permute-start(f32[16,128]{1,0:T(8,128)S(1)} %get-tuple-element.112.refs_2_.refs_0_.refs_4_), channel_id=1, source_target_pairs={{0,2},{1,3},{2,0},{3,1},{4,6},{5,7},{6,4},{7,5},{8,10},{9,11},{10,... | collective-permute-start | bytes 24584 | tf_op jit(solution)/shard_map/ppermute | solution.py:865
  78.6 2.6 %collective-permute-start.24 = (f32[4,32,8,128]{3,2,1,0:T(8,128)S(1)}, f32[4,32,8,128]{3,2,1,0:T(8,128)S(1)}, u32[]{:S(2)}, u32[]{:S(2)}) collective-permute-start(f32[4,32,8,128]{3,2,1,0:T(8,128)S(1)} %stack_y.2.same), channel_id=1, source_target_pairs={{0,4},{4,0},{8,12},{12,8},{16,20},{20,16},{24,28},{28,24},{1,5},{5... | collective-permute-start | bytes 1572872 | tf_op jit(solution)/shard_map/ppermute | solution.py:886
  81.2 3.0 %collective-permute-start.21 = (f32[8,8,128]{2,1,0:T(8,128)S(1)}, f32[8,8,128]{2,1,0:T(8,128)S(1)}, u32[]{:S(2)}, u32[]{:S(2)}) collective-permute-start(f32[8,8,128]{2,1,0:T(8,128)S(1)} %gather_z.3.refs_0_), channel_id=1, source_target_pairs={{0,32},{32,64},{64,96},{96,0},{1,33},{33,65},{65,97},{97,1},{2,34}... | collective-permute-start | bytes 98312 | tf_op jit(solution)/shard_map/ppermute | solution.py:865
  85.3 3.3 %collective-permute-done.22.refs_2_ = f32[8,8,128]{2,1,0:T(8,128)S(1)} collective-permute-done((f32[8,8,128]{2,1,0:T(8,128)S(1)}, f32[8,8,128]{2,1,0:T(8,128)S(1)}, u32[]{:S(2)}, u32[]{:S(2)}) %collective-permute-start.22) | collective-permute-done | bytes 32800 | tf_op jit(solution)/shard_map/ppermute | solution.py:865
  88.8 1.9 %collective-permute-start.25 = (f32[32,8,128]{2,1,0:T(8,128)S(1)}, f32[32,8,128]{2,1,0:T(8,128)S(1)}, u32[]{:S(2)}, u32[]{:S(2)}) collective-permute-start(f32[32,8,128]{2,1,0:T(8,128)S(1)} %gather_x.3.refs_0_.refs_4_), channel_id=1, source_target_pairs={{0,8},{4,12},{8,16},{12,20},{16,24},{20,28},{24,0},{28,4},{1,9},{5... | collective-permute-start | bytes 393224 | tf_op jit(solution)/shard_map/ppermute | solution.py:865
  91.0 2.1 %collective-permute-start.27 = (f32[32,8,128]{2,1,0:T(8,128)S(1)}, f32[32,8,128]{2,1,0:T(8,128)S(1)}, u32[]{:S(2)}, u32[]{:S(2)}) collective-permute-start(f32[32,8,128]{2,1,0:T(8,128)S(1)} %gather_x.3.refs_0_.refs_4_), channel_id=1, source_target_pairs={{0,24},{4,28},{8,0},{12,4},{16,8},{20,12},{24,16},{28,20},{1,25},{... | collective-permute-start | bytes 393224 | tf_op jit(solution)/shard_map/ppermute | solution.py:865
  93.9 3.0 %collective-permute-done.26.refs_2_ = f32[32,8,128]{2,1,0:T(8,128)S(1)} collective-permute-done((f32[32,8,128]{2,1,0:T(8,128)S(1)}, f32[32,8,128]{2,1,0:T(8,128)S(1)}, u32[]{:S(2)}, u32[]{:S(2)}) %collective-permute-start.26) | collective-permute-done | bytes 131104 | tf_op jit(solution)/shard_map/ppermute | solution.py:865
  96.9 2.8 %collective-permute-start.28 = (f32[4,32,8,128]{3,2,1,0:T(8,128)S(1)}, f32[4,32,8,128]{3,2,1,0:T(8,128)S(1)}, u32[]{:S(2)}, u32[]{:S(2)}) collective-permute-start(f32[4,32,8,128]{3,2,1,0:T(8,128)S(1)} %stack_y.3.same), channel_id=1, source_target_pairs={{0,4},{4,0},{8,12},{12,8},{16,20},{20,16},{24,28},{28,24},{1,5},{5... | collective-permute-start | bytes 1572872 | tf_op jit(solution)/shard_map/ppermute | solution.py:886
  99.8 3.6 %coarse_prepare.1 = (f32[6,32,64,128]{3,2,1,0:T(8,128)S(1)}, f32[32,64,128]{2,1,0:T(8,128)S(1)}, f32[32,64,128]{2,1,0:T(8,128)S(1)}, f32[6,16,32,128]{3,2,1,0:T(...) custom-call(f32[4,32,8,128]{3,2,1,0:T(8,128)S(1)} %stack_y.2.same, ...), custom_call_target="tpu_custom_call" | custom-call | tf_op jit(solution)/shard_map/coarse_prepare/pallas_call | solution.py:963
  103.3 9.3 %bottom.1.c2 = f32[18,24,128]{2,1,0:T(8,128)S(1)} custom-call(f32[4,32,8,128]{3,2,1,0:T(8,128)S(1)} %stack_y.3.same, f32[4,32,8,128]{3,2,1,0:T(8,128)S(1)} %collective-permute-done.28.sibling, f32[6,32,64,128]{3,2,1,0:T(8,128)S(1)} %get-tuple-element.123.g, f32[32,64,128]{2,1,0:T(8,128)S(1)} %get-tuple-element.124.inv, ...), custom_call_target="tpu_custom_call" | custom-call | tf_op jit(solution)/shard_map/bottom/pallas_call | solution.py:970
  112.7 3.7 %level1_up.1.c1 = f32[24,24,128]{2,1,0:T(8,128)S(1)} custom-call(f32[18,24,128]{2,1,0:T(8,128)S(1)} %bottom.1.c2, f32[6,36,40,128]{3,2,1,0:T(8,128)S(1)} %get-tuple-element.130.g, f32[36,40,128]{2,1,0:T(8,128)S(1)} %get-tuple-element.131.sp, f32[36,40,128]{2,1,0:T(8,128)S(1)} %get-tuple-element.132.beta, f32[36,40,128]{2,1,0:T(8,128)S(1)} %get-tuple-element.133.iterate), custom_call_target="tpu_custom_call" | custom-call | tf_op jit(solution)/shard_map/level1_up/pallas_call | solution.py:973
  116.3 10.0 %level0_up.1 = f32[32,32,128]{2,1,0:T(8,128)} custom-call(f32[24,24,128]{2,1,0:T(8,128)S(1)} %level1_up.1.c1, f32[48,48,128]{2,1,0:T(8,128)S(1)} %get-tuple-element.87.beta, f32[7,48,48,128]{3,2,1,0:T(8,128)S(1)} %get-tuple-element.134.g_main, f32[6,6,48,128]{3,2,1,0:T(8,128)S(1)} %get-tuple-element.135.g_strip, f32[48,48,128]{2,1,0:T(8,128)S(1)} %get-tuple-element.136.sp, ...), custom_call_target="tpu_custom_call" | custom-call | tf_op jit(solution)/shard_map/level0_up/pallas_call | solution.py:980
  (53 shorter events, 16.2 us)
Async XLA Ops:
  0.0 10.6 %copy-start.1 = (f32[32,32,128]{2,1,0:T(8,128)S(1)}, f32[32,32,128]{2,1,0:T(8,128)}, u32[]{:S(2)}) copy-start(f32[32,32,128]{2,1,0:T(8,128)} %src) | copy-start | bytes 1572868
  0.0 4.9 %copy-start = (f32[32,32,128]{2,1,0:T(8,128)S(1)}, f32[32,32,128]{2,1,0:T(8,128)}, u32[]{:S(2)}) copy-start(f32[32,32,128]{2,1,0:T(8,128)} %beta.1) | copy-start | bytes 1572868
  2.1 8.5 %collective-permute-start.1 = (f32[2,8,32,128]{3,2,1,0:T(8,128)S(1)}, f32[2,8,32,128]{3,2,1,0:T(8,128)S(1)}, u32[]{:S(2)}, u32[]{:S(2)}) collective-permute-start(f32[2,8,32,128]{3,2,1,0:T(8,128)S(1)} %get-tuple-element.76._), channel_id=1, source_target_pairs={{0,96},{32,0},{64,32},{96,64},{1,97},{33,1},{65,33},{97,65},{2,98}... | collective-permute-start | bytes 786440 | tf_op jit(solution)/shard_map/ppermute | solution.py:865
  2.7 7.8 %collective-permute-start = (f32[2,8,32,128]{3,2,1,0:T(8,128)S(1)}, f32[2,8,32,128]{3,2,1,0:T(8,128)S(1)}, u32[]{:S(2)}, u32[]{:S(2)}) collective-permute-start(f32[2,8,32,128]{3,2,1,0:T(8,128)S(1)} %get-tuple-element.75), channel_id=1, source_target_pairs={{0,32},{32,64},{64,96},{96,0},{1,33},{33,65},{65,97},{97,1},{2,34}... | collective-permute-start | bytes 786440 | tf_op jit(solution)/shard_map/ppermute | solution.py:865
  5.4 4.1 %collective-permute-start.2 = (f32[16,128]{1,0:T(8,128)S(1)}, f32[16,128]{1,0:T(8,128)S(1)}, u32[]{:S(2)}, u32[]{:S(2)}) collective-permute-start(f32[16,128]{1,0:T(8,128)S(1)} %coarse_beta.1.mine), channel_id=1, source_target_pairs={{0,1},{1,2},{2,3},{3,0},{4,5},{5,6},{6,7},{7,4},{8,9},{9,10},{10,1... | collective-permute-start | bytes 24584 | tf_op jit(solution)/shard_map/ppermute | solution.py:865
  10.7 8.8 %collective-permute-start.4 = (f32[2,48,8,128]{3,2,1,0:T(8,128)S(1)}, f32[2,48,8,128]{3,2,1,0:T(8,128)S(1)}, u32[]{:S(2)}, u32[]{:S(2)}) collective-permute-start(f32[2,48,8,128]{3,2,1,0:T(8,128)S(1)} %get-tuple-element.82.refs_2_), channel_id=1, source_target_pairs={{0,28},{4,0},{8,4},{12,8},{16,12},{20,16},{24,20},{28,24},{1,29},{... | collective-permute-start | bytes 1179656 | tf_op jit(solution)/shard_map/ppermute | solution.py:865
  12.3 7.3 %collective-permute-start.3 = (f32[2,48,8,128]{3,2,1,0:T(8,128)S(1)}, f32[2,48,8,128]{3,2,1,0:T(8,128)S(1)}, u32[]{:S(2)}, u32[]{:S(2)}) collective-permute-start(f32[2,48,8,128]{3,2,1,0:T(8,128)S(1)} %get-tuple-element.81), channel_id=1, source_target_pairs={{0,4},{4,8},{8,12},{12,16},{16,20},{20,24},{24,28},{28,0},{1,5},{5... | collective-permute-start | bytes 1179656 | tf_op jit(solution)/shard_map/ppermute | solution.py:865
  13.9 4.1 %collective-permute-start.5 = (f32[2,16,128]{2,1,0:T(8,128)S(1)}, f32[2,16,128]{2,1,0:T(8,128)S(1)}, u32[]{:S(2)}, u32[]{:S(2)}) collective-permute-start(f32[2,16,128]{2,1,0:T(8,128)S(1)} %pair.3.refs_0_), channel_id=1, source_target_pairs={{0,2},{1,3},{2,0},{3,1},{4,6},{5,7},{6,4},{7,5},{8,10},{9,11},{10,... | collective-permute-start | bytes 49160 | tf_op jit(solution)/shard_map/ppermute | solution.py:865
  21.1 6.6 %collective-permute-start.6 = (f32[6,48,128]{2,1,0:T(8,128)S(1)}, f32[6,48,128]{2,1,0:T(8,128)S(1)}, u32[]{:S(2)}, u32[]{:S(2)}) collective-permute-start(f32[6,48,128]{2,1,0:T(8,128)S(1)} %get-tuple-element.88), channel_id=1, source_target_pairs={{0,1},{1,2},{2,3},{3,0},{4,5},{5,6},{6,7},{7,4},{8,9},{9,10},{10,1... | collective-permute-start | bytes 442376 | tf_op jit(solution)/shard_map/ppermute | solution.py:865
  22.5 5.2 %collective-permute-start.7 = (f32[6,48,128]{2,1,0:T(8,128)S(1)}, f32[6,48,128]{2,1,0:T(8,128)S(1)}, u32[]{:S(2)}, u32[]{:S(2)}) collective-permute-start(f32[6,48,128]{2,1,0:T(8,128)S(1)} %get-tuple-element.89._), channel_id=1, source_target_pairs={{0,3},{1,0},{2,1},{3,2},{4,7},{5,4},{6,5},{7,6},{8,11},{9,8},{10,9... | collective-permute-start | bytes 442376 | tf_op jit(solution)/shard_map/ppermute | solution.py:865
  24.0 3.7 %collective-permute-start.8 = (f32[8,8,128]{2,1,0:T(8,128)S(1)}, f32[8,8,128]{2,1,0:T(8,128)S(1)}, u32[]{:S(2)}, u32[]{:S(2)}) collective-permute-start(f32[8,8,128]{2,1,0:T(8,128)S(1)} %gather_z.2.mine), channel_id=1, source_target_pairs={{0,32},{32,64},{64,96},{96,0},{1,33},{33,65},{65,97},{97,1},{2,34}... | collective-permute-start | bytes 98312 | tf_op jit(solution)/shard_map/ppermute | solution.py:865
  39.9 4.9 %collective-permute-start.10 = (f32[10,16,128]{2,1,0:T(8,128)S(1)}, f32[10,16,128]{2,1,0:T(8,128)S(1)}, u32[]{:S(2)}, u32[]{:S(2)}) collective-permute-start(f32[10,16,128]{2,1,0:T(8,128)S(1)} %get-tuple-element.95), channel_id=1, source_target_pairs={{0,96},{32,0},{64,32},{96,64},{1,97},{33,1},{65,33},{97,65},{2,98}... | collective-permute-start | bytes 245768 | tf_op jit(solution)/shard_map/ppermute | solution.py:865
  40.0 4.8 %collective-permute-start.9 = (f32[10,16,128]{2,1,0:T(8,128)S(1)}, f32[10,16,128]{2,1,0:T(8,128)S(1)}, u32[]{:S(2)}, u32[]{:S(2)}) collective-permute-start(f32[10,16,128]{2,1,0:T(8,128)S(1)} %get-tuple-element.94), channel_id=1, source_target_pairs={{0,32},{32,64},{64,96},{96,0},{1,33},{33,65},{65,97},{97,1},{2,34}... | collective-permute-start | bytes 245768 | tf_op jit(solution)/shard_map/ppermute | solution.py:865
  44.8 10.8 %collective-permute-start.11 = (f32[360,128]{1,0:T(8,128)S(1)}, f32[360,128]{1,0:T(8,128)S(1)}, u32[]{:S(2)}, u32[]{:S(2)}) collective-permute-start(f32[360,128]{1,0:T(8,128)S(1)} %get-tuple-element.96), channel_id=1, source_target_pairs={{0,4},{4,8},{8,12},{12,16},{16,20},{20,24},{24,28},{28,0},{1,5},{5... | collective-permute-start | bytes 552968 | tf_op jit(solution)/shard_map/ppermute | solution.py:865
  48.7 6.9 %collective-permute-start.12 = (f32[360,128]{1,0:T(8,128)S(1)}, f32[360,128]{1,0:T(8,128)S(1)}, u32[]{:S(2)}, u32[]{:S(2)}) collective-permute-start(f32[360,128]{1,0:T(8,128)S(1)} %get-tuple-element.97.refs_2_), channel_id=1, source_target_pairs={{0,28},{4,0},{8,4},{12,8},{16,12},{20,16},{24,20},{28,24},{1,29},{... | collective-permute-start | bytes 552968 | tf_op jit(solution)/shard_map/ppermute | solution.py:865
  50.7 4.9 %collective-permute-start.13 = (f32[2,8,8,128]{3,2,1,0:T(8,128)S(1)}, f32[2,8,8,128]{3,2,1,0:T(8,128)S(1)}, u32[]{:S(2)}, u32[]{:S(2)}) collective-permute-start(f32[2,8,8,128]{3,2,1,0:T(8,128)S(1)} %pair.4.refs_0_), channel_id=1, source_target_pairs={{0,64},{32,96},{64,0},{96,32},{1,65},{33,97},{65,1},{97,33},{2,66}... | collective-permute-start | bytes 196616 | tf_op jit(solution)/shard_map/ppermute | solution.py:865
  56.4 6.2 %collective-permute-start.16 = (f32[32,8,128]{2,1,0:T(8,128)S(1)}, f32[32,8,128]{2,1,0:T(8,128)S(1)}, u32[]{:S(2)}, u32[]{:S(2)}) collective-permute-start(f32[32,8,128]{2,1,0:T(8,128)S(1)} %gather_x.2.mine), channel_id=1, source_target_pairs={{0,8},{4,12},{8,16},{12,20},{16,24},{20,28},{24,0},{28,4},{1,9},{5... | collective-permute-start | bytes 393224 | tf_op jit(solution)/shard_map/ppermute | solution.py:865
  56.8 5.9 %collective-permute-start.14 = (f32[6,40,128]{2,1,0:T(8,128)S(1)}, f32[6,40,128]{2,1,0:T(8,128)S(1)}, u32[]{:S(2)}, u32[]{:S(2)}) collective-permute-start(f32[6,40,128]{2,1,0:T(8,128)S(1)} %get-tuple-element.103), channel_id=1, source_target_pairs={{0,1},{1,2},{2,3},{3,0},{4,5},{5,6},{6,7},{7,4},{8,9},{9,10},{10,1... | collective-permute-start | bytes 368648 | tf_op jit(solution)/shard_map/ppermute | solution.py:865
  56.9 5.8 %collective-permute-start.15 = (f32[6,40,128]{2,1,0:T(8,128)S(1)}, f32[6,40,128]{2,1,0:T(8,128)S(1)}, u32[]{:S(2)}, u32[]{:S(2)}) collective-permute-start(f32[6,40,128]{2,1,0:T(8,128)S(1)} %get-tuple-element.104._), channel_id=1, source_target_pairs={{0,3},{1,0},{2,1},{3,2},{4,7},{5,4},{6,5},{7,6},{8,11},{9,8},{10,9... | collective-permute-start | bytes 368648 | tf_op jit(solution)/shard_map/ppermute | solution.py:865
  66.9 10.2 %collective-permute-start.20 = (f32[2,32,8,128]{3,2,1,0:T(8,128)S(1)}, f32[2,32,8,128]{3,2,1,0:T(8,128)S(1)}, u32[]{:S(2)}, u32[]{:S(2)}) collective-permute-start(f32[2,32,8,128]{3,2,1,0:T(8,128)S(1)} %pair.5.refs_0_), channel_id=1, source_target_pairs={{0,16},{4,20},{8,24},{12,28},{16,0},{20,4},{24,8},{28,12},{1,17},{... | collective-permute-start | bytes 786440 | tf_op jit(solution)/shard_map/ppermute | solution.py:865
  72.0 5.1 %collective-permute-start.17 = (f32[16,128]{1,0:T(8,128)S(1)}, f32[16,128]{1,0:T(8,128)S(1)}, u32[]{:S(2)}, u32[]{:S(2)}) collective-permute-start(f32[16,128]{1,0:T(8,128)S(1)} %get-tuple-element.112.refs_2_.refs_0_.refs_4_), channel_id=1, source_target_pairs={{0,1},{1,2},{2,3},{3,0},{4,5},{5,6},{6,7},{7,4},{8,9},{9,10},{10,1... | collective-permute-start | bytes 24584 | tf_op jit(solution)/shard_map/ppermute | solution.py:865
  72.0 5.1 %collective-permute-start.18 = (f32[16,128]{1,0:T(8,128)S(1)}, f32[16,128]{1,0:T(8,128)S(1)}, u32[]{:S(2)}, u32[]{:S(2)}) collective-permute-start(f32[16,128]{1,0:T(8,128)S(1)} %get-tuple-element.112.refs_2_.refs_0_.refs_4_), channel_id=1, source_target_pairs={{0,2},{1,3},{2,0},{3,1},{4,6},{5,7},{6,4},{7,5},{8,10},{9,11},{10,... | collective-permute-start | bytes 24584 | tf_op jit(solution)/shard_map/ppermute | solution.py:865
  75.7 2.8 %collective-permute-start.19 = (f32[16,128]{1,0:T(8,128)S(1)}, f32[16,128]{1,0:T(8,128)S(1)}, u32[]{:S(2)}, u32[]{:S(2)}) collective-permute-start(f32[16,128]{1,0:T(8,128)S(1)} %get-tuple-element.112.refs_2_.refs_0_.refs_4_), channel_id=1, source_target_pairs={{0,3},{1,0},{2,1},{3,2},{4,7},{5,4},{6,5},{7,6},{8,11},{9,8},{10,9... | collective-permute-start | bytes 24584 | tf_op jit(solution)/shard_map/ppermute | solution.py:865
  78.6 10.2 %collective-permute-start.24 = (f32[4,32,8,128]{3,2,1,0:T(8,128)S(1)}, f32[4,32,8,128]{3,2,1,0:T(8,128)S(1)}, u32[]{:S(2)}, u32[]{:S(2)}) collective-permute-start(f32[4,32,8,128]{3,2,1,0:T(8,128)S(1)} %stack_y.2.same), channel_id=1, source_target_pairs={{0,4},{4,0},{8,12},{12,8},{16,20},{20,16},{24,28},{28,24},{1,5},{5... | collective-permute-start | bytes 1572872 | tf_op jit(solution)/shard_map/ppermute | solution.py:886
  81.2 4.1 %collective-permute-start.21 = (f32[8,8,128]{2,1,0:T(8,128)S(1)}, f32[8,8,128]{2,1,0:T(8,128)S(1)}, u32[]{:S(2)}, u32[]{:S(2)}) collective-permute-start(f32[8,8,128]{2,1,0:T(8,128)S(1)} %gather_z.3.refs_0_), channel_id=1, source_target_pairs={{0,32},{32,64},{64,96},{96,0},{1,33},{33,65},{65,97},{97,1},{2,34}... | collective-permute-start | bytes 98312 | tf_op jit(solution)/shard_map/ppermute | solution.py:865
  84.2 4.4 %collective-permute-start.22 = (f32[8,8,128]{2,1,0:T(8,128)S(1)}, f32[8,8,128]{2,1,0:T(8,128)S(1)}, u32[]{:S(2)}, u32[]{:S(2)}) collective-permute-start(f32[8,8,128]{2,1,0:T(8,128)S(1)} %gather_z.3.refs_0_), channel_id=1, source_target_pairs={{0,64},{32,96},{64,0},{96,32},{1,65},{33,97},{65,1},{97,33},{2,66}... | collective-permute-start | bytes 98312 | tf_op jit(solution)/shard_map/ppermute | solution.py:865
  84.4 4.3 %collective-permute-start.23 = (f32[8,8,128]{2,1,0:T(8,128)S(1)}, f32[8,8,128]{2,1,0:T(8,128)S(1)}, u32[]{:S(2)}, u32[]{:S(2)}) collective-permute-start(f32[8,8,128]{2,1,0:T(8,128)S(1)} %gather_z.3.refs_0_), channel_id=1, source_target_pairs={{0,96},{32,0},{64,32},{96,64},{1,97},{33,1},{65,33},{97,65},{2,98}... | collective-permute-start | bytes 98312 | tf_op jit(solution)/shard_map/ppermute | solution.py:865
  88.8 5.1 %collective-permute-start.25 = (f32[32,8,128]{2,1,0:T(8,128)S(1)}, f32[32,8,128]{2,1,0:T(8,128)S(1)}, u32[]{:S(2)}, u32[]{:S(2)}) collective-permute-start(f32[32,8,128]{2,1,0:T(8,128)S(1)} %gather_x.3.refs_0_.refs_4_), channel_id=1, source_target_pairs={{0,8},{4,12},{8,16},{12,20},{16,24},{20,28},{24,0},{28,4},{1,9},{5... | collective-permute-start | bytes 393224 | tf_op jit(solution)/shard_map/ppermute | solution.py:865
  90.6 6.3 %collective-permute-start.26 = (f32[32,8,128]{2,1,0:T(8,128)S(1)}, f32[32,8,128]{2,1,0:T(8,128)S(1)}, u32[]{:S(2)}, u32[]{:S(2)}) collective-permute-start(f32[32,8,128]{2,1,0:T(8,128)S(1)} %gather_x.3.refs_0_.refs_4_), channel_id=1, source_target_pairs={{0,16},{4,20},{8,24},{12,28},{16,0},{20,4},{24,8},{28,12},{1,17},{... | collective-permute-start | bytes 393224 | tf_op jit(solution)/shard_map/ppermute | solution.py:865
  91.0 5.9 %collective-permute-start.27 = (f32[32,8,128]{2,1,0:T(8,128)S(1)}, f32[32,8,128]{2,1,0:T(8,128)S(1)}, u32[]{:S(2)}, u32[]{:S(2)}) collective-permute-start(f32[32,8,128]{2,1,0:T(8,128)S(1)} %gather_x.3.refs_0_.refs_4_), channel_id=1, source_target_pairs={{0,24},{4,28},{8,0},{12,4},{16,8},{20,12},{24,16},{28,20},{1,25},{... | collective-permute-start | bytes 393224 | tf_op jit(solution)/shard_map/ppermute | solution.py:865
  96.9 6.4 %collective-permute-start.28 = (f32[4,32,8,128]{3,2,1,0:T(8,128)S(1)}, f32[4,32,8,128]{3,2,1,0:T(8,128)S(1)}, u32[]{:S(2)}, u32[]{:S(2)}) collective-permute-start(f32[4,32,8,128]{3,2,1,0:T(8,128)S(1)} %stack_y.3.same), channel_id=1, source_target_pairs={{0,4},{4,0},{8,12},{12,8},{16,20},{20,16},{24,28},{28,24},{1,5},{5... | collective-permute-start | bytes 1572872 | tf_op jit(solution)/shard_map/ppermute | solution.py:886

commit v9 on v7

--- a/solution.py
+++ b/solution.py
@@ -202,7 +202,7 @@
     return [s * inverse for s in sums], inverse, total
 
 
-def level0_setup(b_pad, bt_pad, ghost, src, src_t, g_main, g_strip, sp, sp_t, total):
+def level0_setup(b_pad, bt_pad, ghost, src, src_t, g_main, g_strip, sp, sp_t, total, v, t, u, u_t, first):
     strip_ghosts(b_pad, ghost)
     lane = lanes_of(48)
 
@@ -227,9 +227,11 @@
         g_main[4, x] = jnp.where(lane == 0, 0.0, faces[4])
         g_main[5, x] = jnp.where(lane == 127, 0.0, faces[5])
         g_main[6, x] = jnp.where(lane == 0, faces[4], jnp.where(lane == 127, faces[5], 0.0))
-        sp[x] = src[x] * (2.0 * inverse)
-        if total is not None:
-            total[x] = tot
+        scaled = src[x] * (2.0 * inverse)
+        sp[x] = scaled
+        u[x] = first * scaled
+        v[x + 1, 8:56, :] = first * scaled
+        total[x] = tot
 
     loop(0, 48, 6, body)
     for xx in range(6):
@@ -241,7 +243,10 @@
         )
         for i in range(6):
             g_strip[i, xx] = faces[i]
-        sp_t[xx] = src_t[xx] * (2.0 * inverse)
+        scaled = src_t[xx] * (2.0 * inverse)
+        sp_t[xx] = scaled
+        u_t[xx] = first * scaled
+        t[xx, 8:56, :] = first * scaled
 
 
 def block_rest(v, t, g_main, sp, x, skip=0):
@@ -271,7 +276,7 @@
         u[x] = new
         v_out[x + 1, 8:56, :] = here + new
 
-    loop(low, high, 6, body)
+    loop(low, high, 4, body)
     for xx in range(6):
         here = t[xx, 8:56, :]
         before, after = strip_sides(t, xx)
@@ -326,8 +331,6 @@
     vm(50, 64, 128),
     vm(6, 64, 128),
     vm(50, 64, 128),
-    vm(50, 64, 128),
-    vm(6, 64, 128),
     vm(6, 64, 128),
     vm(6, 48, 128),
     vm(48, 48, 128),
@@ -339,8 +342,8 @@
 
 
 def level0_down(
-    src, beta, z_lo, z_hi, iter_out, iter_t_out, c_out, c_lo, c_hi, g_main, g_strip, sp, sp_t, bt_out,
-    b_pad, bt_pad, va, vb, ta, tb, ghost, u, u_t, src_t, total, rows,
+    src, beta, z_lo, z_hi, vb, tb, c_out, c_lo, c_hi, g_main, g_strip, sp, sp_t, bt_out,
+    b_pad, bt_pad, va, ta, ghost, u, u_t, src_t, total, rows,
 ):
     for ref in (b_pad, va, vb):
         clear_edges(ref, 48, 48)
@@ -350,28 +353,21 @@
     unpack_strip(z_lo, z_hi, src_t, bt_pad)
     for xx in range(6):
         bt_out[xx] = bt_pad[xx, 8:56, :]
-    level0_setup(b_pad, bt_pad, ghost, src, src_t, g_main, g_strip, sp, sp_t, total)
-
-    first = RECIPE[0][1]
-
-    def start(x):
-        u[x] = first * sp[x]
-        va[x + 1, 8:56, :] = u[x]
-
-    loop(0, 48, 8, start)
-    for xx in range(6):
-        u_t[xx] = first * sp_t[xx]
-        ta[xx, 8:56, :] = u_t[xx]
+    level0_setup(
+        b_pad, bt_pad, ghost, src, src_t, g_main, g_strip, sp, sp_t, total, va, ta, u, u_t, RECIPE[0][1]
+    )
+    for x in (0, 1, 46, 47):
+        vb[x + 1, 8:56, :] = jnp.zeros((48, 128), F32)
     bufs = [(va, ta), (vb, tb)]
     for k in range(1, SMOOTH):
         (v, t), (w, s) = bufs
         retain, factor = RECIPE[k]
-        level0_step(v, t, w, s, ghost, g_main, g_strip, sp, sp_t, u, u_t, 0, 48, retain, factor)
+        level0_step(
+            v, t, w, s, ghost, g_main, g_strip, sp, sp_t, u, u_t, 1 + k, 47 - k, retain, factor
+        )
         bufs = [(w, s), (v, t)]
     v, t = bufs[0]
-    iter_out[...] = v[1:49, 8:56, :]
-    for xx in range(6):
-        iter_t_out[xx] = t[xx, 8:56, :]
+    assert v is vb and t is tb
 
     to_low = pick(lambda r, c: r // 2 == c)
     to_high = pick(lambda r, c: r // 2 + 64 == c)
@@ -523,7 +519,6 @@
 LEVEL1_SCRATCH = [
     vm(38, 56, 128),
     vm(38, 56, 128),
-    vm(38, 56, 128),
     vm(36, 40, 128),
     vm(36, 40, 128),
     vm(36, 40, 128),
@@ -560,15 +555,15 @@
 
 
 def level1_down(
-    ext, z_lo, z_hi, iter_out, chunk, g, sp, beta_out,
-    b_pad, va, vb, u, src, total, rows,
+    ext, z_lo, z_hi, vb, chunk, g, sp, beta_out,
+    b_pad, va, u, src, total, rows,
 ):
     for ref in (b_pad, va, vb):
         clear_edges(ref, 36, 40)
     level1_unpack(ext, z_lo, z_hi, src, b_pad, beta_out)
     ring_weights(b_pad, src, g, sp, total, 36, 40, 4.0)
     v = ring_cheb(va, vb, g, sp, u, 36, 40, RECIPE, True)
-    iter_out[...] = v[1:37, 8:48, :]
+    assert v is vb
     summed = []
     for x2 in range(8):
         parts = []
@@ -792,7 +787,7 @@
         rows[x2, pl.ds(1, 18, stride=2), :] = part
         for half in range(2):
             x = 2 * x2 + half
-            va[x + 1, 8:48, :] = jnp.where(beta[x] > 0.0, iterate[x] + rows[x2], 0.0)
+            va[x + 1, 8:48, :] = jnp.where(beta[x] > 0.0, iterate[x + 1, 8:48, :] + rows[x2], 0.0)
 
     loop(0, 18, 12, prolong)
     v = ring_cheb(va, vb, g, sp, u, 36, 40, RECIPE, False)
@@ -815,7 +810,7 @@
         rows[x1, pl.ds(1, 24, stride=2), :] = wide
         for half in range(2):
             x = 2 * x1 + half
-            va[x + 1, 8:56, :] = jnp.where(beta[x] > 0.0, iterate[x] + rows[x1], 0.0)
+            va[x + 1, 8:56, :] = jnp.where(beta[x] > 0.0, iterate[x + 1, 8:56, :] + rows[x1], 0.0)
 
     loop(0, 24, 12, prolong)
 
@@ -834,7 +829,7 @@
         rows[m, pl.ds(1, 24, stride=2), :] = acc
         for half in range(2):
             xx = 2 * m + half
-            ta[xx, 8:56, :] = jnp.where(beta_t[xx] > 0.0, iterate_t[xx] + rows[m], 0.0)
+            ta[xx, 8:56, :] = jnp.where(beta_t[xx] > 0.0, iterate_t[xx, 8:56, :] + rows[m], 0.0)
 
     loop(0, 3, 36, prolong_strip)
     for x in [*range(6), *range(42, 48)]:
@@ -913,8 +908,8 @@
     iter0, iter0_t, c, lo, hi, *ready = call(
         level0_down,
         (
-            whole,
-            strip,
+            sds(50, 64, 128),
+            sds(6, 64, 128),
             sds(16, 16, 128),
             sds(10, 16, 128),
             sds(10, 16, 128),
@@ -946,7 +941,7 @@
     level1 = sds(36, 40, 128)
     iter1, chunk, g1, sp1, beta1 = call(
         level1_down,
-        (level1, sds(16, 128), sds(6, 36, 40, 128), level1, level1),
+        (sds(38, 56, 128), sds(16, 128), sds(6, 36, 40, 128), level1, level1),
         LEVEL1_SCRATCH,
         name="level1_down",
         mib=8,

time: 127 us -> 126 us (level)
  no operation moved by 1% of the time
where the time goes in v9:
time: 126 us; the launch traced here: 125 us
  starting transfers between devices  47.8 us (38%)
  Pallas kernels  45.5 us (36%)
  waiting for transfers between devices  29.2 us (23%)
  local copies, waits for them, and re-layouts  2.07 us (2%)
    ppermute x27, starting transfers between devices, ring(): lax.ppermute(value, axis, [(i, (i + step) % count) for i in range(count)])  40 us
    ppermute x27, waiting for transfers between devices, ring(): lax.ppermute(value, axis, [(i, (i + step) % count) for i in range(count)])  29.2 us
    pallas_call x1, Pallas kernels, per_device(): call(level0_down, (sds(50, 64, 128), sds(6, 64, 128), sds(16, 16, 128), s...  11.7 us
    pallas_call x1, Pallas kernels, per_device(): call(level0_up, sds(32, 32, 128), [vm(50, 64, 128), vm(50, 64, 128), vm(6...  9.82 us
    pallas_call x1, Pallas kernels, per_device(): call(bottom, sds(18, 24, 128), BOTTOM_SCRATCH, name='bottom', mib=18)  9.26 us
    ppermute x2, starting transfers between devices, across(): lax.ppermute(value, 'gy', [(i, i + 1 - 2 * (i % 2)) for i in range(count)])  7.84 us
    pallas_call x1, Pallas kernels, per_device(): call(level1_down, (sds(38, 56, 128), sds(16, 128), sds(6, 36, 40, 128), l...  4.15 us
    pallas_call x1, Pallas kernels, per_device(): call(level1_up, sds(24, 24, 128), [vm(38, 56, 128), vm(38, 56, 128), vm(3...  3.65 us
  transfers between devices with their start and end apart: 29, of which 19 were waited for; matrix products, arithmetic and copies ran while one was open for 0% of the time, Pallas kernels for 3%

profile of v9, /device:TPU:7, one launch (start us, length us, event | category | flops | bytes accessed | tf_op | source)
XLA Modules:
  0.0 124.8 jit_solution(5156919851184269242)
XLA Ops:
  2.7 2.1 %collective-permute-start = (f32[2,8,32,128]{3,2,1,0:T(8,128)S(1)}, f32[2,8,32,128]{3,2,1,0:T(8,128)S(1)}, u32[]{:S(2)}, u32[]{:S(2)}) collective-permute-start(f32[2,8,32,128]{3,2,1,0:T(8,128)S(1)} %get-tuple-element.72), channel_id=1, source_target_pairs={{0,32},{32,64},{64,96},{96,0},{1,33},{33,65},{65,97},{97,1},{2,34}... | collective-permute-start | bytes 786440 | tf_op jit(solution)/shard_map/ppermute | solution.py:860
  5.4 1.3 %collective-permute-start.2 = (f32[16,128]{1,0:T(8,128)S(1)}, f32[16,128]{1,0:T(8,128)S(1)}, u32[]{:S(2)}, u32[]{:S(2)}) collective-permute-start(f32[16,128]{1,0:T(8,128)S(1)} %coarse_beta.1.mine), channel_id=1, source_target_pairs={{0,1},{1,2},{2,3},{3,0},{4,5},{5,6},{6,7},{7,4},{8,9},{9,10},{10,1... | collective-permute-start | bytes 24584 | tf_op jit(solution)/shard_map/ppermute | solution.py:860
  6.7 2.8 %collective-permute-done.2.other = f32[16,128]{1,0:T(8,128)S(1)} collective-permute-done((f32[16,128]{1,0:T(8,128)S(1)}, f32[16,128]{1,0:T(8,128)S(1)}, u32[]{:S(2)}, u32[]{:S(2)}) %collective-permute-start.2) | collective-permute-done | bytes 8224 | tf_op jit(solution)/shard_map/ppermute | solution.py:860
  10.7 3.1 %collective-permute-start.3 = (f32[2,48,8,128]{3,2,1,0:T(8,128)S(1)}, f32[2,48,8,128]{3,2,1,0:T(8,128)S(1)}, u32[]{:S(2)}, u32[]{:S(2)}) collective-permute-start(f32[2,48,8,128]{3,2,1,0:T(8,128)S(1)} %get-tuple-element.78), channel_id=1, source_target_pairs={{0,4},{4,8},{8,12},{12,16},{16,20},{20,24},{24,28},{28,0},{1,5},{5... | collective-permute-start | bytes 1179656 | tf_op jit(solution)/shard_map/ppermute | solution.py:860
  13.8 2.9 %collective-permute-start.5 = (f32[2,16,128]{2,1,0:T(8,128)S(1)}, f32[2,16,128]{2,1,0:T(8,128)S(1)}, u32[]{:S(2)}, u32[]{:S(2)}) collective-permute-start(f32[2,16,128]{2,1,0:T(8,128)S(1)} %pair.3.refs_0_), channel_id=1, source_target_pairs={{0,2},{1,3},{2,0},{3,1},{4,6},{5,7},{6,4},{7,5},{8,10},{9,11},{10,... | collective-permute-start | bytes 49160 | tf_op jit(solution)/shard_map/ppermute | solution.py:860
  18.5 2.5 %collective-permute-done.4.y_hi = f32[2,48,8,128]{3,2,1,0:T(8,128)S(1)} collective-permute-done((f32[2,48,8,128]{3,2,1,0:T(8,128)S(1)}, f32[2,48,8,128]{3,2,1,0:T(8,128)S(1)}, u32[]{:S(2)}, u32[]{:S(2)}) %collective-permute-start.4) | collective-permute-done | bytes 393248 | tf_op jit(solution)/shard_map/ppermute | solution.py:860
  21.0 1.5 %pack_z.1 = (f32[48,48,128]{2,1,0:T(8,128)S(1)}, f32[48,48,128]{2,1,0:T(8,128)S(1)}, f32[6,48,128]{2,1,0:T(8,128)S(1)}, f32[6,48,128]{2,1,0:T(8,128)S(1)}) custom-call(f32[48,32,128]{2,1,0:T(8,128)S(1)} %get-tuple-element.76.s_mid, f32[48,32,128]{2,1,0:T(8,128)S(1)} %get-tuple-element.77.b_mid, f32[2,48,8,128]{3,2,1,0:T(8,128)S(1)} %collective-permute-done.3.y_lo, ...), custom_call_target="tpu_custom_call" | custom-call | tf_op jit(solution)/shard_map/pack_z/pallas_call | solution.py:902
  22.5 1.4 %collective-permute-start.6 = (f32[6,48,128]{2,1,0:T(8,128)S(1)}, f32[6,48,128]{2,1,0:T(8,128)S(1)}, u32[]{:S(2)}, u32[]{:S(2)}) collective-permute-start(f32[6,48,128]{2,1,0:T(8,128)S(1)} %get-tuple-element.85), channel_id=1, source_target_pairs={{0,1},{1,2},{2,3},{3,0},{4,5},{5,6},{6,7},{7,4},{8,9},{9,10},{10,1... | collective-permute-start | bytes 442376 | tf_op jit(solution)/shard_map/ppermute | solution.py:860
  23.9 1.5 %collective-permute-start.7 = (f32[6,48,128]{2,1,0:T(8,128)S(1)}, f32[6,48,128]{2,1,0:T(8,128)S(1)}, u32[]{:S(2)}, u32[]{:S(2)}) collective-permute-start(f32[6,48,128]{2,1,0:T(8,128)S(1)} %get-tuple-element.86._), channel_id=1, source_target_pairs={{0,3},{1,0},{2,1},{3,2},{4,7},{5,4},{6,5},{7,6},{8,11},{9,8},{10,9... | collective-permute-start | bytes 442376 | tf_op jit(solution)/shard_map/ppermute | solution.py:860
  25.4 2.7 %collective-permute-start.8 = (f32[8,8,128]{2,1,0:T(8,128)S(1)}, f32[8,8,128]{2,1,0:T(8,128)S(1)}, u32[]{:S(2)}, u32[]{:S(2)}) collective-permute-start(f32[8,8,128]{2,1,0:T(8,128)S(1)} %gather_z.2.mine), channel_id=1, source_target_pairs={{0,32},{32,64},{64,96},{96,0},{1,33},{33,65},{65,97},{97,1},{2,34}... | collective-permute-start | bytes 98312 | tf_op jit(solution)/shard_map/ppermute | solution.py:860
  29.7 11.7 %level0_down.1 = (f32[50,64,128]{2,1,0:T(8,128)S(1)}, f32[6,64,128]{2,1,0:T(8,128)S(1)}, f32[16,16,128]{2,1,0:T(8,128)S(1)}, f32[10,16,128]{2,1,0:T(8,128)S(1)},...) custom-call(f32[48,48,128]{2,1,0:T(8,128)S(1)} %get-tuple-element.83, ...), custom_call_target="tpu_custom_call" | custom-call | tf_op jit(solution)/shard_map/level0_down/pallas_call | solution.py:908
  41.4 2.8 %collective-permute-start.9 = (f32[10,16,128]{2,1,0:T(8,128)S(1)}, f32[10,16,128]{2,1,0:T(8,128)S(1)}, u32[]{:S(2)}, u32[]{:S(2)}) collective-permute-start(f32[10,16,128]{2,1,0:T(8,128)S(1)} %get-tuple-element.91), channel_id=1, source_target_pairs={{0,32},{32,64},{64,96},{96,0},{1,33},{33,65},{65,97},{97,1},{2,34}... | collective-permute-start | bytes 245768 | tf_op jit(solution)/shard_map/ppermute | solution.py:860
  45.4 3.9 %collective-permute-done.11.refs_1_ = f32[2,8,8,128]{3,2,1,0:T(8,128)S(1)} collective-permute-done((f32[2,8,8,128]{3,2,1,0:T(8,128)S(1)}, f32[2,8,8,128]{3,2,1,0:T(8,128)S(1)}, u32[]{:S(2)}, u32[]{:S(2)}) %collective-permute-start.11) | collective-permute-done | bytes 65568 | tf_op jit(solution)/shard_map/ppermute | solution.py:860
  49.4 2.3 %collective-permute-start.12 = (f32[360,128]{1,0:T(8,128)S(1)}, f32[360,128]{1,0:T(8,128)S(1)}, u32[]{:S(2)}, u32[]{:S(2)}) collective-permute-start(f32[360,128]{1,0:T(8,128)S(1)} %get-tuple-element.97), channel_id=1, source_target_pairs={{0,4},{4,8},{8,12},{12,16},{16,20},{20,24},{24,28},{28,0},{1,5},{5... | collective-permute-start | bytes 552968 | tf_op jit(solution)/shard_map/ppermute | solution.py:860
  51.7 1.6 %collective-permute-start.14 = (f32[32,8,128]{2,1,0:T(8,128)S(1)}, f32[32,8,128]{2,1,0:T(8,128)S(1)}, u32[]{:S(2)}, u32[]{:S(2)}) collective-permute-start(f32[32,8,128]{2,1,0:T(8,128)S(1)} %gather_x.2.mine), channel_id=1, source_target_pairs={{0,8},{4,12},{8,16},{12,20},{16,24},{20,28},{24,0},{28,4},{1,9},{5... | collective-permute-start | bytes 393224 | tf_op jit(solution)/shard_map/ppermute | solution.py:860
  53.3 4.9 %collective-permute-done.14.other = f32[32,8,128]{2,1,0:T(8,128)S(1)} collective-permute-done((f32[32,8,128]{2,1,0:T(8,128)S(1)}, f32[32,8,128]{2,1,0:T(8,128)S(1)}, u32[]{:S(2)}, u32[]{:S(2)}) %collective-permute-start.14) | collective-permute-done | bytes 131104 | tf_op jit(solution)/shard_map/ppermute | solution.py:860
  59.1 2.5 %collective-permute-start.17 = (f32[2,32,8,128]{3,2,1,0:T(8,128)S(1)}, f32[2,32,8,128]{3,2,1,0:T(8,128)S(1)}, u32[]{:S(2)}, u32[]{:S(2)}) collective-permute-start(f32[2,32,8,128]{3,2,1,0:T(8,128)S(1)} %pair.5.refs_0_), channel_id=1, source_target_pairs={{0,16},{4,20},{8,24},{12,28},{16,0},{20,4},{24,8},{28,12},{1,17},{... | collective-permute-start | bytes 786440 | tf_op jit(solution)/shard_map/ppermute | solution.py:860
  62.6 1.7 %collective-permute-start.16 = (f32[6,40,128]{2,1,0:T(8,128)S(1)}, f32[6,40,128]{2,1,0:T(8,128)S(1)}, u32[]{:S(2)}, u32[]{:S(2)}) collective-permute-start(f32[6,40,128]{2,1,0:T(8,128)S(1)} %get-tuple-element.104.refs_2_), channel_id=1, source_target_pairs={{0,3},{1,0},{2,1},{3,2},{4,7},{5,4},{6,5},{7,6},{8,11},{9,8},{10,9... | collective-permute-start | bytes 368648 | tf_op jit(solution)/shard_map/ppermute | solution.py:860
  64.3 2.1 %collective-permute-done.17.refs_1_ = f32[2,32,8,128]{3,2,1,0:T(8,128)S(1)} collective-permute-done((f32[2,32,8,128]{3,2,1,0:T(8,128)S(1)}, f32[2,32,8,128]{3,2,1,0:T(8,128)S(1)}, u32[]{:S(2)}, u32[]{:S(2)}) %collective-permute-start.17) | collective-permute-done | bytes 262176 | tf_op jit(solution)/shard_map/ppermute | solution.py:860
  66.9 4.1 %level1_down.1 = (f32[38,56,128]{2,1,0:T(8,128)S(1)}, f32[16,128]{1,0:T(8,128)S(1)}, f32[6,36,40,128]{3,2,1,0:T(8,128)S(1)}, f32[36,40,128]{2,1,0:T(8,128)S(1)}, f32[36,40,128]{2,1,0:T(8,128)S(1)}) custom-call(f32[36,40,128]{2,1,0:T(8,128)S(1)} %get-tuple-element.102.ext, f32[6,40,128]{2,1,0:T(8,128)S(1)} %collective-permute-done.15.z_lo, ...), custom_call_target="tpu_custom_call" | custom-call | tf_op jit(solution)/shard_map/level1_down/pallas_call | solution.py:942
  71.0 2.7 %collective-permute-start.21 = (f32[4,32,8,128]{3,2,1,0:T(8,128)S(1)}, f32[4,32,8,128]{3,2,1,0:T(8,128)S(1)}, u32[]{:S(2)}, u32[]{:S(2)}) collective-permute-start(f32[4,32,8,128]{3,2,1,0:T(8,128)S(1)} %stack_y.2.same), channel_id=1, source_target_pairs={{0,4},{4,0},{8,12},{12,8},{16,20},{20,16},{24,28},{28,24},{1,5},{5... | collective-permute-start | bytes 1572872 | tf_op jit(solution)/shard_map/ppermute | solution.py:881
  74.7 2.6 %collective-permute-start.19 = (f32[16,128]{1,0:T(8,128)S(1)}, f32[16,128]{1,0:T(8,128)S(1)}, u32[]{:S(2)}, u32[]{:S(2)}) collective-permute-start(f32[16,128]{1,0:T(8,128)S(1)} %get-tuple-element.112.refs_0_.refs_4_), channel_id=1, source_target_pairs={{0,2},{1,3},{2,0},{3,1},{4,6},{5,7},{6,4},{7,5},{8,10},{9,11},{10,... | collective-permute-start | bytes 24584 | tf_op jit(solution)/shard_map/ppermute | solution.py:860
  79.9 1.6 %collective-permute-start.22 = (f32[8,8,128]{2,1,0:T(8,128)S(1)}, f32[8,8,128]{2,1,0:T(8,128)S(1)}, u32[]{:S(2)}, u32[]{:S(2)}) collective-permute-start(f32[8,8,128]{2,1,0:T(8,128)S(1)} %gather_z.3.refs_0_), channel_id=1, source_target_pairs={{0,32},{32,64},{64,96},{96,0},{1,33},{33,65},{65,97},{97,1},{2,34}... | collective-permute-start | bytes 98312 | tf_op jit(solution)/shard_map/ppermute | solution.py:860
  82.8 3.1 %collective-permute-done.23.refs_2_ = f32[8,8,128]{2,1,0:T(8,128)S(1)} collective-permute-done((f32[8,8,128]{2,1,0:T(8,128)S(1)}, f32[8,8,128]{2,1,0:T(8,128)S(1)}, u32[]{:S(2)}, u32[]{:S(2)}) %collective-permute-start.23) | collective-permute-done | bytes 32800 | tf_op jit(solution)/shard_map/ppermute | solution.py:860
  86.9 2.5 %collective-permute-start.26 = (f32[32,8,128]{2,1,0:T(8,128)S(1)}, f32[32,8,128]{2,1,0:T(8,128)S(1)}, u32[]{:S(2)}, u32[]{:S(2)}) collective-permute-start(f32[32,8,128]{2,1,0:T(8,128)S(1)} %gather_x.3.refs_0_.refs_4_), channel_id=1, source_target_pairs={{0,16},{4,20},{8,24},{12,28},{16,0},{20,4},{24,8},{28,12},{1,17},{... | collective-permute-start | bytes 393224 | tf_op jit(solution)/shard_map/ppermute | solution.py:860
  89.4 1.3 %collective-permute-start.27 = (f32[32,8,128]{2,1,0:T(8,128)S(1)}, f32[32,8,128]{2,1,0:T(8,128)S(1)}, u32[]{:S(2)}, u32[]{:S(2)}) collective-permute-start(f32[32,8,128]{2,1,0:T(8,128)S(1)} %gather_x.3.refs_0_.refs_4_), channel_id=1, source_target_pairs={{0,24},{4,28},{8,0},{12,4},{16,8},{20,12},{24,16},{28,20},{1,25},{... | collective-permute-start | bytes 393224 | tf_op jit(solution)/shard_map/ppermute | solution.py:860
  91.3 1.8 %collective-permute-done.26.refs_2_ = f32[32,8,128]{2,1,0:T(8,128)S(1)} collective-permute-done((f32[32,8,128]{2,1,0:T(8,128)S(1)}, f32[32,8,128]{2,1,0:T(8,128)S(1)}, u32[]{:S(2)}, u32[]{:S(2)}) %collective-permute-start.26) | collective-permute-done | bytes 131104 | tf_op jit(solution)/shard_map/ppermute | solution.py:860
  93.3 5.2 %collective-permute-start.28 = (f32[4,32,8,128]{3,2,1,0:T(8,128)S(1)}, f32[4,32,8,128]{3,2,1,0:T(8,128)S(1)}, u32[]{:S(2)}, u32[]{:S(2)}) collective-permute-start(f32[4,32,8,128]{3,2,1,0:T(8,128)S(1)} %stack_y.3.same), channel_id=1, source_target_pairs={{0,4},{4,0},{8,12},{12,8},{16,20},{20,16},{24,28},{28,24},{1,5},{5... | collective-permute-start | bytes 1572872 | tf_op jit(solution)/shard_map/ppermute | solution.py:881
  98.5 3.5 %coarse_prepare.1 = (f32[6,32,64,128]{3,2,1,0:T(8,128)S(1)}, f32[32,64,128]{2,1,0:T(8,128)S(1)}, f32[32,64,128]{2,1,0:T(8,128)S(1)}, f32[6,16,32,128]{3,2,1,0:T(...) custom-call(f32[4,32,8,128]{3,2,1,0:T(8,128)S(1)} %stack_y.2.same, ...), custom_call_target="tpu_custom_call" | custom-call | tf_op jit(solution)/shard_map/coarse_prepare/pallas_call | solution.py:956
  102.1 9.3 %bottom.1.c2 = f32[18,24,128]{2,1,0:T(8,128)S(1)} custom-call(f32[4,32,8,128]{3,2,1,0:T(8,128)S(1)} %stack_y.3.same, f32[4,32,8,128]{3,2,1,0:T(8,128)S(1)} %collective-permute-done.28.sibling, f32[6,32,64,128]{3,2,1,0:T(8,128)S(1)} %get-tuple-element.117.g, f32[32,64,128]{2,1,0:T(8,128)S(1)} %get-tuple-element.118.inv, ...), custom_call_target="tpu_custom_call" | custom-call | tf_op jit(solution)/shard_map/bottom/pallas_call | solution.py:963
  111.3 3.7 %level1_up.1.c1 = f32[24,24,128]{2,1,0:T(8,128)S(1)} custom-call(f32[18,24,128]{2,1,0:T(8,128)S(1)} %bottom.1.c2, f32[6,36,40,128]{3,2,1,0:T(8,128)S(1)} %get-tuple-element.124.g, f32[36,40,128]{2,1,0:T(8,128)S(1)} %get-tuple-element.125.sp, f32[36,40,128]{2,1,0:T(8,128)S(1)} %get-tuple-element.126.beta, f32[38,56,128]{2,1,0:T(8,128)S(1)} %get-tuple-element.127.iterate), custom_call_target="tpu_custom_call" | custom-call | tf_op jit(solution)/shard_map/level1_up/pallas_call | solution.py:966
  115.0 9.8 %level0_up.1 = f32[32,32,128]{2,1,0:T(8,128)} custom-call(f32[24,24,128]{2,1,0:T(8,128)S(1)} %level1_up.1.c1, f32[48,48,128]{2,1,0:T(8,128)S(1)} %get-tuple-element.84.beta, f32[7,48,48,128]{3,2,1,0:T(8,128)S(1)} %get-tuple-element.128.g_main, f32[6,6,48,128]{3,2,1,0:T(8,128)S(1)} %get-tuple-element.129.g_strip, f32[48,48,128]{2,1,0:T(8,128)S(1)} %get-tuple-element.130.sp, ...), custom_call_target="tpu_custom_call" | custom-call | tf_op jit(solution)/shard_map/level0_up/pallas_call | solution.py:973
  (53 shorter events, 18.0 us)
Async XLA Ops:
  0.0 10.6 %copy-start.1 = (f32[32,32,128]{2,1,0:T(8,128)S(1)}, f32[32,32,128]{2,1,0:T(8,128)}, u32[]{:S(2)}) copy-start(f32[32,32,128]{2,1,0:T(8,128)} %src) | copy-start | bytes 1572868
  0.0 4.9 %copy-start = (f32[32,32,128]{2,1,0:T(8,128)S(1)}, f32[32,32,128]{2,1,0:T(8,128)}, u32[]{:S(2)}) copy-start(f32[32,32,128]{2,1,0:T(8,128)} %beta.1) | copy-start | bytes 1572868
  2.1 8.5 %collective-permute-start.1 = (f32[2,8,32,128]{3,2,1,0:T(8,128)S(1)}, f32[2,8,32,128]{3,2,1,0:T(8,128)S(1)}, u32[]{:S(2)}, u32[]{:S(2)}) collective-permute-start(f32[2,8,32,128]{3,2,1,0:T(8,128)S(1)} %get-tuple-element.73._), channel_id=1, source_target_pairs={{0,96},{32,0},{64,32},{96,64},{1,97},{33,1},{65,33},{97,65},{2,98}... | collective-permute-start | bytes 786440 | tf_op jit(solution)/shard_map/ppermute | solution.py:860
  2.7 7.8 %collective-permute-start = (f32[2,8,32,128]{3,2,1,0:T(8,128)S(1)}, f32[2,8,32,128]{3,2,1,0:T(8,128)S(1)}, u32[]{:S(2)}, u32[]{:S(2)}) collective-permute-start(f32[2,8,32,128]{3,2,1,0:T(8,128)S(1)} %get-tuple-element.72), channel_id=1, source_target_pairs={{0,32},{32,64},{64,96},{96,0},{1,33},{33,65},{65,97},{97,1},{2,34}... | collective-permute-start | bytes 786440 | tf_op jit(solution)/shard_map/ppermute | solution.py:860
  5.4 4.1 %collective-permute-start.2 = (f32[16,128]{1,0:T(8,128)S(1)}, f32[16,128]{1,0:T(8,128)S(1)}, u32[]{:S(2)}, u32[]{:S(2)}) collective-permute-start(f32[16,128]{1,0:T(8,128)S(1)} %coarse_beta.1.mine), channel_id=1, source_target_pairs={{0,1},{1,2},{2,3},{3,0},{4,5},{5,6},{6,7},{7,4},{8,9},{9,10},{10,1... | collective-permute-start | bytes 24584 | tf_op jit(solution)/shard_map/ppermute | solution.py:860
  10.7 7.8 %collective-permute-start.3 = (f32[2,48,8,128]{3,2,1,0:T(8,128)S(1)}, f32[2,48,8,128]{3,2,1,0:T(8,128)S(1)}, u32[]{:S(2)}, u32[]{:S(2)}) collective-permute-start(f32[2,48,8,128]{3,2,1,0:T(8,128)S(1)} %get-tuple-element.78), channel_id=1, source_target_pairs={{0,4},{4,8},{8,12},{12,16},{16,20},{20,24},{24,28},{28,0},{1,5},{5... | collective-permute-start | bytes 1179656 | tf_op jit(solution)/shard_map/ppermute | solution.py:860
  13.8 7.2 %collective-permute-start.4 = (f32[2,48,8,128]{3,2,1,0:T(8,128)S(1)}, f32[2,48,8,128]{3,2,1,0:T(8,128)S(1)}, u32[]{:S(2)}, u32[]{:S(2)}) collective-permute-start(f32[2,48,8,128]{3,2,1,0:T(8,128)S(1)} %get-tuple-element.79.refs_2_), channel_id=1, source_target_pairs={{0,28},{4,0},{8,4},{12,8},{16,12},{20,16},{24,20},{28,24},{1,29},{... | collective-permute-start | bytes 1179656 | tf_op jit(solution)/shard_map/ppermute | solution.py:860
  13.8 4.1 %collective-permute-start.5 = (f32[2,16,128]{2,1,0:T(8,128)S(1)}, f32[2,16,128]{2,1,0:T(8,128)S(1)}, u32[]{:S(2)}, u32[]{:S(2)}) collective-permute-start(f32[2,16,128]{2,1,0:T(8,128)S(1)} %pair.3.refs_0_), channel_id=1, source_target_pairs={{0,2},{1,3},{2,0},{3,1},{4,6},{5,7},{6,4},{7,5},{8,10},{9,11},{10,... | collective-permute-start | bytes 49160 | tf_op jit(solution)/shard_map/ppermute | solution.py:860
  22.5 7.1 %collective-permute-start.6 = (f32[6,48,128]{2,1,0:T(8,128)S(1)}, f32[6,48,128]{2,1,0:T(8,128)S(1)}, u32[]{:S(2)}, u32[]{:S(2)}) collective-permute-start(f32[6,48,128]{2,1,0:T(8,128)S(1)} %get-tuple-element.85), channel_id=1, source_target_pairs={{0,1},{1,2},{2,3},{3,0},{4,5},{5,6},{6,7},{7,4},{8,9},{9,10},{10,1... | collective-permute-start | bytes 442376 | tf_op jit(solution)/shard_map/ppermute | solution.py:860
  23.9 5.8 %collective-permute-start.7 = (f32[6,48,128]{2,1,0:T(8,128)S(1)}, f32[6,48,128]{2,1,0:T(8,128)S(1)}, u32[]{:S(2)}, u32[]{:S(2)}) collective-permute-start(f32[6,48,128]{2,1,0:T(8,128)S(1)} %get-tuple-element.86._), channel_id=1, source_target_pairs={{0,3},{1,0},{2,1},{3,2},{4,7},{5,4},{6,5},{7,6},{8,11},{9,8},{10,9... | collective-permute-start | bytes 442376 | tf_op jit(solution)/shard_map/ppermute | solution.py:860
  25.4 3.7 %collective-permute-start.8 = (f32[8,8,128]{2,1,0:T(8,128)S(1)}, f32[8,8,128]{2,1,0:T(8,128)S(1)}, u32[]{:S(2)}, u32[]{:S(2)}) collective-permute-start(f32[8,8,128]{2,1,0:T(8,128)S(1)} %gather_z.2.mine), channel_id=1, source_target_pairs={{0,32},{32,64},{64,96},{96,0},{1,33},{33,65},{65,97},{97,1},{2,34}... | collective-permute-start | bytes 98312 | tf_op jit(solution)/shard_map/ppermute | solution.py:860
  41.3 8.0 %collective-permute-start.10 = (f32[10,16,128]{2,1,0:T(8,128)S(1)}, f32[10,16,128]{2,1,0:T(8,128)S(1)}, u32[]{:S(2)}, u32[]{:S(2)}) collective-permute-start(f32[10,16,128]{2,1,0:T(8,128)S(1)} %get-tuple-element.92.refs_2_), channel_id=1, source_target_pairs={{0,96},{32,0},{64,32},{96,64},{1,97},{33,1},{65,33},{97,65},{2,98}... | collective-permute-start | bytes 245768 | tf_op jit(solution)/shard_map/ppermute | solution.py:860
  41.4 7.9 %collective-permute-start.9 = (f32[10,16,128]{2,1,0:T(8,128)S(1)}, f32[10,16,128]{2,1,0:T(8,128)S(1)}, u32[]{:S(2)}, u32[]{:S(2)}) collective-permute-start(f32[10,16,128]{2,1,0:T(8,128)S(1)} %get-tuple-element.91), channel_id=1, source_target_pairs={{0,32},{32,64},{64,96},{96,0},{1,33},{33,65},{65,97},{97,1},{2,34}... | collective-permute-start | bytes 245768 | tf_op jit(solution)/shard_map/ppermute | solution.py:860
  44.3 5.0 %collective-permute-start.11 = (f32[2,8,8,128]{3,2,1,0:T(8,128)S(1)}, f32[2,8,8,128]{3,2,1,0:T(8,128)S(1)}, u32[]{:S(2)}, u32[]{:S(2)}) collective-permute-start(f32[2,8,8,128]{3,2,1,0:T(8,128)S(1)} %pair.4.refs_0_), channel_id=1, source_target_pairs={{0,64},{32,96},{64,0},{96,32},{1,65},{33,97},{65,1},{97,33},{2,66}... | collective-permute-start | bytes 196616 | tf_op jit(solution)/shard_map/ppermute | solution.py:860
  49.4 8.9 %collective-permute-start.12 = (f32[360,128]{1,0:T(8,128)S(1)}, f32[360,128]{1,0:T(8,128)S(1)}, u32[]{:S(2)}, u32[]{:S(2)}) collective-permute-start(f32[360,128]{1,0:T(8,128)S(1)} %get-tuple-element.97), channel_id=1, source_target_pairs={{0,4},{4,8},{8,12},{12,16},{16,20},{20,24},{24,28},{28,0},{1,5},{5... | collective-permute-start | bytes 552968 | tf_op jit(solution)/shard_map/ppermute | solution.py:860
  51.7 6.6 %collective-permute-start.13 = (f32[360,128]{1,0:T(8,128)S(1)}, f32[360,128]{1,0:T(8,128)S(1)}, u32[]{:S(2)}, u32[]{:S(2)}) collective-permute-start(f32[360,128]{1,0:T(8,128)S(1)} %get-tuple-element.98._), channel_id=1, source_target_pairs={{0,28},{4,0},{8,4},{12,8},{16,12},{20,16},{24,20},{28,24},{1,29},{... | collective-permute-start | bytes 552968 | tf_op jit(solution)/shard_map/ppermute | solution.py:860
  51.7 6.6 %collective-permute-start.14 = (f32[32,8,128]{2,1,0:T(8,128)S(1)}, f32[32,8,128]{2,1,0:T(8,128)S(1)}, u32[]{:S(2)}, u32[]{:S(2)}) collective-permute-start(f32[32,8,128]{2,1,0:T(8,128)S(1)} %gather_x.2.mine), channel_id=1, source_target_pairs={{0,8},{4,12},{8,16},{12,20},{16,24},{20,28},{24,0},{28,4},{1,9},{5... | collective-permute-start | bytes 393224 | tf_op jit(solution)/shard_map/ppermute | solution.py:860
  59.1 7.4 %collective-permute-start.17 = (f32[2,32,8,128]{3,2,1,0:T(8,128)S(1)}, f32[2,32,8,128]{3,2,1,0:T(8,128)S(1)}, u32[]{:S(2)}, u32[]{:S(2)}) collective-permute-start(f32[2,32,8,128]{3,2,1,0:T(8,128)S(1)} %pair.5.refs_0_), channel_id=1, source_target_pairs={{0,16},{4,20},{8,24},{12,28},{16,0},{20,4},{24,8},{28,12},{1,17},{... | collective-permute-start | bytes 786440 | tf_op jit(solution)/shard_map/ppermute | solution.py:860
  61.6 5.2 %collective-permute-start.15 = (f32[6,40,128]{2,1,0:T(8,128)S(1)}, f32[6,40,128]{2,1,0:T(8,128)S(1)}, u32[]{:S(2)}, u32[]{:S(2)}) collective-permute-start(f32[6,40,128]{2,1,0:T(8,128)S(1)} %get-tuple-element.103), channel_id=1, source_target_pairs={{0,1},{1,2},{2,3},{3,0},{4,5},{5,6},{6,7},{7,4},{8,9},{9,10},{10,1... | collective-permute-start | bytes 368648 | tf_op jit(solution)/shard_map/ppermute | solution.py:860
  62.6 4.3 %collective-permute-start.16 = (f32[6,40,128]{2,1,0:T(8,128)S(1)}, f32[6,40,128]{2,1,0:T(8,128)S(1)}, u32[]{:S(2)}, u32[]{:S(2)}) collective-permute-start(f32[6,40,128]{2,1,0:T(8,128)S(1)} %get-tuple-element.104.refs_2_), channel_id=1, source_target_pairs={{0,3},{1,0},{2,1},{3,2},{4,7},{5,4},{6,5},{7,6},{8,11},{9,8},{10,9... | collective-permute-start | bytes 368648 | tf_op jit(solution)/shard_map/ppermute | solution.py:860
  71.0 8.8 %collective-permute-start.21 = (f32[4,32,8,128]{3,2,1,0:T(8,128)S(1)}, f32[4,32,8,128]{3,2,1,0:T(8,128)S(1)}, u32[]{:S(2)}, u32[]{:S(2)}) collective-permute-start(f32[4,32,8,128]{3,2,1,0:T(8,128)S(1)} %stack_y.2.same), channel_id=1, source_target_pairs={{0,4},{4,0},{8,12},{12,8},{16,20},{20,16},{24,28},{28,24},{1,5},{5... | collective-permute-start | bytes 1572872 | tf_op jit(solution)/shard_map/ppermute | solution.py:881
  73.7 4.4 %collective-permute-start.18 = (f32[16,128]{1,0:T(8,128)S(1)}, f32[16,128]{1,0:T(8,128)S(1)}, u32[]{:S(2)}, u32[]{:S(2)}) collective-permute-start(f32[16,128]{1,0:T(8,128)S(1)} %get-tuple-element.112.refs_0_.refs_4_), channel_id=1, source_target_pairs={{0,1},{1,2},{2,3},{3,0},{4,5},{5,6},{6,7},{7,4},{8,9},{9,10},{10,1... | collective-permute-start | bytes 24584 | tf_op jit(solution)/shard_map/ppermute | solution.py:860
  74.7 4.0 %collective-permute-start.19 = (f32[16,128]{1,0:T(8,128)S(1)}, f32[16,128]{1,0:T(8,128)S(1)}, u32[]{:S(2)}, u32[]{:S(2)}) collective-permute-start(f32[16,128]{1,0:T(8,128)S(1)} %get-tuple-element.112.refs_0_.refs_4_), channel_id=1, source_target_pairs={{0,2},{1,3},{2,0},{3,1},{4,6},{5,7},{6,4},{7,5},{8,10},{9,11},{10,... | collective-permute-start | bytes 24584 | tf_op jit(solution)/shard_map/ppermute | solution.py:860
  77.3 2.5 %collective-permute-start.20 = (f32[16,128]{1,0:T(8,128)S(1)}, f32[16,128]{1,0:T(8,128)S(1)}, u32[]{:S(2)}, u32[]{:S(2)}) collective-permute-start(f32[16,128]{1,0:T(8,128)S(1)} %get-tuple-element.112.refs_0_.refs_4_), channel_id=1, source_target_pairs={{0,3},{1,0},{2,1},{3,2},{4,7},{5,4},{6,5},{7,6},{8,11},{9,8},{10,9... | collective-permute-start | bytes 24584 | tf_op jit(solution)/shard_map/ppermute | solution.py:860
  79.9 2.8 %collective-permute-start.22 = (f32[8,8,128]{2,1,0:T(8,128)S(1)}, f32[8,8,128]{2,1,0:T(8,128)S(1)}, u32[]{:S(2)}, u32[]{:S(2)}) collective-permute-start(f32[8,8,128]{2,1,0:T(8,128)S(1)} %gather_z.3.refs_0_), channel_id=1, source_target_pairs={{0,32},{32,64},{64,96},{96,0},{1,33},{33,65},{65,97},{97,1},{2,34}... | collective-permute-start | bytes 98312 | tf_op jit(solution)/shard_map/ppermute | solution.py:860
  81.6 4.3 %collective-permute-start.23 = (f32[8,8,128]{2,1,0:T(8,128)S(1)}, f32[8,8,128]{2,1,0:T(8,128)S(1)}, u32[]{:S(2)}, u32[]{:S(2)}) collective-permute-start(f32[8,8,128]{2,1,0:T(8,128)S(1)} %gather_z.3.refs_0_), channel_id=1, source_target_pairs={{0,64},{32,96},{64,0},{96,32},{1,65},{33,97},{65,1},{97,33},{2,66}... | collective-permute-start | bytes 98312 | tf_op jit(solution)/shard_map/ppermute | solution.py:860
  82.1 4.1 %collective-permute-start.24 = (f32[8,8,128]{2,1,0:T(8,128)S(1)}, f32[8,8,128]{2,1,0:T(8,128)S(1)}, u32[]{:S(2)}, u32[]{:S(2)}) collective-permute-start(f32[8,8,128]{2,1,0:T(8,128)S(1)} %gather_z.3.refs_0_), channel_id=1, source_target_pairs={{0,96},{32,0},{64,32},{96,64},{1,97},{33,1},{65,33},{97,65},{2,98}... | collective-permute-start | bytes 98312 | tf_op jit(solution)/shard_map/ppermute | solution.py:860
  86.2 5.1 %collective-permute-start.25 = (f32[32,8,128]{2,1,0:T(8,128)S(1)}, f32[32,8,128]{2,1,0:T(8,128)S(1)}, u32[]{:S(2)}, u32[]{:S(2)}) collective-permute-start(f32[32,8,128]{2,1,0:T(8,128)S(1)} %gather_x.3.refs_0_.refs_4_), channel_id=1, source_target_pairs={{0,8},{4,12},{8,16},{12,20},{16,24},{20,28},{24,0},{28,4},{1,9},{5... | collective-permute-start | bytes 393224 | tf_op jit(solution)/shard_map/ppermute | solution.py:860
  86.9 6.2 %collective-permute-start.26 = (f32[32,8,128]{2,1,0:T(8,128)S(1)}, f32[32,8,128]{2,1,0:T(8,128)S(1)}, u32[]{:S(2)}, u32[]{:S(2)}) collective-permute-start(f32[32,8,128]{2,1,0:T(8,128)S(1)} %gather_x.3.refs_0_.refs_4_), channel_id=1, source_target_pairs={{0,16},{4,20},{8,24},{12,28},{16,0},{20,4},{24,8},{28,12},{1,17},{... | collective-permute-start | bytes 393224 | tf_op jit(solution)/shard_map/ppermute | solution.py:860
  89.4 3.9 %collective-permute-start.27 = (f32[32,8,128]{2,1,0:T(8,128)S(1)}, f32[32,8,128]{2,1,0:T(8,128)S(1)}, u32[]{:S(2)}, u32[]{:S(2)}) collective-permute-start(f32[32,8,128]{2,1,0:T(8,128)S(1)} %gather_x.3.refs_0_.refs_4_), channel_id=1, source_target_pairs={{0,24},{4,28},{8,0},{12,4},{16,8},{20,12},{24,16},{28,20},{1,25},{... | collective-permute-start | bytes 393224 | tf_op jit(solution)/shard_map/ppermute | solution.py:860
  93.3 8.7 %collective-permute-start.28 = (f32[4,32,8,128]{3,2,1,0:T(8,128)S(1)}, f32[4,32,8,128]{3,2,1,0:T(8,128)S(1)}, u32[]{:S(2)}, u32[]{:S(2)}) collective-permute-start(f32[4,32,8,128]{3,2,1,0:T(8,128)S(1)} %stack_y.3.same), channel_id=1, source_target_pairs={{0,4},{4,0},{8,12},{12,8},{16,20},{20,16},{24,28},{28,24},{1,5},{5... | collective-permute-start | bytes 1572872 | tf_op jit(solution)/shard_map/ppermute | solution.py:881

commit v10 on v9

--- a/solution.py
+++ b/solution.py
@@ -925,19 +925,18 @@
     )(src_ext, beta_ext, z_lo, z_hi)
     x_lo, x_hi = trade(lo, hi, "gx")
     beta2_pair, _ = lax.optimization_barrier((beta2_pair, lo))
-    beta2_slab = gather(gather_x, [beta2_pair, ring(beta2_pair, "gx", 2)], lo, 32, 8, 128)
-    x_lo, x_hi, beta2_slab = lax.optimization_barrier((x_lo, x_hi, beta2_slab))
+    beta2_far = ring(beta2_pair, "gx", 2)
     lo, hi = call(pack1_y, (sds(360, 128), sds(360, 128)), name="pack1_y")(c, x_lo, x_hi)
     y_lo, y_hi = trade(lo, hi, "gy")
-    beta2_pair = gather(pair, [beta2_slab, ring(beta2_slab, "gy", 2)], lo, 2, 32, 8, 128)
-    y_lo, y_hi, beta2_pair = lax.optimization_barrier((y_lo, y_hi, beta2_pair))
+    beta2_slab = gather(gather_x, [beta2_pair, beta2_far], lo, 32, 8, 128)
+    y_lo, y_hi, beta2_slab = lax.optimization_barrier((y_lo, y_hi, beta2_slab))
     ext, lo, hi = call(
         pack1_z, (sds(36, 40, 128), sds(6, 40, 128), sds(6, 40, 128)), name="pack1_z"
     )(c, x_lo, x_hi, y_lo, y_hi)
     z1_lo, z1_hi = trade(lo, hi, "gz")
-    beta2_pair, _ = lax.optimization_barrier((beta2_pair, lo))
-    beta2_stack = gather(stack_y, [beta2_pair, ring(beta2_pair, "gy", 4)], lo, 4, 32, 8, 128)
-    z1_lo, z1_hi, beta2_stack = lax.optimization_barrier((z1_lo, z1_hi, beta2_stack))
+    beta2_slab, _ = lax.optimization_barrier((beta2_slab, lo))
+    beta2_pair = gather(pair, [beta2_slab, ring(beta2_slab, "gy", 2)], lo, 2, 32, 8, 128)
+    z1_lo, z1_hi, beta2_pair = lax.optimization_barrier((z1_lo, z1_hi, beta2_pair))
     level1 = sds(36, 40, 128)
     iter1, chunk, g1, sp1, beta1 = call(
         level1_down,
@@ -947,11 +946,16 @@
         mib=8,
     )(ext, z1_lo, z1_hi)
     parts = around(chunk, "gz")
-    beta2_stack, _ = lax.optimization_barrier((beta2_stack, chunk))
-    *parts, beta2_other = lax.optimization_barrier((*parts, across(beta2_stack)))
+    beta2_pair, _ = lax.optimization_barrier((beta2_pair, chunk))
+    beta2_far = ring(beta2_pair, "gy", 4)
     parts = around(gather(gather_z, parts, chunk, 8, 8, 128), "gx")
+    beta2_stack = gather(stack_y, [beta2_pair, beta2_far], chunk, 4, 32, 8, 128)
+    *parts, beta2_stack = lax.optimization_barrier((*parts, beta2_stack))
     slab = gather(gather_x, parts, chunk, 32, 8, 128)
-    stack = gather(stack_y, chips(slab), slab, 4, 32, 8, 128)
+    parts = chips(slab)
+    beta2_sent, _ = lax.optimization_barrier((beta2_stack, slab))
+    *parts, beta2_other = lax.optimization_barrier((*parts, across(beta2_sent)))
+    stack = gather(stack_y, parts, slab, 4, 32, 8, 128)
     stack_other = across(stack)
     coarse = call(
         coarse_prepare,

time: 126 us -> 128 us (1.016)
  starting transfers between devices: 47.8 us -> 53.5 us
  waiting for transfers between devices: 29.2 us -> 25.6 us
    ppermute x27, starting transfers between devices: 40 us -> 47.8 us  [ring(): lax.ppermute(value, axis, [(i, (i + step) % count) for i in range(count)])]
    ppermute x27, waiting for transfers between devices: 29.2 us -> 25.6 us  [ring(): lax.ppermute(value, axis, [(i, (i + step) % count) for i in range(count)])]
    ppermute x2, starting transfers between devices: 7.84 us -> 5.77 us  [across(): lax.ppermute(value, 'gy', [(i, i + 1 - 2 * (i % 2)) for i in range(count)])]
  transfers between devices with their start and end apart: 29 -> 29, of which waited for: 19 -> 16; matrix products, arithmetic and copies ran while one was open for 0% -> 0% of each run, Pallas kernels for 3% -> 3%
where the time goes in v10:
time: 128 us; the launch traced here: 127 us
  starting transfers between devices  53.5 us (42%)
  Pallas kernels  45.5 us (36%)
  waiting for transfers between devices  25.6 us (20%)
  local copies, waits for them, and re-layouts  2.07 us (2%)
    ppermute x27, starting transfers between devices, ring(): lax.ppermute(value, axis, [(i, (i + step) % count) for i in range(count)])  47.8 us
    ppermute x27, waiting for transfers between devices, ring(): lax.ppermute(value, axis, [(i, (i + step) % count) for i in range(count)])  25.6 us
    pallas_call x1, Pallas kernels, per_device(): call(level0_down, (sds(50, 64, 128), sds(6, 64, 128), sds(16, 16, 128), s...  11.7 us
    pallas_call x1, Pallas kernels, per_device(): call(level0_up, sds(32, 32, 128), [vm(50, 64, 128), vm(50, 64, 128), vm(6...  9.82 us
    pallas_call x1, Pallas kernels, per_device(): call(bottom, sds(18, 24, 128), BOTTOM_SCRATCH, name='bottom', mib=18)  9.26 us
    ppermute x2, starting transfers between devices, across(): lax.ppermute(value, 'gy', [(i, i + 1 - 2 * (i % 2)) for i in range(count)])  5.77 us
    pallas_call x1, Pallas kernels, per_device(): call(level1_down, (sds(38, 56, 128), sds(16, 128), sds(6, 36, 40, 128), l...  4.15 us
    pallas_call x1, Pallas kernels, per_device(): call(level1_up, sds(24, 24, 128), [vm(38, 56, 128), vm(38, 56, 128), vm(3...  3.65 us
  transfers between devices with their start and end apart: 29, of which 16 were waited for; matrix products, arithmetic and copies ran while one was open for 0% of the time, Pallas kernels for 3%

profile of v10, /device:TPU:7, one launch (start us, length us, event | category | flops | bytes accessed | tf_op | source)
XLA Modules:
  0.0 127.0 jit_solution(13208169478386652711)
XLA Ops:
  2.7 2.1 %collective-permute-start = (f32[2,8,32,128]{3,2,1,0:T(8,128)S(1)}, f32[2,8,32,128]{3,2,1,0:T(8,128)S(1)}, u32[]{:S(2)}, u32[]{:S(2)}) collective-permute-start(f32[2,8,32,128]{3,2,1,0:T(8,128)S(1)} %get-tuple-element.75), channel_id=1, source_target_pairs={{0,32},{32,64},{64,96},{96,0},{1,33},{33,65},{65,97},{97,1},{2,34}... | collective-permute-start | bytes 786440 | tf_op jit(solution)/shard_map/ppermute | solution.py:860
  6.7 2.8 %collective-permute-done.2.other = f32[16,128]{1,0:T(8,128)S(1)} collective-permute-done((f32[16,128]{1,0:T(8,128)S(1)}, f32[16,128]{1,0:T(8,128)S(1)}, u32[]{:S(2)}, u32[]{:S(2)}) %collective-permute-start.2) | collective-permute-done | bytes 8224 | tf_op jit(solution)/shard_map/ppermute | solution.py:860
  10.7 1.6 %collective-permute-start.4 = (f32[2,48,8,128]{3,2,1,0:T(8,128)S(1)}, f32[2,48,8,128]{3,2,1,0:T(8,128)S(1)}, u32[]{:S(2)}, u32[]{:S(2)}) collective-permute-start(f32[2,48,8,128]{3,2,1,0:T(8,128)S(1)} %get-tuple-element.82.refs_2_), channel_id=1, source_target_pairs={{0,28},{4,0},{8,4},{12,8},{16,12},{20,16},{24,20},{28,24},{1,29},{... | collective-permute-start | bytes 1179656 | tf_op jit(solution)/shard_map/ppermute | solution.py:860
  12.3 1.5 %collective-permute-start.3 = (f32[2,48,8,128]{3,2,1,0:T(8,128)S(1)}, f32[2,48,8,128]{3,2,1,0:T(8,128)S(1)}, u32[]{:S(2)}, u32[]{:S(2)}) collective-permute-start(f32[2,48,8,128]{3,2,1,0:T(8,128)S(1)} %get-tuple-element.81), channel_id=1, source_target_pairs={{0,4},{4,8},{8,12},{12,16},{16,20},{20,24},{24,28},{28,0},{1,5},{5... | collective-permute-start | bytes 1179656 | tf_op jit(solution)/shard_map/ppermute | solution.py:860
  13.9 2.9 %collective-permute-start.5 = (f32[2,16,128]{2,1,0:T(8,128)S(1)}, f32[2,16,128]{2,1,0:T(8,128)S(1)}, u32[]{:S(2)}, u32[]{:S(2)}) collective-permute-start(f32[2,16,128]{2,1,0:T(8,128)S(1)} %pair.3.refs_0_), channel_id=1, source_target_pairs={{0,2},{1,3},{2,0},{3,1},{4,6},{5,7},{6,4},{7,5},{8,10},{9,11},{10,... | collective-permute-start | bytes 49160 | tf_op jit(solution)/shard_map/ppermute | solution.py:860
  18.1 1.5 %collective-permute-done.4.y_hi = f32[2,48,8,128]{3,2,1,0:T(8,128)S(1)} collective-permute-done((f32[2,48,8,128]{3,2,1,0:T(8,128)S(1)}, f32[2,48,8,128]{3,2,1,0:T(8,128)S(1)}, u32[]{:S(2)}, u32[]{:S(2)}) %collective-permute-start.4) | collective-permute-done | bytes 393248 | tf_op jit(solution)/shard_map/ppermute | solution.py:860
  19.6 1.5 %pack_z.1 = (f32[48,48,128]{2,1,0:T(8,128)S(1)}, f32[48,48,128]{2,1,0:T(8,128)S(1)}, f32[6,48,128]{2,1,0:T(8,128)S(1)}, f32[6,48,128]{2,1,0:T(8,128)S(1)}) custom-call(f32[48,32,128]{2,1,0:T(8,128)S(1)} %get-tuple-element.79.s_mid, f32[48,32,128]{2,1,0:T(8,128)S(1)} %get-tuple-element.80.b_mid, f32[2,48,8,128]{3,2,1,0:T(8,128)S(1)} %collective-permute-done.3.y_lo, ...), custom_call_target="tpu_custom_call" | custom-call | tf_op jit(solution)/shard_map/pack_z/pallas_call | solution.py:902
  22.5 1.5 %collective-permute-start.7 = (f32[6,48,128]{2,1,0:T(8,128)S(1)}, f32[6,48,128]{2,1,0:T(8,128)S(1)}, u32[]{:S(2)}, u32[]{:S(2)}) collective-permute-start(f32[6,48,128]{2,1,0:T(8,128)S(1)} %get-tuple-element.89._), channel_id=1, source_target_pairs={{0,3},{1,0},{2,1},{3,2},{4,7},{5,4},{6,5},{7,6},{8,11},{9,8},{10,9... | collective-permute-start | bytes 442376 | tf_op jit(solution)/shard_map/ppermute | solution.py:860
  24.0 2.7 %collective-permute-start.8 = (f32[8,8,128]{2,1,0:T(8,128)S(1)}, f32[8,8,128]{2,1,0:T(8,128)S(1)}, u32[]{:S(2)}, u32[]{:S(2)}) collective-permute-start(f32[8,8,128]{2,1,0:T(8,128)S(1)} %gather_z.2.mine), channel_id=1, source_target_pairs={{0,32},{32,64},{64,96},{96,0},{1,33},{33,65},{65,97},{97,1},{2,34}... | collective-permute-start | bytes 98312 | tf_op jit(solution)/shard_map/ppermute | solution.py:860
  27.7 11.7 %level0_down.1 = (f32[50,64,128]{2,1,0:T(8,128)S(1)}, f32[6,64,128]{2,1,0:T(8,128)S(1)}, f32[16,16,128]{2,1,0:T(8,128)S(1)}, f32[10,16,128]{2,1,0:T(8,128)S(1)},...) custom-call(f32[48,48,128]{2,1,0:T(8,128)S(1)} %get-tuple-element.86, ...), custom_call_target="tpu_custom_call" | custom-call | tf_op jit(solution)/shard_map/level0_down/pallas_call | solution.py:908
  39.5 3.0 %collective-permute-start.9 = (f32[10,16,128]{2,1,0:T(8,128)S(1)}, f32[10,16,128]{2,1,0:T(8,128)S(1)}, u32[]{:S(2)}, u32[]{:S(2)}) collective-permute-start(f32[10,16,128]{2,1,0:T(8,128)S(1)} %get-tuple-element.94), channel_id=1, source_target_pairs={{0,32},{32,64},{64,96},{96,0},{1,33},{33,65},{65,97},{97,1},{2,34}... | collective-permute-start | bytes 245768 | tf_op jit(solution)/shard_map/ppermute | solution.py:860
  42.5 1.7 %collective-permute-done.10.from_hi.x_hi = f32[10,16,128]{2,1,0:T(8,128)S(1)} collective-permute-done((f32[10,16,128]{2,1,0:T(8,128)S(1)}, f32[10,16,128]{2,1,0:T(8,128)S(1)}, u32[]{:S(2)}, u32[]{:S(2)}) %collective-permute-start.10) | collective-permute-done | bytes 81952 | tf_op jit(solution)/shard_map/ppermute | solution.py:860
  44.3 3.9 %collective-permute-start.11 = (f32[360,128]{1,0:T(8,128)S(1)}, f32[360,128]{1,0:T(8,128)S(1)}, u32[]{:S(2)}, u32[]{:S(2)}) collective-permute-start(f32[360,128]{1,0:T(8,128)S(1)} %get-tuple-element.96), channel_id=1, source_target_pairs={{0,4},{4,8},{8,12},{12,16},{16,20},{20,24},{24,28},{28,0},{1,5},{5... | collective-permute-start | bytes 552968 | tf_op jit(solution)/shard_map/ppermute | solution.py:860
  48.2 2.0 %collective-permute-start.12 = (f32[360,128]{1,0:T(8,128)S(1)}, f32[360,128]{1,0:T(8,128)S(1)}, u32[]{:S(2)}, u32[]{:S(2)}) collective-permute-start(f32[360,128]{1,0:T(8,128)S(1)} %get-tuple-element.97.refs_2_), channel_id=1, source_target_pairs={{0,28},{4,0},{8,4},{12,8},{16,12},{20,16},{24,20},{28,24},{1,29},{... | collective-permute-start | bytes 552968 | tf_op jit(solution)/shard_map/ppermute | solution.py:860
  50.2 3.2 %collective-permute-start.13 = (f32[2,8,8,128]{3,2,1,0:T(8,128)S(1)}, f32[2,8,8,128]{3,2,1,0:T(8,128)S(1)}, u32[]{:S(2)}, u32[]{:S(2)}) collective-permute-start(f32[2,8,8,128]{3,2,1,0:T(8,128)S(1)} %pair.4.refs_0_), channel_id=1, source_target_pairs={{0,64},{32,96},{64,0},{96,32},{1,65},{33,97},{65,1},{97,33},{2,66}... | collective-permute-start | bytes 196616 | tf_op jit(solution)/shard_map/ppermute | solution.py:860
  53.4 1.7 %collective-permute-done.13.refs_1_ = f32[2,8,8,128]{3,2,1,0:T(8,128)S(1)} collective-permute-done((f32[2,8,8,128]{3,2,1,0:T(8,128)S(1)}, f32[2,8,8,128]{3,2,1,0:T(8,128)S(1)}, u32[]{:S(2)}, u32[]{:S(2)}) %collective-permute-start.13) | collective-permute-done | bytes 65568 | tf_op jit(solution)/shard_map/ppermute | solution.py:860
  56.3 2.6 %collective-permute-start.15 = (f32[6,40,128]{2,1,0:T(8,128)S(1)}, f32[6,40,128]{2,1,0:T(8,128)S(1)}, u32[]{:S(2)}, u32[]{:S(2)}) collective-permute-start(f32[6,40,128]{2,1,0:T(8,128)S(1)} %get-tuple-element.104._), channel_id=1, source_target_pairs={{0,3},{1,0},{2,1},{3,2},{4,7},{5,4},{6,5},{7,6},{8,11},{9,8},{10,9... | collective-permute-start | bytes 368648 | tf_op jit(solution)/shard_map/ppermute | solution.py:860
  58.9 3.2 %collective-permute-done.16.other = f32[32,8,128]{2,1,0:T(8,128)S(1)} collective-permute-done((f32[32,8,128]{2,1,0:T(8,128)S(1)}, f32[32,8,128]{2,1,0:T(8,128)S(1)}, u32[]{:S(2)}, u32[]{:S(2)}) %collective-permute-start.16) | collective-permute-done | bytes 131104 | tf_op jit(solution)/shard_map/ppermute | solution.py:860
  62.2 4.2 %level1_down.1 = (f32[38,56,128]{2,1,0:T(8,128)S(1)}, f32[16,128]{1,0:T(8,128)S(1)}, f32[6,36,40,128]{3,2,1,0:T(8,128)S(1)}, f32[36,40,128]{2,1,0:T(8,128)S(1)}, f32[36,40,128]{2,1,0:T(8,128)S(1)}) custom-call(f32[36,40,128]{2,1,0:T(8,128)S(1)} %get-tuple-element.102.ext, f32[6,40,128]{2,1,0:T(8,128)S(1)} %collective-permute-done.14.z_lo, ...), custom_call_target="tpu_custom_call" | custom-call | tf_op jit(solution)/shard_map/level1_down/pallas_call | solution.py:941
  66.3 5.2 %collective-permute-start.23 = (f32[2,32,8,128]{3,2,1,0:T(8,128)S(1)}, f32[2,32,8,128]{3,2,1,0:T(8,128)S(1)}, u32[]{:S(2)}, u32[]{:S(2)}) collective-permute-start(f32[2,32,8,128]{3,2,1,0:T(8,128)S(1)} %pair.5.refs_0_), channel_id=1, source_target_pairs={{0,16},{4,20},{8,24},{12,28},{16,0},{20,4},{24,8},{28,12},{1,17},{... | collective-permute-start | bytes 786440 | tf_op jit(solution)/shard_map/ppermute | solution.py:860
  71.5 3.6 %collective-permute-start.18 = (f32[16,128]{1,0:T(8,128)S(1)}, f32[16,128]{1,0:T(8,128)S(1)}, u32[]{:S(2)}, u32[]{:S(2)}) collective-permute-start(f32[16,128]{1,0:T(8,128)S(1)} %get-tuple-element.109.refs_0_.refs_4_.refs_2_), channel_id=1, source_target_pairs={{0,2},{1,3},{2,0},{3,1},{4,6},{5,7},{6,4},{7,5},{8,10},{9,11},{10,... | collective-permute-start | bytes 24584 | tf_op jit(solution)/shard_map/ppermute | solution.py:860
  78.1 2.9 %collective-permute-start.20 = (f32[8,8,128]{2,1,0:T(8,128)S(1)}, f32[8,8,128]{2,1,0:T(8,128)S(1)}, u32[]{:S(2)}, u32[]{:S(2)}) collective-permute-start(f32[8,8,128]{2,1,0:T(8,128)S(1)} %gather_z.3.refs_0_), channel_id=1, source_target_pairs={{0,32},{32,64},{64,96},{96,0},{1,33},{33,65},{65,97},{97,1},{2,34}... | collective-permute-start | bytes 98312 | tf_op jit(solution)/shard_map/ppermute | solution.py:860
  82.0 3.3 %collective-permute-done.21.refs_2_ = f32[8,8,128]{2,1,0:T(8,128)S(1)} collective-permute-done((f32[8,8,128]{2,1,0:T(8,128)S(1)}, f32[8,8,128]{2,1,0:T(8,128)S(1)}, u32[]{:S(2)}, u32[]{:S(2)}) %collective-permute-start.21) | collective-permute-done | bytes 32800 | tf_op jit(solution)/shard_map/ppermute | solution.py:860
  85.5 4.3 %collective-permute-start.27 = (f32[4,32,8,128]{3,2,1,0:T(8,128)S(1)}, f32[4,32,8,128]{3,2,1,0:T(8,128)S(1)}, u32[]{:S(2)}, u32[]{:S(2)}) collective-permute-start(f32[4,32,8,128]{3,2,1,0:T(8,128)S(1)} %stack_y.2.same), channel_id=1, source_target_pairs={{0,4},{4,0},{8,12},{12,8},{16,20},{20,16},{24,28},{28,24},{1,5},{5... | collective-permute-start | bytes 1572872 | tf_op jit(solution)/shard_map/ppermute | solution.py:881
  89.8 1.8 %collective-permute-start.24 = (f32[32,8,128]{2,1,0:T(8,128)S(1)}, f32[32,8,128]{2,1,0:T(8,128)S(1)}, u32[]{:S(2)}, u32[]{:S(2)}) collective-permute-start(f32[32,8,128]{2,1,0:T(8,128)S(1)} %gather_x.3.refs_0_.refs_4_), channel_id=1, source_target_pairs={{0,8},{4,12},{8,16},{12,20},{16,24},{20,28},{24,0},{28,4},{1,9},{5... | collective-permute-start | bytes 393224 | tf_op jit(solution)/shard_map/ppermute | solution.py:860
  92.1 2.0 %collective-permute-start.26 = (f32[32,8,128]{2,1,0:T(8,128)S(1)}, f32[32,8,128]{2,1,0:T(8,128)S(1)}, u32[]{:S(2)}, u32[]{:S(2)}) collective-permute-start(f32[32,8,128]{2,1,0:T(8,128)S(1)} %gather_x.3.refs_0_.refs_4_), channel_id=1, source_target_pairs={{0,24},{4,28},{8,0},{12,4},{16,8},{20,12},{24,16},{28,20},{1,25},{... | collective-permute-start | bytes 393224 | tf_op jit(solution)/shard_map/ppermute | solution.py:860
  94.0 2.2 %collective-permute-done.24.refs_1_ = f32[32,8,128]{2,1,0:T(8,128)S(1)} collective-permute-done((f32[32,8,128]{2,1,0:T(8,128)S(1)}, f32[32,8,128]{2,1,0:T(8,128)S(1)}, u32[]{:S(2)}, u32[]{:S(2)}) %collective-permute-start.24) | collective-permute-done | bytes 131104 | tf_op jit(solution)/shard_map/ppermute | solution.py:860
  96.3 2.1 %collective-permute-done.25.refs_2_ = f32[32,8,128]{2,1,0:T(8,128)S(1)} collective-permute-done((f32[32,8,128]{2,1,0:T(8,128)S(1)}, f32[32,8,128]{2,1,0:T(8,128)S(1)}, u32[]{:S(2)}, u32[]{:S(2)}) %collective-permute-start.25) | collective-permute-done | bytes 131104 | tf_op jit(solution)/shard_map/ppermute | solution.py:860
  100.7 3.5 %coarse_prepare.1 = (f32[6,32,64,128]{3,2,1,0:T(8,128)S(1)}, f32[32,64,128]{2,1,0:T(8,128)S(1)}, f32[32,64,128]{2,1,0:T(8,128)S(1)}, f32[6,16,32,128]{3,2,1,0:T(...) custom-call(f32[4,32,8,128]{3,2,1,0:T(8,128)S(1)} %stack_y.2.same, ...), custom_call_target="tpu_custom_call" | custom-call | tf_op jit(solution)/shard_map/coarse_prepare/pallas_call | solution.py:960
  104.3 9.3 %bottom.1.c2 = f32[18,24,128]{2,1,0:T(8,128)S(1)} custom-call(f32[4,32,8,128]{3,2,1,0:T(8,128)S(1)} %stack_y.3.same, f32[4,32,8,128]{3,2,1,0:T(8,128)S(1)} %collective-permute-done.28.sibling, f32[6,32,64,128]{3,2,1,0:T(8,128)S(1)} %get-tuple-element.123.g, f32[32,64,128]{2,1,0:T(8,128)S(1)} %get-tuple-element.124.inv, ...), custom_call_target="tpu_custom_call" | custom-call | tf_op jit(solution)/shard_map/bottom/pallas_call | solution.py:967
  113.5 3.7 %level1_up.1.c1 = f32[24,24,128]{2,1,0:T(8,128)S(1)} custom-call(f32[18,24,128]{2,1,0:T(8,128)S(1)} %bottom.1.c2, f32[6,36,40,128]{3,2,1,0:T(8,128)S(1)} %get-tuple-element.130.g, f32[36,40,128]{2,1,0:T(8,128)S(1)} %get-tuple-element.131.sp, f32[36,40,128]{2,1,0:T(8,128)S(1)} %get-tuple-element.132.beta, f32[38,56,128]{2,1,0:T(8,128)S(1)} %get-tuple-element.133.iterate), custom_call_target="tpu_custom_call" | custom-call | tf_op jit(solution)/shard_map/level1_up/pallas_call | solution.py:970
  117.2 9.8 %level0_up.1 = f32[32,32,128]{2,1,0:T(8,128)} custom-call(f32[24,24,128]{2,1,0:T(8,128)S(1)} %level1_up.1.c1, f32[48,48,128]{2,1,0:T(8,128)S(1)} %get-tuple-element.87.beta, f32[7,48,48,128]{3,2,1,0:T(8,128)S(1)} %get-tuple-element.134.g_main, f32[6,6,48,128]{3,2,1,0:T(8,128)S(1)} %get-tuple-element.135.g_strip, f32[48,48,128]{2,1,0:T(8,128)S(1)} %get-tuple-element.136.sp, ...), custom_call_target="tpu_custom_call" | custom-call | tf_op jit(solution)/shard_map/level0_up/pallas_call | solution.py:977
  (53 shorter events, 17.8 us)
Async XLA Ops:
  0.0 10.6 %copy-start.1 = (f32[32,32,128]{2,1,0:T(8,128)S(1)}, f32[32,32,128]{2,1,0:T(8,128)}, u32[]{:S(2)}) copy-start(f32[32,32,128]{2,1,0:T(8,128)} %src) | copy-start | bytes 1572868
  0.0 4.9 %copy-start = (f32[32,32,128]{2,1,0:T(8,128)S(1)}, f32[32,32,128]{2,1,0:T(8,128)}, u32[]{:S(2)}) copy-start(f32[32,32,128]{2,1,0:T(8,128)} %beta.1) | copy-start | bytes 1572868
  2.1 8.5 %collective-permute-start.1 = (f32[2,8,32,128]{3,2,1,0:T(8,128)S(1)}, f32[2,8,32,128]{3,2,1,0:T(8,128)S(1)}, u32[]{:S(2)}, u32[]{:S(2)}) collective-permute-start(f32[2,8,32,128]{3,2,1,0:T(8,128)S(1)} %get-tuple-element.76._), channel_id=1, source_target_pairs={{0,96},{32,0},{64,32},{96,64},{1,97},{33,1},{65,33},{97,65},{2,98}... | collective-permute-start | bytes 786440 | tf_op jit(solution)/shard_map/ppermute | solution.py:860
  2.7 7.8 %collective-permute-start = (f32[2,8,32,128]{3,2,1,0:T(8,128)S(1)}, f32[2,8,32,128]{3,2,1,0:T(8,128)S(1)}, u32[]{:S(2)}, u32[]{:S(2)}) collective-permute-start(f32[2,8,32,128]{3,2,1,0:T(8,128)S(1)} %get-tuple-element.75), channel_id=1, source_target_pairs={{0,32},{32,64},{64,96},{96,0},{1,33},{33,65},{65,97},{97,1},{2,34}... | collective-permute-start | bytes 786440 | tf_op jit(solution)/shard_map/ppermute | solution.py:860
  5.4 4.1 %collective-permute-start.2 = (f32[16,128]{1,0:T(8,128)S(1)}, f32[16,128]{1,0:T(8,128)S(1)}, u32[]{:S(2)}, u32[]{:S(2)}) collective-permute-start(f32[16,128]{1,0:T(8,128)S(1)} %coarse_beta.1.mine), channel_id=1, source_target_pairs={{0,1},{1,2},{2,3},{3,0},{4,5},{5,6},{6,7},{7,4},{8,9},{9,10},{10,1... | collective-permute-start | bytes 24584 | tf_op jit(solution)/shard_map/ppermute | solution.py:860
  10.7 8.8 %collective-permute-start.4 = (f32[2,48,8,128]{3,2,1,0:T(8,128)S(1)}, f32[2,48,8,128]{3,2,1,0:T(8,128)S(1)}, u32[]{:S(2)}, u32[]{:S(2)}) collective-permute-start(f32[2,48,8,128]{3,2,1,0:T(8,128)S(1)} %get-tuple-element.82.refs_2_), channel_id=1, source_target_pairs={{0,28},{4,0},{8,4},{12,8},{16,12},{20,16},{24,20},{28,24},{1,29},{... | collective-permute-start | bytes 1179656 | tf_op jit(solution)/shard_map/ppermute | solution.py:860
  12.3 7.3 %collective-permute-start.3 = (f32[2,48,8,128]{3,2,1,0:T(8,128)S(1)}, f32[2,48,8,128]{3,2,1,0:T(8,128)S(1)}, u32[]{:S(2)}, u32[]{:S(2)}) collective-permute-start(f32[2,48,8,128]{3,2,1,0:T(8,128)S(1)} %get-tuple-element.81), channel_id=1, source_target_pairs={{0,4},{4,8},{8,12},{12,16},{16,20},{20,24},{24,28},{28,0},{1,5},{5... | collective-permute-start | bytes 1179656 | tf_op jit(solution)/shard_map/ppermute | solution.py:860
  13.9 4.1 %collective-permute-start.5 = (f32[2,16,128]{2,1,0:T(8,128)S(1)}, f32[2,16,128]{2,1,0:T(8,128)S(1)}, u32[]{:S(2)}, u32[]{:S(2)}) collective-permute-start(f32[2,16,128]{2,1,0:T(8,128)S(1)} %pair.3.refs_0_), channel_id=1, source_target_pairs={{0,2},{1,3},{2,0},{3,1},{4,6},{5,7},{6,4},{7,5},{8,10},{9,11},{10,... | collective-permute-start | bytes 49160 | tf_op jit(solution)/shard_map/ppermute | solution.py:860
  21.1 6.6 %collective-permute-start.6 = (f32[6,48,128]{2,1,0:T(8,128)S(1)}, f32[6,48,128]{2,1,0:T(8,128)S(1)}, u32[]{:S(2)}, u32[]{:S(2)}) collective-permute-start(f32[6,48,128]{2,1,0:T(8,128)S(1)} %get-tuple-element.88), channel_id=1, source_target_pairs={{0,1},{1,2},{2,3},{3,0},{4,5},{5,6},{6,7},{7,4},{8,9},{9,10},{10,1... | collective-permute-start | bytes 442376 | tf_op jit(solution)/shard_map/ppermute | solution.py:860
  22.5 5.2 %collective-permute-start.7 = (f32[6,48,128]{2,1,0:T(8,128)S(1)}, f32[6,48,128]{2,1,0:T(8,128)S(1)}, u32[]{:S(2)}, u32[]{:S(2)}) collective-permute-start(f32[6,48,128]{2,1,0:T(8,128)S(1)} %get-tuple-element.89._), channel_id=1, source_target_pairs={{0,3},{1,0},{2,1},{3,2},{4,7},{5,4},{6,5},{7,6},{8,11},{9,8},{10,9... | collective-permute-start | bytes 442376 | tf_op jit(solution)/shard_map/ppermute | solution.py:860
  24.0 3.7 %collective-permute-start.8 = (f32[8,8,128]{2,1,0:T(8,128)S(1)}, f32[8,8,128]{2,1,0:T(8,128)S(1)}, u32[]{:S(2)}, u32[]{:S(2)}) collective-permute-start(f32[8,8,128]{2,1,0:T(8,128)S(1)} %gather_z.2.mine), channel_id=1, source_target_pairs={{0,32},{32,64},{64,96},{96,0},{1,33},{33,65},{65,97},{97,1},{2,34}... | collective-permute-start | bytes 98312 | tf_op jit(solution)/shard_map/ppermute | solution.py:860
  39.4 4.9 %collective-permute-start.10 = (f32[10,16,128]{2,1,0:T(8,128)S(1)}, f32[10,16,128]{2,1,0:T(8,128)S(1)}, u32[]{:S(2)}, u32[]{:S(2)}) collective-permute-start(f32[10,16,128]{2,1,0:T(8,128)S(1)} %get-tuple-element.95), channel_id=1, source_target_pairs={{0,96},{32,0},{64,32},{96,64},{1,97},{33,1},{65,33},{97,65},{2,98}... | collective-permute-start | bytes 245768 | tf_op jit(solution)/shard_map/ppermute | solution.py:860
  39.5 4.8 %collective-permute-start.9 = (f32[10,16,128]{2,1,0:T(8,128)S(1)}, f32[10,16,128]{2,1,0:T(8,128)S(1)}, u32[]{:S(2)}, u32[]{:S(2)}) collective-permute-start(f32[10,16,128]{2,1,0:T(8,128)S(1)} %get-tuple-element.94), channel_id=1, source_target_pairs={{0,32},{32,64},{64,96},{96,0},{1,33},{33,65},{65,97},{97,1},{2,34}... | collective-permute-start | bytes 245768 | tf_op jit(solution)/shard_map/ppermute | solution.py:860
  44.3 10.8 %collective-permute-start.11 = (f32[360,128]{1,0:T(8,128)S(1)}, f32[360,128]{1,0:T(8,128)S(1)}, u32[]{:S(2)}, u32[]{:S(2)}) collective-permute-start(f32[360,128]{1,0:T(8,128)S(1)} %get-tuple-element.96), channel_id=1, source_target_pairs={{0,4},{4,8},{8,12},{12,16},{16,20},{20,24},{24,28},{28,0},{1,5},{5... | collective-permute-start | bytes 552968 | tf_op jit(solution)/shard_map/ppermute | solution.py:860
  48.2 6.9 %collective-permute-start.12 = (f32[360,128]{1,0:T(8,128)S(1)}, f32[360,128]{1,0:T(8,128)S(1)}, u32[]{:S(2)}, u32[]{:S(2)}) collective-permute-start(f32[360,128]{1,0:T(8,128)S(1)} %get-tuple-element.97.refs_2_), channel_id=1, source_target_pairs={{0,28},{4,0},{8,4},{12,8},{16,12},{20,16},{24,20},{28,24},{1,29},{... | collective-permute-start | bytes 552968 | tf_op jit(solution)/shard_map/ppermute | solution.py:860
  50.2 4.9 %collective-permute-start.13 = (f32[2,8,8,128]{3,2,1,0:T(8,128)S(1)}, f32[2,8,8,128]{3,2,1,0:T(8,128)S(1)}, u32[]{:S(2)}, u32[]{:S(2)}) collective-permute-start(f32[2,8,8,128]{3,2,1,0:T(8,128)S(1)} %pair.4.refs_0_), channel_id=1, source_target_pairs={{0,64},{32,96},{64,0},{96,32},{1,65},{33,97},{65,1},{97,33},{2,66}... | collective-permute-start | bytes 196616 | tf_op jit(solution)/shard_map/ppermute | solution.py:860
  55.9 6.2 %collective-permute-start.16 = (f32[32,8,128]{2,1,0:T(8,128)S(1)}, f32[32,8,128]{2,1,0:T(8,128)S(1)}, u32[]{:S(2)}, u32[]{:S(2)}) collective-permute-start(f32[32,8,128]{2,1,0:T(8,128)S(1)} %gather_x.2.mine), channel_id=1, source_target_pairs={{0,8},{4,12},{8,16},{12,20},{16,24},{20,28},{24,0},{28,4},{1,9},{5... | collective-permute-start | bytes 393224 | tf_op jit(solution)/shard_map/ppermute | solution.py:860
  56.3 5.9 %collective-permute-start.14 = (f32[6,40,128]{2,1,0:T(8,128)S(1)}, f32[6,40,128]{2,1,0:T(8,128)S(1)}, u32[]{:S(2)}, u32[]{:S(2)}) collective-permute-start(f32[6,40,128]{2,1,0:T(8,128)S(1)} %get-tuple-element.103), channel_id=1, source_target_pairs={{0,1},{1,2},{2,3},{3,0},{4,5},{5,6},{6,7},{7,4},{8,9},{9,10},{10,1... | collective-permute-start | bytes 368648 | tf_op jit(solution)/shard_map/ppermute | solution.py:860
  56.3 5.8 %collective-permute-start.15 = (f32[6,40,128]{2,1,0:T(8,128)S(1)}, f32[6,40,128]{2,1,0:T(8,128)S(1)}, u32[]{:S(2)}, u32[]{:S(2)}) collective-permute-start(f32[6,40,128]{2,1,0:T(8,128)S(1)} %get-tuple-element.104._), channel_id=1, source_target_pairs={{0,3},{1,0},{2,1},{3,2},{4,7},{5,4},{6,5},{7,6},{8,11},{9,8},{10,9... | collective-permute-start | bytes 368648 | tf_op jit(solution)/shard_map/ppermute | solution.py:860
  66.3 15.6 %collective-permute-start.23 = (f32[2,32,8,128]{3,2,1,0:T(8,128)S(1)}, f32[2,32,8,128]{3,2,1,0:T(8,128)S(1)}, u32[]{:S(2)}, u32[]{:S(2)}) collective-permute-start(f32[2,32,8,128]{3,2,1,0:T(8,128)S(1)} %pair.5.refs_0_), channel_id=1, source_target_pairs={{0,16},{4,20},{8,24},{12,28},{16,0},{20,4},{24,8},{28,12},{1,17},{... | collective-permute-start | bytes 786440 | tf_op jit(solution)/shard_map/ppermute | solution.py:860
  71.5 4.0 %collective-permute-start.17 = (f32[16,128]{1,0:T(8,128)S(1)}, f32[16,128]{1,0:T(8,128)S(1)}, u32[]{:S(2)}, u32[]{:S(2)}) collective-permute-start(f32[16,128]{1,0:T(8,128)S(1)} %get-tuple-element.109.refs_0_.refs_4_.refs_2_), channel_id=1, source_target_pairs={{0,1},{1,2},{2,3},{3,0},{4,5},{5,6},{6,7},{7,4},{8,9},{9,10},{10,1... | collective-permute-start | bytes 24584 | tf_op jit(solution)/shard_map/ppermute | solution.py:860
  71.5 5.1 %collective-permute-start.18 = (f32[16,128]{1,0:T(8,128)S(1)}, f32[16,128]{1,0:T(8,128)S(1)}, u32[]{:S(2)}, u32[]{:S(2)}) collective-permute-start(f32[16,128]{1,0:T(8,128)S(1)} %get-tuple-element.109.refs_0_.refs_4_.refs_2_), channel_id=1, source_target_pairs={{0,2},{1,3},{2,0},{3,1},{4,6},{5,7},{6,4},{7,5},{8,10},{9,11},{10,... | collective-permute-start | bytes 24584 | tf_op jit(solution)/shard_map/ppermute | solution.py:860
  75.2 2.8 %collective-permute-start.19 = (f32[16,128]{1,0:T(8,128)S(1)}, f32[16,128]{1,0:T(8,128)S(1)}, u32[]{:S(2)}, u32[]{:S(2)}) collective-permute-start(f32[16,128]{1,0:T(8,128)S(1)} %get-tuple-element.109.refs_0_.refs_4_.refs_2_), channel_id=1, source_target_pairs={{0,3},{1,0},{2,1},{3,2},{4,7},{5,4},{6,5},{7,6},{8,11},{9,8},{10,9... | collective-permute-start | bytes 24584 | tf_op jit(solution)/shard_map/ppermute | solution.py:860
  78.1 3.9 %collective-permute-start.20 = (f32[8,8,128]{2,1,0:T(8,128)S(1)}, f32[8,8,128]{2,1,0:T(8,128)S(1)}, u32[]{:S(2)}, u32[]{:S(2)}) collective-permute-start(f32[8,8,128]{2,1,0:T(8,128)S(1)} %gather_z.3.refs_0_), channel_id=1, source_target_pairs={{0,32},{32,64},{64,96},{96,0},{1,33},{33,65},{65,97},{97,1},{2,34}... | collective-permute-start | bytes 98312 | tf_op jit(solution)/shard_map/ppermute | solution.py:860
  80.9 4.4 %collective-permute-start.21 = (f32[8,8,128]{2,1,0:T(8,128)S(1)}, f32[8,8,128]{2,1,0:T(8,128)S(1)}, u32[]{:S(2)}, u32[]{:S(2)}) collective-permute-start(f32[8,8,128]{2,1,0:T(8,128)S(1)} %gather_z.3.refs_0_), channel_id=1, source_target_pairs={{0,64},{32,96},{64,0},{96,32},{1,65},{33,97},{65,1},{97,33},{2,66}... | collective-permute-start | bytes 98312 | tf_op jit(solution)/shard_map/ppermute | solution.py:860
  81.2 4.3 %collective-permute-start.22 = (f32[8,8,128]{2,1,0:T(8,128)S(1)}, f32[8,8,128]{2,1,0:T(8,128)S(1)}, u32[]{:S(2)}, u32[]{:S(2)}) collective-permute-start(f32[8,8,128]{2,1,0:T(8,128)S(1)} %gather_z.3.refs_0_), channel_id=1, source_target_pairs={{0,96},{32,0},{64,32},{96,64},{1,97},{33,1},{65,33},{97,65},{2,98}... | collective-permute-start | bytes 98312 | tf_op jit(solution)/shard_map/ppermute | solution.py:860
  85.5 13.6 %collective-permute-start.27 = (f32[4,32,8,128]{3,2,1,0:T(8,128)S(1)}, f32[4,32,8,128]{3,2,1,0:T(8,128)S(1)}, u32[]{:S(2)}, u32[]{:S(2)}) collective-permute-start(f32[4,32,8,128]{3,2,1,0:T(8,128)S(1)} %stack_y.2.same), channel_id=1, source_target_pairs={{0,4},{4,0},{8,12},{12,8},{16,20},{20,16},{24,28},{28,24},{1,5},{5... | collective-permute-start | bytes 1572872 | tf_op jit(solution)/shard_map/ppermute | solution.py:881
  89.8 6.4 %collective-permute-start.24 = (f32[32,8,128]{2,1,0:T(8,128)S(1)}, f32[32,8,128]{2,1,0:T(8,128)S(1)}, u32[]{:S(2)}, u32[]{:S(2)}) collective-permute-start(f32[32,8,128]{2,1,0:T(8,128)S(1)} %gather_x.3.refs_0_.refs_4_), channel_id=1, source_target_pairs={{0,8},{4,12},{8,16},{12,20},{16,24},{20,28},{24,0},{28,4},{1,9},{5... | collective-permute-start | bytes 393224 | tf_op jit(solution)/shard_map/ppermute | solution.py:860
  91.6 6.8 %collective-permute-start.25 = (f32[32,8,128]{2,1,0:T(8,128)S(1)}, f32[32,8,128]{2,1,0:T(8,128)S(1)}, u32[]{:S(2)}, u32[]{:S(2)}) collective-permute-start(f32[32,8,128]{2,1,0:T(8,128)S(1)} %gather_x.3.refs_0_.refs_4_), channel_id=1, source_target_pairs={{0,16},{4,20},{8,24},{12,28},{16,0},{20,4},{24,8},{28,12},{1,17},{... | collective-permute-start | bytes 393224 | tf_op jit(solution)/shard_map/ppermute | solution.py:860
  92.1 7.1 %collective-permute-start.26 = (f32[32,8,128]{2,1,0:T(8,128)S(1)}, f32[32,8,128]{2,1,0:T(8,128)S(1)}, u32[]{:S(2)}, u32[]{:S(2)}) collective-permute-start(f32[32,8,128]{2,1,0:T(8,128)S(1)} %gather_x.3.refs_0_.refs_4_), channel_id=1, source_target_pairs={{0,24},{4,28},{8,0},{12,4},{16,8},{20,12},{24,16},{28,20},{1,25},{... | collective-permute-start | bytes 393224 | tf_op jit(solution)/shard_map/ppermute | solution.py:860
  99.2 5.0 %collective-permute-start.28 = (f32[4,32,8,128]{3,2,1,0:T(8,128)S(1)}, f32[4,32,8,128]{3,2,1,0:T(8,128)S(1)}, u32[]{:S(2)}, u32[]{:S(2)}) collective-permute-start(f32[4,32,8,128]{3,2,1,0:T(8,128)S(1)} %stack_y.3.same), channel_id=1, source_target_pairs={{0,4},{4,0},{8,12},{12,8},{16,20},{20,16},{24,28},{28,24},{1,5},{5... | collective-permute-start | bytes 1572872 | tf_op jit(solution)/shard_map/ppermute | solution.py:881

commit v11 on v9

--- a/solution.py
+++ b/solution.py
@@ -484,7 +484,7 @@
     return here, rest
 
 
-def ring_step(v, v_out, g, sp, u, planes, rows, retain, factor):
+def ring_step(v, v_out, g, sp, u, low, high, rows, retain, factor):
     def body(x):
         here, rest = ring_rest(v, g, sp, x, rows)
         new = factor * rest
@@ -493,7 +493,7 @@
         u[x] = new
         v_out[x + 1, 8 : 8 + rows, :] = here + new
 
-    loop(0, planes, rows // 16, body)
+    loop(low, high, rows // 16, body)
 
 
 def ring_zero_start(v, u, sp, planes, rows, factor):
@@ -504,14 +504,17 @@
     loop(0, planes, rows // 8, body)
 
 
-def ring_cheb(va, vb, g, sp, u, planes, rows, recipe, from_zero):
+def ring_cheb(va, vb, g, sp, u, planes, rows, recipe, from_zero, trim=None):
     begin = 0
     if from_zero:
         ring_zero_start(va, u, sp, planes, rows, recipe[0][1])
         begin = 1
     for k in range(begin, len(recipe)):
         retain, factor = recipe[k]
-        ring_step(va, vb, g, sp, u, planes, rows, None if k == 0 else retain, factor)
+        skip = 0 if trim is None else trim + k
+        ring_step(
+            va, vb, g, sp, u, skip, planes - skip, rows, None if k == 0 else retain, factor
+        )
         va, vb = vb, va
     return va
 
@@ -562,7 +565,9 @@
         clear_edges(ref, 36, 40)
     level1_unpack(ext, z_lo, z_hi, src, b_pad, beta_out)
     ring_weights(b_pad, src, g, sp, total, 36, 40, 4.0)
-    v = ring_cheb(va, vb, g, sp, u, 36, 40, RECIPE, True)
+    for x in (0, 1, 34, 35):
+        vb[x + 1, 8:48, :] = jnp.zeros((40, 128), F32)
+    v = ring_cheb(va, vb, g, sp, u, 36, 40, RECIPE, True, trim=1)
     assert v is vb
     summed = []
     for x2 in range(8):
@@ -743,7 +748,7 @@
         spw[x] = s2[plane, pl.ds(row, 24), :] * invw[x]
 
     loop(0, 22, 6, window)
-    c2 = ring_cheb(wa, wb, gw, spw, uw, 22, 24, RECIPE, False)
+    c2 = ring_cheb(wa, wb, gw, spw, uw, 22, 24, RECIPE, False, trim=1)
     shift = (128 - iz * 32) % 128
     for x in range(18):
         out[x] = roll(c2[x + 3, 8:32, :], shift)
@@ -790,7 +795,7 @@
             va[x + 1, 8:48, :] = jnp.where(beta[x] > 0.0, iterate[x + 1, 8:48, :] + rows[x2], 0.0)
 
     loop(0, 18, 12, prolong)
-    v = ring_cheb(va, vb, g, sp, u, 36, 40, RECIPE, False)
+    v = ring_cheb(va, vb, g, sp, u, 36, 40, RECIPE, False, trim=5)
     out[...] = v[7:31, 14:38, :]
 
 
@@ -841,7 +846,7 @@
         if k == 0:
             retain = None
         if k < SMOOTH - 1:
-            low, high = (4, 44) if k < 2 else (6, 42)
+            low, high = 5 + k, 43 - k
             level0_step(
                 v, t, w, s, ghost, g_main, g_strip, sp, sp_t, u, u_t, low, high, retain, factor
             )

time: 126 us -> 125 us (level)
  Pallas kernels: 45.5 us -> 44 us
where the time goes in v11:
time: 125 us; the launch traced here: 123 us
  starting transfers between devices  47.8 us (38%)
  Pallas kernels  44 us (35%)
  waiting for transfers between devices  29.2 us (23%)
  local copies, waits for them, and re-layouts  2.07 us (2%)
    ppermute x27, starting transfers between devices, ring(): lax.ppermute(value, axis, [(i, (i + step) % count) for i in range(count)])  40 us
    ppermute x27, waiting for transfers between devices, ring(): lax.ppermute(value, axis, [(i, (i + step) % count) for i in range(count)])  29.2 us
    pallas_call x1, Pallas kernels, per_device(): call(level0_down, (sds(50, 64, 128), sds(6, 64, 128), sds(16, 16, 128), s...  11.7 us
    pallas_call x1, Pallas kernels, per_device(): call(level0_up, sds(32, 32, 128), [vm(50, 64, 128), vm(50, 64, 128), vm(6...  9.49 us
    pallas_call x1, Pallas kernels, per_device(): call(bottom, sds(18, 24, 128), BOTTOM_SCRATCH, name='bottom', mib=18)  9.1 us
    ppermute x2, starting transfers between devices, across(): lax.ppermute(value, 'gy', [(i, i + 1 - 2 * (i % 2)) for i in range(count)])  7.81 us
    pallas_call x1, Pallas kernels, per_device(): call(level1_down, (sds(38, 56, 128), sds(16, 128), sds(6, 36, 40, 128), l...  3.99 us
    pallas_call x1, Pallas kernels, per_device(): call(coarse_prepare, tuple((sds(*shape) for shape in COARSE_SHAPES)), COA...  3.55 us
  transfers between devices with their start and end apart: 29, of which 19 were waited for; matrix products, arithmetic and copies ran while one was open for 0% of the time, Pallas kernels for 3%

profile of v11, /device:TPU:7, one launch (start us, length us, event | category | flops | bytes accessed | tf_op | source)
XLA Modules:
  0.0 123.3 jit_solution(5430601987017945150)
XLA Ops:
  2.7 2.1 %collective-permute-start = (f32[2,8,32,128]{3,2,1,0:T(8,128)S(1)}, f32[2,8,32,128]{3,2,1,0:T(8,128)S(1)}, u32[]{:S(2)}, u32[]{:S(2)}) collective-permute-start(f32[2,8,32,128]{3,2,1,0:T(8,128)S(1)} %get-tuple-element.72), channel_id=1, source_target_pairs={{0,32},{32,64},{64,96},{96,0},{1,33},{33,65},{65,97},{97,1},{2,34}... | collective-permute-start | bytes 786440 | tf_op jit(solution)/shard_map/ppermute | solution.py:865
  5.4 1.3 %collective-permute-start.2 = (f32[16,128]{1,0:T(8,128)S(1)}, f32[16,128]{1,0:T(8,128)S(1)}, u32[]{:S(2)}, u32[]{:S(2)}) collective-permute-start(f32[16,128]{1,0:T(8,128)S(1)} %coarse_beta.1.mine), channel_id=1, source_target_pairs={{0,1},{1,2},{2,3},{3,0},{4,5},{5,6},{6,7},{7,4},{8,9},{9,10},{10,1... | collective-permute-start | bytes 24584 | tf_op jit(solution)/shard_map/ppermute | solution.py:865
  6.7 2.8 %collective-permute-done.2.other = f32[16,128]{1,0:T(8,128)S(1)} collective-permute-done((f32[16,128]{1,0:T(8,128)S(1)}, f32[16,128]{1,0:T(8,128)S(1)}, u32[]{:S(2)}, u32[]{:S(2)}) %collective-permute-start.2) | collective-permute-done | bytes 8224 | tf_op jit(solution)/shard_map/ppermute | solution.py:865
  10.7 3.1 %collective-permute-start.3 = (f32[2,48,8,128]{3,2,1,0:T(8,128)S(1)}, f32[2,48,8,128]{3,2,1,0:T(8,128)S(1)}, u32[]{:S(2)}, u32[]{:S(2)}) collective-permute-start(f32[2,48,8,128]{3,2,1,0:T(8,128)S(1)} %get-tuple-element.78), channel_id=1, source_target_pairs={{0,4},{4,8},{8,12},{12,16},{16,20},{20,24},{24,28},{28,0},{1,5},{5... | collective-permute-start | bytes 1179656 | tf_op jit(solution)/shard_map/ppermute | solution.py:865
  13.8 2.9 %collective-permute-start.5 = (f32[2,16,128]{2,1,0:T(8,128)S(1)}, f32[2,16,128]{2,1,0:T(8,128)S(1)}, u32[]{:S(2)}, u32[]{:S(2)}) collective-permute-start(f32[2,16,128]{2,1,0:T(8,128)S(1)} %pair.3.refs_0_), channel_id=1, source_target_pairs={{0,2},{1,3},{2,0},{3,1},{4,6},{5,7},{6,4},{7,5},{8,10},{9,11},{10,... | collective-permute-start | bytes 49160 | tf_op jit(solution)/shard_map/ppermute | solution.py:865
  18.5 2.5 %collective-permute-done.4.y_hi = f32[2,48,8,128]{3,2,1,0:T(8,128)S(1)} collective-permute-done((f32[2,48,8,128]{3,2,1,0:T(8,128)S(1)}, f32[2,48,8,128]{3,2,1,0:T(8,128)S(1)}, u32[]{:S(2)}, u32[]{:S(2)}) %collective-permute-start.4) | collective-permute-done | bytes 393248 | tf_op jit(solution)/shard_map/ppermute | solution.py:865
  21.0 1.5 %pack_z.1 = (f32[48,48,128]{2,1,0:T(8,128)S(1)}, f32[48,48,128]{2,1,0:T(8,128)S(1)}, f32[6,48,128]{2,1,0:T(8,128)S(1)}, f32[6,48,128]{2,1,0:T(8,128)S(1)}) custom-call(f32[48,32,128]{2,1,0:T(8,128)S(1)} %get-tuple-element.76.s_mid, f32[48,32,128]{2,1,0:T(8,128)S(1)} %get-tuple-element.77.b_mid, f32[2,48,8,128]{3,2,1,0:T(8,128)S(1)} %collective-permute-done.3.y_lo, ...), custom_call_target="tpu_custom_call" | custom-call | tf_op jit(solution)/shard_map/pack_z/pallas_call | solution.py:907
  22.5 1.4 %collective-permute-start.6 = (f32[6,48,128]{2,1,0:T(8,128)S(1)}, f32[6,48,128]{2,1,0:T(8,128)S(1)}, u32[]{:S(2)}, u32[]{:S(2)}) collective-permute-start(f32[6,48,128]{2,1,0:T(8,128)S(1)} %get-tuple-element.85), channel_id=1, source_target_pairs={{0,1},{1,2},{2,3},{3,0},{4,5},{5,6},{6,7},{7,4},{8,9},{9,10},{10,1... | collective-permute-start | bytes 442376 | tf_op jit(solution)/shard_map/ppermute | solution.py:865
  23.9 1.5 %collective-permute-start.7 = (f32[6,48,128]{2,1,0:T(8,128)S(1)}, f32[6,48,128]{2,1,0:T(8,128)S(1)}, u32[]{:S(2)}, u32[]{:S(2)}) collective-permute-start(f32[6,48,128]{2,1,0:T(8,128)S(1)} %get-tuple-element.86._), channel_id=1, source_target_pairs={{0,3},{1,0},{2,1},{3,2},{4,7},{5,4},{6,5},{7,6},{8,11},{9,8},{10,9... | collective-permute-start | bytes 442376 | tf_op jit(solution)/shard_map/ppermute | solution.py:865
  25.4 2.7 %collective-permute-start.8 = (f32[8,8,128]{2,1,0:T(8,128)S(1)}, f32[8,8,128]{2,1,0:T(8,128)S(1)}, u32[]{:S(2)}, u32[]{:S(2)}) collective-permute-start(f32[8,8,128]{2,1,0:T(8,128)S(1)} %gather_z.2.mine), channel_id=1, source_target_pairs={{0,32},{32,64},{64,96},{96,0},{1,33},{33,65},{65,97},{97,1},{2,34}... | collective-permute-start | bytes 98312 | tf_op jit(solution)/shard_map/ppermute | solution.py:865
  29.7 11.7 %level0_down.1 = (f32[50,64,128]{2,1,0:T(8,128)S(1)}, f32[6,64,128]{2,1,0:T(8,128)S(1)}, f32[16,16,128]{2,1,0:T(8,128)S(1)}, f32[10,16,128]{2,1,0:T(8,128)S(1)},...) custom-call(f32[48,48,128]{2,1,0:T(8,128)S(1)} %get-tuple-element.83, ...), custom_call_target="tpu_custom_call" | custom-call | tf_op jit(solution)/shard_map/level0_down/pallas_call | solution.py:913
  41.4 2.8 %collective-permute-start.9 = (f32[10,16,128]{2,1,0:T(8,128)S(1)}, f32[10,16,128]{2,1,0:T(8,128)S(1)}, u32[]{:S(2)}, u32[]{:S(2)}) collective-permute-start(f32[10,16,128]{2,1,0:T(8,128)S(1)} %get-tuple-element.91), channel_id=1, source_target_pairs={{0,32},{32,64},{64,96},{96,0},{1,33},{33,65},{65,97},{97,1},{2,34}... | collective-permute-start | bytes 245768 | tf_op jit(solution)/shard_map/ppermute | solution.py:865
  45.4 3.9 %collective-permute-done.11.refs_1_ = f32[2,8,8,128]{3,2,1,0:T(8,128)S(1)} collective-permute-done((f32[2,8,8,128]{3,2,1,0:T(8,128)S(1)}, f32[2,8,8,128]{3,2,1,0:T(8,128)S(1)}, u32[]{:S(2)}, u32[]{:S(2)}) %collective-permute-start.11) | collective-permute-done | bytes 65568 | tf_op jit(solution)/shard_map/ppermute | solution.py:865
  49.4 2.3 %collective-permute-start.12 = (f32[360,128]{1,0:T(8,128)S(1)}, f32[360,128]{1,0:T(8,128)S(1)}, u32[]{:S(2)}, u32[]{:S(2)}) collective-permute-start(f32[360,128]{1,0:T(8,128)S(1)} %get-tuple-element.97), channel_id=1, source_target_pairs={{0,4},{4,8},{8,12},{12,16},{16,20},{20,24},{24,28},{28,0},{1,5},{5... | collective-permute-start | bytes 552968 | tf_op jit(solution)/shard_map/ppermute | solution.py:865
  51.7 1.6 %collective-permute-start.14 = (f32[32,8,128]{2,1,0:T(8,128)S(1)}, f32[32,8,128]{2,1,0:T(8,128)S(1)}, u32[]{:S(2)}, u32[]{:S(2)}) collective-permute-start(f32[32,8,128]{2,1,0:T(8,128)S(1)} %gather_x.2.mine), channel_id=1, source_target_pairs={{0,8},{4,12},{8,16},{12,20},{16,24},{20,28},{24,0},{28,4},{1,9},{5... | collective-permute-start | bytes 393224 | tf_op jit(solution)/shard_map/ppermute | solution.py:865
  53.3 4.9 %collective-permute-done.14.other = f32[32,8,128]{2,1,0:T(8,128)S(1)} collective-permute-done((f32[32,8,128]{2,1,0:T(8,128)S(1)}, f32[32,8,128]{2,1,0:T(8,128)S(1)}, u32[]{:S(2)}, u32[]{:S(2)}) %collective-permute-start.14) | collective-permute-done | bytes 131104 | tf_op jit(solution)/shard_map/ppermute | solution.py:865
  59.1 2.5 %collective-permute-start.17 = (f32[2,32,8,128]{3,2,1,0:T(8,128)S(1)}, f32[2,32,8,128]{3,2,1,0:T(8,128)S(1)}, u32[]{:S(2)}, u32[]{:S(2)}) collective-permute-start(f32[2,32,8,128]{3,2,1,0:T(8,128)S(1)} %pair.5.refs_0_), channel_id=1, source_target_pairs={{0,16},{4,20},{8,24},{12,28},{16,0},{20,4},{24,8},{28,12},{1,17},{... | collective-permute-start | bytes 786440 | tf_op jit(solution)/shard_map/ppermute | solution.py:865
  62.6 1.7 %collective-permute-start.16 = (f32[6,40,128]{2,1,0:T(8,128)S(1)}, f32[6,40,128]{2,1,0:T(8,128)S(1)}, u32[]{:S(2)}, u32[]{:S(2)}) collective-permute-start(f32[6,40,128]{2,1,0:T(8,128)S(1)} %get-tuple-element.104.refs_2_), channel_id=1, source_target_pairs={{0,3},{1,0},{2,1},{3,2},{4,7},{5,4},{6,5},{7,6},{8,11},{9,8},{10,9... | collective-permute-start | bytes 368648 | tf_op jit(solution)/shard_map/ppermute | solution.py:865
  64.3 2.1 %collective-permute-done.17.refs_1_ = f32[2,32,8,128]{3,2,1,0:T(8,128)S(1)} collective-permute-done((f32[2,32,8,128]{3,2,1,0:T(8,128)S(1)}, f32[2,32,8,128]{3,2,1,0:T(8,128)S(1)}, u32[]{:S(2)}, u32[]{:S(2)}) %collective-permute-start.17) | collective-permute-done | bytes 262176 | tf_op jit(solution)/shard_map/ppermute | solution.py:865
  66.9 4.0 %level1_down.1 = (f32[38,56,128]{2,1,0:T(8,128)S(1)}, f32[16,128]{1,0:T(8,128)S(1)}, f32[6,36,40,128]{3,2,1,0:T(8,128)S(1)}, f32[36,40,128]{2,1,0:T(8,128)S(1)}, f32[36,40,128]{2,1,0:T(8,128)S(1)}) custom-call(f32[36,40,128]{2,1,0:T(8,128)S(1)} %get-tuple-element.102.ext, f32[6,40,128]{2,1,0:T(8,128)S(1)} %collective-permute-done.15.z_lo, ...), custom_call_target="tpu_custom_call" | custom-call | tf_op jit(solution)/shard_map/level1_down/pallas_call | solution.py:947
  70.9 2.6 %collective-permute-start.21 = (f32[4,32,8,128]{3,2,1,0:T(8,128)S(1)}, f32[4,32,8,128]{3,2,1,0:T(8,128)S(1)}, u32[]{:S(2)}, u32[]{:S(2)}) collective-permute-start(f32[4,32,8,128]{3,2,1,0:T(8,128)S(1)} %stack_y.2.same), channel_id=1, source_target_pairs={{0,4},{4,0},{8,12},{12,8},{16,20},{20,16},{24,28},{28,24},{1,5},{5... | collective-permute-start | bytes 1572872 | tf_op jit(solution)/shard_map/ppermute | solution.py:886
  74.5 2.6 %collective-permute-start.19 = (f32[16,128]{1,0:T(8,128)S(1)}, f32[16,128]{1,0:T(8,128)S(1)}, u32[]{:S(2)}, u32[]{:S(2)}) collective-permute-start(f32[16,128]{1,0:T(8,128)S(1)} %get-tuple-element.112.refs_0_.refs_4_), channel_id=1, source_target_pairs={{0,2},{1,3},{2,0},{3,1},{4,6},{5,7},{6,4},{7,5},{8,10},{9,11},{10,... | collective-permute-start | bytes 24584 | tf_op jit(solution)/shard_map/ppermute | solution.py:865
  79.7 1.6 %collective-permute-start.22 = (f32[8,8,128]{2,1,0:T(8,128)S(1)}, f32[8,8,128]{2,1,0:T(8,128)S(1)}, u32[]{:S(2)}, u32[]{:S(2)}) collective-permute-start(f32[8,8,128]{2,1,0:T(8,128)S(1)} %gather_z.3.refs_0_), channel_id=1, source_target_pairs={{0,32},{32,64},{64,96},{96,0},{1,33},{33,65},{65,97},{97,1},{2,34}... | collective-permute-start | bytes 98312 | tf_op jit(solution)/shard_map/ppermute | solution.py:865
  82.6 3.1 %collective-permute-done.23.refs_2_ = f32[8,8,128]{2,1,0:T(8,128)S(1)} collective-permute-done((f32[8,8,128]{2,1,0:T(8,128)S(1)}, f32[8,8,128]{2,1,0:T(8,128)S(1)}, u32[]{:S(2)}, u32[]{:S(2)}) %collective-permute-start.23) | collective-permute-done | bytes 32800 | tf_op jit(solution)/shard_map/ppermute | solution.py:865
  86.7 2.5 %collective-permute-start.26 = (f32[32,8,128]{2,1,0:T(8,128)S(1)}, f32[32,8,128]{2,1,0:T(8,128)S(1)}, u32[]{:S(2)}, u32[]{:S(2)}) collective-permute-start(f32[32,8,128]{2,1,0:T(8,128)S(1)} %gather_x.3.refs_0_.refs_4_), channel_id=1, source_target_pairs={{0,16},{4,20},{8,24},{12,28},{16,0},{20,4},{24,8},{28,12},{1,17},{... | collective-permute-start | bytes 393224 | tf_op jit(solution)/shard_map/ppermute | solution.py:865
  89.2 1.3 %collective-permute-start.27 = (f32[32,8,128]{2,1,0:T(8,128)S(1)}, f32[32,8,128]{2,1,0:T(8,128)S(1)}, u32[]{:S(2)}, u32[]{:S(2)}) collective-permute-start(f32[32,8,128]{2,1,0:T(8,128)S(1)} %gather_x.3.refs_0_.refs_4_), channel_id=1, source_target_pairs={{0,24},{4,28},{8,0},{12,4},{16,8},{20,12},{24,16},{28,20},{1,25},{... | collective-permute-start | bytes 393224 | tf_op jit(solution)/shard_map/ppermute | solution.py:865
  91.1 1.8 %collective-permute-done.26.refs_2_ = f32[32,8,128]{2,1,0:T(8,128)S(1)} collective-permute-done((f32[32,8,128]{2,1,0:T(8,128)S(1)}, f32[32,8,128]{2,1,0:T(8,128)S(1)}, u32[]{:S(2)}, u32[]{:S(2)}) %collective-permute-start.26) | collective-permute-done | bytes 131104 | tf_op jit(solution)/shard_map/ppermute | solution.py:865
  93.1 5.2 %collective-permute-start.28 = (f32[4,32,8,128]{3,2,1,0:T(8,128)S(1)}, f32[4,32,8,128]{3,2,1,0:T(8,128)S(1)}, u32[]{:S(2)}, u32[]{:S(2)}) collective-permute-start(f32[4,32,8,128]{3,2,1,0:T(8,128)S(1)} %stack_y.3.same), channel_id=1, source_target_pairs={{0,4},{4,0},{8,12},{12,8},{16,20},{20,16},{24,28},{28,24},{1,5},{5... | collective-permute-start | bytes 1572872 | tf_op jit(solution)/shard_map/ppermute | solution.py:886
  98.3 3.5 %coarse_prepare.1 = (f32[6,32,64,128]{3,2,1,0:T(8,128)S(1)}, f32[32,64,128]{2,1,0:T(8,128)S(1)}, f32[32,64,128]{2,1,0:T(8,128)S(1)}, f32[6,16,32,128]{3,2,1,0:T(...) custom-call(f32[4,32,8,128]{3,2,1,0:T(8,128)S(1)} %stack_y.2.same, ...), custom_call_target="tpu_custom_call" | custom-call | tf_op jit(solution)/shard_map/coarse_prepare/pallas_call | solution.py:961
  101.9 9.1 %bottom.1.c2 = f32[18,24,128]{2,1,0:T(8,128)S(1)} custom-call(f32[4,32,8,128]{3,2,1,0:T(8,128)S(1)} %stack_y.3.same, f32[4,32,8,128]{3,2,1,0:T(8,128)S(1)} %collective-permute-done.28.sibling, f32[6,32,64,128]{3,2,1,0:T(8,128)S(1)} %get-tuple-element.117.g, f32[32,64,128]{2,1,0:T(8,128)S(1)} %get-tuple-element.118.inv, ...), custom_call_target="tpu_custom_call" | custom-call | tf_op jit(solution)/shard_map/bottom/pallas_call | solution.py:968
  111.0 2.8 %level1_up.1.c1 = f32[24,24,128]{2,1,0:T(8,128)S(1)} custom-call(f32[18,24,128]{2,1,0:T(8,128)S(1)} %bottom.1.c2, f32[6,36,40,128]{3,2,1,0:T(8,128)S(1)} %get-tuple-element.124.g, f32[36,40,128]{2,1,0:T(8,128)S(1)} %get-tuple-element.125.sp, f32[36,40,128]{2,1,0:T(8,128)S(1)} %get-tuple-element.126.beta, f32[38,56,128]{2,1,0:T(8,128)S(1)} %get-tuple-element.127.iterate), custom_call_target="tpu_custom_call" | custom-call | tf_op jit(solution)/shard_map/level1_up/pallas_call | solution.py:971
  113.8 9.5 %level0_up.1 = f32[32,32,128]{2,1,0:T(8,128)} custom-call(f32[24,24,128]{2,1,0:T(8,128)S(1)} %level1_up.1.c1, f32[48,48,128]{2,1,0:T(8,128)S(1)} %get-tuple-element.84.beta, f32[7,48,48,128]{3,2,1,0:T(8,128)S(1)} %get-tuple-element.128.g_main, f32[6,6,48,128]{3,2,1,0:T(8,128)S(1)} %get-tuple-element.129.g_strip, f32[48,48,128]{2,1,0:T(8,128)S(1)} %get-tuple-element.130.sp, ...), custom_call_target="tpu_custom_call" | custom-call | tf_op jit(solution)/shard_map/level0_up/pallas_call | solution.py:978
  (53 shorter events, 18.0 us)
Async XLA Ops:
  0.0 10.6 %copy-start.1 = (f32[32,32,128]{2,1,0:T(8,128)S(1)}, f32[32,32,128]{2,1,0:T(8,128)}, u32[]{:S(2)}) copy-start(f32[32,32,128]{2,1,0:T(8,128)} %src) | copy-start | bytes 1572868
  0.0 4.9 %copy-start = (f32[32,32,128]{2,1,0:T(8,128)S(1)}, f32[32,32,128]{2,1,0:T(8,128)}, u32[]{:S(2)}) copy-start(f32[32,32,128]{2,1,0:T(8,128)} %beta.1) | copy-start | bytes 1572868
  2.1 8.5 %collective-permute-start.1 = (f32[2,8,32,128]{3,2,1,0:T(8,128)S(1)}, f32[2,8,32,128]{3,2,1,0:T(8,128)S(1)}, u32[]{:S(2)}, u32[]{:S(2)}) collective-permute-start(f32[2,8,32,128]{3,2,1,0:T(8,128)S(1)} %get-tuple-element.73._), channel_id=1, source_target_pairs={{0,96},{32,0},{64,32},{96,64},{1,97},{33,1},{65,33},{97,65},{2,98}... | collective-permute-start | bytes 786440 | tf_op jit(solution)/shard_map/ppermute | solution.py:865
  2.7 7.8 %collective-permute-start = (f32[2,8,32,128]{3,2,1,0:T(8,128)S(1)}, f32[2,8,32,128]{3,2,1,0:T(8,128)S(1)}, u32[]{:S(2)}, u32[]{:S(2)}) collective-permute-start(f32[2,8,32,128]{3,2,1,0:T(8,128)S(1)} %get-tuple-element.72), channel_id=1, source_target_pairs={{0,32},{32,64},{64,96},{96,0},{1,33},{33,65},{65,97},{97,1},{2,34}... | collective-permute-start | bytes 786440 | tf_op jit(solution)/shard_map/ppermute | solution.py:865
  5.4 4.1 %collective-permute-start.2 = (f32[16,128]{1,0:T(8,128)S(1)}, f32[16,128]{1,0:T(8,128)S(1)}, u32[]{:S(2)}, u32[]{:S(2)}) collective-permute-start(f32[16,128]{1,0:T(8,128)S(1)} %coarse_beta.1.mine), channel_id=1, source_target_pairs={{0,1},{1,2},{2,3},{3,0},{4,5},{5,6},{6,7},{7,4},{8,9},{9,10},{10,1... | collective-permute-start | bytes 24584 | tf_op jit(solution)/shard_map/ppermute | solution.py:865
  10.7 7.8 %collective-permute-start.3 = (f32[2,48,8,128]{3,2,1,0:T(8,128)S(1)}, f32[2,48,8,128]{3,2,1,0:T(8,128)S(1)}, u32[]{:S(2)}, u32[]{:S(2)}) collective-permute-start(f32[2,48,8,128]{3,2,1,0:T(8,128)S(1)} %get-tuple-element.78), channel_id=1, source_target_pairs={{0,4},{4,8},{8,12},{12,16},{16,20},{20,24},{24,28},{28,0},{1,5},{5... | collective-permute-start | bytes 1179656 | tf_op jit(solution)/shard_map/ppermute | solution.py:865
  13.8 7.2 %collective-permute-start.4 = (f32[2,48,8,128]{3,2,1,0:T(8,128)S(1)}, f32[2,48,8,128]{3,2,1,0:T(8,128)S(1)}, u32[]{:S(2)}, u32[]{:S(2)}) collective-permute-start(f32[2,48,8,128]{3,2,1,0:T(8,128)S(1)} %get-tuple-element.79.refs_2_), channel_id=1, source_target_pairs={{0,28},{4,0},{8,4},{12,8},{16,12},{20,16},{24,20},{28,24},{1,29},{... | collective-permute-start | bytes 1179656 | tf_op jit(solution)/shard_map/ppermute | solution.py:865
  13.8 4.1 %collective-permute-start.5 = (f32[2,16,128]{2,1,0:T(8,128)S(1)}, f32[2,16,128]{2,1,0:T(8,128)S(1)}, u32[]{:S(2)}, u32[]{:S(2)}) collective-permute-start(f32[2,16,128]{2,1,0:T(8,128)S(1)} %pair.3.refs_0_), channel_id=1, source_target_pairs={{0,2},{1,3},{2,0},{3,1},{4,6},{5,7},{6,4},{7,5},{8,10},{9,11},{10,... | collective-permute-start | bytes 49160 | tf_op jit(solution)/shard_map/ppermute | solution.py:865
  22.5 7.1 %collective-permute-start.6 = (f32[6,48,128]{2,1,0:T(8,128)S(1)}, f32[6,48,128]{2,1,0:T(8,128)S(1)}, u32[]{:S(2)}, u32[]{:S(2)}) collective-permute-start(f32[6,48,128]{2,1,0:T(8,128)S(1)} %get-tuple-element.85), channel_id=1, source_target_pairs={{0,1},{1,2},{2,3},{3,0},{4,5},{5,6},{6,7},{7,4},{8,9},{9,10},{10,1... | collective-permute-start | bytes 442376 | tf_op jit(solution)/shard_map/ppermute | solution.py:865
  23.9 5.8 %collective-permute-start.7 = (f32[6,48,128]{2,1,0:T(8,128)S(1)}, f32[6,48,128]{2,1,0:T(8,128)S(1)}, u32[]{:S(2)}, u32[]{:S(2)}) collective-permute-start(f32[6,48,128]{2,1,0:T(8,128)S(1)} %get-tuple-element.86._), channel_id=1, source_target_pairs={{0,3},{1,0},{2,1},{3,2},{4,7},{5,4},{6,5},{7,6},{8,11},{9,8},{10,9... | collective-permute-start | bytes 442376 | tf_op jit(solution)/shard_map/ppermute | solution.py:865
  25.4 3.7 %collective-permute-start.8 = (f32[8,8,128]{2,1,0:T(8,128)S(1)}, f32[8,8,128]{2,1,0:T(8,128)S(1)}, u32[]{:S(2)}, u32[]{:S(2)}) collective-permute-start(f32[8,8,128]{2,1,0:T(8,128)S(1)} %gather_z.2.mine), channel_id=1, source_target_pairs={{0,32},{32,64},{64,96},{96,0},{1,33},{33,65},{65,97},{97,1},{2,34}... | collective-permute-start | bytes 98312 | tf_op jit(solution)/shard_map/ppermute | solution.py:865
  41.3 8.0 %collective-permute-start.10 = (f32[10,16,128]{2,1,0:T(8,128)S(1)}, f32[10,16,128]{2,1,0:T(8,128)S(1)}, u32[]{:S(2)}, u32[]{:S(2)}) collective-permute-start(f32[10,16,128]{2,1,0:T(8,128)S(1)} %get-tuple-element.92.refs_2_), channel_id=1, source_target_pairs={{0,96},{32,0},{64,32},{96,64},{1,97},{33,1},{65,33},{97,65},{2,98}... | collective-permute-start | bytes 245768 | tf_op jit(solution)/shard_map/ppermute | solution.py:865
  41.4 7.9 %collective-permute-start.9 = (f32[10,16,128]{2,1,0:T(8,128)S(1)}, f32[10,16,128]{2,1,0:T(8,128)S(1)}, u32[]{:S(2)}, u32[]{:S(2)}) collective-permute-start(f32[10,16,128]{2,1,0:T(8,128)S(1)} %get-tuple-element.91), channel_id=1, source_target_pairs={{0,32},{32,64},{64,96},{96,0},{1,33},{33,65},{65,97},{97,1},{2,34}... | collective-permute-start | bytes 245768 | tf_op jit(solution)/shard_map/ppermute | solution.py:865
  44.3 5.0 %collective-permute-start.11 = (f32[2,8,8,128]{3,2,1,0:T(8,128)S(1)}, f32[2,8,8,128]{3,2,1,0:T(8,128)S(1)}, u32[]{:S(2)}, u32[]{:S(2)}) collective-permute-start(f32[2,8,8,128]{3,2,1,0:T(8,128)S(1)} %pair.4.refs_0_), channel_id=1, source_target_pairs={{0,64},{32,96},{64,0},{96,32},{1,65},{33,97},{65,1},{97,33},{2,66}... | collective-permute-start | bytes 196616 | tf_op jit(solution)/shard_map/ppermute | solution.py:865
  49.4 8.9 %collective-permute-start.12 = (f32[360,128]{1,0:T(8,128)S(1)}, f32[360,128]{1,0:T(8,128)S(1)}, u32[]{:S(2)}, u32[]{:S(2)}) collective-permute-start(f32[360,128]{1,0:T(8,128)S(1)} %get-tuple-element.97), channel_id=1, source_target_pairs={{0,4},{4,8},{8,12},{12,16},{16,20},{20,24},{24,28},{28,0},{1,5},{5... | collective-permute-start | bytes 552968 | tf_op jit(solution)/shard_map/ppermute | solution.py:865
  51.7 6.6 %collective-permute-start.13 = (f32[360,128]{1,0:T(8,128)S(1)}, f32[360,128]{1,0:T(8,128)S(1)}, u32[]{:S(2)}, u32[]{:S(2)}) collective-permute-start(f32[360,128]{1,0:T(8,128)S(1)} %get-tuple-element.98._), channel_id=1, source_target_pairs={{0,28},{4,0},{8,4},{12,8},{16,12},{20,16},{24,20},{28,24},{1,29},{... | collective-permute-start | bytes 552968 | tf_op jit(solution)/shard_map/ppermute | solution.py:865
  51.7 6.6 %collective-permute-start.14 = (f32[32,8,128]{2,1,0:T(8,128)S(1)}, f32[32,8,128]{2,1,0:T(8,128)S(1)}, u32[]{:S(2)}, u32[]{:S(2)}) collective-permute-start(f32[32,8,128]{2,1,0:T(8,128)S(1)} %gather_x.2.mine), channel_id=1, source_target_pairs={{0,8},{4,12},{8,16},{12,20},{16,24},{20,28},{24,0},{28,4},{1,9},{5... | collective-permute-start | bytes 393224 | tf_op jit(solution)/shard_map/ppermute | solution.py:865
  59.1 7.4 %collective-permute-start.17 = (f32[2,32,8,128]{3,2,1,0:T(8,128)S(1)}, f32[2,32,8,128]{3,2,1,0:T(8,128)S(1)}, u32[]{:S(2)}, u32[]{:S(2)}) collective-permute-start(f32[2,32,8,128]{3,2,1,0:T(8,128)S(1)} %pair.5.refs_0_), channel_id=1, source_target_pairs={{0,16},{4,20},{8,24},{12,28},{16,0},{20,4},{24,8},{28,12},{1,17},{... | collective-permute-start | bytes 786440 | tf_op jit(solution)/shard_map/ppermute | solution.py:865
  61.6 5.2 %collective-permute-start.15 = (f32[6,40,128]{2,1,0:T(8,128)S(1)}, f32[6,40,128]{2,1,0:T(8,128)S(1)}, u32[]{:S(2)}, u32[]{:S(2)}) collective-permute-start(f32[6,40,128]{2,1,0:T(8,128)S(1)} %get-tuple-element.103), channel_id=1, source_target_pairs={{0,1},{1,2},{2,3},{3,0},{4,5},{5,6},{6,7},{7,4},{8,9},{9,10},{10,1... | collective-permute-start | bytes 368648 | tf_op jit(solution)/shard_map/ppermute | solution.py:865
  62.6 4.3 %collective-permute-start.16 = (f32[6,40,128]{2,1,0:T(8,128)S(1)}, f32[6,40,128]{2,1,0:T(8,128)S(1)}, u32[]{:S(2)}, u32[]{:S(2)}) collective-permute-start(f32[6,40,128]{2,1,0:T(8,128)S(1)} %get-tuple-element.104.refs_2_), channel_id=1, source_target_pairs={{0,3},{1,0},{2,1},{3,2},{4,7},{5,4},{6,5},{7,6},{8,11},{9,8},{10,9... | collective-permute-start | bytes 368648 | tf_op jit(solution)/shard_map/ppermute | solution.py:865
  70.9 8.7 %collective-permute-start.21 = (f32[4,32,8,128]{3,2,1,0:T(8,128)S(1)}, f32[4,32,8,128]{3,2,1,0:T(8,128)S(1)}, u32[]{:S(2)}, u32[]{:S(2)}) collective-permute-start(f32[4,32,8,128]{3,2,1,0:T(8,128)S(1)} %stack_y.2.same), channel_id=1, source_target_pairs={{0,4},{4,0},{8,12},{12,8},{16,20},{20,16},{24,28},{28,24},{1,5},{5... | collective-permute-start | bytes 1572872 | tf_op jit(solution)/shard_map/ppermute | solution.py:886
  73.5 4.4 %collective-permute-start.18 = (f32[16,128]{1,0:T(8,128)S(1)}, f32[16,128]{1,0:T(8,128)S(1)}, u32[]{:S(2)}, u32[]{:S(2)}) collective-permute-start(f32[16,128]{1,0:T(8,128)S(1)} %get-tuple-element.112.refs_0_.refs_4_), channel_id=1, source_target_pairs={{0,1},{1,2},{2,3},{3,0},{4,5},{5,6},{6,7},{7,4},{8,9},{9,10},{10,1... | collective-permute-start | bytes 24584 | tf_op jit(solution)/shard_map/ppermute | solution.py:865
  74.5 4.0 %collective-permute-start.19 = (f32[16,128]{1,0:T(8,128)S(1)}, f32[16,128]{1,0:T(8,128)S(1)}, u32[]{:S(2)}, u32[]{:S(2)}) collective-permute-start(f32[16,128]{1,0:T(8,128)S(1)} %get-tuple-element.112.refs_0_.refs_4_), channel_id=1, source_target_pairs={{0,2},{1,3},{2,0},{3,1},{4,6},{5,7},{6,4},{7,5},{8,10},{9,11},{10,... | collective-permute-start | bytes 24584 | tf_op jit(solution)/shard_map/ppermute | solution.py:865
  77.1 2.5 %collective-permute-start.20 = (f32[16,128]{1,0:T(8,128)S(1)}, f32[16,128]{1,0:T(8,128)S(1)}, u32[]{:S(2)}, u32[]{:S(2)}) collective-permute-start(f32[16,128]{1,0:T(8,128)S(1)} %get-tuple-element.112.refs_0_.refs_4_), channel_id=1, source_target_pairs={{0,3},{1,0},{2,1},{3,2},{4,7},{5,4},{6,5},{7,6},{8,11},{9,8},{10,9... | collective-permute-start | bytes 24584 | tf_op jit(solution)/shard_map/ppermute | solution.py:865
  79.7 2.8 %collective-permute-start.22 = (f32[8,8,128]{2,1,0:T(8,128)S(1)}, f32[8,8,128]{2,1,0:T(8,128)S(1)}, u32[]{:S(2)}, u32[]{:S(2)}) collective-permute-start(f32[8,8,128]{2,1,0:T(8,128)S(1)} %gather_z.3.refs_0_), channel_id=1, source_target_pairs={{0,32},{32,64},{64,96},{96,0},{1,33},{33,65},{65,97},{97,1},{2,34}... | collective-permute-start | bytes 98312 | tf_op jit(solution)/shard_map/ppermute | solution.py:865
  81.4 4.3 %collective-permute-start.23 = (f32[8,8,128]{2,1,0:T(8,128)S(1)}, f32[8,8,128]{2,1,0:T(8,128)S(1)}, u32[]{:S(2)}, u32[]{:S(2)}) collective-permute-start(f32[8,8,128]{2,1,0:T(8,128)S(1)} %gather_z.3.refs_0_), channel_id=1, source_target_pairs={{0,64},{32,96},{64,0},{96,32},{1,65},{33,97},{65,1},{97,33},{2,66}... | collective-permute-start | bytes 98312 | tf_op jit(solution)/shard_map/ppermute | solution.py:865
  81.9 4.1 %collective-permute-start.24 = (f32[8,8,128]{2,1,0:T(8,128)S(1)}, f32[8,8,128]{2,1,0:T(8,128)S(1)}, u32[]{:S(2)}, u32[]{:S(2)}) collective-permute-start(f32[8,8,128]{2,1,0:T(8,128)S(1)} %gather_z.3.refs_0_), channel_id=1, source_target_pairs={{0,96},{32,0},{64,32},{96,64},{1,97},{33,1},{65,33},{97,65},{2,98}... | collective-permute-start | bytes 98312 | tf_op jit(solution)/shard_map/ppermute | solution.py:865
  86.0 5.1 %collective-permute-start.25 = (f32[32,8,128]{2,1,0:T(8,128)S(1)}, f32[32,8,128]{2,1,0:T(8,128)S(1)}, u32[]{:S(2)}, u32[]{:S(2)}) collective-permute-start(f32[32,8,128]{2,1,0:T(8,128)S(1)} %gather_x.3.refs_0_.refs_4_), channel_id=1, source_target_pairs={{0,8},{4,12},{8,16},{12,20},{16,24},{20,28},{24,0},{28,4},{1,9},{5... | collective-permute-start | bytes 393224 | tf_op jit(solution)/shard_map/ppermute | solution.py:865
  86.7 6.2 %collective-permute-start.26 = (f32[32,8,128]{2,1,0:T(8,128)S(1)}, f32[32,8,128]{2,1,0:T(8,128)S(1)}, u32[]{:S(2)}, u32[]{:S(2)}) collective-permute-start(f32[32,8,128]{2,1,0:T(8,128)S(1)} %gather_x.3.refs_0_.refs_4_), channel_id=1, source_target_pairs={{0,16},{4,20},{8,24},{12,28},{16,0},{20,4},{24,8},{28,12},{1,17},{... | collective-permute-start | bytes 393224 | tf_op jit(solution)/shard_map/ppermute | solution.py:865
  89.2 3.9 %collective-permute-start.27 = (f32[32,8,128]{2,1,0:T(8,128)S(1)}, f32[32,8,128]{2,1,0:T(8,128)S(1)}, u32[]{:S(2)}, u32[]{:S(2)}) collective-permute-start(f32[32,8,128]{2,1,0:T(8,128)S(1)} %gather_x.3.refs_0_.refs_4_), channel_id=1, source_target_pairs={{0,24},{4,28},{8,0},{12,4},{16,8},{20,12},{24,16},{28,20},{1,25},{... | collective-permute-start | bytes 393224 | tf_op jit(solution)/shard_map/ppermute | solution.py:865
  93.1 8.7 %collective-permute-start.28 = (f32[4,32,8,128]{3,2,1,0:T(8,128)S(1)}, f32[4,32,8,128]{3,2,1,0:T(8,128)S(1)}, u32[]{:S(2)}, u32[]{:S(2)}) collective-permute-start(f32[4,32,8,128]{3,2,1,0:T(8,128)S(1)} %stack_y.3.same), channel_id=1, source_target_pairs={{0,4},{4,0},{8,12},{12,8},{16,20},{20,16},{24,28},{28,24},{1,5},{5... | collective-permute-start | bytes 1572872 | tf_op jit(solution)/shard_map/ppermute | solution.py:886
